TPU v7x, 512 devices: a whole 4x4x16 slice. The times are simulated.
512 devices in a mesh: dp: 16 (over x_hi, y, core), tensor: 32 (over z, x_lo).
Axes of the slice: x: 4 (x_hi: 2, x_lo: 2; x = x_hi * 2 + x_lo), y: 4, z: 16, core: 2. Of those that a mesh axis runs over, the one named last changes fastest.
Arguments:
- features: bfloat16 [8192, 16384], P('tensor', 'dp'), may hold values from -6 to 6
- up_blocks: bfloat16 [64, 128, 512], P('tensor', 'dp'), may hold values from -0.5 to 0.5
- down_blocks: bfloat16 [64, 512, 128], P('tensor', 'dp'), may hold values from -0.25 to 0.25
- out_cotangent: bfloat16 [8192, 16384], P('tensor', 'dp'), may hold values from -6 to 6
Outputs:
- mixed: bfloat16 [8192, 16384], P('tensor', 'dp')
- feature_grad: bfloat16 [8192, 16384], P('tensor', 'dp')
- up_grad: float32 [64, 128, 512], P('tensor', 'dp')
- down_grad: float32 [64, 512, 128], P('tensor', 'dp')
All inputs are finite; a program needn't handle non-finite values.
Results may differ from a plain program's by a relative error of at most 0.023.
Values may be sent and summed in bfloat16 or wider, within the bound.
No kernel may reach another device: no remote copies, remote signals or barrier semaphores. Data moves between devices by JAX's collectives and lax.ppermute only.
A program may use at most 64 MiB of HBM per device.

v0:
```python
import jax
import jax.numpy as jnp
from jax import lax
from jax.sharding import PartitionSpec as P

NB = 64
BIN = 128
BOUT = 512
J_UP = 8
J_DN = 2


def gelu_value(v):
    return 0.5 * v * (1.0 + lax.erf(v * 0.7071067811865476))


def gelu_slope(v):
    return (
        0.5 * (1.0 + lax.erf(v * 0.7071067811865476))
        + v * jnp.exp(-0.5 * v * v) * 0.3989422804014327
    )


def per_device(features, up_blocks, down_blocks, out_cotangent):
    local_blocks = up_blocks.shape[0]
    tok_local = features.shape[1]
    dp_count = lax.axis_size("dp")
    x_local = features.reshape(local_blocks, BIN, tok_local)
    down_whole = lax.all_gather(down_blocks, "dp", axis=1, tiled=True)
    down_four = down_whole.reshape(local_blocks, BOUT, NB, J_DN)
    piece = lax.all_gather(up_blocks, "dp", axis=1, tiled=True)
    rows_now = piece.shape[1]
    x_rows = x_local
    pre_sum = jnp.einsum(
        "bkgj,bkt->gbjt",
        piece.reshape(local_blocks, rows_now, NB, J_UP),
        x_rows,
        preferred_element_type=jnp.float32,
    )
    pre = pre_sum.astype(jnp.bfloat16)
    received = lax.all_to_all(pre, "tensor", split_axis=0, concat_axis=1, tiled=True)
    items = received.shape[3]
    permuted = received.reshape(local_blocks, BOUT, items)
    hidden_act = gelu_value(permuted.astype(jnp.float32)).astype(jnp.bfloat16)
    blockout = jnp.einsum(
        "gmt,gmbj->bgjt", hidden_act, down_four, preferred_element_type=jnp.float32
    ).astype(jnp.bfloat16)
    returned = lax.all_to_all(blockout, "tensor", split_axis=0, concat_axis=1, tiled=True)
    permuted, act, mixed_blocks = (permuted, hidden_act, returned.reshape(local_blocks, BIN, items))
    mixed = mixed_blocks.reshape(local_blocks * BIN, tok_local)
    shaped = out_cotangent.reshape(local_blocks, NB, J_DN, tok_local)
    dblock = lax.all_to_all(shaped, "tensor", split_axis=1, concat_axis=0, tiled=True)
    dact = jnp.einsum("gmbj,bgjt->gmt", down_four, dblock, preferred_element_type=jnp.float32)
    dperm = (dact * gelu_slope(permuted.astype(jnp.float32))).astype(jnp.bfloat16)
    term = jnp.einsum("gmt,bgjt->mgbj", act, dblock, preferred_element_type=jnp.float32)
    down_share = lax.psum_scatter(
        term.reshape(BOUT // dp_count * lax.axis_size("dp"), local_blocks, BIN).astype(
            jnp.bfloat16
        ),
        "dp",
        scatter_dimension=0,
        tiled=True,
    ).astype(jnp.float32)
    down_grad = down_share.transpose(1, 0, 2)
    dpre = lax.all_to_all(
        dperm.reshape(local_blocks, NB, J_UP, tok_local),
        "tensor",
        split_axis=1,
        concat_axis=0,
        tiled=True,
    )
    x_rows = x_local
    term = jnp.einsum("bkt,gbjt->kbgj", x_rows, dpre, preferred_element_type=jnp.float32)
    up_share = lax.psum_scatter(
        term.reshape(BIN // dp_count * lax.axis_size("dp"), local_blocks, BOUT).astype(
            jnp.bfloat16
        ),
        "dp",
        scatter_dimension=0,
        tiled=True,
    ).astype(jnp.float32)
    up_grad = up_share.transpose(1, 0, 2)
    piece = lax.all_gather(up_blocks, "dp", axis=1, tiled=True)
    rows_now = piece.shape[1]
    fgrad = jnp.einsum(
        "bkgj,gbjt->bkt",
        piece.reshape(local_blocks, rows_now, NB, J_UP),
        dpre,
        preferred_element_type=jnp.float32,
    ).astype(jnp.bfloat16)
    feature_grad = fgrad.reshape(local_blocks * BIN, tok_local)
    return (mixed, feature_grad, up_grad, down_grad)


def solution(mesh):
    placed = (
        P("tensor", "dp"),
        P("tensor", "dp", None),
        P("tensor", "dp", None),
        P("tensor", "dp"),
    )
    return jax.shard_map(
        per_device,
        mesh=mesh,
        in_specs=placed,
        out_specs=(
            P("tensor", "dp"),
            P("tensor", "dp"),
            P("tensor", "dp", None),
            P("tensor", "dp", None),
        ),
        check_vma=False,
    )
```

profile of v0, /device:TPU:1, one launch (start us, length us, event | category | flops | bytes accessed | tf_op | source)
XLA Modules:
  0.0 537.9 jit_solution(7308746396229365794)
XLA Ops:
  7.2 1.3 reshape.41
  9.6 17.0 %all-to-all-start.2 = ((bf16[2,64,2,1024]{3,2,0,1:T(2,128)(2,1)}), bf16[2,64,2,1024]{3,2,0,1:T(2,128)(2,1)S(1)}, u32[]{:S(2)}, u32[]{:S(2)}) async-start(bf16[2,64,2,1024]{3,2,0,1:T(2,128)(2,1)} %copy.54), calls=%async_computation.2 | async-start | bytes 1048576 | tf_op jit(solution)/shard_map/all_to_all | solution.py:52
  27.3 25.8 %all_gather.7 = bf16[2,128,512]{2,0,1:T(2,128)(2,1)S(1)} all-gather(bf16[2,8,512]{2,0,1:T(2,128)(2,1)S(1)} %copy.45), channel_id=1, replica_groups=mesh['dp'=16,'tensor'=32] {'dp'}, dimensions={1}, use_global_device_ids=true | all-gather | bytes 278528 | tf_op jit(solution)/shard_map/all_gather | solution.py:31
  54.1 2.5 copy.48
  57.6 11.2 %all-to-all-start = ((bf16[64,2,8,1024]{3,2,1,0:T(8,128)(2,1)}), bf16[64,2,8,1024]{3,2,1,0:T(8,128)(2,1)S(1)}, u32[]{:S(2)}, u32[]{:S(2)}) async-start(bf16[64,2,8,1024]{3,2,1,0:T(8,128)(2,1)} %copy.48), calls=%async_computation | async-start | bytes 4194304 | tf_op jit(solution)/shard_map/all_to_all | solution.py:41
  68.8 22.2 %all_gather.8 = bf16[2,512,128]{2,1,0:T(8,128)(2,1)} all-gather(bf16[2,32,128]{2,1,0:T(8,128)(2,1)S(1)} %copy-done.4), channel_id=1, replica_groups=mesh['dp'=16,'tensor'=32] {'dp'}, dimensions={1}, use_global_device_ids=true | all-gather | bytes 278528 | tf_op jit(solution)/shard_map/all_gather | solution.py:29
  91.0 1.8 copy.50
  95.3 70.4 %all-to-all-done = bf16[64,2,8,1024]{3,2,1,0:T(8,128)(2,1)S(1)} async-done(((bf16[64,2,8,1024]{3,2,1,0:T(8,128)(2,1)}), bf16[64,2,8,1024]{3,2,1,0:T(8,128)(2,1)S(1)}, u32[]{:S(2)}, u32[]{:S(2)}) %all-to-all-start) | async-done | bytes 2097184 | tf_op jit(solution)/shard_map/all_to_all | solution.py:41
  167.3 1.5 fusion.14
  168.9 1.6 copy.58
  170.4 6.7 %all-to-all-start.3 = ((bf16[2,64,8,1024]{3,2,0,1:T(8,128)(2,1)}), bf16[2,64,8,1024]{3,2,0,1:T(8,128)(2,1)}, u32[]{:S(2)}, u32[]{:S(2)}) async-start(bf16[2,64,8,1024]{3,2,0,1:T(8,128)(2,1)} %copy.58), calls=%async_computation.3 | async-start | bytes 4194304 | tf_op jit(solution)/shard_map/all_to_all | solution.py:65
  177.6 1.3 copy.52
  178.9 94.1 %all-to-all-done.3 = bf16[2,64,8,1024]{3,2,0,1:T(8,128)(2,1)} async-done(((bf16[2,64,8,1024]{3,2,0,1:T(8,128)(2,1)}), bf16[2,64,8,1024]{3,2,0,1:T(8,128)(2,1)}, u32[]{:S(2)}, u32[]{:S(2)}) %all-to-all-start.3) | async-done | bytes 2097184 | tf_op jit(solution)/shard_map/all_to_all | solution.py:65
  273.0 7.2 %all-to-all-start.1 = ((bf16[64,2,2,1024]{3,2,1,0:T(2,128)(2,1)}), bf16[64,2,2,1024]{3,2,1,0:T(2,128)(2,1)S(1)}, u32[]{:S(2)}, u32[]{:S(2)}) async-start(bf16[64,2,2,1024]{3,2,1,0:T(2,128)(2,1)} %copy.52), calls=%async_computation.1 | async-start | bytes 1048576 | tf_op jit(solution)/shard_map/all_to_all | solution.py:48
  280.3 1.3 dynamic-slice
  282.2 1.9 fusion.26
  285.7 5.1 copy.84
  290.7 2.7 all_to_all.55
  295.1 1.8 copy.74
  296.9 140.1 %all-reduce.3.cloned.1.call-done = bf16[512,2,128]{2,1,0:T(2,128)(2,1)} async-done(((bf16[512,2,128]{2,1,0:T(2,128)(2,1)}), bf16[512,2,128]{2,1,0:T(2,128)(2,1)}) %all-reduce.3.cloned.1.call-update) | async-done | bytes 262160
  439.5 2.0 reshape_reshape.3
  441.5 1.3 fusion.15
  442.8 86.9 %reduce-scatter.4.cloned.1.call-done = bf16[8,1024]{1,0:T(8,128)(2,1)} async-done(((bf16[128,1024]{1,0:T(8,128)(2,1)}), bf16[8,1024]{1,0:T(8,128)(2,1)}) %reduce-scatter.4.cloned.1.call-update) | async-done | bytes 16400
  529.7 1.3 convert_bitcast_fusion.2
  (32 shorter events, 14.1 us)
Async XLA Ops:
  7.2 46.2 %copy-start = (bf16[256,1024]{1,0:T(8,128)(2,1)S(1)}, bf16[256,1024]{1,0:T(8,128)(2,1)}, u32[]{:S(2)}) copy-start(bf16[256,1024]{1,0:T(8,128)(2,1)} %param.4) | copy-start | bytes 1572868
  9.6 47.9 %all-to-all-start.2 = ((bf16[2,64,2,1024]{3,2,0,1:T(2,128)(2,1)}), bf16[2,64,2,1024]{3,2,0,1:T(2,128)(2,1)S(1)}, u32[]{:S(2)}, u32[]{:S(2)}) async-start(bf16[2,64,2,1024]{3,2,0,1:T(2,128)(2,1)} %copy.54), calls=%async_computation.2 | async-start | bytes 1048576 | tf_op jit(solution)/shard_map/all_to_all | solution.py:52
  54.0 14.7 %copy-start.4 = (bf16[2,32,128]{2,1,0:T(8,128)(2,1)S(1)}, bf16[2,32,128]{2,1,0:T(8,128)(2,1)}, u32[]{:S(2)}) copy-start(bf16[2,32,128]{2,1,0:T(8,128)(2,1)} %param.6) | copy-start | bytes 49156
  57.6 108.1 %all-to-all-start = ((bf16[64,2,8,1024]{3,2,1,0:T(8,128)(2,1)}), bf16[64,2,8,1024]{3,2,1,0:T(8,128)(2,1)S(1)}, u32[]{:S(2)}, u32[]{:S(2)}) async-start(bf16[64,2,8,1024]{3,2,1,0:T(8,128)(2,1)} %copy.48), calls=%async_computation | async-start | bytes 4194304 | tf_op jit(solution)/shard_map/all_to_all | solution.py:41
  95.3 72.0 %copy-start.1 = (bf16[64,2,2,1024]{3,0,2,1:T(8,128)(2,1)}, bf16[64,2,2,1024]{3,0,2,1:T(8,128)(2,1)S(1)}, u32[]{:S(2)}) copy-start(bf16[64,2,2,1024]{3,0,2,1:T(8,128)(2,1)S(1)} %all_to_all.51) | copy-start | bytes 1572868
  166.1 1.2 copy-start.2
  168.9 8.3 %copy-start.3 = (bf16[2,512,128]{1,0,2:T(2,128)(2,1)S(1)}, bf16[2,512,128]{1,0,2:T(2,128)(2,1)}, u32[]{:S(2)}) copy-start(bf16[2,512,128]{1,0,2:T(2,128)(2,1)} %copy.50) | copy-start | bytes 786436
  170.4 102.5 %all-to-all-start.3 = ((bf16[2,64,8,1024]{3,2,0,1:T(8,128)(2,1)}), bf16[2,64,8,1024]{3,2,0,1:T(8,128)(2,1)}, u32[]{:S(2)}, u32[]{:S(2)}) async-start(bf16[2,64,8,1024]{3,2,0,1:T(8,128)(2,1)} %copy.58), calls=%async_computation.3 | async-start | bytes 4194304 | tf_op jit(solution)/shard_map/all_to_all | solution.py:65
  273.0 165.3 %all-to-all-start.1 = ((bf16[64,2,2,1024]{3,2,1,0:T(2,128)(2,1)}), bf16[64,2,2,1024]{3,2,1,0:T(2,128)(2,1)S(1)}, u32[]{:S(2)}, u32[]{:S(2)}) async-start(bf16[64,2,2,1024]{3,2,1,0:T(2,128)(2,1)} %copy.52), calls=%async_computation.1 | async-start | bytes 1048576 | tf_op jit(solution)/shard_map/all_to_all | solution.py:48
  280.2 156.7 %all-reduce.3.cloned.1.call-start = ((), (), s32[]{:S(2)}) async-start(), calls=%async_computation.6 | async-start | bytes 524288
  285.4 244.3 %reduce-scatter.4.cloned.1.call-start = ((), (), s32[]{:S(2)}) async-start(), calls=%async_computation.5 | async-start | bytes 278528
Sparse Core Ops, SparseCore 0:
  285.5 151.3 all-reduce.2
  442.2 87.4 reduce-scatter.3
where the time goes:
time: 539 us; the launch traced here: 538 us
  waiting for transfers between devices  392 us (73%)
  blocking collectives  48 us (9%)
  starting transfers between devices  42.3 us (8%)
  local copies, waits for them, and re-layouts  30.5 us (6%)
  between operations  14.9 us (3%)
  matrix products  6.53 us (1%)
    unnamed x4, waiting for transfers between devices  227 us
    all_to_all x1, waiting for transfers between devices, per_device(): lax.all_to_all(dperm.reshape(local_blocks, NB, J_UP, tok_local), 'tensor'...  94.1 us
    all_to_all x1, waiting for transfers between devices, per_device(): lax.all_to_all(pre, 'tensor', split_axis=0, concat_axis=1, tiled=True)  70.4 us
    all_gather x1, blocking collectives, per_device(): piece = lax.all_gather(up_blocks, 'dp', axis=1, tiled=True)  25.8 us
    all_gather x1, blocking collectives, per_device(): down_whole = lax.all_gather(down_blocks, 'dp', axis=1, tiled=True)  22.2 us
    all_to_all x1, starting transfers between devices, per_device(): lax.all_to_all(shaped, 'tensor', split_axis=1, concat_axis=0, tiled=True)  17 us
    all_to_all x1, starting transfers between devices, per_device(): lax.all_to_all(pre, 'tensor', split_axis=0, concat_axis=1, tiled=True)  11.2 us
  transfers between devices with their start and end apart: 6, of which 5 were waited for; matrix products, arithmetic and copies ran while one was open for 5% of the time, Pallas kernels for 0%

commit v1 on v0

v1 whole, which is shorter than its diff:
```python
import jax
import jax.numpy as jnp
from jax import lax
from jax.sharding import PartitionSpec as P

NB = 64
BIN = 128
BOUT = 512
J_UP = 8
J_DN = 2
F32 = jnp.float32
BF16 = jnp.bfloat16


def gelu_value(v):
    return 0.5 * v * (1.0 + lax.erf(v * 0.7071067811865476))


def gelu_slope(v):
    return (
        0.5 * (1.0 + lax.erf(v * 0.7071067811865476))
        + v * jnp.exp(-0.5 * v * v) * 0.3989422804014327
    )


def exchange(x):
    return lax.all_to_all(x, "tensor", split_axis=0, concat_axis=0, tiled=True)


def gather_rows(up_blocks, down_blocks):
    n = lax.axis_size("dp")
    nb, ru, wu = up_blocks.shape
    rd, wd = down_blocks.shape[1:]
    both = jnp.concatenate([up_blocks, down_blocks.reshape(nb, ru, wu)], axis=0)
    sent = jnp.broadcast_to(both, (n,) + both.shape)
    got = lax.all_to_all(sent, "dp", split_axis=0, concat_axis=0, tiled=True)
    up = got[:, :nb].transpose(1, 0, 2, 3).reshape(nb, n * ru, wu)
    down = got[:, nb:].reshape(n, nb, rd, wd).transpose(1, 0, 2, 3).reshape(nb, n * rd, wd)
    return up, down


def sum_rows(up_term, down_term):
    n = lax.axis_size("dp")
    nb, hu, wu = up_term.shape
    hd, wd = down_term.shape[1:]
    ru, rd = hu // n, hd // n
    u = up_term.astype(BF16).reshape(nb, n, ru, wu).transpose(1, 0, 2, 3)
    d = down_term.astype(BF16).reshape(nb, n, ru, wu).transpose(1, 0, 2, 3)
    got = lax.all_to_all(
        jnp.concatenate([u, d], axis=1), "dp", split_axis=0, concat_axis=0, tiled=True
    )
    s = jnp.sum(got.astype(F32), axis=0)
    return s[:nb], s[nb:].reshape(nb, rd, wd)


def per_device(features, up_blocks, down_blocks, out_cotangent):
    nb = up_blocks.shape[0]
    t = features.shape[1]
    n = NB // nb
    up, down = gather_rows(up_blocks, down_blocks)
    x = features.reshape(nb, BIN, t)
    pre = jnp.einsum(
        "bkgj,bkt->gbjt", up.reshape(nb, BIN, NB, J_UP), x, preferred_element_type=F32
    ).astype(BF16)
    permuted = exchange(pre.reshape(n, nb, nb, J_UP, t))
    permuted = permuted.transpose(1, 0, 2, 3, 4).reshape(nb, BOUT, t)
    cot = out_cotangent.reshape(nb, n, nb, J_DN, t).transpose(1, 2, 0, 3, 4)
    dblock = exchange(cot).transpose(1, 0, 2, 3, 4).reshape(nb, BIN, t)
    pf = permuted.astype(F32)
    act = gelu_value(pf).astype(BF16)
    dact = jnp.einsum("gmc,gct->gmt", down, dblock, preferred_element_type=F32)
    dperm = (dact * gelu_slope(pf)).astype(BF16)
    dpre = exchange(dperm.reshape(nb, n, nb, J_UP, t).transpose(1, 2, 0, 3, 4))
    dpre = dpre.transpose(1, 0, 2, 3, 4).reshape(nb, BOUT, t)
    blockout = jnp.einsum("gmc,gmt->gct", down, act, preferred_element_type=F32).astype(BF16)
    mixed = exchange(blockout.reshape(nb, n, nb, J_DN, t).transpose(1, 2, 0, 3, 4))
    mixed = mixed.transpose(1, 0, 2, 3, 4).reshape(nb * BIN, t)
    down_term = jnp.einsum("gmt,gct->gmc", act, dblock, preferred_element_type=F32)
    up_term = jnp.einsum("bkt,bnt->bkn", x, dpre, preferred_element_type=F32)
    fgrad = jnp.einsum("bkn,bnt->bkt", up, dpre, preferred_element_type=F32).astype(BF16)
    up_grad, down_grad = sum_rows(up_term, down_term)
    return mixed, fgrad.reshape(nb * BIN, t), up_grad, down_grad


def solution(mesh):
    flat = P("tensor", "dp")
    rows = P("tensor", "dp", None)
    return jax.shard_map(
        per_device,
        mesh=mesh,
        in_specs=(flat, rows, rows, flat),
        out_specs=(flat, flat, rows, rows),
        check_vma=False,
    )
```

time: 539 us -> 339 us (0.63)
  waiting for transfers between devices: 392 us -> 236 us
  blocking collectives: 48 us -> 0 us
  between operations: 14.9 us -> 0.82 us
  starting transfers between devices: 42.3 us -> 51.9 us
  local copies, waits for them, and re-layouts: 30.5 us -> 36.6 us
    unnamed x4 -> x0, waiting for transfers between devices: 227 us -> none
    all_to_all x4 -> x6, waiting for transfers between devices: 165 us -> 236 us  [the longest x4 221 us: exchange(): return lax.all_to_all(x, 'tensor', split_axis=0, concat_axis=0, tiled=True)]
    all_gather x2 -> x0, blocking collectives: 48 us -> none  [the longest x1 25.8 us: per_device(): piece = lax.all_gather(up_blocks, 'dp', axis=1, tiled=True)]
    reshape x3 -> x11, local copies, waits for them, and re-layouts: 4.02 us -> 16 us  [the longest x2 2.6 us: per_device(): blockout.reshape(nb, n, nb, J_DN, t).transpose(1, 2, 0, 3, 4)]
    all_to_all x5 -> x0, local copies, waits for them, and re-layouts: 11.4 us -> none  [the longest x2 7.82 us: per_device(): lax.all_to_all(dperm.reshape(local_blocks, NB, J_UP, tok_local), 'tensor'...]
    all_to_all x4 -> x6, starting transfers between devices: 42.1 us -> 51.9 us  [the longest x4 34.1 us: exchange(): return lax.all_to_all(x, 'tensor', split_axis=0, concat_axis=0, tiled=True)]
    another operation x1 -> x2, local copies, waits for them, and re-layouts: 2.03 us -> 10.5 us  [per_device(): up.reshape(nb, BIN, NB, J_UP)]
    transpose x0 -> x7, local copies, waits for them, and re-layouts: none -> 8.01 us  [the longest x1 1.87 us: per_device(): dpre = dpre.transpose(1, 0, 2, 3, 4).reshape(nb, BOUT, t)]
  transfers between devices with their start and end apart: 6 -> 6, of which waited for: 5 -> 6; matrix products, arithmetic and copies ran while one was open for 5% -> 12% of each run, Pallas kernels for 0% -> 0%
where the time goes in v1:
time: 339 us; the launch traced here: 338 us
  waiting for transfers between devices  236 us (70%)
  starting transfers between devices  51.9 us (15%)
  local copies, waits for them, and re-layouts  36.6 us (11%)
  matrix products  7.99 us (2%)
  other arithmetic  4.35 us (1%)
    all_to_all x4, waiting for transfers between devices, exchange(): return lax.all_to_all(x, 'tensor', split_axis=0, concat_axis=0, tiled=True)  221 us
    all_to_all x4, starting transfers between devices, exchange(): return lax.all_to_all(x, 'tensor', split_axis=0, concat_axis=0, tiled=True)  34.1 us
    another operation x2, local copies, waits for them, and re-layouts, per_device(): up.reshape(nb, BIN, NB, J_UP)  10.5 us
    all_to_all x1, starting transfers between devices, gather_rows(): got = lax.all_to_all(sent, 'dp', split_axis=0, concat_axis=0, tiled=True)  10.2 us
    all_to_all x1, waiting for transfers between devices, gather_rows(): got = lax.all_to_all(sent, 'dp', split_axis=0, concat_axis=0, tiled=True)  8.78 us
    all_to_all x1, starting transfers between devices, sum_rows(): lax.all_to_all(jnp.concatenate([u, d], axis=1), 'dp', split_axis=0, conca...  7.47 us
    all_to_all x1, waiting for transfers between devices, sum_rows(): lax.all_to_all(jnp.concatenate([u, d], axis=1), 'dp', split_axis=0, conca...  6.97 us
  transfers between devices with their start and end apart: 6, of which 6 were waited for; matrix products, arithmetic and copies ran while one was open for 12% of the time, Pallas kernels for 0%

profile of v1, /device:TPU:1, one launch (start us, length us, event | category | flops | bytes accessed | tf_op | source)
XLA Modules:
  0.0 338.0 jit_solution(3798027171147751376)
XLA Ops:
  3.0 10.2 %all-to-all-start = ((bf16[16,4,8,512]{3,2,1,0:T(8,128)(2,1)}), bf16[16,4,8,512]{3,2,1,0:T(8,128)(2,1)S(1)}, u32[]{:S(2)}, u32[]{:S(2)}) async-start(bf16[16,4,8,512]{3,2,1,0:T(8,128)(2,1)} %broadcast_in_dim.3), calls=%async_computation | async-start | bytes 1048576 | tf_op jit(solution)/shard_map/all_to_all | solution.py:36
  15.9 8.8 %all-to-all-done = bf16[16,4,8,512]{3,2,1,0:T(8,128)(2,1)S(1)} async-done(((bf16[16,4,8,512]{3,2,1,0:T(8,128)(2,1)}), bf16[16,4,8,512]{3,2,1,0:T(8,128)(2,1)S(1)}, u32[]{:S(2)}, u32[]{:S(2)}) %all-to-all-start) | async-done | bytes 524320 | tf_op jit(solution)/shard_map/all_to_all | solution.py:36
  24.6 13.4 %all-to-all-start.3 = ((bf16[32,2,2,2,1024]{4,3,2,1,0:T(2,128)(2,1)}), bf16[32,2,2,2,1024]{4,3,2,1,0:T(2,128)(2,1)S(1)}, u32[]{:S(2)}, u32[]{:S(2)}) async-start(bf16[32,2,2,2,1024]{4,3,2,1,0:T(2,128)(2,1)} %copy.45), calls=%async_computation.3 | async-start | bytes 1048576 | tf_op jit(solution)/shard_map/all_to_all | solution.py:27
  38.7 4.7 %copy.53 = bf16[2,16,8,512]{2,1,3,0:T(8,128)(2,1)} copy(bf16[2,16,8,512]{3,2,0,1:T(8,128)(2,1)S(1)} %get-tuple-element.6) | data formatting | bytes 524288 | tf_op jit(solution)/shard_map/reshape;reshape | solution.py:63
  43.5 5.8 %reshape.77 = bf16[2,128,64,8]{1,3,2,0:T(8,128)(2,1)S(1)} reshape(bf16[2,16,8,512]{2,1,3,0:T(8,128)(2,1)} %copy.53) | data formatting | bytes 524288 | tf_op jit(solution)/shard_map/reshape;reshape | solution.py:63
  50.0 1.5 copy.39
  51.5 16.9 %all-to-all-done.3 = bf16[32,2,2,2,1024]{4,3,2,1,0:T(2,128)(2,1)S(1)} async-done(((bf16[32,2,2,2,1024]{4,3,2,1,0:T(2,128)(2,1)}), bf16[32,2,2,2,1024]{4,3,2,1,0:T(2,128)(2,1)S(1)}, u32[]{:S(2)}, u32[]{:S(2)}) %all-to-all-start.3) | async-done | bytes 524320 | tf_op jit(solution)/shard_map/all_to_all | solution.py:27
  68.4 5.5 %all-to-all-start.1 = ((bf16[32,2,2,8,1024]{4,3,1,2,0:T(8,128)(2,1)}), bf16[32,2,2,8,1024]{4,3,1,2,0:T(8,128)(2,1)S(1)}, u32[]{:S(2)}, u32[]{:S(2)}) async-start(bf16[32,2,2,8,1024]{4,3,1,2,0:T(8,128)(2,1)} %copy.39), calls=%async_computation.1 | async-start | bytes 4194304 | tf_op jit(solution)/shard_map/all_to_all | solution.py:27
  73.9 1.8 reshape.60
  75.7 1.7 copy.36
  78.6 2.0 reshape.68
  80.6 89.2 %all-to-all-done.1 = bf16[32,2,2,8,1024]{4,3,1,2,0:T(8,128)(2,1)S(1)} async-done(((bf16[32,2,2,8,1024]{4,3,1,2,0:T(8,128)(2,1)}), bf16[32,2,2,8,1024]{4,3,1,2,0:T(8,128)(2,1)S(1)}, u32[]{:S(2)}, u32[]{:S(2)}) %all-to-all-start.1) | async-done | bytes 2097184 | tf_op jit(solution)/shard_map/all_to_all | solution.py:27
  172.1 1.5 fusion.5
  173.6 1.5 copy.63
  175.1 7.5 %all-to-all-start.4 = ((bf16[32,2,2,8,1024]{4,3,1,2,0:T(8,128)(2,1)}), bf16[32,2,2,8,1024]{4,3,1,2,0:T(8,128)(2,1)}, u32[]{:S(2)}, u32[]{:S(2)}) async-start(bf16[32,2,2,8,1024]{4,3,1,2,0:T(8,128)(2,1)} %bitcast.72), calls=%async_computation.4 | async-start | bytes 4194304 | tf_op jit(solution)/shard_map/all_to_all | solution.py:27
  186.5 91.9 %all-to-all-done.4 = bf16[32,2,2,8,1024]{4,3,1,2,0:T(8,128)(2,1)} async-done(((bf16[32,2,2,8,1024]{4,3,1,2,0:T(8,128)(2,1)}), bf16[32,2,2,8,1024]{4,3,1,2,0:T(8,128)(2,1)}, u32[]{:S(2)}, u32[]{:S(2)}) %all-to-all-start.4) | async-done | bytes 2097184 | tf_op jit(solution)/shard_map/all_to_all | solution.py:27
  278.4 7.8 %all-to-all-start.2 = ((bf16[32,2,2,2,1024]{4,3,1,2,0:T(2,128)(2,1)}), bf16[32,2,2,2,1024]{4,3,1,2,0:T(2,128)(2,1)S(1)}, u32[]{:S(2)}, u32[]{:S(2)}) async-start(bf16[32,2,2,2,1024]{4,3,1,2,0:T(2,128)(2,1)} %bitcast.77), calls=%async_computation.2 | async-start | bytes 1048576 | tf_op jit(solution)/shard_map/all_to_all | solution.py:27
  286.2 2.5 convolution_convert_fusion.3
  288.7 1.8 reshape.73
  290.5 1.9 copy.48
  294.1 22.6 %all-to-all-done.2 = bf16[32,2,2,2,1024]{4,3,1,2,0:T(2,128)(2,1)S(1)} async-done(((bf16[32,2,2,2,1024]{4,3,1,2,0:T(2,128)(2,1)}), bf16[32,2,2,2,1024]{4,3,1,2,0:T(2,128)(2,1)S(1)}, u32[]{:S(2)}, u32[]{:S(2)}) %all-to-all-start.2) | async-done | bytes 524320 | tf_op jit(solution)/shard_map/all_to_all | solution.py:27
  316.7 7.5 %all-to-all-start.5 = ((bf16[16,4,8,512]{3,2,1,0:T(8,128)(2,1)}), bf16[16,4,8,512]{3,2,1,0:T(8,128)(2,1)}, u32[]{:S(2)}, u32[]{:S(2)}) async-start(bf16[16,4,8,512]{3,2,1,0:T(8,128)(2,1)} %pad_maximum_fusion), calls=%async_computation.5 | async-start | bytes 1048576 | tf_op jit(solution)/shard_map/all_to_all | solution.py:49
  325.4 2.0 reshape.65
  328.6 7.0 %all-to-all-done.5 = bf16[16,4,8,512]{3,2,1,0:T(8,128)(2,1)} async-done(((bf16[16,4,8,512]{3,2,1,0:T(8,128)(2,1)}), bf16[16,4,8,512]{3,2,1,0:T(8,128)(2,1)}, u32[]{:S(2)}, u32[]{:S(2)}) %all-to-all-start.5) | async-done | bytes 524320 | tf_op jit(solution)/shard_map/all_to_all | solution.py:49
  (30 shorter events, 20.2 us)
Async XLA Ops:
  0.6 48.7 %copy-start = (bf16[256,1024]{1,0:T(8,128)(2,1)S(1)}, bf16[256,1024]{1,0:T(8,128)(2,1)}, u32[]{:S(2)}) copy-start(bf16[256,1024]{1,0:T(8,128)(2,1)} %param.4) | copy-start | bytes 1572868
  3.0 21.6 %all-to-all-start = ((bf16[16,4,8,512]{3,2,1,0:T(8,128)(2,1)}), bf16[16,4,8,512]{3,2,1,0:T(8,128)(2,1)S(1)}, u32[]{:S(2)}, u32[]{:S(2)}) async-start(bf16[16,4,8,512]{3,2,1,0:T(8,128)(2,1)} %broadcast_in_dim.3), calls=%async_computation | async-start | bytes 1048576 | tf_op jit(solution)/shard_map/all_to_all | solution.py:36
  24.6 43.8 %all-to-all-start.3 = ((bf16[32,2,2,2,1024]{4,3,2,1,0:T(2,128)(2,1)}), bf16[32,2,2,2,1024]{4,3,2,1,0:T(2,128)(2,1)S(1)}, u32[]{:S(2)}, u32[]{:S(2)}) async-start(bf16[32,2,2,2,1024]{4,3,2,1,0:T(2,128)(2,1)} %copy.45), calls=%async_computation.3 | async-start | bytes 1048576 | tf_op jit(solution)/shard_map/all_to_all | solution.py:27
  68.4 101.4 %all-to-all-start.1 = ((bf16[32,2,2,8,1024]{4,3,1,2,0:T(8,128)(2,1)}), bf16[32,2,2,8,1024]{4,3,1,2,0:T(8,128)(2,1)S(1)}, u32[]{:S(2)}, u32[]{:S(2)}) async-start(bf16[32,2,2,8,1024]{4,3,1,2,0:T(8,128)(2,1)} %copy.39), calls=%async_computation.1 | async-start | bytes 4194304 | tf_op jit(solution)/shard_map/all_to_all | solution.py:27
  170.9 1.2 copy-start.2
  170.9 1.2 copy-start.3
  175.1 103.3 %all-to-all-start.4 = ((bf16[32,2,2,8,1024]{4,3,1,2,0:T(8,128)(2,1)}), bf16[32,2,2,8,1024]{4,3,1,2,0:T(8,128)(2,1)}, u32[]{:S(2)}, u32[]{:S(2)}) async-start(bf16[32,2,2,8,1024]{4,3,1,2,0:T(8,128)(2,1)} %bitcast.72), calls=%async_computation.4 | async-start | bytes 4194304 | tf_op jit(solution)/shard_map/all_to_all | solution.py:27
  278.4 38.3 %all-to-all-start.2 = ((bf16[32,2,2,2,1024]{4,3,1,2,0:T(2,128)(2,1)}), bf16[32,2,2,2,1024]{4,3,1,2,0:T(2,128)(2,1)S(1)}, u32[]{:S(2)}, u32[]{:S(2)}) async-start(bf16[32,2,2,2,1024]{4,3,1,2,0:T(2,128)(2,1)} %bitcast.77), calls=%async_computation.2 | async-start | bytes 1048576 | tf_op jit(solution)/shard_map/all_to_all | solution.py:27
  290.5 2.7 copy-start.1
  316.7 18.9 %all-to-all-start.5 = ((bf16[16,4,8,512]{3,2,1,0:T(8,128)(2,1)}), bf16[16,4,8,512]{3,2,1,0:T(8,128)(2,1)}, u32[]{:S(2)}, u32[]{:S(2)}) async-start(bf16[16,4,8,512]{3,2,1,0:T(8,128)(2,1)} %pad_maximum_fusion), calls=%async_computation.5 | async-start | bytes 1048576 | tf_op jit(solution)/shard_map/all_to_all | solution.py:49

commit v2 on v1

--- a/solution.py
+++ b/solution.py
@@ -23,8 +23,54 @@
     )
 
 
+DEVICES = ("dp", "tensor")
+
+
+class Plan:
+    def __init__(self):
+        def index(xh, y, c, z, xl):
+            return (((xh * 4 + y) * 2 + c) * 16 + z) * 2 + xl
+
+        shuffle, mirror, weights, place = [], [], [], {}
+        for z in range(16):
+            for t in range(16):
+                xh, y, c = t >> 3, (t >> 1) & 3, t & 1
+                label = 8 * c + 4 * xh + y
+                moved = (label + z) % 16
+                c2, xh2, y2 = moved >> 3, (moved >> 2) & 1, moved & 3
+                for xl in range(2):
+                    xl2 = xl if xh2 == xh else 1 - xl
+                    mid = index(xh2, y2, c2, z, xl2)
+                    end = index(xh2, y2, c2, label, xl2)
+                    shuffle.append((index(xh, y, c, z, xl), mid))
+                    mirror.append((mid, end))
+                    weights.append((index(xh2, y2, c2, z, xl), end))
+                    place[label, 2 * z + xl] = end
+        self.shuffle, self.mirror, self.weights = shuffle, mirror, weights
+        self.layers = [[place[t, k] for k in range(32)] for t in range(16)]
+
+
+PLAN = Plan()
+
+
+def back(pairs):
+    return [(b, a) for a, b in pairs]
+
+
 def exchange(x):
-    return lax.all_to_all(x, "tensor", split_axis=0, concat_axis=0, tiled=True)
+    return lax.all_to_all(
+        x, DEVICES, split_axis=0, concat_axis=0, tiled=True, axis_index_groups=PLAN.layers
+    )
+
+
+def to_work(x):
+    return lax.ppermute(lax.ppermute(x, DEVICES, PLAN.shuffle), DEVICES, PLAN.mirror)
+
+
+def to_store(x):
+    return lax.ppermute(
+        lax.ppermute(x, DEVICES, back(PLAN.mirror)), DEVICES, back(PLAN.shuffle)
+    )
 
 
 def gather_rows(up_blocks, down_blocks):
@@ -34,8 +80,10 @@
     both = jnp.concatenate([up_blocks, down_blocks.reshape(nb, ru, wu)], axis=0)
     sent = jnp.broadcast_to(both, (n,) + both.shape)
     got = lax.all_to_all(sent, "dp", split_axis=0, concat_axis=0, tiled=True)
-    up = got[:, :nb].transpose(1, 0, 2, 3).reshape(nb, n * ru, wu)
-    down = got[:, nb:].reshape(n, nb, rd, wd).transpose(1, 0, 2, 3).reshape(nb, n * rd, wd)
+    up = lax.ppermute(got[:, :nb], DEVICES, PLAN.weights)
+    down = lax.ppermute(got[:, nb:], DEVICES, PLAN.weights)
+    up = up.transpose(1, 0, 2, 3).reshape(nb, n * ru, wu)
+    down = down.reshape(n, nb, rd, wd).transpose(1, 0, 2, 3).reshape(nb, n * rd, wd)
     return up, down
 
 
@@ -46,6 +94,8 @@
     ru, rd = hu // n, hd // n
     u = up_term.astype(BF16).reshape(nb, n, ru, wu).transpose(1, 0, 2, 3)
     d = down_term.astype(BF16).reshape(nb, n, ru, wu).transpose(1, 0, 2, 3)
+    u = lax.ppermute(u, DEVICES, back(PLAN.weights))
+    d = lax.ppermute(d, DEVICES, back(PLAN.weights))
     got = lax.all_to_all(
         jnp.concatenate([u, d], axis=1), "dp", split_axis=0, concat_axis=0, tiled=True
     )
@@ -58,7 +108,8 @@
     t = features.shape[1]
     n = NB // nb
     up, down = gather_rows(up_blocks, down_blocks)
-    x = features.reshape(nb, BIN, t)
+    x = to_work(features).reshape(nb, BIN, t)
+    out_cotangent = to_work(out_cotangent)
     pre = jnp.einsum(
         "bkgj,bkt->gbjt", up.reshape(nb, BIN, NB, J_UP), x, preferred_element_type=F32
     ).astype(BF16)
@@ -79,7 +130,7 @@
     up_term = jnp.einsum("bkt,bnt->bkn", x, dpre, preferred_element_type=F32)
     fgrad = jnp.einsum("bkn,bnt->bkt", up, dpre, preferred_element_type=F32).astype(BF16)
     up_grad, down_grad = sum_rows(up_term, down_term)
-    return mixed, fgrad.reshape(nb * BIN, t), up_grad, down_grad
+    return to_store(mixed), to_store(fgrad.reshape(nb * BIN, t)), up_grad, down_grad
 
 
 def solution(mesh):

time: 339 us -> 314 us (0.926)
  the two profiles are of different devices: /device:TPU:1 before, /device:TPU:89 now
where the time goes in v2:
time: 314 us; the launch traced here: 313 us
  starting transfers between devices  206 us (66%)
  waiting for transfers between devices  62.9 us (20%)
  local copies, waits for them, and re-layouts  27.5 us (9%)
  matrix products  9.03 us (3%)
  other arithmetic  6.29 us (2%)
    all_to_all x4, starting transfers between devices, exchange(): lax.all_to_all(x, DEVICES, split_axis=0, concat_axis=0, tiled=True, axis_...  74.3 us
    all_to_all x1, starting transfers between devices, sum_rows(): lax.all_to_all(jnp.concatenate([u, d], axis=1), 'dp', split_axis=0, conca...  45.5 us
    ppermute x2, starting transfers between devices, to_work(): lax.ppermute(lax.ppermute(x, DEVICES, PLAN.shuffle), DEVICES, PLAN.mirror)  30.4 us
    all_to_all x4, waiting for transfers between devices, exchange(): lax.all_to_all(x, DEVICES, split_axis=0, concat_axis=0, tiled=True, axis_...  27.6 us
    ppermute x2, starting transfers between devices, to_store(): lax.ppermute(x, DEVICES, back(PLAN.mirror))  14.4 us
    ppermute x1, waiting for transfers between devices, gather_rows(): down = lax.ppermute(got[:, nb:], DEVICES, PLAN.weights)  14.3 us
    another operation x2, local copies, waits for them, and re-layouts, per_device(): up.reshape(nb, BIN, NB, J_UP)  10.5 us
    ppermute x2, waiting for transfers between devices, to_store(): lax.ppermute(lax.ppermute(x, DEVICES, back(PLAN.mirror)), DEVICES, back(P...  10 us
  transfers between devices with their start and end apart: 18, of which 9 were waited for; matrix products, arithmetic and copies ran while one was open for 11% of the time, Pallas kernels for 0%

profile of v2, /device:TPU:89, one launch (start us, length us, event | category | flops | bytes accessed | tf_op | source)
XLA Modules:
  0.0 312.7 jit_solution(17151244271173341365)
XLA Ops:
  0.6 5.1 %collective-permute-start.6 = (bf16[256,1024]{1,0:T(8,128)(2,1)}, bf16[256,1024]{1,0:T(8,128)(2,1)S(1)}, u32[]{:S(2)}, u32[]{:S(2)}) collective-permute-start(bf16[256,1024]{1,0:T(8,128)(2,1)} %param.7), channel_id=1, source_target_pairs={{0,0},{1,1},{32,32},{33,33},{64,64},{65,65},{96,96},{97,97},{128,1... | collective-permute-start | bytes 1572872 | tf_op jit(solution)/shard_map/ppermute | solution.py:67
  5.7 3.9 %collective-permute-start.2 = (bf16[256,1024]{1,0:T(8,128)(2,1)}, bf16[256,1024]{1,0:T(8,128)(2,1)S(1)}, u32[]{:S(2)}, u32[]{:S(2)}) collective-permute-start(bf16[256,1024]{1,0:T(8,128)(2,1)} %param.4), channel_id=1, source_target_pairs={{0,0},{1,1},{32,32},{33,33},{64,64},{65,65},{96,96},{97,97},{128,1... | collective-permute-start | bytes 1572872 | tf_op jit(solution)/shard_map/ppermute | solution.py:67
  11.9 5.6 %all-to-all-start = ((bf16[16,4,8,512]{3,2,1,0:T(8,128)(2,1)}), bf16[16,4,8,512]{3,2,1,0:T(8,128)(2,1)S(1)}, u32[]{:S(2)}, u32[]{:S(2)}) async-start(bf16[16,4,8,512]{3,2,1,0:T(8,128)(2,1)} %broadcast_in_dim.3), calls=%async_computation | async-start | bytes 1048576 | tf_op jit(solution)/shard_map/all_to_all | solution.py:82
  17.5 18.4 %collective-permute-start.7 = (bf16[256,1024]{1,0:T(8,128)(2,1)S(1)}, bf16[256,1024]{1,0:T(8,128)(2,1)S(1)}, u32[]{:S(2)}, u32[]{:S(2)}) collective-permute-start(bf16[256,1024]{1,0:T(8,128)(2,1)S(1)} %collective-permute-done.6), channel_id=1, source_target_pairs={{0,0},{1,1},{32,48},{33,49},{64,66},{65,67},{96,114},{97,115},{128... | collective-permute-start | bytes 1572872 | tf_op jit(solution)/shard_map/ppermute | solution.py:67
  35.9 12.0 %collective-permute-start.3 = (bf16[256,1024]{1,0:T(8,128)(2,1)S(1)}, bf16[256,1024]{1,0:T(8,128)(2,1)S(1)}, u32[]{:S(2)}, u32[]{:S(2)}) collective-permute-start(bf16[256,1024]{1,0:T(8,128)(2,1)S(1)} %collective-permute-done.2), channel_id=1, source_target_pairs={{0,0},{1,1},{32,48},{33,49},{64,66},{65,67},{96,114},{97,115},{128... | collective-permute-start | bytes 1572872 | tf_op jit(solution)/shard_map/ppermute | solution.py:67
  51.5 41.3 %all-to-all-start.3 = ((bf16[32,2,2,2,1024]{4,3,2,1,0:T(2,128)(2,1)}), bf16[32,2,2,2,1024]{4,3,2,1,0:T(2,128)(2,1)S(1)}, u32[]{:S(2)}, u32[]{:S(2)}) async-start(bf16[32,2,2,2,1024]{4,3,2,1,0:T(2,128)(2,1)} %copy.45), calls=%async_computation.3 | async-start | bytes 1048576 | tf_op jit(solution)/shard_map/all_to_all | solution.py:61
  92.8 4.7 %copy.53 = bf16[2,16,8,512]{2,1,3,0:T(8,128)(2,1)} copy(bf16[2,16,8,512]{3,2,0,1:T(8,128)(2,1)S(1)} %bitcast.83) | data formatting | bytes 524288 | tf_op jit(solution)/shard_map/reshape;reshape | solution.py:114
  97.4 5.8 %reshape.77 = bf16[2,128,64,8]{1,3,2,0:T(8,128)(2,1)S(1)} reshape(bf16[2,16,8,512]{2,1,3,0:T(8,128)(2,1)} %copy.53) | data formatting | bytes 524288 | tf_op jit(solution)/shard_map/reshape;reshape | solution.py:114
  106.7 17.3 %all-to-all-start.1 = ((bf16[32,2,2,8,1024]{4,3,1,2,0:T(8,128)(2,1)}), bf16[32,2,2,8,1024]{4,3,1,2,0:T(8,128)(2,1)S(1)}, u32[]{:S(2)}, u32[]{:S(2)}) async-start(bf16[32,2,2,8,1024]{4,3,1,2,0:T(8,128)(2,1)} %copy.39), calls=%async_computation.1 | async-start | bytes 4194304 | tf_op jit(solution)/shard_map/all_to_all | solution.py:61
  124.0 8.0 %collective-permute-start = (bf16[16,2,8,512]{3,2,1,0:T(8,128)(2,1)S(1)}, bf16[16,2,8,512]{3,2,1,0:T(8,128)(2,1)S(1)}, u32[]{:S(2)}, u32[]{:S(2)}) collective-permute-start(bf16[16,2,8,512]{3,2,1,0:T(8,128)(2,1)S(1)} %get-tuple-element.7), channel_id=1, source_target_pairs={{0,0},{1,1},{32,48},{33,49},{64,66},{65,67},{96,114},{97,115},{128... | collective-permute-start | bytes 786440 | tf_op jit(solution)/shard_map/ppermute | solution.py:84
  132.0 14.3 %collective-permute-done = bf16[16,2,8,512]{3,2,1,0:T(8,128)(2,1)S(1)} collective-permute-done((bf16[16,2,8,512]{3,2,1,0:T(8,128)(2,1)S(1)}, bf16[16,2,8,512]{3,2,1,0:T(8,128)(2,1)S(1)}, u32[]{:S(2)}, u32[]{:S(2)}) %collective-permute-start) | collective-permute-done | bytes 262176 | tf_op jit(solution)/shard_map/ppermute | solution.py:84
  148.5 5.4 %all-to-all-done.1 = bf16[32,2,2,8,1024]{4,3,1,2,0:T(8,128)(2,1)S(1)} async-done(((bf16[32,2,2,8,1024]{4,3,1,2,0:T(8,128)(2,1)}), bf16[32,2,2,8,1024]{4,3,1,2,0:T(8,128)(2,1)S(1)}, u32[]{:S(2)}, u32[]{:S(2)}) %all-to-all-start.1) | async-done | bytes 2097184 | tf_op jit(solution)/shard_map/all_to_all | solution.py:61
  160.4 11.0 %all-to-all-start.2 = ((bf16[32,2,2,2,1024]{4,3,1,2,0:T(2,128)(2,1)}), bf16[32,2,2,2,1024]{4,3,1,2,0:T(2,128)(2,1)S(1)}, u32[]{:S(2)}, u32[]{:S(2)}) async-start(bf16[32,2,2,2,1024]{4,3,1,2,0:T(2,128)(2,1)} %bitcast.69), calls=%async_computation.2 | async-start | bytes 1048576 | tf_op jit(solution)/shard_map/all_to_all | solution.py:61
  171.4 5.1 %fusion.5 = bf16[2,512,1024]{2,1,0:T(8,128)(2,1)S(1)} fusion(f32[2,32,2,8,1024]{4,3,2,1,0:T(8,128)} %copy-done, f32[2,512,1024]{2,1,0:T(8,128)} %get-tuple-element.5, bf16[2,512,128]{2,1,0:T(8,128)(2,1)} %bitcast.84, bf16[2,128,1024]{2,1,0:T(8,128)(2,1)} %reshape.68), kind=kOutput, calls=%fused_computation.6 | convolution fusion | flops 276824064 | bytes 11272192 | tf_op jit(solution)/shard_map/gmc,gct->gmt/dot_general | solution.py:122
  178.1 4.5 %all-to-all-done.2 = bf16[32,2,2,2,1024]{4,3,1,2,0:T(2,128)(2,1)S(1)} async-done(((bf16[32,2,2,2,1024]{4,3,1,2,0:T(2,128)(2,1)}), bf16[32,2,2,2,1024]{4,3,1,2,0:T(2,128)(2,1)S(1)}, u32[]{:S(2)}, u32[]{:S(2)}) %all-to-all-start.2) | async-done | bytes 524320 | tf_op jit(solution)/shard_map/all_to_all | solution.py:61
  182.6 4.7 %all-to-all-start.4 = ((bf16[32,2,2,8,1024]{4,3,1,2,0:T(8,128)(2,1)}), bf16[32,2,2,8,1024]{4,3,1,2,0:T(8,128)(2,1)}, u32[]{:S(2)}, u32[]{:S(2)}) async-start(bf16[32,2,2,8,1024]{4,3,1,2,0:T(8,128)(2,1)} %bitcast.74), calls=%async_computation.4 | async-start | bytes 4194304 | tf_op jit(solution)/shard_map/all_to_all | solution.py:61
  190.0 6.9 %collective-permute-start.11 = (bf16[16,2,8,512]{3,2,1,0:T(8,128)(2,1)S(1)}, bf16[16,2,8,512]{3,2,1,0:T(8,128)(2,1)}, u32[]{:S(2)}, u32[]{:S(2)}) collective-permute-start(bf16[16,2,8,512]{3,2,1,0:T(8,128)(2,1)S(1)} %bitcast.87), channel_id=1, source_target_pairs={{0,0},{1,1},{48,32},{49,33},{66,64},{67,65},{114,96},{115,97},{132... | collective-permute-start | bytes 786440 | tf_op jit(solution)/shard_map/ppermute | solution.py:98
  197.4 6.2 %collective-permute-start.4 = (bf16[256,1024]{1,0:T(8,128)(2,1)S(1)}, bf16[256,1024]{1,0:T(8,128)(2,1)}, u32[]{:S(2)}, u32[]{:S(2)}) collective-permute-start(bf16[256,1024]{1,0:T(8,128)(2,1)S(1)} %reshape.65), channel_id=1, source_target_pairs={{0,0},{1,1},{48,32},{49,33},{66,64},{67,65},{114,96},{115,97},{132... | collective-permute-start | bytes 1572872 | tf_op jit(solution)/shard_map/ppermute | solution.py:72
  203.6 16.6 %all-to-all-done.4 = bf16[32,2,2,8,1024]{4,3,1,2,0:T(8,128)(2,1)} async-done(((bf16[32,2,2,8,1024]{4,3,1,2,0:T(8,128)(2,1)}), bf16[32,2,2,8,1024]{4,3,1,2,0:T(8,128)(2,1)}, u32[]{:S(2)}, u32[]{:S(2)}) %all-to-all-start.4) | async-done | bytes 2097184 | tf_op jit(solution)/shard_map/all_to_all | solution.py:61
  222.8 4.9 %collective-permute-start.10 = (bf16[16,2,8,512]{3,2,1,0:T(8,128)(2,1)S(1)}, bf16[16,2,8,512]{3,2,1,0:T(8,128)(2,1)S(1)}, u32[]{:S(2)}, u32[]{:S(2)}) collective-permute-start(bf16[16,2,8,512]{3,2,1,0:T(8,128)(2,1)S(1)} %bitcast.88), channel_id=1, source_target_pairs={{0,0},{1,1},{48,32},{49,33},{66,64},{67,65},{114,96},{115,97},{132... | collective-permute-start | bytes 786440 | tf_op jit(solution)/shard_map/ppermute | solution.py:97
  228.2 8.2 %collective-permute-start.8 = (bf16[256,1024]{1,0:T(8,128)(2,1)S(1)}, bf16[256,1024]{1,0:T(8,128)(2,1)}, u32[]{:S(2)}, u32[]{:S(2)}) collective-permute-start(bf16[256,1024]{1,0:T(8,128)(2,1)S(1)} %bitcast.86), channel_id=1, source_target_pairs={{0,0},{1,1},{48,32},{49,33},{66,64},{67,65},{114,96},{115,97},{132... | collective-permute-start | bytes 1572872 | tf_op jit(solution)/shard_map/ppermute | solution.py:72
  243.8 45.5 %all-to-all-start.5 = ((bf16[16,4,8,512]{3,2,1,0:T(8,128)(2,1)}), bf16[16,4,8,512]{3,2,1,0:T(8,128)(2,1)S(1)}, u32[]{:S(2)}, u32[]{:S(2)}) async-start(bf16[16,4,8,512]{3,2,1,0:T(8,128)(2,1)} %pad_maximum_fusion), calls=%async_computation.5 | async-start | bytes 1048576 | tf_op jit(solution)/shard_map/all_to_all | solution.py:99
  292.4 7.3 %all-to-all-done.5 = bf16[16,4,8,512]{3,2,1,0:T(8,128)(2,1)S(1)} async-done(((bf16[16,4,8,512]{3,2,1,0:T(8,128)(2,1)}), bf16[16,4,8,512]{3,2,1,0:T(8,128)(2,1)S(1)}, u32[]{:S(2)}, u32[]{:S(2)}) %all-to-all-start.5) | async-done | bytes 524320 | tf_op jit(solution)/shard_map/all_to_all | solution.py:99
  301.1 10.0 %collective-permute-done.9 = bf16[256,1024]{1,0:T(8,128)(2,1)S(1)} collective-permute-done((bf16[256,1024]{1,0:T(8,128)(2,1)}, bf16[256,1024]{1,0:T(8,128)(2,1)S(1)}, u32[]{:S(2)}, u32[]{:S(2)}) %collective-permute-start.9) | collective-permute-done | bytes 524320 | tf_op jit(solution)/shard_map/ppermute | solution.py:71
  (59 shorter events, 38.9 us)
Async XLA Ops:
  0.6 16.9 %collective-permute-start.6 = (bf16[256,1024]{1,0:T(8,128)(2,1)}, bf16[256,1024]{1,0:T(8,128)(2,1)S(1)}, u32[]{:S(2)}, u32[]{:S(2)}) collective-permute-start(bf16[256,1024]{1,0:T(8,128)(2,1)} %param.7), channel_id=1, source_target_pairs={{0,0},{1,1},{32,32},{33,33},{64,64},{65,65},{96,96},{97,97},{128,1... | collective-permute-start | bytes 1572872 | tf_op jit(solution)/shard_map/ppermute | solution.py:67
  5.7 30.2 %collective-permute-start.2 = (bf16[256,1024]{1,0:T(8,128)(2,1)}, bf16[256,1024]{1,0:T(8,128)(2,1)S(1)}, u32[]{:S(2)}, u32[]{:S(2)}) collective-permute-start(bf16[256,1024]{1,0:T(8,128)(2,1)} %param.4), channel_id=1, source_target_pairs={{0,0},{1,1},{32,32},{33,33},{64,64},{65,65},{96,96},{97,97},{128,1... | collective-permute-start | bytes 1572872 | tf_op jit(solution)/shard_map/ppermute | solution.py:67
  11.9 36.0 %all-to-all-start = ((bf16[16,4,8,512]{3,2,1,0:T(8,128)(2,1)}), bf16[16,4,8,512]{3,2,1,0:T(8,128)(2,1)S(1)}, u32[]{:S(2)}, u32[]{:S(2)}) async-start(bf16[16,4,8,512]{3,2,1,0:T(8,128)(2,1)} %broadcast_in_dim.3), calls=%async_computation | async-start | bytes 1048576 | tf_op jit(solution)/shard_map/all_to_all | solution.py:82
  17.5 32.4 %collective-permute-start.7 = (bf16[256,1024]{1,0:T(8,128)(2,1)S(1)}, bf16[256,1024]{1,0:T(8,128)(2,1)S(1)}, u32[]{:S(2)}, u32[]{:S(2)}) collective-permute-start(bf16[256,1024]{1,0:T(8,128)(2,1)S(1)} %collective-permute-done.6), channel_id=1, source_target_pairs={{0,0},{1,1},{32,48},{33,49},{64,66},{65,67},{96,114},{97,115},{128... | collective-permute-start | bytes 1572872 | tf_op jit(solution)/shard_map/ppermute | solution.py:67
  35.9 67.4 %collective-permute-start.3 = (bf16[256,1024]{1,0:T(8,128)(2,1)S(1)}, bf16[256,1024]{1,0:T(8,128)(2,1)S(1)}, u32[]{:S(2)}, u32[]{:S(2)}) collective-permute-start(bf16[256,1024]{1,0:T(8,128)(2,1)S(1)} %collective-permute-done.2), channel_id=1, source_target_pairs={{0,0},{1,1},{32,48},{33,49},{64,66},{65,67},{96,114},{97,115},{128... | collective-permute-start | bytes 1572872 | tf_op jit(solution)/shard_map/ppermute | solution.py:67
  48.0 44.8 %collective-permute-start.1 = (bf16[16,2,8,512]{3,2,1,0:T(8,128)(2,1)S(1)}, bf16[16,2,8,512]{3,2,1,0:T(8,128)(2,1)S(1)}, u32[]{:S(2)}, u32[]{:S(2)}) collective-permute-start(bf16[16,2,8,512]{3,2,1,0:T(8,128)(2,1)S(1)} %get-tuple-element.6), channel_id=1, source_target_pairs={{0,0},{1,1},{32,48},{33,49},{64,66},{65,67},{96,114},{97,115},{128... | collective-permute-start | bytes 786440 | tf_op jit(solution)/shard_map/ppermute | solution.py:83
  51.5 55.2 %all-to-all-start.3 = ((bf16[32,2,2,2,1024]{4,3,2,1,0:T(2,128)(2,1)}), bf16[32,2,2,2,1024]{4,3,2,1,0:T(2,128)(2,1)S(1)}, u32[]{:S(2)}, u32[]{:S(2)}) async-start(bf16[32,2,2,2,1024]{4,3,2,1,0:T(2,128)(2,1)} %copy.45), calls=%async_computation.3 | async-start | bytes 1048576 | tf_op jit(solution)/shard_map/all_to_all | solution.py:61
  103.3 3.4 %copy-start.1 = (bf16[256,1024]{1,0:T(8,128)(2,1)}, bf16[256,1024]{1,0:T(8,128)(2,1)S(1)}, u32[]{:S(2)}) copy-start(bf16[256,1024]{1,0:T(8,128)(2,1)S(1)} %collective-permute-done.3) | copy-start | bytes 1572868
  106.7 47.3 %all-to-all-start.1 = ((bf16[32,2,2,8,1024]{4,3,1,2,0:T(8,128)(2,1)}), bf16[32,2,2,8,1024]{4,3,1,2,0:T(8,128)(2,1)S(1)}, u32[]{:S(2)}, u32[]{:S(2)}) async-start(bf16[32,2,2,8,1024]{4,3,1,2,0:T(8,128)(2,1)} %copy.39), calls=%async_computation.1 | async-start | bytes 4194304 | tf_op jit(solution)/shard_map/all_to_all | solution.py:61
  124.0 22.3 %collective-permute-start = (bf16[16,2,8,512]{3,2,1,0:T(8,128)(2,1)S(1)}, bf16[16,2,8,512]{3,2,1,0:T(8,128)(2,1)S(1)}, u32[]{:S(2)}, u32[]{:S(2)}) collective-permute-start(bf16[16,2,8,512]{3,2,1,0:T(8,128)(2,1)S(1)} %get-tuple-element.7), channel_id=1, source_target_pairs={{0,0},{1,1},{32,48},{33,49},{64,66},{65,67},{96,114},{97,115},{128... | collective-permute-start | bytes 786440 | tf_op jit(solution)/shard_map/ppermute | solution.py:84
  155.1 3.3 %copy-start = (f32[2,32,2,8,1024]{4,3,2,1,0:T(8,128)}, f32[2,32,2,8,1024]{4,3,2,1,0:T(8,128)S(1)}, u32[]{:S(2)}) copy-start(f32[2,32,2,8,1024]{4,3,2,1,0:T(8,128)S(1)} %copy.40) | copy-start | bytes 12582916
  155.1 3.3 %copy-start.3 = (bf16[2,16,32,128]{3,2,1,0:T(8,128)(2,1)S(1)}, bf16[2,16,32,128]{3,2,1,0:T(8,128)(2,1)}, u32[]{:S(2)}) copy-start(bf16[2,16,32,128]{3,2,1,0:T(8,128)(2,1)} %copy.36) | copy-start | bytes 786436
  160.4 22.1 %all-to-all-start.2 = ((bf16[32,2,2,2,1024]{4,3,1,2,0:T(2,128)(2,1)}), bf16[32,2,2,2,1024]{4,3,1,2,0:T(2,128)(2,1)S(1)}, u32[]{:S(2)}, u32[]{:S(2)}) async-start(bf16[32,2,2,2,1024]{4,3,1,2,0:T(2,128)(2,1)} %bitcast.69), calls=%async_computation.2 | async-start | bytes 1048576 | tf_op jit(solution)/shard_map/all_to_all | solution.py:61
  176.6 10.7 %copy-start.4 = (bf16[2,128,1024]{2,1,0:T(8,128)(2,1)S(1)}, bf16[2,128,1024]{2,1,0:T(8,128)(2,1)}, u32[]{:S(2)}) copy-start(bf16[2,128,1024]{2,1,0:T(8,128)(2,1)} %reshape.68) | copy-start | bytes 1572868
  182.6 37.6 %all-to-all-start.4 = ((bf16[32,2,2,8,1024]{4,3,1,2,0:T(8,128)(2,1)}), bf16[32,2,2,8,1024]{4,3,1,2,0:T(8,128)(2,1)}, u32[]{:S(2)}, u32[]{:S(2)}) async-start(bf16[32,2,2,8,1024]{4,3,1,2,0:T(8,128)(2,1)} %bitcast.74), calls=%async_computation.4 | async-start | bytes 4194304 | tf_op jit(solution)/shard_map/all_to_all | solution.py:61
  188.8 33.2 %copy-start.2 = (bf16[256,1024]{1,0:T(8,128)(2,1)S(1)}, bf16[256,1024]{1,0:T(8,128)(2,1)}, u32[]{:S(2)}) copy-start(bf16[256,1024]{1,0:T(8,128)(2,1)} %copy-done.1) | copy-start | bytes 1572868
  190.0 49.5 %collective-permute-start.11 = (bf16[16,2,8,512]{3,2,1,0:T(8,128)(2,1)S(1)}, bf16[16,2,8,512]{3,2,1,0:T(8,128)(2,1)}, u32[]{:S(2)}, u32[]{:S(2)}) collective-permute-start(bf16[16,2,8,512]{3,2,1,0:T(8,128)(2,1)S(1)} %bitcast.87), channel_id=1, source_target_pairs={{0,0},{1,1},{48,32},{49,33},{66,64},{67,65},{114,96},{115,97},{132... | collective-permute-start | bytes 786440 | tf_op jit(solution)/shard_map/ppermute | solution.py:98
  197.4 40.1 %collective-permute-start.4 = (bf16[256,1024]{1,0:T(8,128)(2,1)S(1)}, bf16[256,1024]{1,0:T(8,128)(2,1)}, u32[]{:S(2)}, u32[]{:S(2)}) collective-permute-start(bf16[256,1024]{1,0:T(8,128)(2,1)S(1)} %reshape.65), channel_id=1, source_target_pairs={{0,0},{1,1},{48,32},{49,33},{66,64},{67,65},{114,96},{115,97},{132... | collective-permute-start | bytes 1572872 | tf_op jit(solution)/shard_map/ppermute | solution.py:72
  222.8 19.1 %collective-permute-start.10 = (bf16[16,2,8,512]{3,2,1,0:T(8,128)(2,1)S(1)}, bf16[16,2,8,512]{3,2,1,0:T(8,128)(2,1)S(1)}, u32[]{:S(2)}, u32[]{:S(2)}) collective-permute-start(bf16[16,2,8,512]{3,2,1,0:T(8,128)(2,1)S(1)} %bitcast.88), channel_id=1, source_target_pairs={{0,0},{1,1},{48,32},{49,33},{66,64},{67,65},{114,96},{115,97},{132... | collective-permute-start | bytes 786440 | tf_op jit(solution)/shard_map/ppermute | solution.py:97
  228.2 61.1 %collective-permute-start.8 = (bf16[256,1024]{1,0:T(8,128)(2,1)S(1)}, bf16[256,1024]{1,0:T(8,128)(2,1)}, u32[]{:S(2)}, u32[]{:S(2)}) collective-permute-start(bf16[256,1024]{1,0:T(8,128)(2,1)S(1)} %bitcast.86), channel_id=1, source_target_pairs={{0,0},{1,1},{48,32},{49,33},{66,64},{67,65},{114,96},{115,97},{132... | collective-permute-start | bytes 1572872 | tf_op jit(solution)/shard_map/ppermute | solution.py:72
  237.6 54.8 %collective-permute-start.5 = (bf16[256,1024]{1,0:T(8,128)(2,1)}, bf16[256,1024]{1,0:T(8,128)(2,1)S(1)}, u32[]{:S(2)}, u32[]{:S(2)}) collective-permute-start(bf16[256,1024]{1,0:T(8,128)(2,1)} %collective-permute-done.4), channel_id=1, source_target_pairs={{0,0},{1,1},{32,32},{33,33},{64,64},{65,65},{96,96},{97,97},{128,1... | collective-permute-start | bytes 1572872 | tf_op jit(solution)/shard_map/ppermute | solution.py:71
  243.8 56.0 %all-to-all-start.5 = ((bf16[16,4,8,512]{3,2,1,0:T(8,128)(2,1)}), bf16[16,4,8,512]{3,2,1,0:T(8,128)(2,1)S(1)}, u32[]{:S(2)}, u32[]{:S(2)}) async-start(bf16[16,4,8,512]{3,2,1,0:T(8,128)(2,1)} %pad_maximum_fusion), calls=%async_computation.5 | async-start | bytes 1048576 | tf_op jit(solution)/shard_map/all_to_all | solution.py:99
  289.3 21.8 %collective-permute-start.9 = (bf16[256,1024]{1,0:T(8,128)(2,1)}, bf16[256,1024]{1,0:T(8,128)(2,1)S(1)}, u32[]{:S(2)}, u32[]{:S(2)}) collective-permute-start(bf16[256,1024]{1,0:T(8,128)(2,1)} %collective-permute-done.8), channel_id=1, source_target_pairs={{0,0},{1,1},{32,32},{33,33},{64,64},{65,65},{96,96},{97,97},{128,1... | collective-permute-start | bytes 1572872 | tf_op jit(solution)/shard_map/ppermute | solution.py:71

commit v3 on v2

--- a/solution.py
+++ b/solution.py
@@ -63,8 +63,16 @@
     )
 
 
-def to_work(x):
-    return lax.ppermute(lax.ppermute(x, DEVICES, PLAN.shuffle), DEVICES, PLAN.mirror)
+def after(x, *others):
+    return lax.optimization_barrier((x,) + others)[0]
+
+
+def shuffle(x):
+    return lax.ppermute(x, DEVICES, PLAN.shuffle)
+
+
+def mirror(x):
+    return lax.ppermute(x, DEVICES, PLAN.mirror)
 
 
 def to_store(x):
@@ -76,18 +84,19 @@
 def gather_rows(up_blocks, down_blocks):
     n = lax.axis_size("dp")
     nb, ru, wu = up_blocks.shape
-    rd, wd = down_blocks.shape[1:]
     both = jnp.concatenate([up_blocks, down_blocks.reshape(nb, ru, wu)], axis=0)
     sent = jnp.broadcast_to(both, (n,) + both.shape)
     got = lax.all_to_all(sent, "dp", split_axis=0, concat_axis=0, tiled=True)
-    up = lax.ppermute(got[:, :nb], DEVICES, PLAN.weights)
-    down = lax.ppermute(got[:, nb:], DEVICES, PLAN.weights)
-    up = up.transpose(1, 0, 2, 3).reshape(nb, n * ru, wu)
-    down = down.reshape(n, nb, rd, wd).transpose(1, 0, 2, 3).reshape(nb, n * rd, wd)
-    return up, down
+    return got[:, :nb], got[:, nb:]
 
 
-def sum_rows(up_term, down_term):
+def whole(rows, height, width):
+    n, nb = rows.shape[:2]
+    rows = lax.ppermute(rows, DEVICES, PLAN.weights)
+    return rows.reshape(n, nb, height // n, width).transpose(1, 0, 2, 3).reshape(nb, height, width)
+
+
+def sum_rows(up_term, down_term, gate):
     n = lax.axis_size("dp")
     nb, hu, wu = up_term.shape
     hd, wd = down_term.shape[1:]
@@ -96,9 +105,8 @@
     d = down_term.astype(BF16).reshape(nb, n, ru, wu).transpose(1, 0, 2, 3)
     u = lax.ppermute(u, DEVICES, back(PLAN.weights))
     d = lax.ppermute(d, DEVICES, back(PLAN.weights))
-    got = lax.all_to_all(
-        jnp.concatenate([u, d], axis=1), "dp", split_axis=0, concat_axis=0, tiled=True
-    )
+    both = after(jnp.concatenate([u, d], axis=1), gate)
+    got = lax.all_to_all(both, "dp", split_axis=0, concat_axis=0, tiled=True)
     s = jnp.sum(got.astype(F32), axis=0)
     return s[:nb], s[nb:].reshape(nb, rd, wd)
 
@@ -107,30 +115,40 @@
     nb = up_blocks.shape[0]
     t = features.shape[1]
     n = NB // nb
-    up, down = gather_rows(up_blocks, down_blocks)
-    x = to_work(features).reshape(nb, BIN, t)
-    out_cotangent = to_work(out_cotangent)
-    pre = jnp.einsum(
-        "bkgj,bkt->gbjt", up.reshape(nb, BIN, NB, J_UP), x, preferred_element_type=F32
-    ).astype(BF16)
-    permuted = exchange(pre.reshape(n, nb, nb, J_UP, t))
+    moved = shuffle(features)
+    up_rows, down_rows = gather_rows(up_blocks, down_blocks)
+    moved_cot = shuffle(after(out_cotangent, moved, up_rows))
+    x_flat = mirror(moved)
+    up = whole(up_rows, BIN, BOUT)
+    cot = mirror(after(moved_cot, x_flat))
+    x = after(x_flat, moved_cot).reshape(nb, BIN, t)
+    pre = jnp.einsum("bkn,bkt->bnt", up, x, preferred_element_type=F32).astype(BF16)
+    permuted = exchange(pre.reshape(nb, n, nb, J_UP, t).transpose(1, 2, 0, 3, 4))
+    down = whole(after(down_rows, up), BOUT, BIN)
+    cot = after(cot, permuted).reshape(nb, n, nb, J_DN, t).transpose(1, 2, 0, 3, 4)
+    dblock = exchange(cot)
     permuted = permuted.transpose(1, 0, 2, 3, 4).reshape(nb, BOUT, t)
-    cot = out_cotangent.reshape(nb, n, nb, J_DN, t).transpose(1, 2, 0, 3, 4)
-    dblock = exchange(cot).transpose(1, 0, 2, 3, 4).reshape(nb, BIN, t)
     pf = permuted.astype(F32)
     act = gelu_value(pf).astype(BF16)
+    blockout = jnp.einsum("gmc,gmt->gct", down, act, preferred_element_type=F32).astype(BF16)
+    blockout = blockout.reshape(nb, n, nb, J_DN, t).transpose(1, 2, 0, 3, 4)
+    mixed = exchange(after(blockout, dblock))
+    dblock = dblock.transpose(1, 0, 2, 3, 4).reshape(nb, BIN, t)
     dact = jnp.einsum("gmc,gct->gmt", down, dblock, preferred_element_type=F32)
     dperm = (dact * gelu_slope(pf)).astype(BF16)
-    dpre = exchange(dperm.reshape(nb, n, nb, J_UP, t).transpose(1, 2, 0, 3, 4))
+    dperm = dperm.reshape(nb, n, nb, J_UP, t).transpose(1, 2, 0, 3, 4)
+    dpre = exchange(after(dperm, mixed))
+    mixed = to_store(mixed.transpose(1, 0, 2, 3, 4).reshape(nb * BIN, t))
+    down_term = jnp.einsum("gmt,gct->gmc", act, dblock, preferred_element_type=F32)
     dpre = dpre.transpose(1, 0, 2, 3, 4).reshape(nb, BOUT, t)
-    blockout = jnp.einsum("gmc,gmt->gct", down, act, preferred_element_type=F32).astype(BF16)
-    mixed = exchange(blockout.reshape(nb, n, nb, J_DN, t).transpose(1, 2, 0, 3, 4))
-    mixed = mixed.transpose(1, 0, 2, 3, 4).reshape(nb * BIN, t)
-    down_term = jnp.einsum("gmt,gct->gmc", act, dblock, preferred_element_type=F32)
+    fgrad = jnp.einsum("bkn,bnt->bkt", up, dpre, preferred_element_type=F32).astype(BF16)
+    fgrad = fgrad.reshape(nb * BIN, t)
+    dpre = after(dpre, fgrad)
     up_term = jnp.einsum("bkt,bnt->bkn", x, dpre, preferred_element_type=F32)
-    fgrad = jnp.einsum("bkn,bnt->bkt", up, dpre, preferred_element_type=F32).astype(BF16)
-    up_grad, down_grad = sum_rows(up_term, down_term)
-    return to_store(mixed), to_store(fgrad.reshape(nb * BIN, t)), up_grad, down_grad
+    fgrad = lax.ppermute(fgrad, DEVICES, back(PLAN.mirror))
+    up_grad, down_grad = sum_rows(up_term, down_term, fgrad)
+    fgrad = lax.ppermute(fgrad, DEVICES, back(PLAN.shuffle))
+    return mixed, fgrad, up_grad, down_grad
 
 
 def solution(mesh):

time: 314 us -> 319 us (1.016)
  the two profiles are of different devices: /device:TPU:89 before, /device:TPU:102 now
where the time goes in v3:
time: 319 us; the launch traced here: 317 us
  starting transfers between devices  166 us (52%)
  waiting for transfers between devices  120 us (38%)
  local copies, waits for them, and re-layouts  16.4 us (5%)
  matrix products  9.09 us (3%)
  other arithmetic  5.33 us (2%)
    all_to_all x4, starting transfers between devices, exchange(): lax.all_to_all(x, DEVICES, split_axis=0, concat_axis=0, tiled=True, axis_...  68.3 us
    all_to_all x1, starting transfers between devices, sum_rows(): got = lax.all_to_all(both, 'dp', split_axis=0, concat_axis=0, tiled=True)  39.5 us
    ppermute x2, waiting for transfers between devices, whole(): rows = lax.ppermute(rows, DEVICES, PLAN.weights)  30.7 us
    all_to_all x4, waiting for transfers between devices, exchange(): lax.all_to_all(x, DEVICES, split_axis=0, concat_axis=0, tiled=True, axis_...  27.5 us
    ppermute x2, waiting for transfers between devices, shuffle(): return lax.ppermute(x, DEVICES, PLAN.shuffle)  16.7 us
    ppermute x1, starting transfers between devices, to_store(): lax.ppermute(lax.ppermute(x, DEVICES, back(PLAN.mirror)), DEVICES, back(P...  14.5 us
    ppermute x2, waiting for transfers between devices, mirror(): return lax.ppermute(x, DEVICES, PLAN.mirror)  13.9 us
    ppermute x2, starting transfers between devices, whole(): rows = lax.ppermute(rows, DEVICES, PLAN.weights)  10.2 us
  transfers between devices with their start and end apart: 18, of which 14 were waited for; matrix products, arithmetic and copies ran while one was open for 7% of the time, Pallas kernels for 0%

profile of v3, /device:TPU:102, one launch (start us, length us, event | category | flops | bytes accessed | tf_op | source)
XLA Modules:
  0.0 317.5 jit_solution(16966321971902759926)
XLA Ops:
  2.9 7.5 %all-to-all-start = ((bf16[16,4,8,512]{3,2,1,0:T(8,128)(2,1)}), bf16[16,4,8,512]{3,2,1,0:T(8,128)(2,1)S(1)}, u32[]{:S(2)}, u32[]{:S(2)}) async-start(bf16[16,4,8,512]{3,2,1,0:T(8,128)(2,1)} %broadcast_in_dim.3), calls=%async_computation | async-start | bytes 1048576 | tf_op jit(solution)/shard_map/all_to_all | solution.py:89
  10.4 4.6 %collective-permute-start.2 = (bf16[256,1024]{1,0:T(8,128)(2,1)}, bf16[256,1024]{1,0:T(8,128)(2,1)S(1)}, u32[]{:S(2)}, u32[]{:S(2)}) collective-permute-start(bf16[256,1024]{1,0:T(8,128)(2,1)} %param.4), channel_id=1, source_target_pairs={{0,0},{1,1},{32,32},{33,33},{64,64},{65,65},{96,96},{97,97},{128,1... | collective-permute-start | bytes 1572872 | tf_op jit(solution)/shard_map/ppermute | solution.py:71
  15.0 5.0 %all-to-all-done = bf16[16,4,8,512]{3,2,1,0:T(8,128)(2,1)S(1)} async-done(((bf16[16,4,8,512]{3,2,1,0:T(8,128)(2,1)}), bf16[16,4,8,512]{3,2,1,0:T(8,128)(2,1)S(1)}, u32[]{:S(2)}, u32[]{:S(2)}) %all-to-all-start) | async-done | bytes 524320 | tf_op jit(solution)/shard_map/all_to_all | solution.py:89
  20.1 9.9 %collective-permute-done.2 = bf16[256,1024]{1,0:T(8,128)(2,1)S(1)} collective-permute-done((bf16[256,1024]{1,0:T(8,128)(2,1)}, bf16[256,1024]{1,0:T(8,128)(2,1)S(1)}, u32[]{:S(2)}, u32[]{:S(2)}) %collective-permute-start.2) | collective-permute-done | bytes 524320 | tf_op jit(solution)/shard_map/ppermute | solution.py:71
  29.9 4.3 %collective-permute-start.4 = (bf16[256,1024]{1,0:T(8,128)(2,1)}, bf16[256,1024]{1,0:T(8,128)(2,1)S(1)}, u32[]{:S(2)}, u32[]{:S(2)}) collective-permute-start(bf16[256,1024]{1,0:T(8,128)(2,1)} %param.7), channel_id=1, source_target_pairs={{0,0},{1,1},{32,32},{33,33},{64,64},{65,65},{96,96},{97,97},{128,1... | collective-permute-start | bytes 1572872 | tf_op jit(solution)/shard_map/ppermute | solution.py:71
  36.1 5.1 %collective-permute-start = (bf16[16,2,8,512]{3,2,0,1:T(8,128)(2,1)S(1)}, bf16[16,2,8,512]{3,2,0,1:T(8,128)(2,1)S(1)}, u32[]{:S(2)}, u32[]{:S(2)}) collective-permute-start(bf16[16,2,8,512]{3,2,0,1:T(8,128)(2,1)S(1)} %copy.51), channel_id=1, source_target_pairs={{0,0},{1,1},{32,48},{33,49},{64,66},{65,67},{96,114},{97,115},{128... | collective-permute-start | bytes 786440 | tf_op jit(solution)/shard_map/ppermute | solution.py:95
  41.2 6.8 %collective-permute-done.4 = bf16[256,1024]{1,0:T(8,128)(2,1)S(1)} collective-permute-done((bf16[256,1024]{1,0:T(8,128)(2,1)}, bf16[256,1024]{1,0:T(8,128)(2,1)S(1)}, u32[]{:S(2)}, u32[]{:S(2)}) %collective-permute-start.4) | collective-permute-done | bytes 524320 | tf_op jit(solution)/shard_map/ppermute | solution.py:71
  48.0 13.9 %collective-permute-done.3 = bf16[256,1024]{1,0:T(8,128)(2,1)S(1)} collective-permute-done((bf16[256,1024]{1,0:T(8,128)(2,1)S(1)}, bf16[256,1024]{1,0:T(8,128)(2,1)S(1)}, u32[]{:S(2)}, u32[]{:S(2)}) %collective-permute-start.3) | collective-permute-done | bytes 524320 | tf_op jit(solution)/shard_map/ppermute | solution.py:75
  61.9 9.8 %collective-permute-done = bf16[16,2,8,512]{3,2,0,1:T(8,128)(2,1)S(1)} collective-permute-done((bf16[16,2,8,512]{3,2,0,1:T(8,128)(2,1)S(1)}, bf16[16,2,8,512]{3,2,0,1:T(8,128)(2,1)S(1)}, u32[]{:S(2)}, u32[]{:S(2)}) %collective-permute-start) | collective-permute-done | bytes 262176 | tf_op jit(solution)/shard_map/ppermute | solution.py:95
  74.0 25.2 %all-to-all-start.1 = ((bf16[32,2,2,8,1024]{4,3,1,2,0:T(8,128)(2,1)}), bf16[32,2,2,8,1024]{4,3,1,2,0:T(8,128)(2,1)S(1)}, u32[]{:S(2)}, u32[]{:S(2)}) async-start(bf16[32,2,2,8,1024]{4,3,1,2,0:T(8,128)(2,1)} %bitcast.65), calls=%async_computation.1 | async-start | bytes 4194304 | tf_op jit(solution)/shard_map/all_to_all | solution.py:61
  101.2 5.1 %collective-permute-start.1 = (bf16[16,2,8,512]{3,2,1,0:T(8,128)(2,1)S(1)}, bf16[16,2,8,512]{3,2,1,0:T(8,128)(2,1)S(1)}, u32[]{:S(2)}, u32[]{:S(2)}) collective-permute-start(bf16[16,2,8,512]{3,2,1,0:T(8,128)(2,1)S(1)} %get-tuple-element.13), channel_id=1, source_target_pairs={{0,0},{1,1},{32,48},{33,49},{64,66},{65,67},{96,114},{97,115},{128... | collective-permute-start | bytes 786440 | tf_op jit(solution)/shard_map/ppermute | solution.py:95
  106.3 20.9 %collective-permute-done.1 = bf16[16,2,8,512]{3,2,1,0:T(8,128)(2,1)S(1)} collective-permute-done((bf16[16,2,8,512]{3,2,1,0:T(8,128)(2,1)S(1)}, bf16[16,2,8,512]{3,2,1,0:T(8,128)(2,1)S(1)}, u32[]{:S(2)}, u32[]{:S(2)}) %collective-permute-start.1) | collective-permute-done | bytes 262176 | tf_op jit(solution)/shard_map/ppermute | solution.py:95
  129.7 29.5 %all-to-all-start.2 = ((bf16[32,2,2,2,1024]{4,3,2,1,0:T(2,128)(2,1)}), bf16[32,2,2,2,1024]{4,3,2,1,0:T(2,128)(2,1)S(1)}, u32[]{:S(2)}, u32[]{:S(2)}) async-start(bf16[32,2,2,2,1024]{4,3,2,1,0:T(2,128)(2,1)} %copy.42), calls=%async_computation.2 | async-start | bytes 1048576 | tf_op jit(solution)/shard_map/all_to_all | solution.py:61
  160.3 3.2 %fusion.7 = (bf16[2,512,1024]{2,1,0:T(8,128)(2,1)S(1)}, f32[2,512,1024]{2,1,0:T(8,128)}) fusion(f32[2,32,2,8,1024]{4,3,2,1,0:T(8,128)S(1)} %copy.39), kind=kLoop, calls=%fused_computation.10 | loop fusion | flops 5242880 | bytes 10485760 | tf_op jit(solution)/shard_map/convert_element_type | solution.py:132
  169.6 6.8 %all-to-all-start.3 = ((bf16[32,2,2,2,1024]{4,3,1,2,0:T(2,128)(2,1)}), bf16[32,2,2,2,1024]{4,3,1,2,0:T(2,128)(2,1)S(1)}, u32[]{:S(2)}, u32[]{:S(2)}) async-start(bf16[32,2,2,2,1024]{4,3,1,2,0:T(2,128)(2,1)} %bitcast.59), calls=%async_computation.3 | async-start | bytes 1048576 | tf_op jit(solution)/shard_map/all_to_all | solution.py:61
  176.4 5.1 %fusion.5 = bf16[2,512,1024]{2,1,0:T(8,128)(2,1)S(1)} fusion(f32[2,32,2,8,1024]{4,3,2,1,0:T(8,128)} %copy-done, f32[2,512,1024]{2,1,0:T(8,128)} %get-tuple-element.23, bf16[2,512,128]{2,1,0:T(8,128)(2,1)S(1)} %bitcast.75, bf16[2,128,1024]{2,1,0:T(8,128)(2,1)} %reshape.68), kind=kOutput, calls=%fused_computation.6 | convolution fusion | flops 276824064 | bytes 11272192 | tf_op jit(solution)/shard_map/gmc,gct->gmt/dot_general | solution.py:137
  185.4 6.9 %all-to-all-start.4 = ((bf16[32,2,2,8,1024]{4,3,1,2,0:T(8,128)(2,1)}), bf16[32,2,2,8,1024]{4,3,1,2,0:T(8,128)(2,1)}, u32[]{:S(2)}, u32[]{:S(2)}) async-start(bf16[32,2,2,8,1024]{4,3,1,2,0:T(8,128)(2,1)} %bitcast.64), calls=%async_computation.4 | async-start | bytes 4194304 | tf_op jit(solution)/shard_map/all_to_all | solution.py:61
  195.7 5.1 %collective-permute-start.6 = (bf16[256,1024]{1,0:T(8,128)(2,1)S(1)}, bf16[256,1024]{1,0:T(8,128)(2,1)}, u32[]{:S(2)}, u32[]{:S(2)}) collective-permute-start(bf16[256,1024]{1,0:T(8,128)(2,1)S(1)} %reshape.67), channel_id=1, source_target_pairs={{0,0},{1,1},{48,32},{49,33},{66,64},{67,65},{114,96},{115,97},{132... | collective-permute-start | bytes 1572872 | tf_op jit(solution)/shard_map/ppermute | solution.py:80
  200.9 23.5 %all-to-all-done.4 = bf16[32,2,2,8,1024]{4,3,1,2,0:T(8,128)(2,1)} async-done(((bf16[32,2,2,8,1024]{4,3,1,2,0:T(8,128)(2,1)}), bf16[32,2,2,8,1024]{4,3,1,2,0:T(8,128)(2,1)}, u32[]{:S(2)}, u32[]{:S(2)}) %all-to-all-start.4) | async-done | bytes 2097184 | tf_op jit(solution)/shard_map/all_to_all | solution.py:61
  234.0 14.5 %collective-permute-start.7 = (bf16[256,1024]{1,0:T(8,128)(2,1)}, bf16[256,1024]{1,0:T(8,128)(2,1)S(1)}, u32[]{:S(2)}, u32[]{:S(2)}) collective-permute-start(bf16[256,1024]{1,0:T(8,128)(2,1)} %collective-permute-done.6), channel_id=1, source_target_pairs={{0,0},{1,1},{32,32},{33,33},{64,64},{65,65},{96,96},{97,97},{128,1... | collective-permute-start | bytes 1572872 | tf_op jit(solution)/shard_map/ppermute | solution.py:79
  248.5 6.3 %collective-permute-done.10 = bf16[16,2,8,512]{3,2,1,0:T(8,128)(2,1)S(1)} collective-permute-done((bf16[16,2,8,512]{3,2,1,0:T(8,128)(2,1)S(1)}, bf16[16,2,8,512]{3,2,1,0:T(8,128)(2,1)S(1)}, u32[]{:S(2)}, u32[]{:S(2)}) %collective-permute-start.10) | collective-permute-done | bytes 262176 | tf_op jit(solution)/shard_map/ppermute | solution.py:106
  255.7 39.5 %all-to-all-start.5 = ((bf16[16,4,8,512]{3,2,1,0:T(8,128)(2,1)}), bf16[16,4,8,512]{3,2,1,0:T(8,128)(2,1)S(1)}, u32[]{:S(2)}, u32[]{:S(2)}) async-start(bf16[16,4,8,512]{3,2,1,0:T(8,128)(2,1)} %pad_maximum_fusion), calls=%async_computation.5 | async-start | bytes 1048576 | tf_op jit(solution)/shard_map/all_to_all | solution.py:109
  297.1 7.6 %all-to-all-done.5 = bf16[16,4,8,512]{3,2,1,0:T(8,128)(2,1)S(1)} async-done(((bf16[16,4,8,512]{3,2,1,0:T(8,128)(2,1)}), bf16[16,4,8,512]{3,2,1,0:T(8,128)(2,1)S(1)}, u32[]{:S(2)}, u32[]{:S(2)}) %all-to-all-start.5) | async-done | bytes 524320 | tf_op jit(solution)/shard_map/all_to_all | solution.py:109
  306.0 9.9 %collective-permute-done.9 = bf16[256,1024]{1,0:T(8,128)(2,1)S(1)} collective-permute-done((bf16[256,1024]{1,0:T(8,128)(2,1)S(1)}, bf16[256,1024]{1,0:T(8,128)(2,1)S(1)}, u32[]{:S(2)}, u32[]{:S(2)}) %collective-permute-start.9) | collective-permute-done | bytes 524320 | tf_op jit(solution)/shard_map/ppermute | solution.py:150
  (62 shorter events, 40.8 us)
Async XLA Ops:
  2.9 17.0 %all-to-all-start = ((bf16[16,4,8,512]{3,2,1,0:T(8,128)(2,1)}), bf16[16,4,8,512]{3,2,1,0:T(8,128)(2,1)S(1)}, u32[]{:S(2)}, u32[]{:S(2)}) async-start(bf16[16,4,8,512]{3,2,1,0:T(8,128)(2,1)} %broadcast_in_dim.3), calls=%async_computation | async-start | bytes 1048576 | tf_op jit(solution)/shard_map/all_to_all | solution.py:89
  10.4 19.5 %collective-permute-start.2 = (bf16[256,1024]{1,0:T(8,128)(2,1)}, bf16[256,1024]{1,0:T(8,128)(2,1)S(1)}, u32[]{:S(2)}, u32[]{:S(2)}) collective-permute-start(bf16[256,1024]{1,0:T(8,128)(2,1)} %param.4), channel_id=1, source_target_pairs={{0,0},{1,1},{32,32},{33,33},{64,64},{65,65},{96,96},{97,97},{128,1... | collective-permute-start | bytes 1572872 | tf_op jit(solution)/shard_map/ppermute | solution.py:71
  29.9 18.1 %collective-permute-start.4 = (bf16[256,1024]{1,0:T(8,128)(2,1)}, bf16[256,1024]{1,0:T(8,128)(2,1)S(1)}, u32[]{:S(2)}, u32[]{:S(2)}) collective-permute-start(bf16[256,1024]{1,0:T(8,128)(2,1)} %param.7), channel_id=1, source_target_pairs={{0,0},{1,1},{32,32},{33,33},{64,64},{65,65},{96,96},{97,97},{128,1... | collective-permute-start | bytes 1572872 | tf_op jit(solution)/shard_map/ppermute | solution.py:71
  34.2 27.7 %collective-permute-start.3 = (bf16[256,1024]{1,0:T(8,128)(2,1)S(1)}, bf16[256,1024]{1,0:T(8,128)(2,1)S(1)}, u32[]{:S(2)}, u32[]{:S(2)}) collective-permute-start(bf16[256,1024]{1,0:T(8,128)(2,1)S(1)} %collective-permute-done.2), channel_id=1, source_target_pairs={{0,0},{1,1},{32,48},{33,49},{64,66},{65,67},{96,114},{97,115},{128... | collective-permute-start | bytes 1572872 | tf_op jit(solution)/shard_map/ppermute | solution.py:75
  36.1 35.6 %collective-permute-start = (bf16[16,2,8,512]{3,2,0,1:T(8,128)(2,1)S(1)}, bf16[16,2,8,512]{3,2,0,1:T(8,128)(2,1)S(1)}, u32[]{:S(2)}, u32[]{:S(2)}) collective-permute-start(bf16[16,2,8,512]{3,2,0,1:T(8,128)(2,1)S(1)} %copy.51), channel_id=1, source_target_pairs={{0,0},{1,1},{32,48},{33,49},{64,66},{65,67},{96,114},{97,115},{128... | collective-permute-start | bytes 786440 | tf_op jit(solution)/shard_map/ppermute | solution.py:95
  48.0 23.7 %copy-start.6 = (bf16[256,1024]{1,0:T(8,128)(2,1)}, bf16[256,1024]{1,0:T(8,128)(2,1)S(1)}, u32[]{:S(2)}) copy-start(bf16[256,1024]{1,0:T(8,128)(2,1)S(1)} %collective-permute-done.4) | copy-start | bytes 1572868
  61.9 9.8 %copy-start.1 = (bf16[256,1024]{1,0:T(8,128)(2,1)}, bf16[256,1024]{1,0:T(8,128)(2,1)S(1)}, u32[]{:S(2)}) copy-start(bf16[256,1024]{1,0:T(8,128)(2,1)S(1)} %collective-permute-done.3) | copy-start | bytes 1572868
  74.0 54.1 %all-to-all-start.1 = ((bf16[32,2,2,8,1024]{4,3,1,2,0:T(8,128)(2,1)}), bf16[32,2,2,8,1024]{4,3,1,2,0:T(8,128)(2,1)S(1)}, u32[]{:S(2)}, u32[]{:S(2)}) async-start(bf16[32,2,2,8,1024]{4,3,1,2,0:T(8,128)(2,1)} %bitcast.65), calls=%async_computation.1 | async-start | bytes 4194304 | tf_op jit(solution)/shard_map/all_to_all | solution.py:61
  99.2 28.1 %collective-permute-start.5 = (bf16[256,1024]{1,0:T(8,128)(2,1)}, bf16[256,1024]{1,0:T(8,128)(2,1)S(1)}, u32[]{:S(2)}, u32[]{:S(2)}) collective-permute-start(bf16[256,1024]{1,0:T(8,128)(2,1)} %copy-done.6), channel_id=1, source_target_pairs={{0,0},{1,1},{32,48},{33,49},{64,66},{65,67},{96,114},{97,115},{128... | collective-permute-start | bytes 1572872 | tf_op jit(solution)/shard_map/ppermute | solution.py:75
  101.2 26.0 %collective-permute-start.1 = (bf16[16,2,8,512]{3,2,1,0:T(8,128)(2,1)S(1)}, bf16[16,2,8,512]{3,2,1,0:T(8,128)(2,1)S(1)}, u32[]{:S(2)}, u32[]{:S(2)}) collective-permute-start(bf16[16,2,8,512]{3,2,1,0:T(8,128)(2,1)S(1)} %get-tuple-element.13), channel_id=1, source_target_pairs={{0,0},{1,1},{32,48},{33,49},{64,66},{65,67},{96,114},{97,115},{128... | collective-permute-start | bytes 786440 | tf_op jit(solution)/shard_map/ppermute | solution.py:95
  129.7 38.5 %all-to-all-start.2 = ((bf16[32,2,2,2,1024]{4,3,2,1,0:T(2,128)(2,1)}), bf16[32,2,2,2,1024]{4,3,2,1,0:T(2,128)(2,1)S(1)}, u32[]{:S(2)}, u32[]{:S(2)}) async-start(bf16[32,2,2,2,1024]{4,3,2,1,0:T(2,128)(2,1)} %copy.42), calls=%async_computation.2 | async-start | bytes 1048576 | tf_op jit(solution)/shard_map/all_to_all | solution.py:61
  160.3 3.3 %copy-start = (f32[2,32,2,8,1024]{4,3,2,1,0:T(8,128)}, f32[2,32,2,8,1024]{4,3,2,1,0:T(8,128)S(1)}, u32[]{:S(2)}) copy-start(f32[2,32,2,8,1024]{4,3,2,1,0:T(8,128)S(1)} %copy.39) | copy-start | bytes 12582916
  169.6 15.9 %all-to-all-start.3 = ((bf16[32,2,2,2,1024]{4,3,1,2,0:T(2,128)(2,1)}), bf16[32,2,2,2,1024]{4,3,1,2,0:T(2,128)(2,1)S(1)}, u32[]{:S(2)}, u32[]{:S(2)}) async-start(bf16[32,2,2,2,1024]{4,3,1,2,0:T(2,128)(2,1)} %bitcast.59), calls=%async_computation.3 | async-start | bytes 1048576 | tf_op jit(solution)/shard_map/all_to_all | solution.py:61
  181.4 10.8 %copy-start.5 = (bf16[2,128,1024]{2,1,0:T(8,128)(2,1)S(1)}, bf16[2,128,1024]{2,1,0:T(8,128)(2,1)}, u32[]{:S(2)}) copy-start(bf16[2,128,1024]{2,1,0:T(8,128)(2,1)} %reshape.68) | copy-start | bytes 1572868
  185.4 38.9 %all-to-all-start.4 = ((bf16[32,2,2,8,1024]{4,3,1,2,0:T(8,128)(2,1)}), bf16[32,2,2,8,1024]{4,3,1,2,0:T(8,128)(2,1)}, u32[]{:S(2)}, u32[]{:S(2)}) async-start(bf16[32,2,2,8,1024]{4,3,1,2,0:T(8,128)(2,1)} %bitcast.64), calls=%async_computation.4 | async-start | bytes 4194304 | tf_op jit(solution)/shard_map/all_to_all | solution.py:61
  193.0 33.1 %copy-start.4 = (bf16[16,2,8,512]{3,2,0,1:T(8,128)(2,1)S(1)}, bf16[16,2,8,512]{3,2,0,1:T(8,128)(2,1)}, u32[]{:S(2)}) copy-start(bf16[16,2,8,512]{3,2,0,1:T(8,128)(2,1)} %copy-done.3) | copy-start | bytes 786436
  193.2 55.3 %collective-permute-start.11 = (bf16[16,2,8,512]{3,2,1,0:T(8,128)(2,1)S(1)}, bf16[16,2,8,512]{3,2,1,0:T(8,128)(2,1)S(1)}, u32[]{:S(2)}, u32[]{:S(2)}) collective-permute-start(bf16[16,2,8,512]{3,2,1,0:T(8,128)(2,1)S(1)} %bitcast.77), channel_id=1, source_target_pairs={{0,0},{1,1},{48,32},{49,33},{66,64},{67,65},{114,96},{115,97},{132... | collective-permute-start | bytes 786440 | tf_op jit(solution)/shard_map/ppermute | solution.py:107
  195.5 33.0 %copy-start.2 = (bf16[256,1024]{1,0:T(8,128)(2,1)S(1)}, bf16[256,1024]{1,0:T(8,128)(2,1)}, u32[]{:S(2)}) copy-start(bf16[256,1024]{1,0:T(8,128)(2,1)} %copy-done.1) | copy-start | bytes 1572868
  195.7 38.2 %collective-permute-start.6 = (bf16[256,1024]{1,0:T(8,128)(2,1)S(1)}, bf16[256,1024]{1,0:T(8,128)(2,1)}, u32[]{:S(2)}, u32[]{:S(2)}) collective-permute-start(bf16[256,1024]{1,0:T(8,128)(2,1)S(1)} %reshape.67), channel_id=1, source_target_pairs={{0,0},{1,1},{48,32},{49,33},{66,64},{67,65},{114,96},{115,97},{132... | collective-permute-start | bytes 1572872 | tf_op jit(solution)/shard_map/ppermute | solution.py:80
  226.6 29.1 %collective-permute-start.8 = (bf16[256,1024]{1,0:T(8,128)(2,1)S(1)}, bf16[256,1024]{1,0:T(8,128)(2,1)S(1)}, u32[]{:S(2)}, u32[]{:S(2)}) collective-permute-start(bf16[256,1024]{1,0:T(8,128)(2,1)S(1)} %bitcast.76), channel_id=1, source_target_pairs={{0,0},{1,1},{48,32},{49,33},{66,64},{67,65},{114,96},{115,97},{132... | collective-permute-start | bytes 1572872 | tf_op jit(solution)/shard_map/ppermute | solution.py:148
  229.4 25.5 %collective-permute-start.10 = (bf16[16,2,8,512]{3,2,1,0:T(8,128)(2,1)S(1)}, bf16[16,2,8,512]{3,2,1,0:T(8,128)(2,1)S(1)}, u32[]{:S(2)}, u32[]{:S(2)}) collective-permute-start(bf16[16,2,8,512]{3,2,1,0:T(8,128)(2,1)S(1)} %bitcast.78), channel_id=1, source_target_pairs={{0,0},{1,1},{48,32},{49,33},{66,64},{67,65},{114,96},{115,97},{132... | collective-permute-start | bytes 786440 | tf_op jit(solution)/shard_map/ppermute | solution.py:106
  234.0 63.1 %collective-permute-start.7 = (bf16[256,1024]{1,0:T(8,128)(2,1)}, bf16[256,1024]{1,0:T(8,128)(2,1)S(1)}, u32[]{:S(2)}, u32[]{:S(2)}) collective-permute-start(bf16[256,1024]{1,0:T(8,128)(2,1)} %collective-permute-done.6), channel_id=1, source_target_pairs={{0,0},{1,1},{32,32},{33,33},{64,64},{65,65},{96,96},{97,97},{128,1... | collective-permute-start | bytes 1572872 | tf_op jit(solution)/shard_map/ppermute | solution.py:79
  255.7 49.0 %all-to-all-start.5 = ((bf16[16,4,8,512]{3,2,1,0:T(8,128)(2,1)}), bf16[16,4,8,512]{3,2,1,0:T(8,128)(2,1)S(1)}, u32[]{:S(2)}, u32[]{:S(2)}) async-start(bf16[16,4,8,512]{3,2,1,0:T(8,128)(2,1)} %pad_maximum_fusion), calls=%async_computation.5 | async-start | bytes 1048576 | tf_op jit(solution)/shard_map/all_to_all | solution.py:109
  295.2 20.7 %collective-permute-start.9 = (bf16[256,1024]{1,0:T(8,128)(2,1)S(1)}, bf16[256,1024]{1,0:T(8,128)(2,1)S(1)}, u32[]{:S(2)}, u32[]{:S(2)}) collective-permute-start(bf16[256,1024]{1,0:T(8,128)(2,1)S(1)} %collective-permute-done.8), channel_id=1, source_target_pairs={{0,0},{1,1},{32,32},{33,33},{64,64},{65,65},{96,96},{97,97},{128,1... | collective-permute-start | bytes 1572872 | tf_op jit(solution)/shard_map/ppermute | solution.py:150
  (1 other events, 0.8 us)

commit v4 on v3

v4 whole, which is shorter than its diff:
```python
import jax
import jax.numpy as jnp
from jax import lax
from jax.sharding import PartitionSpec as P

NB = 64
BIN = 128
BOUT = 512
J_UP = 8
J_DN = 2
F32 = jnp.float32
BF16 = jnp.bfloat16


def gelu_value(v):
    return 0.5 * v * (1.0 + lax.erf(v * 0.7071067811865476))


def gelu_slope(v):
    return (
        0.5 * (1.0 + lax.erf(v * 0.7071067811865476))
        + v * jnp.exp(-0.5 * v * v) * 0.3989422804014327
    )


DEVICES = ("dp", "tensor")


class Plan:
    def __init__(self):
        def index(xh, y, c, z, xl):
            return (((xh * 4 + y) * 2 + c) * 16 + z) * 2 + xl

        def side(z, xh, xl):
            return xl if xh == (z >> 2) & 1 else 1 - xl

        def at(label):
            return (label >> 2) & 1, label & 3, label >> 3

        spots = [(z, *at(k), xl) for z in range(16) for k in range(16) for xl in range(2)]
        shuffle, mirror, place = [], [], {}
        for z in range(16):
            for label in range(16):
                xh, y, c = at(label)
                xh2, y2, c2 = at((label + z) % 16)
                for xl in range(2):
                    xl2 = side(label, xh2, xl)
                    mid = index(xh2, y2, c2, z, xl2)
                    end = index(xh2, y2, c2, label, xl2)
                    shuffle.append((index(xh, y, c, z, xl), mid))
                    mirror.append((mid, end))
                    place[label, 2 * z + xl] = end
        self.shuffle, self.mirror = shuffle, mirror
        self.layers = [[place[t, k] for k in range(32)] for t in range(16)]
        self.planes = [
            [index(*at(k), z, side(z, at(k)[0], xl)) for k in range(16)]
            for z in range(16)
            for xl in range(2)
        ]
        self.columns = [
            [index(*at(k), z, side(z, at(k)[0], xl)) for z in range(16)]
            for k in range(16)
            for xl in range(2)
        ]
        self.swap = [
            (index(xh, y, c, z, xl), index(xh, y, c, z, side(z, xh, xl)))
            for z, xh, y, c, xl in spots
        ]


PLAN = Plan()


def back(pairs):
    return [(b, a) for a, b in pairs]


def exchange(x, groups):
    return lax.all_to_all(
        x, DEVICES, split_axis=0, concat_axis=0, tiled=True, axis_index_groups=groups
    )


def roll(x, shift):
    return lax.dynamic_slice_in_dim(jnp.concatenate([x, x]), shift, x.shape[0])


def layer():
    return lax.axis_index("tensor") // 2


def after(x, *others):
    return lax.optimization_barrier((x,) + others)[0]


def shuffle(x):
    return lax.ppermute(x, DEVICES, PLAN.shuffle)


def mirror(x):
    return lax.ppermute(x, DEVICES, PLAN.mirror)


def unmirror(x):
    return lax.ppermute(x, DEVICES, back(PLAN.mirror))


def unshuffle(x):
    return lax.ppermute(x, DEVICES, back(PLAN.shuffle))


def gather_rows(up_blocks, down_blocks, gate):
    n = lax.axis_size("dp")
    nb, ru, wu = up_blocks.shape
    rd, wd = down_blocks.shape[1:]
    both = jnp.concatenate([up_blocks, down_blocks.reshape(nb, ru, wu)], axis=0)
    both = lax.ppermute(both, DEVICES, PLAN.swap)
    got = exchange(jnp.broadcast_to(both, (n,) + both.shape), PLAN.columns)
    got = exchange(roll(after(got, gate), n - layer()), PLAN.planes)
    got = got.reshape(2, 2, 4, 2 * nb, ru, wu).transpose(3, 1, 2, 0, 4, 5)
    up = got[:nb].reshape(nb, n * ru, wu)
    down = got[nb:].reshape(nb, n, rd, wd).reshape(nb, n * rd, wd)
    return up, down


def sum_rows(up_term, down_term, gate):
    n = lax.axis_size("dp")
    nb, hu, wu = up_term.shape
    hd, wd = down_term.shape[1:]
    ru, rd = hu // n, hd // n
    u = up_term.astype(BF16).reshape(nb, 2, 4, 2, ru, wu).transpose(3, 1, 2, 0, 4, 5)
    d = down_term.astype(BF16).reshape(nb, 2, 4, 2, ru, wu).transpose(3, 1, 2, 0, 4, 5)
    both = jnp.concatenate([u, d], axis=3).reshape(n, 2 * nb, ru, wu)
    got = roll(exchange(both, PLAN.planes), layer())
    s = jnp.sum(exchange(after(got, gate), PLAN.columns).astype(F32), axis=0)
    s = lax.ppermute(s, DEVICES, PLAN.swap)
    return s[:nb], s[nb:].reshape(nb, rd, wd)


def per_device(features, up_blocks, down_blocks, out_cotangent):
    nb = up_blocks.shape[0]
    t = features.shape[1]
    n = NB // nb
    x = mirror(shuffle(features))
    cot = mirror(shuffle(out_cotangent))
    up, down = gather_rows(up_blocks, down_blocks, x)
    x = x.reshape(nb, BIN, t)
    cot = cot.reshape(nb, n, nb, J_DN, t).transpose(1, 2, 0, 3, 4)
    pre = jnp.einsum("bkn,bkt->bnt", up, x, preferred_element_type=F32).astype(BF16)
    pre = pre.reshape(nb, n, nb, J_UP, t).transpose(1, 2, 0, 3, 4)
    sent = jnp.concatenate(
        [pre.reshape(n, nb * nb, J_UP, t), cot.reshape(n, 1, nb * nb * J_DN, t)], axis=1
    )
    got = exchange(sent, PLAN.layers)
    permuted = got[:, : nb * nb].reshape(n, nb, nb, J_UP, t)
    permuted = permuted.transpose(1, 0, 2, 3, 4).reshape(nb, BOUT, t)
    dblock = got[:, nb * nb].reshape(n, nb, nb, J_DN, t)
    dblock = dblock.transpose(1, 0, 2, 3, 4).reshape(nb, BIN, t)
    pf = permuted.astype(F32)
    act = gelu_value(pf).astype(BF16)
    blockout = jnp.einsum("gmc,gmt->gct", down, act, preferred_element_type=F32).astype(BF16)
    blockout = blockout.reshape(nb, n, nb, J_DN, t).transpose(1, 2, 0, 3, 4)
    mixed = exchange(blockout, PLAN.layers)
    dact = jnp.einsum("gmc,gct->gmt", down, dblock, preferred_element_type=F32)
    dperm = (dact * gelu_slope(pf)).astype(BF16)
    dperm = dperm.reshape(nb, n, nb, J_UP, t).transpose(1, 2, 0, 3, 4)
    dpre = exchange(after(dperm, mixed), PLAN.layers)
    mixed = unmirror(mixed.transpose(1, 0, 2, 3, 4).reshape(nb * BIN, t))
    down_term = jnp.einsum("gmt,gct->gmc", act, dblock, preferred_element_type=F32)
    dpre = after(dpre, mixed).transpose(1, 0, 2, 3, 4).reshape(nb, BOUT, t)
    fgrad = jnp.einsum("bkn,bnt->bkt", up, dpre, preferred_element_type=F32).astype(BF16)
    fgrad = fgrad.reshape(nb * BIN, t)
    dpre = after(dpre, fgrad)
    fgrad = unmirror(fgrad)
    up_term = jnp.einsum("bkt,bnt->bkn", x, dpre, preferred_element_type=F32)
    up_grad, down_grad = sum_rows(up_term, down_term, fgrad)
    return unshuffle(mixed), unshuffle(fgrad), up_grad, down_grad


def solution(mesh):
    flat = P("tensor", "dp")
    rows = P("tensor", "dp", None)
    return jax.shard_map(
        per_device,
        mesh=mesh,
        in_specs=(flat, rows, rows, flat),
        out_specs=(flat, flat, rows, rows),
        check_vma=False,
    )
```

time: 319 us -> 319 us (level)
  the two profiles are of different devices: /device:TPU:102 before, /device:TPU:1 now
where the time goes in v4:
time: 319 us; the launch traced here: 315 us
  waiting for transfers between devices  162 us (51%)
  starting transfers between devices  119 us (37%)
  local copies, waits for them, and re-layouts  14.5 us (5%)
  matrix products  9.42 us (3%)
  other arithmetic  9.15 us (3%)
    all_to_all x7, waiting for transfers between devices, exchange(): lax.all_to_all(x, DEVICES, split_axis=0, concat_axis=0, tiled=True, axis_...  97 us
    all_to_all x7, starting transfers between devices, exchange(): lax.all_to_all(x, DEVICES, split_axis=0, concat_axis=0, tiled=True, axis_...  91.3 us
    ppermute x2, waiting for transfers between devices, unmirror(): return lax.ppermute(x, DEVICES, back(PLAN.mirror))  46 us
    ppermute x2, waiting for transfers between devices, mirror(): return lax.ppermute(x, DEVICES, PLAN.mirror)  19.2 us
    ppermute x2, starting transfers between devices, mirror(): return lax.ppermute(x, DEVICES, PLAN.mirror)  16.9 us
  transfers between devices with their start and end apart: 17, of which 9 were waited for; matrix products, arithmetic and copies ran while one was open for 4% of the time, Pallas kernels for 0%

profile of v4, /device:TPU:1, one launch (start us, length us, event | category | flops | bytes accessed | tf_op | source)
XLA Modules:
  0.0 315.5 jit_solution(15890818002504144497)
XLA Ops:
  3.6 18.1 %all-to-all-start = ((bf16[16,4,8,512]{3,2,1,0:T(8,128)(2,1)}), bf16[16,4,8,512]{3,2,1,0:T(8,128)(2,1)S(1)}, u32[]{:S(2)}, u32[]{:S(2)}) async-start(bf16[16,4,8,512]{3,2,1,0:T(8,128)(2,1)} %broadcast_in_dim.3), calls=%async_computation | async-start | bytes 1048576 | tf_op jit(solution)/shard_map/all_to_all | solution.py:79
  25.1 14.8 %collective-permute-start.2 = (bf16[256,1024]{1,0:T(8,128)(2,1)S(1)}, bf16[256,1024]{1,0:T(8,128)(2,1)S(1)}, u32[]{:S(2)}, u32[]{:S(2)}) collective-permute-start(bf16[256,1024]{1,0:T(8,128)(2,1)S(1)} %collective-permute-done.1), channel_id=1, source_target_pairs={{0,0},{1,1},{64,66},{65,67},{128,132},{129,133},{192,198},{193,199... | collective-permute-start | bytes 1572872 | tf_op jit(solution)/shard_map/ppermute | solution.py:101
  40.0 2.0 collective-permute-start.4
  42.0 19.2 %collective-permute-done.2 = bf16[256,1024]{1,0:T(8,128)(2,1)S(1)} collective-permute-done((bf16[256,1024]{1,0:T(8,128)(2,1)S(1)}, bf16[256,1024]{1,0:T(8,128)(2,1)S(1)}, u32[]{:S(2)}, u32[]{:S(2)}) %collective-permute-start.2) | collective-permute-done | bytes 524320 | tf_op jit(solution)/shard_map/ppermute | solution.py:101
  62.2 43.7 %all-to-all-start.1 = ((bf16[16,4,8,512]{3,2,1,0:T(8,128)(2,1)}), bf16[16,4,8,512]{3,2,1,0:T(8,128)(2,1)S(1)}, u32[]{:S(2)}, u32[]{:S(2)}) async-start(bf16[16,4,8,512]{3,2,1,0:T(8,128)(2,1)} %fusion.11), calls=%async_computation.1 | async-start | bytes 1048576 | tf_op jit(solution)/shard_map/all_to_all | solution.py:79
  106.6 11.1 %all-to-all-done.1 = bf16[16,4,8,512]{3,2,1,0:T(8,128)(2,1)S(1)} async-done(((bf16[16,4,8,512]{3,2,1,0:T(8,128)(2,1)}), bf16[16,4,8,512]{3,2,1,0:T(8,128)(2,1)S(1)}, u32[]{:S(2)}, u32[]{:S(2)}) %all-to-all-start.1) | async-done | bytes 524320 | tf_op jit(solution)/shard_map/all_to_all | solution.py:79
  118.7 1.8 pad_maximum_fusion
  120.5 4.0 %all-to-all-start.2 = ((bf16[32,5,8,1024]{3,2,1,0:T(8,128)(2,1)}), bf16[32,5,8,1024]{3,2,1,0:T(8,128)(2,1)S(1)}, u32[]{:S(2)}, u32[]{:S(2)}) async-start(bf16[32,5,8,1024]{3,2,1,0:T(8,128)(2,1)} %pad_maximum_fusion), calls=%async_computation.2 | async-start | bytes 5242880 | tf_op jit(solution)/shard_map/all_to_all | solution.py:79
  125.4 39.7 %all-to-all-done.2 = bf16[32,5,8,1024]{3,2,1,0:T(8,128)(2,1)S(1)} async-done(((bf16[32,5,8,1024]{3,2,1,0:T(8,128)(2,1)}), bf16[32,5,8,1024]{3,2,1,0:T(8,128)(2,1)S(1)}, u32[]{:S(2)}, u32[]{:S(2)}) %all-to-all-start.2) | async-done | bytes 2621472 | tf_op jit(solution)/shard_map/all_to_all | solution.py:79
  168.3 3.2 %fusion.7 = (bf16[2,512,1024]{2,1,0:T(8,128)(2,1)S(1)}, f32[2,512,1024]{2,1,0:T(8,128)}) fusion(f32[2,32,2,8,1024]{4,3,2,1,0:T(8,128)S(1)} %copy.59), kind=kLoop, calls=%fused_computation.11 | loop fusion | flops 5242880 | bytes 10485760 | tf_op jit(solution)/shard_map/convert_element_type | solution.py:160
  173.6 3.9 %all-to-all-start.3 = ((bf16[32,2,2,2,1024]{4,3,1,2,0:T(2,128)(2,1)}), bf16[32,2,2,2,1024]{4,3,1,2,0:T(2,128)(2,1)S(1)}, u32[]{:S(2)}, u32[]{:S(2)}) async-start(bf16[32,2,2,2,1024]{4,3,1,2,0:T(2,128)(2,1)} %bitcast.64), calls=%async_computation.3 | async-start | bytes 1048576 | tf_op jit(solution)/shard_map/all_to_all | solution.py:79
  177.6 5.1 %fusion.5 = bf16[2,512,1024]{2,1,0:T(8,128)(2,1)S(1)} fusion(f32[2,32,2,8,1024]{4,3,2,1,0:T(8,128)} %copy-done, f32[2,512,1024]{2,1,0:T(8,128)} %get-tuple-element.15, bf16[2,512,128]{2,1,0:T(8,128)(2,1)} %reshape_reshape.3, bf16[2,128,1024]{2,1,0:T(8,128)(2,1)} %reshape.78), kind=kOutput, calls=%fused_computation.6 | convolution fusion | flops 276824064 | bytes 11272192 | tf_op jit(solution)/shard_map/gmc,gct->gmt/dot_general | solution.py:164
  184.2 5.4 %all-to-all-done.3 = bf16[32,2,2,2,1024]{4,3,1,2,0:T(2,128)(2,1)S(1)} async-done(((bf16[32,2,2,2,1024]{4,3,1,2,0:T(2,128)(2,1)}), bf16[32,2,2,2,1024]{4,3,1,2,0:T(2,128)(2,1)S(1)}, u32[]{:S(2)}, u32[]{:S(2)}) %all-to-all-start.3) | async-done | bytes 524320 | tf_op jit(solution)/shard_map/all_to_all | solution.py:79
  189.6 4.7 %all-to-all-start.4 = ((bf16[32,2,2,8,1024]{4,3,1,2,0:T(8,128)(2,1)}), bf16[32,2,2,8,1024]{4,3,1,2,0:T(8,128)(2,1)}, u32[]{:S(2)}, u32[]{:S(2)}) async-start(bf16[32,2,2,8,1024]{4,3,1,2,0:T(8,128)(2,1)} %bitcast.68), calls=%async_computation.4 | async-start | bytes 4194304 | tf_op jit(solution)/shard_map/all_to_all | solution.py:79
  194.9 2.1 collective-permute-start.5
  199.0 24.3 %collective-permute-done.5 = bf16[256,1024]{1,0:T(8,128)(2,1)} collective-permute-done((bf16[256,1024]{1,0:T(8,128)(2,1)S(1)}, bf16[256,1024]{1,0:T(8,128)(2,1)}, u32[]{:S(2)}, u32[]{:S(2)}) %collective-permute-start.5) | collective-permute-done | bytes 524320 | tf_op jit(solution)/shard_map/ppermute | solution.py:105
  223.3 3.9 %all-to-all-done.4 = bf16[32,2,2,8,1024]{4,3,1,2,0:T(8,128)(2,1)} async-done(((bf16[32,2,2,8,1024]{4,3,1,2,0:T(8,128)(2,1)}), bf16[32,2,2,8,1024]{4,3,1,2,0:T(8,128)(2,1)}, u32[]{:S(2)}, u32[]{:S(2)}) %all-to-all-start.4) | async-done | bytes 2097184 | tf_op jit(solution)/shard_map/all_to_all | solution.py:79
  227.3 1.8 copy.66
  231.2 8.6 %all-to-all-start.5 = ((bf16[16,4,8,512]{3,2,1,0:T(8,128)(2,1)}), bf16[16,4,8,512]{3,2,1,0:T(8,128)(2,1)S(1)}, u32[]{:S(2)}, u32[]{:S(2)}) async-start(bf16[16,4,8,512]{3,2,1,0:T(8,128)(2,1)} %bitcast.27), calls=%async_computation.5 | async-start | bytes 1048576 | tf_op jit(solution)/shard_map/all_to_all | solution.py:79
  239.8 1.9 collective-permute-start.7
  241.7 9.8 %all-to-all-done.5 = bf16[16,4,8,512]{3,2,1,0:T(8,128)(2,1)S(1)} async-done(((bf16[16,4,8,512]{3,2,1,0:T(8,128)(2,1)}), bf16[16,4,8,512]{3,2,1,0:T(8,128)(2,1)S(1)}, u32[]{:S(2)}, u32[]{:S(2)}) %all-to-all-start.5) | async-done | bytes 524320 | tf_op jit(solution)/shard_map/all_to_all | solution.py:79
  252.6 21.7 %collective-permute-done.7 = bf16[256,1024]{1,0:T(8,128)(2,1)S(1)} collective-permute-done((bf16[256,1024]{1,0:T(8,128)(2,1)S(1)}, bf16[256,1024]{1,0:T(8,128)(2,1)S(1)}, u32[]{:S(2)}, u32[]{:S(2)}) %collective-permute-start.7) | collective-permute-done | bytes 524320 | tf_op jit(solution)/shard_map/ppermute | solution.py:105
  274.2 8.2 %all-to-all-start.6 = ((bf16[16,4,8,512]{3,2,1,0:T(8,128)(2,1)}), bf16[16,4,8,512]{3,2,1,0:T(8,128)(2,1)S(1)}, u32[]{:S(2)}, u32[]{:S(2)}) async-start(bf16[16,4,8,512]{3,2,1,0:T(8,128)(2,1)} %fusion.10), calls=%async_computation.6 | async-start | bytes 1048576 | tf_op jit(solution)/shard_map/all_to_all | solution.py:79
  284.9 27.0 %all-to-all-done.6 = bf16[16,4,8,512]{3,2,1,0:T(8,128)(2,1)S(1)} async-done(((bf16[16,4,8,512]{3,2,1,0:T(8,128)(2,1)}), bf16[16,4,8,512]{3,2,1,0:T(8,128)(2,1)S(1)}, u32[]{:S(2)}, u32[]{:S(2)}) %all-to-all-start.6) | async-done | bytes 524320 | tf_op jit(solution)/shard_map/all_to_all | solution.py:79
  (60 shorter events, 28.3 us)
Async XLA Ops:
  2.1 0.7 collective-permute-start
  3.6 57.6 %all-to-all-start = ((bf16[16,4,8,512]{3,2,1,0:T(8,128)(2,1)}), bf16[16,4,8,512]{3,2,1,0:T(8,128)(2,1)S(1)}, u32[]{:S(2)}, u32[]{:S(2)}) async-start(bf16[16,4,8,512]{3,2,1,0:T(8,128)(2,1)} %broadcast_in_dim.3), calls=%async_computation | async-start | bytes 1048576 | tf_op jit(solution)/shard_map/all_to_all | solution.py:79
  21.7 3.4 %collective-permute-start.1 = (bf16[256,1024]{1,0:T(8,128)(2,1)}, bf16[256,1024]{1,0:T(8,128)(2,1)S(1)}, u32[]{:S(2)}, u32[]{:S(2)}) collective-permute-start(bf16[256,1024]{1,0:T(8,128)(2,1)} %param.4), channel_id=1, source_target_pairs={{0,0},{1,1},{64,64},{65,65},{128,128},{129,129},{192,192},{193,193... | collective-permute-start | bytes 1572872 | tf_op jit(solution)/shard_map/ppermute | solution.py:97
  23.4 16.6 %collective-permute-start.3 = (bf16[256,1024]{1,0:T(8,128)(2,1)}, bf16[256,1024]{1,0:T(8,128)(2,1)S(1)}, u32[]{:S(2)}, u32[]{:S(2)}) collective-permute-start(bf16[256,1024]{1,0:T(8,128)(2,1)} %param.7), channel_id=1, source_target_pairs={{0,0},{1,1},{64,64},{65,65},{128,128},{129,129},{192,192},{193,193... | collective-permute-start | bytes 1572872 | tf_op jit(solution)/shard_map/ppermute | solution.py:97
  25.1 36.1 %collective-permute-start.2 = (bf16[256,1024]{1,0:T(8,128)(2,1)S(1)}, bf16[256,1024]{1,0:T(8,128)(2,1)S(1)}, u32[]{:S(2)}, u32[]{:S(2)}) collective-permute-start(bf16[256,1024]{1,0:T(8,128)(2,1)S(1)} %collective-permute-done.1), channel_id=1, source_target_pairs={{0,0},{1,1},{64,66},{65,67},{128,132},{129,133},{192,198},{193,199... | collective-permute-start | bytes 1572872 | tf_op jit(solution)/shard_map/ppermute | solution.py:101
  40.0 65.9 %collective-permute-start.4 = (bf16[256,1024]{1,0:T(8,128)(2,1)S(1)}, bf16[256,1024]{1,0:T(8,128)(2,1)S(1)}, u32[]{:S(2)}, u32[]{:S(2)}) collective-permute-start(bf16[256,1024]{1,0:T(8,128)(2,1)S(1)} %collective-permute-done.3), channel_id=1, source_target_pairs={{0,0},{1,1},{64,66},{65,67},{128,132},{129,133},{192,198},{193,199... | collective-permute-start | bytes 1572872 | tf_op jit(solution)/shard_map/ppermute | solution.py:101
  61.2 56.6 %copy-start.1 = (bf16[256,1024]{1,0:T(8,128)(2,1)}, bf16[256,1024]{1,0:T(8,128)(2,1)S(1)}, u32[]{:S(2)}) copy-start(bf16[256,1024]{1,0:T(8,128)(2,1)S(1)} %collective-permute-done.2) | copy-start | bytes 1572868
  62.2 55.4 %all-to-all-start.1 = ((bf16[16,4,8,512]{3,2,1,0:T(8,128)(2,1)}), bf16[16,4,8,512]{3,2,1,0:T(8,128)(2,1)S(1)}, u32[]{:S(2)}, u32[]{:S(2)}) async-start(bf16[16,4,8,512]{3,2,1,0:T(8,128)(2,1)} %fusion.11), calls=%async_computation.1 | async-start | bytes 1048576 | tf_op jit(solution)/shard_map/all_to_all | solution.py:79
  120.5 44.7 %all-to-all-start.2 = ((bf16[32,5,8,1024]{3,2,1,0:T(8,128)(2,1)}), bf16[32,5,8,1024]{3,2,1,0:T(8,128)(2,1)S(1)}, u32[]{:S(2)}, u32[]{:S(2)}) async-start(bf16[32,5,8,1024]{3,2,1,0:T(8,128)(2,1)} %pad_maximum_fusion), calls=%async_computation.2 | async-start | bytes 5242880 | tf_op jit(solution)/shard_map/all_to_all | solution.py:79
  168.3 3.3 %copy-start = (f32[2,32,2,8,1024]{4,3,2,1,0:T(8,128)}, f32[2,32,2,8,1024]{4,3,2,1,0:T(8,128)S(1)}, u32[]{:S(2)}) copy-start(f32[2,32,2,8,1024]{4,3,2,1,0:T(8,128)S(1)} %copy.59) | copy-start | bytes 12582916
  168.3 3.3 %copy-start.3 = (bf16[2,512,128]{2,1,0:T(8,128)(2,1)S(1)}, bf16[2,512,128]{2,1,0:T(8,128)(2,1)}, u32[]{:S(2)}) copy-start(bf16[2,512,128]{2,1,0:T(8,128)(2,1)} %reshape_reshape.3) | copy-start | bytes 786436
  173.6 16.0 %all-to-all-start.3 = ((bf16[32,2,2,2,1024]{4,3,1,2,0:T(2,128)(2,1)}), bf16[32,2,2,2,1024]{4,3,1,2,0:T(2,128)(2,1)S(1)}, u32[]{:S(2)}, u32[]{:S(2)}) async-start(bf16[32,2,2,2,1024]{4,3,1,2,0:T(2,128)(2,1)} %bitcast.64), calls=%async_computation.3 | async-start | bytes 1048576 | tf_op jit(solution)/shard_map/all_to_all | solution.py:79
  189.6 37.7 %all-to-all-start.4 = ((bf16[32,2,2,8,1024]{4,3,1,2,0:T(8,128)(2,1)}), bf16[32,2,2,8,1024]{4,3,1,2,0:T(8,128)(2,1)}, u32[]{:S(2)}, u32[]{:S(2)}) async-start(bf16[32,2,2,8,1024]{4,3,1,2,0:T(8,128)(2,1)} %bitcast.68), calls=%async_computation.4 | async-start | bytes 4194304 | tf_op jit(solution)/shard_map/all_to_all | solution.py:79
  194.9 28.4 %collective-permute-start.5 = (bf16[256,1024]{1,0:T(8,128)(2,1)S(1)}, bf16[256,1024]{1,0:T(8,128)(2,1)}, u32[]{:S(2)}, u32[]{:S(2)}) collective-permute-start(bf16[256,1024]{1,0:T(8,128)(2,1)S(1)} %reshape.77), channel_id=1, source_target_pairs={{0,0},{1,1},{66,64},{67,65},{132,128},{133,129},{198,192},{199,193... | collective-permute-start | bytes 1572872 | tf_op jit(solution)/shard_map/ppermute | solution.py:105
  199.0 30.5 %copy-start.2 = (bf16[256,1024]{1,0:T(8,128)(2,1)S(1)}, bf16[256,1024]{1,0:T(8,128)(2,1)}, u32[]{:S(2)}) copy-start(bf16[256,1024]{1,0:T(8,128)(2,1)} %copy-done.1) | copy-start | bytes 1572868
  231.2 20.3 %all-to-all-start.5 = ((bf16[16,4,8,512]{3,2,1,0:T(8,128)(2,1)}), bf16[16,4,8,512]{3,2,1,0:T(8,128)(2,1)S(1)}, u32[]{:S(2)}, u32[]{:S(2)}) async-start(bf16[16,4,8,512]{3,2,1,0:T(8,128)(2,1)} %bitcast.27), calls=%async_computation.5 | async-start | bytes 1048576 | tf_op jit(solution)/shard_map/all_to_all | solution.py:79
  239.8 34.4 %collective-permute-start.7 = (bf16[256,1024]{1,0:T(8,128)(2,1)S(1)}, bf16[256,1024]{1,0:T(8,128)(2,1)S(1)}, u32[]{:S(2)}, u32[]{:S(2)}) collective-permute-start(bf16[256,1024]{1,0:T(8,128)(2,1)S(1)} %bitcast.82), channel_id=1, source_target_pairs={{0,0},{1,1},{66,64},{67,65},{132,128},{133,129},{198,192},{199,193... | collective-permute-start | bytes 1572872 | tf_op jit(solution)/shard_map/ppermute | solution.py:105
  274.2 37.6 %all-to-all-start.6 = ((bf16[16,4,8,512]{3,2,1,0:T(8,128)(2,1)}), bf16[16,4,8,512]{3,2,1,0:T(8,128)(2,1)S(1)}, u32[]{:S(2)}, u32[]{:S(2)}) async-start(bf16[16,4,8,512]{3,2,1,0:T(8,128)(2,1)} %fusion.10), calls=%async_computation.6 | async-start | bytes 1048576 | tf_op jit(solution)/shard_map/all_to_all | solution.py:79
  282.5 30.1 %collective-permute-start.6 = (bf16[256,1024]{1,0:T(8,128)(2,1)}, bf16[256,1024]{1,0:T(8,128)(2,1)S(1)}, u32[]{:S(2)}, u32[]{:S(2)}) collective-permute-start(bf16[256,1024]{1,0:T(8,128)(2,1)} %collective-permute-done.5), channel_id=1, source_target_pairs={{0,0},{1,1},{64,64},{65,65},{128,128},{129,129},{192,192},{193,193... | collective-permute-start | bytes 1572872 | tf_op jit(solution)/shard_map/ppermute | solution.py:109
  284.2 28.4 %collective-permute-start.8 = (bf16[256,1024]{1,0:T(8,128)(2,1)S(1)}, bf16[256,1024]{1,0:T(8,128)(2,1)S(1)}, u32[]{:S(2)}, u32[]{:S(2)}) collective-permute-start(bf16[256,1024]{1,0:T(8,128)(2,1)S(1)} %collective-permute-done.7), channel_id=1, source_target_pairs={{0,0},{1,1},{64,64},{65,65},{128,128},{129,129},{192,192},{193,193... | collective-permute-start | bytes 1572872 | tf_op jit(solution)/shard_map/ppermute | solution.py:109
  312.0 0.7 collective-permute-start.9

commit v5 on v3

--- a/solution.py
+++ b/solution.py
@@ -26,6 +26,10 @@
 DEVICES = ("dp", "tensor")
 
 
+def back(pairs):
+    return [(b, a) for a, b in pairs]
+
+
 class Plan:
     def __init__(self):
         def index(xh, y, c, z, xl):
@@ -47,14 +51,12 @@
                     weights.append((index(xh2, y2, c2, z, xl), end))
                     place[label, 2 * z + xl] = end
         self.shuffle, self.mirror, self.weights = shuffle, mirror, weights
+        outward = dict(back(mirror)), dict(back(shuffle))
+        self.home = [(end, outward[1][mid]) for end, mid in outward[0].items()]
         self.layers = [[place[t, k] for k in range(32)] for t in range(16)]
 
 
 PLAN = Plan()
-
-
-def back(pairs):
-    return [(b, a) for a, b in pairs]
 
 
 def exchange(x):
@@ -75,10 +77,16 @@
     return lax.ppermute(x, DEVICES, PLAN.mirror)
 
 
+def unmirror(x):
+    return lax.ppermute(x, DEVICES, back(PLAN.mirror))
+
+
+def unshuffle(x):
+    return lax.ppermute(x, DEVICES, back(PLAN.shuffle))
+
+
 def to_store(x):
-    return lax.ppermute(
-        lax.ppermute(x, DEVICES, back(PLAN.mirror)), DEVICES, back(PLAN.shuffle)
-    )
+    return lax.ppermute(x, DEVICES, PLAN.home)
 
 
 def gather_rows(up_blocks, down_blocks):
@@ -96,7 +104,7 @@
     return rows.reshape(n, nb, height // n, width).transpose(1, 0, 2, 3).reshape(nb, height, width)
 
 
-def sum_rows(up_term, down_term, gate):
+def sum_rows(up_term, down_term):
     n = lax.axis_size("dp")
     nb, hu, wu = up_term.shape
     hd, wd = down_term.shape[1:]
@@ -105,7 +113,7 @@
     d = down_term.astype(BF16).reshape(nb, n, ru, wu).transpose(1, 0, 2, 3)
     u = lax.ppermute(u, DEVICES, back(PLAN.weights))
     d = lax.ppermute(d, DEVICES, back(PLAN.weights))
-    both = after(jnp.concatenate([u, d], axis=1), gate)
+    both = jnp.concatenate([u, d], axis=1)
     got = lax.all_to_all(both, "dp", split_axis=0, concat_axis=0, tiled=True)
     s = jnp.sum(got.astype(F32), axis=0)
     return s[:nb], s[nb:].reshape(nb, rd, wd)
@@ -116,39 +124,35 @@
     t = features.shape[1]
     n = NB // nb
     moved = shuffle(features)
+    cot = mirror(shuffle(out_cotangent))
     up_rows, down_rows = gather_rows(up_blocks, down_blocks)
-    moved_cot = shuffle(after(out_cotangent, moved, up_rows))
-    x_flat = mirror(moved)
     up = whole(up_rows, BIN, BOUT)
-    cot = mirror(after(moved_cot, x_flat))
-    x = after(x_flat, moved_cot).reshape(nb, BIN, t)
+    x_flat = mirror(after(moved, cot))
+    dblock = exchange(cot.reshape(nb, n, nb, J_DN, t).transpose(1, 2, 0, 3, 4))
+    x = after(x_flat, dblock).reshape(nb, BIN, t)
     pre = jnp.einsum("bkn,bkt->bnt", up, x, preferred_element_type=F32).astype(BF16)
     permuted = exchange(pre.reshape(nb, n, nb, J_UP, t).transpose(1, 2, 0, 3, 4))
-    down = whole(after(down_rows, up), BOUT, BIN)
-    cot = after(cot, permuted).reshape(nb, n, nb, J_DN, t).transpose(1, 2, 0, 3, 4)
-    dblock = exchange(cot)
+    down = whole(after(down_rows, x_flat), BOUT, BIN)
     permuted = permuted.transpose(1, 0, 2, 3, 4).reshape(nb, BOUT, t)
     pf = permuted.astype(F32)
     act = gelu_value(pf).astype(BF16)
     blockout = jnp.einsum("gmc,gmt->gct", down, act, preferred_element_type=F32).astype(BF16)
     blockout = blockout.reshape(nb, n, nb, J_DN, t).transpose(1, 2, 0, 3, 4)
-    mixed = exchange(after(blockout, dblock))
+    mixed = exchange(blockout)
     dblock = dblock.transpose(1, 0, 2, 3, 4).reshape(nb, BIN, t)
     dact = jnp.einsum("gmc,gct->gmt", down, dblock, preferred_element_type=F32)
     dperm = (dact * gelu_slope(pf)).astype(BF16)
     dperm = dperm.reshape(nb, n, nb, J_UP, t).transpose(1, 2, 0, 3, 4)
     dpre = exchange(after(dperm, mixed))
-    mixed = to_store(mixed.transpose(1, 0, 2, 3, 4).reshape(nb * BIN, t))
+    mixed = unmirror(mixed.transpose(1, 0, 2, 3, 4).reshape(nb * BIN, t))
     down_term = jnp.einsum("gmt,gct->gmc", act, dblock, preferred_element_type=F32)
-    dpre = dpre.transpose(1, 0, 2, 3, 4).reshape(nb, BOUT, t)
+    dpre = after(dpre, mixed).transpose(1, 0, 2, 3, 4).reshape(nb, BOUT, t)
     fgrad = jnp.einsum("bkn,bnt->bkt", up, dpre, preferred_element_type=F32).astype(BF16)
     fgrad = fgrad.reshape(nb * BIN, t)
     dpre = after(dpre, fgrad)
     up_term = jnp.einsum("bkt,bnt->bkn", x, dpre, preferred_element_type=F32)
-    fgrad = lax.ppermute(fgrad, DEVICES, back(PLAN.mirror))
-    up_grad, down_grad = sum_rows(up_term, down_term, fgrad)
-    fgrad = lax.ppermute(fgrad, DEVICES, back(PLAN.shuffle))
-    return mixed, fgrad, up_grad, down_grad
+    up_grad, down_grad = sum_rows(up_term, down_term)
+    return unshuffle(mixed), to_store(fgrad), up_grad, down_grad
 
 
 def solution(mesh):

time: 319 us -> 297 us (0.931)
  the two profiles are of different devices: /device:TPU:102 before, /device:TPU:32 now
where the time goes in v5:
time: 297 us; the launch traced here: 296 us
  starting transfers between devices  154 us (52%)
  waiting for transfers between devices  109 us (37%)
  local copies, waits for them, and re-layouts  16.8 us (6%)
  matrix products  9.33 us (3%)
  other arithmetic  5.3 us (2%)
    all_to_all x4, starting transfers between devices, exchange(): lax.all_to_all(x, DEVICES, split_axis=0, concat_axis=0, tiled=True, axis_...  44.2 us
    all_to_all x1, starting transfers between devices, sum_rows(): got = lax.all_to_all(both, 'dp', split_axis=0, concat_axis=0, tiled=True)  41 us
    all_to_all x4, waiting for transfers between devices, exchange(): lax.all_to_all(x, DEVICES, split_axis=0, concat_axis=0, tiled=True, axis_...  27.1 us
    ppermute x2, starting transfers between devices, whole(): rows = lax.ppermute(rows, DEVICES, PLAN.weights)  23.8 us
    ppermute x2, waiting for transfers between devices, whole(): rows = lax.ppermute(rows, DEVICES, PLAN.weights)  18.2 us
    ppermute x2, starting transfers between devices, mirror(): return lax.ppermute(x, DEVICES, PLAN.mirror)  15.1 us
    ppermute x1, waiting for transfers between devices, sum_rows(): u = lax.ppermute(u, DEVICES, back(PLAN.weights))  14.6 us
    ppermute x1, waiting for transfers between devices, unmirror(): return lax.ppermute(x, DEVICES, back(PLAN.mirror))  13.4 us
  transfers between devices with their start and end apart: 17, of which 10 were waited for; matrix products, arithmetic and copies ran while one was open for 7% of the time, Pallas kernels for 0%

profile of v5, /device:TPU:32, one launch (start us, length us, event | category | flops | bytes accessed | tf_op | source)
XLA Modules:
  0.0 295.6 jit_solution(13726653570654164232)
XLA Ops:
  0.6 3.5 %collective-permute-start.1 = (bf16[256,1024]{1,0:T(8,128)(2,1)}, bf16[256,1024]{1,0:T(8,128)(2,1)S(1)}, u32[]{:S(2)}, u32[]{:S(2)}) collective-permute-start(bf16[256,1024]{1,0:T(8,128)(2,1)} %param.7), channel_id=1, source_target_pairs={{0,0},{1,1},{32,32},{33,33},{64,64},{65,65},{96,96},{97,97},{128,1... | collective-permute-start | bytes 1572872 | tf_op jit(solution)/shard_map/ppermute | solution.py:73
  4.1 3.5 %collective-permute-start = (bf16[256,1024]{1,0:T(8,128)(2,1)}, bf16[256,1024]{1,0:T(8,128)(2,1)S(1)}, u32[]{:S(2)}, u32[]{:S(2)}) collective-permute-start(bf16[256,1024]{1,0:T(8,128)(2,1)} %param.4), channel_id=1, source_target_pairs={{0,0},{1,1},{32,32},{33,33},{64,64},{65,65},{96,96},{97,97},{128,1... | collective-permute-start | bytes 1572872 | tf_op jit(solution)/shard_map/ppermute | solution.py:73
  8.4 11.5 %collective-permute-done.1 = bf16[256,1024]{1,0:T(8,128)(2,1)S(1)} collective-permute-done((bf16[256,1024]{1,0:T(8,128)(2,1)}, bf16[256,1024]{1,0:T(8,128)(2,1)S(1)}, u32[]{:S(2)}, u32[]{:S(2)}) %collective-permute-start.1) | collective-permute-done | bytes 524320 | tf_op jit(solution)/shard_map/ppermute | solution.py:73
  19.9 10.8 %collective-permute-start.2 = (bf16[256,1024]{1,0:T(8,128)(2,1)S(1)}, bf16[256,1024]{1,0:T(8,128)(2,1)S(1)}, u32[]{:S(2)}, u32[]{:S(2)}) collective-permute-start(bf16[256,1024]{1,0:T(8,128)(2,1)S(1)} %collective-permute-done.1), channel_id=1, source_target_pairs={{0,0},{1,1},{32,48},{33,49},{64,66},{65,67},{96,114},{97,115},{128... | collective-permute-start | bytes 1572872 | tf_op jit(solution)/shard_map/ppermute | solution.py:77
  32.3 6.5 %all-to-all-start = ((bf16[16,4,8,512]{3,2,1,0:T(8,128)(2,1)}), bf16[16,4,8,512]{3,2,1,0:T(8,128)(2,1)S(1)}, u32[]{:S(2)}, u32[]{:S(2)}) async-start(bf16[16,4,8,512]{3,2,1,0:T(8,128)(2,1)} %broadcast_in_dim.3), calls=%async_computation | async-start | bytes 1048576 | tf_op jit(solution)/shard_map/all_to_all | solution.py:97
  38.8 12.0 %collective-permute-done.2 = bf16[256,1024]{1,0:T(8,128)(2,1)S(1)} collective-permute-done((bf16[256,1024]{1,0:T(8,128)(2,1)S(1)}, bf16[256,1024]{1,0:T(8,128)(2,1)S(1)}, u32[]{:S(2)}, u32[]{:S(2)}) %collective-permute-start.2) | collective-permute-done | bytes 524320 | tf_op jit(solution)/shard_map/ppermute | solution.py:77
  50.9 4.3 %collective-permute-start.3 = (bf16[256,1024]{1,0:T(8,128)(2,1)S(1)}, bf16[256,1024]{1,0:T(8,128)(2,1)S(1)}, u32[]{:S(2)}, u32[]{:S(2)}) collective-permute-start(bf16[256,1024]{1,0:T(8,128)(2,1)S(1)} %collective-permute-done), channel_id=1, source_target_pairs={{0,0},{1,1},{32,48},{33,49},{64,66},{65,67},{96,114},{97,115},{128... | collective-permute-start | bytes 1572872 | tf_op jit(solution)/shard_map/ppermute | solution.py:77
  56.7 14.4 %all-to-all-start.1 = ((bf16[32,2,2,2,1024]{4,3,2,1,0:T(2,128)(2,1)}), bf16[32,2,2,2,1024]{4,3,2,1,0:T(2,128)(2,1)S(1)}, u32[]{:S(2)}, u32[]{:S(2)}) async-start(bf16[32,2,2,2,1024]{4,3,2,1,0:T(2,128)(2,1)} %copy.36), calls=%async_computation.1 | async-start | bytes 1048576 | tf_op jit(solution)/shard_map/all_to_all | solution.py:63
  71.9 18.3 %collective-permute-start.5 = (bf16[16,2,8,512]{3,2,0,1:T(8,128)(2,1)S(1)}, bf16[16,2,8,512]{3,2,0,1:T(8,128)(2,1)S(1)}, u32[]{:S(2)}, u32[]{:S(2)}) collective-permute-start(bf16[16,2,8,512]{3,2,0,1:T(8,128)(2,1)S(1)} %copy.50), channel_id=1, source_target_pairs={{0,0},{1,1},{32,48},{33,49},{64,66},{65,67},{96,114},{97,115},{128... | collective-permute-start | bytes 786440 | tf_op jit(solution)/shard_map/ppermute | solution.py:103
  90.2 7.1 %collective-permute-done.5 = bf16[16,2,8,512]{3,2,0,1:T(8,128)(2,1)S(1)} collective-permute-done((bf16[16,2,8,512]{3,2,0,1:T(8,128)(2,1)S(1)}, bf16[16,2,8,512]{3,2,0,1:T(8,128)(2,1)S(1)}, u32[]{:S(2)}, u32[]{:S(2)}) %collective-permute-start.5) | collective-permute-done | bytes 262176 | tf_op jit(solution)/shard_map/ppermute | solution.py:103
  99.6 18.0 %all-to-all-start.2 = ((bf16[32,2,2,8,1024]{4,3,1,2,0:T(8,128)(2,1)}), bf16[32,2,2,8,1024]{4,3,1,2,0:T(8,128)(2,1)S(1)}, u32[]{:S(2)}, u32[]{:S(2)}) async-start(bf16[32,2,2,8,1024]{4,3,1,2,0:T(8,128)(2,1)} %bitcast.66), calls=%async_computation.2 | async-start | bytes 4194304 | tf_op jit(solution)/shard_map/all_to_all | solution.py:63
  117.6 5.5 %collective-permute-start.4 = (bf16[16,2,8,512]{3,2,1,0:T(8,128)(2,1)}, bf16[16,2,8,512]{3,2,1,0:T(8,128)(2,1)S(1)}, u32[]{:S(2)}, u32[]{:S(2)}) collective-permute-start(bf16[16,2,8,512]{3,2,1,0:T(8,128)(2,1)} %get-tuple-element.11), channel_id=1, source_target_pairs={{0,0},{1,1},{32,48},{33,49},{64,66},{65,67},{96,114},{97,115},{128... | collective-permute-start | bytes 786440 | tf_op jit(solution)/shard_map/ppermute | solution.py:103
  124.4 11.1 %collective-permute-done.4 = bf16[16,2,8,512]{3,2,1,0:T(8,128)(2,1)S(1)} collective-permute-done((bf16[16,2,8,512]{3,2,1,0:T(8,128)(2,1)}, bf16[16,2,8,512]{3,2,1,0:T(8,128)(2,1)S(1)}, u32[]{:S(2)}, u32[]{:S(2)}) %collective-permute-start.4) | collective-permute-done | bytes 262176 | tf_op jit(solution)/shard_map/ppermute | solution.py:103
  135.8 16.3 %all-to-all-done.2 = bf16[32,2,2,8,1024]{4,3,1,2,0:T(8,128)(2,1)S(1)} async-done(((bf16[32,2,2,8,1024]{4,3,1,2,0:T(8,128)(2,1)}), bf16[32,2,2,8,1024]{4,3,1,2,0:T(8,128)(2,1)S(1)}, u32[]{:S(2)}, u32[]{:S(2)}) %all-to-all-start.2) | async-done | bytes 2097184 | tf_op jit(solution)/shard_map/all_to_all | solution.py:63
  158.5 5.8 %all-to-all-start.3 = ((bf16[32,2,2,2,1024]{4,3,1,2,0:T(2,128)(2,1)}), bf16[32,2,2,2,1024]{4,3,1,2,0:T(2,128)(2,1)S(1)}, u32[]{:S(2)}, u32[]{:S(2)}) async-start(bf16[32,2,2,2,1024]{4,3,1,2,0:T(2,128)(2,1)} %bitcast.60), calls=%async_computation.3 | async-start | bytes 1048576 | tf_op jit(solution)/shard_map/all_to_all | solution.py:63
  164.3 5.1 %fusion.5 = bf16[2,512,1024]{2,1,0:T(8,128)(2,1)S(1)} fusion(f32[2,32,2,8,1024]{4,3,2,1,0:T(8,128)} %copy-done, f32[2,512,1024]{2,1,0:T(8,128)} %get-tuple-element.17, bf16[2,512,128]{2,1,0:T(8,128)(2,1)S(1)} %bitcast.76, bf16[2,128,1024]{2,1,0:T(8,128)(2,1)} %reshape.68), kind=kOutput, calls=%fused_computation.6 | convolution fusion | flops 276824064 | bytes 11272192 | tf_op jit(solution)/shard_map/gmc,gct->gmt/dot_general | solution.py:143
  170.9 4.2 %all-to-all-done.3 = bf16[32,2,2,2,1024]{4,3,1,2,0:T(2,128)(2,1)S(1)} async-done(((bf16[32,2,2,2,1024]{4,3,1,2,0:T(2,128)(2,1)}), bf16[32,2,2,2,1024]{4,3,1,2,0:T(2,128)(2,1)S(1)}, u32[]{:S(2)}, u32[]{:S(2)}) %all-to-all-start.3) | async-done | bytes 524320 | tf_op jit(solution)/shard_map/all_to_all | solution.py:63
  175.0 6.0 %all-to-all-start.4 = ((bf16[32,2,2,8,1024]{4,3,1,2,0:T(8,128)(2,1)}), bf16[32,2,2,8,1024]{4,3,1,2,0:T(8,128)(2,1)}, u32[]{:S(2)}, u32[]{:S(2)}) async-start(bf16[32,2,2,8,1024]{4,3,1,2,0:T(8,128)(2,1)} %bitcast.65), calls=%async_computation.4 | async-start | bytes 4194304 | tf_op jit(solution)/shard_map/all_to_all | solution.py:63
  187.5 4.9 %collective-permute-start.10 = (bf16[16,2,8,512]{3,2,1,0:T(8,128)(2,1)S(1)}, bf16[16,2,8,512]{3,2,1,0:T(8,128)(2,1)S(1)}, u32[]{:S(2)}, u32[]{:S(2)}) collective-permute-start(bf16[16,2,8,512]{3,2,1,0:T(8,128)(2,1)S(1)} %bitcast.78), channel_id=1, source_target_pairs={{0,0},{1,1},{48,32},{49,33},{66,64},{67,65},{114,96},{115,97},{132... | collective-permute-start | bytes 786440 | tf_op jit(solution)/shard_map/ppermute | solution.py:115
  192.5 13.4 %collective-permute-done.6 = bf16[256,1024]{1,0:T(8,128)(2,1)S(1)} collective-permute-done((bf16[256,1024]{1,0:T(8,128)(2,1)}, bf16[256,1024]{1,0:T(8,128)(2,1)S(1)}, u32[]{:S(2)}, u32[]{:S(2)}) %collective-permute-start.6) | collective-permute-done | bytes 524320 | tf_op jit(solution)/shard_map/ppermute | solution.py:81
  205.9 6.6 %all-to-all-done.4 = bf16[32,2,2,8,1024]{4,3,1,2,0:T(8,128)(2,1)} async-done(((bf16[32,2,2,8,1024]{4,3,1,2,0:T(8,128)(2,1)}), bf16[32,2,2,8,1024]{4,3,1,2,0:T(8,128)(2,1)}, u32[]{:S(2)}, u32[]{:S(2)}) %all-to-all-start.4) | async-done | bytes 2097184 | tf_op jit(solution)/shard_map/all_to_all | solution.py:63
  223.9 14.6 %collective-permute-done.9 = bf16[16,2,8,512]{3,2,1,0:T(8,128)(2,1)S(1)} collective-permute-done((bf16[16,2,8,512]{3,2,1,0:T(8,128)(2,1)S(1)}, bf16[16,2,8,512]{3,2,1,0:T(8,128)(2,1)S(1)}, u32[]{:S(2)}, u32[]{:S(2)}) %collective-permute-start.9) | collective-permute-done | bytes 262176 | tf_op jit(solution)/shard_map/ppermute | solution.py:114
  239.4 41.0 %all-to-all-start.5 = ((bf16[16,4,8,512]{3,2,1,0:T(8,128)(2,1)}), bf16[16,4,8,512]{3,2,1,0:T(8,128)(2,1)S(1)}, u32[]{:S(2)}, u32[]{:S(2)}) async-start(bf16[16,4,8,512]{3,2,1,0:T(8,128)(2,1)} %pad_maximum_fusion), calls=%async_computation.5 | async-start | bytes 1048576 | tf_op jit(solution)/shard_map/all_to_all | solution.py:117
  280.4 12.3 %all-to-all-done.5 = bf16[16,4,8,512]{3,2,1,0:T(8,128)(2,1)S(1)} async-done(((bf16[16,4,8,512]{3,2,1,0:T(8,128)(2,1)}), bf16[16,4,8,512]{3,2,1,0:T(8,128)(2,1)S(1)}, u32[]{:S(2)}, u32[]{:S(2)}) %all-to-all-start.5) | async-done | bytes 524320 | tf_op jit(solution)/shard_map/all_to_all | solution.py:117
  (56 shorter events, 37.9 us)
Async XLA Ops:
  0.6 19.3 %collective-permute-start.1 = (bf16[256,1024]{1,0:T(8,128)(2,1)}, bf16[256,1024]{1,0:T(8,128)(2,1)S(1)}, u32[]{:S(2)}, u32[]{:S(2)}) collective-permute-start(bf16[256,1024]{1,0:T(8,128)(2,1)} %param.7), channel_id=1, source_target_pairs={{0,0},{1,1},{32,32},{33,33},{64,64},{65,65},{96,96},{97,97},{128,1... | collective-permute-start | bytes 1572872 | tf_op jit(solution)/shard_map/ppermute | solution.py:73
  4.1 34.7 %collective-permute-start = (bf16[256,1024]{1,0:T(8,128)(2,1)}, bf16[256,1024]{1,0:T(8,128)(2,1)S(1)}, u32[]{:S(2)}, u32[]{:S(2)}) collective-permute-start(bf16[256,1024]{1,0:T(8,128)(2,1)} %param.4), channel_id=1, source_target_pairs={{0,0},{1,1},{32,32},{33,33},{64,64},{65,65},{96,96},{97,97},{128,1... | collective-permute-start | bytes 1572872 | tf_op jit(solution)/shard_map/ppermute | solution.py:73
  19.9 31.0 %collective-permute-start.2 = (bf16[256,1024]{1,0:T(8,128)(2,1)S(1)}, bf16[256,1024]{1,0:T(8,128)(2,1)S(1)}, u32[]{:S(2)}, u32[]{:S(2)}) collective-permute-start(bf16[256,1024]{1,0:T(8,128)(2,1)S(1)} %collective-permute-done.1), channel_id=1, source_target_pairs={{0,0},{1,1},{32,48},{33,49},{64,66},{65,67},{96,114},{97,115},{128... | collective-permute-start | bytes 1572872 | tf_op jit(solution)/shard_map/ppermute | solution.py:77
  32.3 24.4 %all-to-all-start = ((bf16[16,4,8,512]{3,2,1,0:T(8,128)(2,1)}), bf16[16,4,8,512]{3,2,1,0:T(8,128)(2,1)S(1)}, u32[]{:S(2)}, u32[]{:S(2)}) async-start(bf16[16,4,8,512]{3,2,1,0:T(8,128)(2,1)} %broadcast_in_dim.3), calls=%async_computation | async-start | bytes 1048576 | tf_op jit(solution)/shard_map/all_to_all | solution.py:97
  50.9 39.3 %collective-permute-start.3 = (bf16[256,1024]{1,0:T(8,128)(2,1)S(1)}, bf16[256,1024]{1,0:T(8,128)(2,1)S(1)}, u32[]{:S(2)}, u32[]{:S(2)}) collective-permute-start(bf16[256,1024]{1,0:T(8,128)(2,1)S(1)} %collective-permute-done), channel_id=1, source_target_pairs={{0,0},{1,1},{32,48},{33,49},{64,66},{65,67},{96,114},{97,115},{128... | collective-permute-start | bytes 1572872 | tf_op jit(solution)/shard_map/ppermute | solution.py:77
  56.7 33.5 %all-to-all-start.1 = ((bf16[32,2,2,2,1024]{4,3,2,1,0:T(2,128)(2,1)}), bf16[32,2,2,2,1024]{4,3,2,1,0:T(2,128)(2,1)S(1)}, u32[]{:S(2)}, u32[]{:S(2)}) async-start(bf16[32,2,2,2,1024]{4,3,2,1,0:T(2,128)(2,1)} %copy.36), calls=%async_computation.1 | async-start | bytes 1048576 | tf_op jit(solution)/shard_map/all_to_all | solution.py:63
  71.9 25.4 %collective-permute-start.5 = (bf16[16,2,8,512]{3,2,0,1:T(8,128)(2,1)S(1)}, bf16[16,2,8,512]{3,2,0,1:T(8,128)(2,1)S(1)}, u32[]{:S(2)}, u32[]{:S(2)}) collective-permute-start(bf16[16,2,8,512]{3,2,0,1:T(8,128)(2,1)S(1)} %copy.50), channel_id=1, source_target_pairs={{0,0},{1,1},{32,48},{33,49},{64,66},{65,67},{96,114},{97,115},{128... | collective-permute-start | bytes 786440 | tf_op jit(solution)/shard_map/ppermute | solution.py:103
  90.2 9.4 %copy-start.1 = (bf16[256,1024]{1,0:T(8,128)(2,1)}, bf16[256,1024]{1,0:T(8,128)(2,1)S(1)}, u32[]{:S(2)}) copy-start(bf16[256,1024]{1,0:T(8,128)(2,1)S(1)} %collective-permute-done.3) | copy-start | bytes 1572868
  97.3 2.3 copy-start.3
  99.6 52.5 %all-to-all-start.2 = ((bf16[32,2,2,8,1024]{4,3,1,2,0:T(8,128)(2,1)}), bf16[32,2,2,8,1024]{4,3,1,2,0:T(8,128)(2,1)S(1)}, u32[]{:S(2)}, u32[]{:S(2)}) async-start(bf16[32,2,2,8,1024]{4,3,1,2,0:T(8,128)(2,1)} %bitcast.66), calls=%async_computation.2 | async-start | bytes 4194304 | tf_op jit(solution)/shard_map/all_to_all | solution.py:63
  117.6 18.0 %collective-permute-start.4 = (bf16[16,2,8,512]{3,2,1,0:T(8,128)(2,1)}, bf16[16,2,8,512]{3,2,1,0:T(8,128)(2,1)S(1)}, u32[]{:S(2)}, u32[]{:S(2)}) collective-permute-start(bf16[16,2,8,512]{3,2,1,0:T(8,128)(2,1)} %get-tuple-element.11), channel_id=1, source_target_pairs={{0,0},{1,1},{32,48},{33,49},{64,66},{65,67},{96,114},{97,115},{128... | collective-permute-start | bytes 786440 | tf_op jit(solution)/shard_map/ppermute | solution.py:103
  153.2 3.3 %copy-start = (f32[2,32,2,8,1024]{4,3,2,1,0:T(8,128)}, f32[2,32,2,8,1024]{4,3,2,1,0:T(8,128)S(1)}, u32[]{:S(2)}) copy-start(f32[2,32,2,8,1024]{4,3,2,1,0:T(8,128)S(1)} %copy.39) | copy-start | bytes 12582916
  158.5 16.5 %all-to-all-start.3 = ((bf16[32,2,2,2,1024]{4,3,1,2,0:T(2,128)(2,1)}), bf16[32,2,2,2,1024]{4,3,1,2,0:T(2,128)(2,1)S(1)}, u32[]{:S(2)}, u32[]{:S(2)}) async-start(bf16[32,2,2,2,1024]{4,3,1,2,0:T(2,128)(2,1)} %bitcast.60), calls=%async_computation.3 | async-start | bytes 1048576 | tf_op jit(solution)/shard_map/all_to_all | solution.py:63
  175.0 37.5 %all-to-all-start.4 = ((bf16[32,2,2,8,1024]{4,3,1,2,0:T(8,128)(2,1)}), bf16[32,2,2,8,1024]{4,3,1,2,0:T(8,128)(2,1)}, u32[]{:S(2)}, u32[]{:S(2)}) async-start(bf16[32,2,2,8,1024]{4,3,1,2,0:T(8,128)(2,1)} %bitcast.65), calls=%async_computation.4 | async-start | bytes 4194304 | tf_op jit(solution)/shard_map/all_to_all | solution.py:63
  182.4 31.9 %copy-start.4 = (bf16[16,2,8,512]{3,2,0,1:T(8,128)(2,1)S(1)}, bf16[16,2,8,512]{3,2,0,1:T(8,128)(2,1)}, u32[]{:S(2)}) copy-start(bf16[16,2,8,512]{3,2,0,1:T(8,128)(2,1)} %copy-done.3) | copy-start | bytes 786436
  182.4 23.5 %collective-permute-start.6 = (bf16[256,1024]{1,0:T(8,128)(2,1)}, bf16[256,1024]{1,0:T(8,128)(2,1)S(1)}, u32[]{:S(2)}, u32[]{:S(2)}) collective-permute-start(bf16[256,1024]{1,0:T(8,128)(2,1)} %reshape.67), channel_id=1, source_target_pairs={{0,0},{1,1},{48,32},{49,33},{66,64},{67,65},{114,96},{115,97},{132... | collective-permute-start | bytes 1572872 | tf_op jit(solution)/shard_map/ppermute | solution.py:81
  187.3 27.4 %copy-start.2 = (bf16[256,1024]{1,0:T(8,128)(2,1)S(1)}, bf16[256,1024]{1,0:T(8,128)(2,1)}, u32[]{:S(2)}) copy-start(bf16[256,1024]{1,0:T(8,128)(2,1)} %copy-done.1) | copy-start | bytes 1572868
  187.5 36.4 %collective-permute-start.10 = (bf16[16,2,8,512]{3,2,1,0:T(8,128)(2,1)S(1)}, bf16[16,2,8,512]{3,2,1,0:T(8,128)(2,1)S(1)}, u32[]{:S(2)}, u32[]{:S(2)}) collective-permute-start(bf16[16,2,8,512]{3,2,1,0:T(8,128)(2,1)S(1)} %bitcast.78), channel_id=1, source_target_pairs={{0,0},{1,1},{48,32},{49,33},{66,64},{67,65},{114,96},{115,97},{132... | collective-permute-start | bytes 786440 | tf_op jit(solution)/shard_map/ppermute | solution.py:115
  215.6 22.9 %collective-permute-start.9 = (bf16[16,2,8,512]{3,2,1,0:T(8,128)(2,1)S(1)}, bf16[16,2,8,512]{3,2,1,0:T(8,128)(2,1)S(1)}, u32[]{:S(2)}, u32[]{:S(2)}) collective-permute-start(bf16[16,2,8,512]{3,2,1,0:T(8,128)(2,1)S(1)} %bitcast.79), channel_id=1, source_target_pairs={{0,0},{1,1},{48,32},{49,33},{66,64},{67,65},{114,96},{115,97},{132... | collective-permute-start | bytes 786440 | tf_op jit(solution)/shard_map/ppermute | solution.py:114
  217.6 62.8 %collective-permute-start.7 = (bf16[256,1024]{1,0:T(8,128)(2,1)S(1)}, bf16[256,1024]{1,0:T(8,128)(2,1)S(1)}, u32[]{:S(2)}, u32[]{:S(2)}) collective-permute-start(bf16[256,1024]{1,0:T(8,128)(2,1)S(1)} %collective-permute-done.6), channel_id=1, source_target_pairs={{0,0},{1,1},{32,32},{33,33},{64,64},{65,65},{96,96},{97,97},{128,1... | collective-permute-start | bytes 1572872 | tf_op jit(solution)/shard_map/ppermute | solution.py:85
  220.6 59.8 %collective-permute-start.8 = (bf16[256,1024]{1,0:T(8,128)(2,1)S(1)}, bf16[256,1024]{1,0:T(8,128)(2,1)S(1)}, u32[]{:S(2)}, u32[]{:S(2)}) collective-permute-start(bf16[256,1024]{1,0:T(8,128)(2,1)S(1)} %bitcast.77), channel_id=1, source_target_pairs={{0,0},{1,1},{48,32},{49,33},{66,64},{67,65},{114,96},{115,97},{132... | collective-permute-start | bytes 1572872 | tf_op jit(solution)/shard_map/ppermute | solution.py:89
  239.4 53.4 %all-to-all-start.5 = ((bf16[16,4,8,512]{3,2,1,0:T(8,128)(2,1)}), bf16[16,4,8,512]{3,2,1,0:T(8,128)(2,1)S(1)}, u32[]{:S(2)}, u32[]{:S(2)}) async-start(bf16[16,4,8,512]{3,2,1,0:T(8,128)(2,1)} %pad_maximum_fusion), calls=%async_computation.5 | async-start | bytes 1048576 | tf_op jit(solution)/shard_map/all_to_all | solution.py:117

commit v6 on v5

v6 whole, which is shorter than its diff:
```python
import jax
import jax.numpy as jnp
from jax import lax
from jax.sharding import PartitionSpec as P

NB = 64
BIN = 128
BOUT = 512
J_UP = 8
J_DN = 2
F32 = jnp.float32
BF16 = jnp.bfloat16


def gelu_value(v):
    return 0.5 * v * (1.0 + lax.erf(v * 0.7071067811865476))


def gelu_slope(v):
    return (
        0.5 * (1.0 + lax.erf(v * 0.7071067811865476))
        + v * jnp.exp(-0.5 * v * v) * 0.3989422804014327
    )


DEVICES = ("dp", "tensor")


def back(pairs):
    return [(b, a) for a, b in pairs]


class Plan:
    def __init__(self):
        def index(xh, y, c, z, xl):
            return (((xh * 4 + y) * 2 + c) * 16 + z) * 2 + xl

        shuffle, mirror, weights, place = [], [], [], {}
        for z in range(16):
            for t in range(16):
                xh, y, c = t >> 3, (t >> 1) & 3, t & 1
                label = 8 * c + 4 * xh + y
                moved = (label + z) % 16
                c2, xh2, y2 = moved >> 3, (moved >> 2) & 1, moved & 3
                for xl in range(2):
                    xl2 = xl if xh2 == xh else 1 - xl
                    mid = index(xh2, y2, c2, z, xl2)
                    end = index(xh2, y2, c2, label, xl2)
                    shuffle.append((index(xh, y, c, z, xl), mid))
                    mirror.append((mid, end))
                    weights.append((index(xh2, y2, c2, z, xl), end))
                    place[label, 2 * z + xl] = end
        self.shuffle, self.mirror, self.weights = shuffle, mirror, weights
        outward = dict(back(mirror)), dict(back(shuffle))
        self.home = [(end, outward[1][mid]) for end, mid in outward[0].items()]
        self.layers = [[place[t, k] for k in range(32)] for t in range(16)]


PLAN = Plan()


def exchange(x):
    return lax.all_to_all(
        x, DEVICES, split_axis=0, concat_axis=0, tiled=True, axis_index_groups=PLAN.layers
    )


def after(x, *others):
    return lax.optimization_barrier((x,) + others)[0]


def shuffle(x):
    return lax.ppermute(x, DEVICES, PLAN.shuffle)


def mirror(x):
    return lax.ppermute(x, DEVICES, PLAN.mirror)


def unmirror(x):
    return lax.ppermute(x, DEVICES, back(PLAN.mirror))


def unshuffle(x):
    return lax.ppermute(x, DEVICES, back(PLAN.shuffle))


def to_store(x):
    return lax.ppermute(x, DEVICES, PLAN.home)


def gather_rows(up_blocks, down_blocks):
    n = lax.axis_size("dp")
    nb, ru, wu = up_blocks.shape
    both = jnp.concatenate([up_blocks, down_blocks.reshape(nb, ru, wu)], axis=0)
    sent = jnp.broadcast_to(both, (n,) + both.shape)
    got = lax.all_to_all(sent, "dp", split_axis=0, concat_axis=0, tiled=True)
    return got[:, :nb], got[:, nb:]


def to_class(rows):
    return lax.ppermute(rows, DEVICES, PLAN.weights)


def from_class(rows):
    return lax.ppermute(rows, DEVICES, back(PLAN.weights))


def per_device(features, up_blocks, down_blocks, out_cotangent):
    nb, ru, wu = up_blocks.shape
    rd, wd = down_blocks.shape[1:]
    t = features.shape[1]
    n = NB // nb
    dp = lax.axis_size("dp")

    moved_cot = shuffle(out_cotangent)
    moved = shuffle(after(features, moved_cot)).reshape(nb, BIN, t)
    cot = mirror(moved_cot)
    up_rows, down_rows = gather_rows(up_blocks, down_blocks)

    def up_of(rows):
        return to_class(rows).reshape(BIN, BOUT)

    up0 = up_of(up_rows[:, 0])
    x0 = mirror(after(moved[0], cot))
    dblock = exchange(cot.reshape(nb, n, nb, J_DN, t).transpose(1, 2, 0, 3, 4))
    dblock = dblock.transpose(1, 0, 2, 3, 4).reshape(nb, BIN, t)
    down = to_class(after(down_rows, x0))
    x1 = mirror(after(moved[1], x0))
    up1 = up_of(after(up_rows[:, 1], x0))

    def pre_of(up, x):
        pre = jnp.einsum("kn,kt->nt", up, x, preferred_element_type=F32).astype(BF16)
        return pre.reshape(n, nb, J_UP, t)

    def hidden(got):
        v = got.transpose(1, 0, 2, 3).reshape(nb, n * J_UP, t).astype(F32)
        return v, gelu_value(v).astype(BF16)

    def backward(v, down):
        dact = jnp.einsum("gmc,gct->gmt", down, dblock, preferred_element_type=F32)
        dperm = (dact * gelu_slope(v)).astype(BF16)
        return dperm.reshape(nb, n, J_UP, t).transpose(1, 0, 2, 3)

    def grads(dpre, up, x):
        dpre = dpre.reshape(BOUT, t)
        fgrad = jnp.einsum("kn,nt->kt", up, dpre, preferred_element_type=F32).astype(BF16)
        dpre = after(dpre, fgrad)
        term = jnp.einsum("kt,nt->kn", x, dpre, preferred_element_type=F32)
        return fgrad, term.astype(BF16).reshape(dp, ru, wu)

    v0, act0 = hidden(exchange(pre_of(up0, after(x0, dblock))))
    down = down.reshape(dp, nb, rd, wd).transpose(1, 0, 2, 3).reshape(nb, n, nb, J_UP, wd)
    down0 = down[:, :, 0].reshape(nb, n * J_UP, wd)
    down1 = down[:, :, 1].reshape(nb, n * J_UP, wd)
    dpre0 = exchange(after(backward(v0, down0), x1))
    v1, act1 = hidden(exchange(after(pre_of(up1, x1), dpre0)))
    fgrad0, u0 = grads(dpre0, up0, x0)
    fgrad0 = to_store(fgrad0)
    u0 = from_class(u0)

    def down_product(down, act):
        return jnp.einsum("gmc,gmt->gct", down, act, preferred_element_type=F32)

    blockout = (down_product(down0, act0) + down_product(down1, act1)).astype(BF16)
    mixed = exchange(blockout.reshape(nb, n, nb, J_DN, t).transpose(1, 2, 0, 3, 4))

    def down_term(act):
        d = jnp.einsum("gmt,gct->gmc", act, dblock, preferred_element_type=F32)
        return d.astype(BF16).reshape(nb, n, 1, J_UP, wd)

    d = jnp.concatenate([down_term(act0), down_term(act1)], axis=2)
    d = from_class(d.reshape(nb, dp, ru, wu).transpose(1, 0, 2, 3))
    dpre1 = exchange(after(backward(v1, down1), mixed, fgrad0, u0))
    mixed = mixed.transpose(1, 0, 2, 3, 4).reshape(nb * BIN, t)
    mixed = unmirror(after(mixed, d))
    fgrad1, u1 = grads(dpre1, up1, x1)
    fgrad1 = to_store(fgrad1)
    u1 = from_class(after(u1, mixed))
    both = jnp.concatenate([u0[:, None], u1[:, None], d], axis=1)
    got = lax.all_to_all(both, "dp", split_axis=0, concat_axis=0, tiled=True)
    s = jnp.sum(got.astype(F32), axis=0)
    return (
        unshuffle(mixed),
        jnp.concatenate([fgrad0, fgrad1], axis=0),
        s[:nb],
        s[nb:].reshape(nb, rd, wd),
    )


def solution(mesh):
    flat = P("tensor", "dp")
    rows = P("tensor", "dp", None)
    return jax.shard_map(
        per_device,
        mesh=mesh,
        in_specs=(flat, rows, rows, flat),
        out_specs=(flat, flat, rows, rows),
        check_vma=False,
    )
```

time: 297 us -> 364 us (1.23)
  the two profiles are of different devices: /device:TPU:32 before, /device:TPU:1 now
where the time goes in v6:
time: 364 us; the launch traced here: 361 us
  starting transfers between devices  175 us (48%)
  waiting for transfers between devices  150 us (41%)
  local copies, waits for them, and re-layouts  17.1 us (5%)
  matrix products  13.2 us (4%)
  other arithmetic  4.89 us (1%)
    all_to_all x6, starting transfers between devices, exchange(): lax.all_to_all(x, DEVICES, split_axis=0, concat_axis=0, tiled=True, axis_...  49.9 us
    ppermute x3, waiting for transfers between devices, from_class(): return lax.ppermute(rows, DEVICES, back(PLAN.weights))  41.5 us
    ppermute x3, starting transfers between devices, mirror(): return lax.ppermute(x, DEVICES, PLAN.mirror)  33.5 us
    ppermute x3, waiting for transfers between devices, to_class(): return lax.ppermute(rows, DEVICES, PLAN.weights)  27.3 us
    ppermute x1, waiting for transfers between devices, unmirror(): return lax.ppermute(x, DEVICES, back(PLAN.mirror))  26.4 us
    ppermute x3, starting transfers between devices, from_class(): return lax.ppermute(rows, DEVICES, back(PLAN.weights))  25 us
    all_to_all x1, starting transfers between devices, gather_rows(): got = lax.all_to_all(sent, 'dp', split_axis=0, concat_axis=0, tiled=True)  21.8 us
    all_to_all x6, waiting for transfers between devices, exchange(): lax.all_to_all(x, DEVICES, split_axis=0, concat_axis=0, tiled=True, axis_...  19.1 us
  transfers between devices with their start and end apart: 23, of which 13 were waited for; matrix products, arithmetic and copies ran while one was open for 6% of the time, Pallas kernels for 0%

profile of v6, /device:TPU:1, one launch (start us, length us, event | category | flops | bytes accessed | tf_op | source)
XLA Modules:
  0.0 361.4 jit_solution(11673797341171289470)
XLA Ops:
  4.8 18.7 %collective-permute-start.2 = (bf16[256,1024]{1,0:T(8,128)(2,1)S(1)}, bf16[256,1024]{1,0:T(8,128)(2,1)S(1)}, u32[]{:S(2)}, u32[]{:S(2)}) collective-permute-start(bf16[256,1024]{1,0:T(8,128)(2,1)S(1)} %collective-permute-done), channel_id=1, source_target_pairs={{0,0},{1,1},{32,48},{33,49},{64,66},{65,67},{96,114},{97,115},{128... | collective-permute-start | bytes 1572872 | tf_op jit(solution)/shard_map/ppermute | solution.py:77
  25.1 21.8 %all-to-all-start = ((bf16[16,4,8,512]{3,2,1,0:T(8,128)(2,1)}), bf16[16,4,8,512]{3,2,1,0:T(8,128)(2,1)S(1)}, u32[]{:S(2)}, u32[]{:S(2)}) async-start(bf16[16,4,8,512]{3,2,1,0:T(8,128)(2,1)} %broadcast_in_dim.9), calls=%async_computation | async-start | bytes 1048576 | tf_op jit(solution)/shard_map/all_to_all | solution.py:97
  48.4 9.7 %all-to-all-done = bf16[16,4,8,512]{3,2,1,0:T(8,128)(2,1)S(1)} async-done(((bf16[16,4,8,512]{3,2,1,0:T(8,128)(2,1)}), bf16[16,4,8,512]{3,2,1,0:T(8,128)(2,1)S(1)}, u32[]{:S(2)}, u32[]{:S(2)}) %all-to-all-start) | async-done | bytes 524320 | tf_op jit(solution)/shard_map/all_to_all | solution.py:97
  58.1 14.7 %all-to-all-start.1 = ((bf16[32,2,2,2,1024]{4,3,2,1,0:T(2,128)(2,1)}), bf16[32,2,2,2,1024]{4,3,2,1,0:T(2,128)(2,1)S(1)}, u32[]{:S(2)}, u32[]{:S(2)}) async-start(bf16[32,2,2,2,1024]{4,3,2,1,0:T(2,128)(2,1)} %copy.37), calls=%async_computation.1 | async-start | bytes 1048576 | tf_op jit(solution)/shard_map/all_to_all | solution.py:63
  72.9 7.0 %collective-permute-start.3 = (bf16[128,1024]{1,0:T(8,128)(2,1)S(1)}, bf16[128,1024]{1,0:T(8,128)(2,1)S(1)}, u32[]{:S(2)}, u32[]{:S(2)}) collective-permute-start(bf16[128,1024]{1,0:T(8,128)(2,1)S(1)} %get-tuple-element.18), channel_id=1, source_target_pairs={{0,0},{1,1},{32,48},{33,49},{64,66},{65,67},{96,114},{97,115},{128... | collective-permute-start | bytes 786440 | tf_op jit(solution)/shard_map/ppermute | solution.py:77
  80.6 7.0 %collective-permute-start.5 = (bf16[16,8,512]{2,1,0:T(8,128)(2,1)S(1)}, bf16[16,8,512]{2,1,0:T(8,128)(2,1)S(1)}, u32[]{:S(2)}, u32[]{:S(2)}) collective-permute-start(bf16[16,8,512]{2,1,0:T(8,128)(2,1)S(1)} %get-tuple-element.31), channel_id=1, source_target_pairs={{0,0},{1,1},{32,48},{33,49},{64,66},{65,67},{96,114},{97,115},{128... | collective-permute-start | bytes 393224 | tf_op jit(solution)/shard_map/ppermute | solution.py:102
  88.2 8.2 %collective-permute-done.3 = bf16[128,1024]{1,0:T(8,128)(2,1)S(1)} collective-permute-done((bf16[128,1024]{1,0:T(8,128)(2,1)S(1)}, bf16[128,1024]{1,0:T(8,128)(2,1)S(1)}, u32[]{:S(2)}, u32[]{:S(2)}) %collective-permute-start.3) | collective-permute-done | bytes 262176 | tf_op jit(solution)/shard_map/ppermute | solution.py:77
  99.4 13.5 %all-to-all-start.2 = ((bf16[32,2,8,1024]{3,2,1,0:T(8,128)(2,1)}), bf16[32,2,8,1024]{3,2,1,0:T(8,128)(2,1)S(1)}, u32[]{:S(2)}, u32[]{:S(2)}) async-start(bf16[32,2,8,1024]{3,2,1,0:T(8,128)(2,1)} %bitcast.7), calls=%async_computation.2 | async-start | bytes 2097152 | tf_op jit(solution)/shard_map/all_to_all | solution.py:63
  112.9 6.2 %collective-permute-start.4 = (bf16[16,2,8,512]{3,2,1,0:T(8,128)(2,1)S(1)}, bf16[16,2,8,512]{3,2,1,0:T(8,128)(2,1)S(1)}, u32[]{:S(2)}, u32[]{:S(2)}) collective-permute-start(bf16[16,2,8,512]{3,2,1,0:T(8,128)(2,1)S(1)} %slice.41), channel_id=1, source_target_pairs={{0,0},{1,1},{32,48},{33,49},{64,66},{65,67},{96,114},{97,115},{128... | collective-permute-start | bytes 786440 | tf_op jit(solution)/shard_map/ppermute | solution.py:102
  119.1 7.8 %collective-permute-start.7 = (bf16[128,1024]{1,0:T(8,128)(2,1)S(1)}, bf16[128,1024]{1,0:T(8,128)(2,1)S(1)}, u32[]{:S(2)}, u32[]{:S(2)}) collective-permute-start(bf16[128,1024]{1,0:T(8,128)(2,1)S(1)} %get-tuple-element.22), channel_id=1, source_target_pairs={{0,0},{1,1},{32,48},{33,49},{64,66},{65,67},{96,114},{97,115},{128... | collective-permute-start | bytes 786440 | tf_op jit(solution)/shard_map/ppermute | solution.py:77
  126.9 14.8 %collective-permute-done.4 = bf16[16,2,8,512]{3,2,1,0:T(8,128)(2,1)S(1)} collective-permute-done((bf16[16,2,8,512]{3,2,1,0:T(8,128)(2,1)S(1)}, bf16[16,2,8,512]{3,2,1,0:T(8,128)(2,1)S(1)}, u32[]{:S(2)}, u32[]{:S(2)}) %collective-permute-start.4) | collective-permute-done | bytes 262176 | tf_op jit(solution)/shard_map/ppermute | solution.py:102
  145.4 6.8 %all-to-all-start.3 = ((bf16[32,2,8,1024]{3,2,1,0:T(8,128)(2,1)}), bf16[32,2,8,1024]{3,2,1,0:T(8,128)(2,1)S(1)}, u32[]{:S(2)}, u32[]{:S(2)}) async-start(bf16[32,2,8,1024]{3,2,1,0:T(8,128)(2,1)} %bitcast.122), calls=%async_computation.3 | async-start | bytes 2097152 | tf_op jit(solution)/shard_map/all_to_all | solution.py:63
  156.5 11.0 %collective-permute-done.6 = bf16[16,8,512]{2,1,0:T(8,128)(2,1)S(1)} collective-permute-done((bf16[16,8,512]{2,1,0:T(8,128)(2,1)S(1)}, bf16[16,8,512]{2,1,0:T(8,128)(2,1)S(1)}, u32[]{:S(2)}, u32[]{:S(2)}) %collective-permute-start.6) | collective-permute-done | bytes 131104 | tf_op jit(solution)/shard_map/ppermute | solution.py:102
  179.5 15.4 %all-to-all-done.4 = bf16[32,2,8,1024]{3,2,1,0:T(8,128)(2,1)} async-done(((bf16[32,2,8,1024]{3,2,1,0:T(8,128)(2,1)}), bf16[32,2,8,1024]{3,2,1,0:T(8,128)(2,1)}, u32[]{:S(2)}, u32[]{:S(2)}) %all-to-all-start.4) | async-done | bytes 1048608 | tf_op jit(solution)/shard_map/all_to_all | solution.py:63
  213.2 9.7 %collective-permute-start.12 = (bf16[16,8,512]{2,1,0:T(8,128)(2,1)S(1)}, bf16[16,8,512]{2,1,0:T(8,128)(2,1)S(1)}, u32[]{:S(2)}, u32[]{:S(2)}) collective-permute-start(bf16[16,8,512]{2,1,0:T(8,128)(2,1)S(1)} %fusion.23), channel_id=1, source_target_pairs={{0,0},{1,1},{48,32},{49,33},{66,64},{67,65},{114,96},{115,97},{132... | collective-permute-start | bytes 393224 | tf_op jit(solution)/shard_map/ppermute | solution.py:106
  226.2 18.2 %collective-permute-done.12 = bf16[16,8,512]{2,1,0:T(8,128)(2,1)S(1)} collective-permute-done((bf16[16,8,512]{2,1,0:T(8,128)(2,1)S(1)}, bf16[16,8,512]{2,1,0:T(8,128)(2,1)S(1)}, u32[]{:S(2)}, u32[]{:S(2)}) %collective-permute-start.12) | collective-permute-done | bytes 131104 | tf_op jit(solution)/shard_map/ppermute | solution.py:106
  253.0 8.3 %collective-permute-start.8 = (bf16[16,2,8,512]{3,2,0,1:T(8,128)(2,1)S(1)}, bf16[16,2,8,512]{3,2,0,1:T(8,128)(2,1)S(1)}, u32[]{:S(2)}, u32[]{:S(2)}) collective-permute-start(bf16[16,2,8,512]{3,2,0,1:T(8,128)(2,1)S(1)} %bitcast.136), channel_id=1, source_target_pairs={{0,0},{1,1},{48,32},{49,33},{66,64},{67,65},{114,96},{115,97},{132... | collective-permute-start | bytes 786440 | tf_op jit(solution)/shard_map/ppermute | solution.py:106
  262.9 17.5 %collective-permute-done.8 = bf16[16,2,8,512]{3,2,0,1:T(8,128)(2,1)S(1)} collective-permute-done((bf16[16,2,8,512]{3,2,0,1:T(8,128)(2,1)S(1)}, bf16[16,2,8,512]{3,2,0,1:T(8,128)(2,1)S(1)}, u32[]{:S(2)}, u32[]{:S(2)}) %collective-permute-start.8) | collective-permute-done | bytes 262176 | tf_op jit(solution)/shard_map/ppermute | solution.py:106
  280.4 7.5 %collective-permute-start.9 = (bf16[256,1024]{1,0:T(8,128)(2,1)S(1)}, bf16[256,1024]{1,0:T(8,128)(2,1)}, u32[]{:S(2)}, u32[]{:S(2)}) collective-permute-start(bf16[256,1024]{1,0:T(8,128)(2,1)S(1)} %reshape.93), channel_id=1, source_target_pairs={{0,0},{1,1},{48,32},{49,33},{66,64},{67,65},{114,96},{115,97},{132... | collective-permute-start | bytes 1572872 | tf_op jit(solution)/shard_map/ppermute | solution.py:81
  288.8 26.4 %collective-permute-done.9 = bf16[256,1024]{1,0:T(8,128)(2,1)} collective-permute-done((bf16[256,1024]{1,0:T(8,128)(2,1)S(1)}, bf16[256,1024]{1,0:T(8,128)(2,1)}, u32[]{:S(2)}, u32[]{:S(2)}) %collective-permute-start.9) | collective-permute-done | bytes 524320 | tf_op jit(solution)/shard_map/ppermute | solution.py:81
  315.2 7.0 %collective-permute-start.14 = (bf16[16,8,512]{2,1,0:T(8,128)(2,1)S(1)}, bf16[16,8,512]{2,1,0:T(8,128)(2,1)S(1)}, u32[]{:S(2)}, u32[]{:S(2)}) collective-permute-start(bf16[16,8,512]{2,1,0:T(8,128)(2,1)S(1)} %fusion.24), channel_id=1, source_target_pairs={{0,0},{1,1},{48,32},{49,33},{66,64},{67,65},{114,96},{115,97},{132... | collective-permute-start | bytes 393224 | tf_op jit(solution)/shard_map/ppermute | solution.py:106
  323.8 5.7 %collective-permute-done.14 = bf16[16,8,512]{2,1,0:T(8,128)(2,1)S(1)} collective-permute-done((bf16[16,8,512]{2,1,0:T(8,128)(2,1)S(1)}, bf16[16,8,512]{2,1,0:T(8,128)(2,1)S(1)}, u32[]{:S(2)}, u32[]{:S(2)}) %collective-permute-start.14) | collective-permute-done | bytes 131104 | tf_op jit(solution)/shard_map/ppermute | solution.py:106
  334.6 6.1 %collective-permute-start.13 = (bf16[128,1024]{1,0:T(8,128)(2,1)S(1)}, bf16[128,1024]{1,0:T(8,128)(2,1)S(1)}, u32[]{:S(2)}, u32[]{:S(2)}) collective-permute-start(bf16[128,1024]{1,0:T(8,128)(2,1)S(1)} %convolution_convert_fusion.2), channel_id=1, source_target_pairs={{0,0},{1,1},{48,32},{49,33},{66,64},{67,65},{114,96},{115,97},{132... | collective-permute-start | bytes 786440 | tf_op jit(solution)/shard_map/ppermute | solution.py:89
  340.7 16.8 %collective-permute-done.13 = bf16[128,1024]{1,0:T(8,128)(2,1)S(1)} collective-permute-done((bf16[128,1024]{1,0:T(8,128)(2,1)S(1)}, bf16[128,1024]{1,0:T(8,128)(2,1)S(1)}, u32[]{:S(2)}, u32[]{:S(2)}) %collective-permute-start.13) | collective-permute-done | bytes 262176 | tf_op jit(solution)/shard_map/ppermute | solution.py:89
  (91 shorter events, 74.3 us)
Async XLA Ops:
  0.6 2.4 collective-permute-start
  3.1 69.8 %collective-permute-start.1 = (bf16[256,1024]{1,0:T(8,128)(2,1)}, bf16[256,1024]{1,0:T(8,128)(2,1)S(1)}, u32[]{:S(2)}, u32[]{:S(2)}) collective-permute-start(bf16[256,1024]{1,0:T(8,128)(2,1)} %param.4), channel_id=1, source_target_pairs={{0,0},{1,1},{32,32},{33,33},{64,64},{65,65},{96,96},{97,97},{128,1... | collective-permute-start | bytes 1572872 | tf_op jit(solution)/shard_map/ppermute | solution.py:73
  4.8 42.1 %collective-permute-start.2 = (bf16[256,1024]{1,0:T(8,128)(2,1)S(1)}, bf16[256,1024]{1,0:T(8,128)(2,1)S(1)}, u32[]{:S(2)}, u32[]{:S(2)}) collective-permute-start(bf16[256,1024]{1,0:T(8,128)(2,1)S(1)} %collective-permute-done), channel_id=1, source_target_pairs={{0,0},{1,1},{32,48},{33,49},{64,66},{65,67},{96,114},{97,115},{128... | collective-permute-start | bytes 1572872 | tf_op jit(solution)/shard_map/ppermute | solution.py:77
  25.1 33.1 %all-to-all-start = ((bf16[16,4,8,512]{3,2,1,0:T(8,128)(2,1)}), bf16[16,4,8,512]{3,2,1,0:T(8,128)(2,1)S(1)}, u32[]{:S(2)}, u32[]{:S(2)}) async-start(bf16[16,4,8,512]{3,2,1,0:T(8,128)(2,1)} %broadcast_in_dim.9), calls=%async_computation | async-start | bytes 1048576 | tf_op jit(solution)/shard_map/all_to_all | solution.py:97
  58.1 29.5 %all-to-all-start.1 = ((bf16[32,2,2,2,1024]{4,3,2,1,0:T(2,128)(2,1)}), bf16[32,2,2,2,1024]{4,3,2,1,0:T(2,128)(2,1)S(1)}, u32[]{:S(2)}, u32[]{:S(2)}) async-start(bf16[32,2,2,2,1024]{4,3,2,1,0:T(2,128)(2,1)} %copy.37), calls=%async_computation.1 | async-start | bytes 1048576 | tf_op jit(solution)/shard_map/all_to_all | solution.py:63
  72.9 23.5 %collective-permute-start.3 = (bf16[128,1024]{1,0:T(8,128)(2,1)S(1)}, bf16[128,1024]{1,0:T(8,128)(2,1)S(1)}, u32[]{:S(2)}, u32[]{:S(2)}) collective-permute-start(bf16[128,1024]{1,0:T(8,128)(2,1)S(1)} %get-tuple-element.18), channel_id=1, source_target_pairs={{0,0},{1,1},{32,48},{33,49},{64,66},{65,67},{96,114},{97,115},{128... | collective-permute-start | bytes 786440 | tf_op jit(solution)/shard_map/ppermute | solution.py:77
  80.6 17.3 %collective-permute-start.5 = (bf16[16,8,512]{2,1,0:T(8,128)(2,1)S(1)}, bf16[16,8,512]{2,1,0:T(8,128)(2,1)S(1)}, u32[]{:S(2)}, u32[]{:S(2)}) collective-permute-start(bf16[16,8,512]{2,1,0:T(8,128)(2,1)S(1)} %get-tuple-element.31), channel_id=1, source_target_pairs={{0,0},{1,1},{32,48},{33,49},{64,66},{65,67},{96,114},{97,115},{128... | collective-permute-start | bytes 393224 | tf_op jit(solution)/shard_map/ppermute | solution.py:102
  88.2 53.7 %copy-start = (bf16[2,128,1024]{2,1,0:T(8,128)(2,1)}, bf16[2,128,1024]{2,1,0:T(8,128)(2,1)S(1)}, u32[]{:S(2)}) copy-start(bf16[2,128,1024]{2,1,0:T(8,128)(2,1)S(1)} %reshape.87) | copy-start | bytes 1572868
  99.4 42.5 %all-to-all-start.2 = ((bf16[32,2,8,1024]{3,2,1,0:T(8,128)(2,1)}), bf16[32,2,8,1024]{3,2,1,0:T(8,128)(2,1)S(1)}, u32[]{:S(2)}, u32[]{:S(2)}) async-start(bf16[32,2,8,1024]{3,2,1,0:T(8,128)(2,1)} %bitcast.7), calls=%async_computation.2 | async-start | bytes 2097152 | tf_op jit(solution)/shard_map/all_to_all | solution.py:63
  112.9 28.8 %collective-permute-start.4 = (bf16[16,2,8,512]{3,2,1,0:T(8,128)(2,1)S(1)}, bf16[16,2,8,512]{3,2,1,0:T(8,128)(2,1)S(1)}, u32[]{:S(2)}, u32[]{:S(2)}) collective-permute-start(bf16[16,2,8,512]{3,2,1,0:T(8,128)(2,1)S(1)} %slice.41), channel_id=1, source_target_pairs={{0,0},{1,1},{32,48},{33,49},{64,66},{65,67},{96,114},{97,115},{128... | collective-permute-start | bytes 786440 | tf_op jit(solution)/shard_map/ppermute | solution.py:102
  119.1 26.2 %collective-permute-start.7 = (bf16[128,1024]{1,0:T(8,128)(2,1)S(1)}, bf16[128,1024]{1,0:T(8,128)(2,1)S(1)}, u32[]{:S(2)}, u32[]{:S(2)}) collective-permute-start(bf16[128,1024]{1,0:T(8,128)(2,1)S(1)} %get-tuple-element.22), channel_id=1, source_target_pairs={{0,0},{1,1},{32,48},{33,49},{64,66},{65,67},{96,114},{97,115},{128... | collective-permute-start | bytes 786440 | tf_op jit(solution)/shard_map/ppermute | solution.py:77
  145.4 27.3 %all-to-all-start.3 = ((bf16[32,2,8,1024]{3,2,1,0:T(8,128)(2,1)}), bf16[32,2,8,1024]{3,2,1,0:T(8,128)(2,1)S(1)}, u32[]{:S(2)}, u32[]{:S(2)}) async-start(bf16[32,2,8,1024]{3,2,1,0:T(8,128)(2,1)} %bitcast.122), calls=%async_computation.3 | async-start | bytes 2097152 | tf_op jit(solution)/shard_map/all_to_all | solution.py:63
  152.2 15.3 %collective-permute-start.6 = (bf16[16,8,512]{2,1,0:T(8,128)(2,1)S(1)}, bf16[16,8,512]{2,1,0:T(8,128)(2,1)S(1)}, u32[]{:S(2)}, u32[]{:S(2)}) collective-permute-start(bf16[16,8,512]{2,1,0:T(8,128)(2,1)S(1)} %copy-done.11), channel_id=1, source_target_pairs={{0,0},{1,1},{32,48},{33,49},{64,66},{65,67},{96,114},{97,115},{128... | collective-permute-start | bytes 393224 | tf_op jit(solution)/shard_map/ppermute | solution.py:102
  172.6 22.3 %all-to-all-start.4 = ((bf16[32,2,8,1024]{3,2,1,0:T(8,128)(2,1)}), bf16[32,2,8,1024]{3,2,1,0:T(8,128)(2,1)}, u32[]{:S(2)}, u32[]{:S(2)}) async-start(bf16[32,2,8,1024]{3,2,1,0:T(8,128)(2,1)} %bitcast.14), calls=%async_computation.4 | async-start | bytes 2097152 | tf_op jit(solution)/shard_map/all_to_all | solution.py:63
  202.3 42.1 %all-to-all-start.5 = ((bf16[32,2,2,2,1024]{4,3,1,2,0:T(2,128)(2,1)}), bf16[32,2,2,2,1024]{4,3,1,2,0:T(2,128)(2,1)}, u32[]{:S(2)}, u32[]{:S(2)}) async-start(bf16[32,2,2,2,1024]{4,3,1,2,0:T(2,128)(2,1)} %bitcast.129), calls=%async_computation.5 | async-start | bytes 1048576 | tf_op jit(solution)/shard_map/all_to_all | solution.py:63
  208.2 36.2 %collective-permute-start.11 = (bf16[128,1024]{1,0:T(8,128)(2,1)S(1)}, bf16[128,1024]{1,0:T(8,128)(2,1)}, u32[]{:S(2)}, u32[]{:S(2)}) collective-permute-start(bf16[128,1024]{1,0:T(8,128)(2,1)S(1)} %convolution_convert_fusion.3), channel_id=1, source_target_pairs={{0,0},{1,1},{48,32},{49,33},{66,64},{67,65},{114,96},{115,97},{132... | collective-permute-start | bytes 786440 | tf_op jit(solution)/shard_map/ppermute | solution.py:89
  213.2 31.2 %collective-permute-start.12 = (bf16[16,8,512]{2,1,0:T(8,128)(2,1)S(1)}, bf16[16,8,512]{2,1,0:T(8,128)(2,1)S(1)}, u32[]{:S(2)}, u32[]{:S(2)}) collective-permute-start(bf16[16,8,512]{2,1,0:T(8,128)(2,1)S(1)} %fusion.23), channel_id=1, source_target_pairs={{0,0},{1,1},{48,32},{49,33},{66,64},{67,65},{114,96},{115,97},{132... | collective-permute-start | bytes 393224 | tf_op jit(solution)/shard_map/ppermute | solution.py:106
  245.0 42.9 %all-to-all-start.6 = ((bf16[32,2,8,1024]{3,2,1,0:T(8,128)(2,1)}), bf16[32,2,8,1024]{3,2,1,0:T(8,128)(2,1)S(1)}, u32[]{:S(2)}, u32[]{:S(2)}) async-start(bf16[32,2,8,1024]{3,2,1,0:T(8,128)(2,1)} %bitcast.128), calls=%async_computation.6 | async-start | bytes 2097152 | tf_op jit(solution)/shard_map/all_to_all | solution.py:63
  253.0 27.4 %collective-permute-start.8 = (bf16[16,2,8,512]{3,2,0,1:T(8,128)(2,1)S(1)}, bf16[16,2,8,512]{3,2,0,1:T(8,128)(2,1)S(1)}, u32[]{:S(2)}, u32[]{:S(2)}) collective-permute-start(bf16[16,2,8,512]{3,2,0,1:T(8,128)(2,1)S(1)} %bitcast.136), channel_id=1, source_target_pairs={{0,0},{1,1},{48,32},{49,33},{66,64},{67,65},{114,96},{115,97},{132... | collective-permute-start | bytes 786440 | tf_op jit(solution)/shard_map/ppermute | solution.py:106
  280.4 34.8 %collective-permute-start.9 = (bf16[256,1024]{1,0:T(8,128)(2,1)S(1)}, bf16[256,1024]{1,0:T(8,128)(2,1)}, u32[]{:S(2)}, u32[]{:S(2)}) collective-permute-start(bf16[256,1024]{1,0:T(8,128)(2,1)S(1)} %reshape.93), channel_id=1, source_target_pairs={{0,0},{1,1},{48,32},{49,33},{66,64},{67,65},{114,96},{115,97},{132... | collective-permute-start | bytes 1572872 | tf_op jit(solution)/shard_map/ppermute | solution.py:81
  315.2 14.4 %collective-permute-start.14 = (bf16[16,8,512]{2,1,0:T(8,128)(2,1)S(1)}, bf16[16,8,512]{2,1,0:T(8,128)(2,1)S(1)}, u32[]{:S(2)}, u32[]{:S(2)}) collective-permute-start(bf16[16,8,512]{2,1,0:T(8,128)(2,1)S(1)} %fusion.24), channel_id=1, source_target_pairs={{0,0},{1,1},{48,32},{49,33},{66,64},{67,65},{114,96},{115,97},{132... | collective-permute-start | bytes 393224 | tf_op jit(solution)/shard_map/ppermute | solution.py:106
  322.1 18.5 %collective-permute-start.10 = (bf16[256,1024]{1,0:T(8,128)(2,1)}, bf16[256,1024]{1,0:T(8,128)(2,1)S(1)}, u32[]{:S(2)}, u32[]{:S(2)}) collective-permute-start(bf16[256,1024]{1,0:T(8,128)(2,1)} %collective-permute-done.9), channel_id=1, source_target_pairs={{0,0},{1,1},{32,32},{33,33},{64,64},{65,65},{96,96},{97,97},{128,1... | collective-permute-start | bytes 1572872 | tf_op jit(solution)/shard_map/ppermute | solution.py:85
  330.5 28.8 %all-to-all-start.7 = ((bf16[16,4,8,512]{3,2,1,0:T(8,128)(2,1)}), bf16[16,4,8,512]{3,2,1,0:T(8,128)(2,1)S(1)}, u32[]{:S(2)}, u32[]{:S(2)}) async-start(bf16[16,4,8,512]{3,2,1,0:T(8,128)(2,1)} %copy.49), calls=%async_computation.7 | async-start | bytes 1048576 | tf_op jit(solution)/shard_map/all_to_all | solution.py:181
  334.6 22.9 %collective-permute-start.13 = (bf16[128,1024]{1,0:T(8,128)(2,1)S(1)}, bf16[128,1024]{1,0:T(8,128)(2,1)S(1)}, u32[]{:S(2)}, u32[]{:S(2)}) collective-permute-start(bf16[128,1024]{1,0:T(8,128)(2,1)S(1)} %convolution_convert_fusion.2), channel_id=1, source_target_pairs={{0,0},{1,1},{48,32},{49,33},{66,64},{67,65},{114,96},{115,97},{132... | collective-permute-start | bytes 786440 | tf_op jit(solution)/shard_map/ppermute | solution.py:89
  (13 other events, 95.6 us)

commit v7 on v4

v7 whole, which is shorter than its diff:
```python
import jax
import jax.numpy as jnp
from jax import lax
from jax.sharding import PartitionSpec as P

NB = 64
BIN = 128
BOUT = 512
J_UP = 8
J_DN = 2
F32 = jnp.float32
BF16 = jnp.bfloat16


def gelu_value(v):
    return 0.5 * v * (1.0 + lax.erf(v * 0.7071067811865476))


def gelu_slope(v):
    return (
        0.5 * (1.0 + lax.erf(v * 0.7071067811865476))
        + v * jnp.exp(-0.5 * v * v) * 0.3989422804014327
    )


DEVICES = ("dp", "tensor")


def back(pairs):
    return [(b, a) for a, b in pairs]


class Plan:
    def __init__(self):
        def index(xh, y, c, z, xl):
            return (((xh * 4 + y) * 2 + c) * 16 + z) * 2 + xl

        def side(z, xh, xl):
            return xl if xh == (z >> 2) & 1 else 1 - xl

        def at(label):
            return (label >> 2) & 1, label & 3, label >> 3

        spots = [(z, *at(k), xl) for z in range(16) for k in range(16) for xl in range(2)]
        shuffle, mirror, weights, home, place = [], [], [], [], {}
        for z in range(16):
            for label in range(16):
                xh, y, c = at(label)
                xh2, y2, c2 = at((label + z) % 16)
                for xl in range(2):
                    xl2 = side(label, xh2, xl)
                    mid = index(xh2, y2, c2, z, xl2)
                    end = index(xh2, y2, c2, label, xl2)
                    shuffle.append((index(xh, y, c, z, xl), mid))
                    mirror.append((mid, end))
                    home.append((end, index(xh, y, c, z, xl)))
                    weights.append((index(xh2, y2, c2, z, xl), end))
                    place[label, 2 * z + xl] = end
        self.shuffle, self.mirror, self.home, self.weights = shuffle, mirror, home, weights
        self.layers = [[place[t, k] for k in range(32)] for t in range(16)]
        self.planes = [
            [index(*at(k), z, side(z, at(k)[0], xl)) for k in range(16)]
            for z in range(16)
            for xl in range(2)
        ]
        self.columns = [
            [index(*at(k), z, side(z, at(k)[0], xl)) for z in range(16)]
            for k in range(16)
            for xl in range(2)
        ]
        self.swap = [
            (index(xh, y, c, z, xl), index(xh, y, c, z, side(z, xh, xl)))
            for z, xh, y, c, xl in spots
        ]


PLAN = Plan()


def exchange(x, groups):
    return lax.all_to_all(
        x, DEVICES, split_axis=0, concat_axis=0, tiled=True, axis_index_groups=groups
    )


def roll(x, shift):
    return lax.dynamic_slice_in_dim(jnp.concatenate([x, x]), shift, x.shape[0])


def layer():
    return lax.axis_index("tensor") // 2


def after(x, *others):
    return lax.optimization_barrier((x,) + others)[0]


def shuffle(x):
    return lax.ppermute(x, DEVICES, PLAN.shuffle)


def mirror(x):
    return lax.ppermute(x, DEVICES, PLAN.mirror)


def unmirror(x):
    return lax.ppermute(x, DEVICES, back(PLAN.mirror))


def unshuffle(x):
    return lax.ppermute(x, DEVICES, back(PLAN.shuffle))


def to_store(x):
    return lax.ppermute(x, DEVICES, PLAN.home)


def gather_rows(up_blocks, down_blocks):
    n = lax.axis_size("dp")
    nb, ru, wu = up_blocks.shape
    rd, wd = down_blocks.shape[1:]
    both = jnp.concatenate([up_blocks, down_blocks.reshape(nb, ru, wu)], axis=0)
    both = lax.ppermute(both, DEVICES, PLAN.swap)
    got = lax.all_gather(both, DEVICES, axis_index_groups=PLAN.columns)
    got = exchange(roll(got, n - layer()), PLAN.planes)
    got = got.reshape(2, 2, 4, 2 * nb, ru, wu).transpose(3, 1, 2, 0, 4, 5)
    up = got[:nb].reshape(nb, n * ru, wu)
    down = got[nb:].reshape(nb, n, rd, wd).reshape(nb, n * rd, wd)
    return up, down


def to_rows(term):
    n = lax.axis_size("dp")
    nb = term.shape[0]
    rows = term.astype(BF16).reshape(nb, n, -1, BOUT).transpose(1, 0, 2, 3)
    return lax.ppermute(rows, DEVICES, back(PLAN.weights))


def sum_rows(up_term, down_term, down_shape):
    both = jnp.concatenate([up_term, down_term], axis=1)
    got = lax.all_to_all(both, "dp", split_axis=0, concat_axis=0, tiled=True)
    s = jnp.sum(got.astype(F32), axis=0)
    nb = down_shape[0]
    return s[:nb], s[nb:].reshape(down_shape)


def per_device(features, up_blocks, down_blocks, out_cotangent):
    nb = up_blocks.shape[0]
    t = features.shape[1]
    n = NB // nb
    moved = shuffle(features)
    moved_cot = shuffle(after(out_cotangent, moved))
    up, down = gather_rows(up_blocks, down_blocks)
    x_flat = mirror(moved)
    cot = mirror(after(moved_cot, x_flat))
    x = after(x_flat, moved_cot).reshape(nb, BIN, t)
    pre = jnp.einsum("bkn,bkt->bnt", up, x, preferred_element_type=F32).astype(BF16)
    permuted = exchange(pre.reshape(nb, n, nb, J_UP, t).transpose(1, 2, 0, 3, 4), PLAN.layers)
    cot = after(cot, permuted).reshape(nb, n, nb, J_DN, t).transpose(1, 2, 0, 3, 4)
    dblock = exchange(cot, PLAN.layers)
    permuted = permuted.transpose(1, 0, 2, 3, 4).reshape(nb, BOUT, t)
    pf = permuted.astype(F32)
    act = gelu_value(pf).astype(BF16)
    blockout = jnp.einsum("gmc,gmt->gct", down, act, preferred_element_type=F32).astype(BF16)
    blockout = blockout.reshape(nb, n, nb, J_DN, t).transpose(1, 2, 0, 3, 4)
    mixed = exchange(after(blockout, dblock), PLAN.layers)
    dblock = dblock.transpose(1, 0, 2, 3, 4).reshape(nb, BIN, t)
    dact = jnp.einsum("gmc,gct->gmt", down, dblock, preferred_element_type=F32)
    dperm = (dact * gelu_slope(pf)).astype(BF16)
    dperm = dperm.reshape(nb, n, nb, J_UP, t).transpose(1, 2, 0, 3, 4)
    down_term = jnp.einsum("gmt,gct->gmc", act, dblock, preferred_element_type=F32)
    down_term = to_rows(down_term)
    dpre = exchange(after(dperm, mixed, down_term), PLAN.layers)
    mixed = unmirror(mixed.transpose(1, 0, 2, 3, 4).reshape(nb * BIN, t))
    dpre = after(dpre, mixed).transpose(1, 0, 2, 3, 4).reshape(nb, BOUT, t)
    fgrad = jnp.einsum("bkn,bnt->bkt", up, dpre, preferred_element_type=F32).astype(BF16)
    fgrad = fgrad.reshape(nb * BIN, t)
    dpre = after(dpre, fgrad)
    up_term = jnp.einsum("bkt,bnt->bkn", x, dpre, preferred_element_type=F32)
    up_term = to_rows(up_term)
    up_grad, down_grad = sum_rows(up_term, down_term, down_blocks.shape)
    return unshuffle(after(mixed, up_term)), to_store(fgrad), up_grad, down_grad


def solution(mesh):
    flat = P("tensor", "dp")
    rows = P("tensor", "dp", None)
    return jax.shard_map(
        per_device,
        mesh=mesh,
        in_specs=(flat, rows, rows, flat),
        out_specs=(flat, flat, rows, rows),
        check_vma=False,
    )
```

time: 319 us -> 312 us (0.978)
  the two profiles are of different devices: /device:TPU:1 before, /device:TPU:45 now
where the time goes in v7:
time: 312 us; the launch traced here: 310 us
  starting transfers between devices  128 us (41%)
  waiting for transfers between devices  115 us (37%)
  blocking collectives  33.7 us (11%)
  local copies, waits for them, and re-layouts  16.5 us (5%)
  matrix products  10 us (3%)
  other arithmetic  6.32 us (2%)
    all_to_all x5, starting transfers between devices, exchange(): lax.all_to_all(x, DEVICES, split_axis=0, concat_axis=0, tiled=True, axis_...  69.3 us
    all_gather x1, blocking collectives, gather_rows(): got = lax.all_gather(both, DEVICES, axis_index_groups=PLAN.columns)  33.7 us
    all_to_all x1, starting transfers between devices, sum_rows(): got = lax.all_to_all(both, 'dp', split_axis=0, concat_axis=0, tiled=True)  30.2 us
    ppermute x1, waiting for transfers between devices, unmirror(): return lax.ppermute(x, DEVICES, back(PLAN.mirror))  29.9 us
    ppermute x2, waiting for transfers between devices, to_rows(): return lax.ppermute(rows, DEVICES, back(PLAN.weights))  27.7 us
    ppermute x2, waiting for transfers between devices, mirror(): return lax.ppermute(x, DEVICES, PLAN.mirror)  23.1 us
    ppermute x1, waiting for transfers between devices, unshuffle(): return lax.ppermute(x, DEVICES, back(PLAN.shuffle))  9.92 us
    ppermute x2, starting transfers between devices, mirror(): return lax.ppermute(x, DEVICES, PLAN.mirror)  9.12 us
  transfers between devices with their start and end apart: 16, of which 10 were waited for; matrix products, arithmetic and copies ran while one was open for 6% of the time, Pallas kernels for 0%

profile of v7, /device:TPU:45, one launch (start us, length us, event | category | flops | bytes accessed | tf_op | source)
XLA Modules:
  0.0 310.4 jit_solution(5137762214584086513)
XLA Ops:
  2.1 2.8 collective-permute-start
  4.9 3.2 %collective-permute-start.1 = (bf16[256,1024]{1,0:T(8,128)(2,1)}, bf16[256,1024]{1,0:T(8,128)(2,1)S(1)}, u32[]{:S(2)}, u32[]{:S(2)}) collective-permute-start(bf16[256,1024]{1,0:T(8,128)(2,1)} %param.4), channel_id=1, source_target_pairs={{0,0},{1,1},{64,64},{65,65},{128,128},{129,129},{192,192},{193,193... | collective-permute-start | bytes 1572872 | tf_op jit(solution)/shard_map/ppermute | solution.py:99
  8.2 33.7 %all-gather = bf16[64,8,512]{2,1,0:T(8,128)(2,1)S(1)} all-gather(bf16[4,8,512]{2,1,0:T(8,128)(2,1)S(1)} %collective-permute-done), channel_id=2, replica_groups={{0,2,4,6,9,11,13,15,16,18,20,22,25,27,29,31},{1,3,5,7,8,10,12,14,17,19,..., dimensions={0}, use_global_device_ids=true | all-gather | bytes 557056 | tf_op jit(solution)/shard_map/all_gather | solution.py:124
  42.8 12.0 %all-to-all-start = ((bf16[16,4,8,512]{3,2,1,0:T(8,128)(2,1)}), bf16[16,4,8,512]{3,2,1,0:T(8,128)(2,1)S(1)}, u32[]{:S(2)}, u32[]{:S(2)}) async-start(bf16[16,4,8,512]{3,2,1,0:T(8,128)(2,1)} %fusion.11), calls=%async_computation | async-start | bytes 1048576 | tf_op jit(solution)/shard_map/all_to_all | solution.py:81
  54.8 3.1 collective-permute-start.3
  57.9 6.5 %collective-permute-start.2 = (bf16[256,1024]{1,0:T(8,128)(2,1)S(1)}, bf16[256,1024]{1,0:T(8,128)(2,1)S(1)}, u32[]{:S(2)}, u32[]{:S(2)}) collective-permute-start(bf16[256,1024]{1,0:T(8,128)(2,1)S(1)} %collective-permute-done.1), channel_id=1, source_target_pairs={{0,0},{1,1},{64,66},{65,67},{128,132},{129,133},{192,198},{193,199... | collective-permute-start | bytes 1572872 | tf_op jit(solution)/shard_map/ppermute | solution.py:103
  64.6 8.6 %collective-permute-done.3 = bf16[256,1024]{1,0:T(8,128)(2,1)} collective-permute-done((bf16[256,1024]{1,0:T(8,128)(2,1)}, bf16[256,1024]{1,0:T(8,128)(2,1)}, u32[]{:S(2)}, u32[]{:S(2)}) %collective-permute-start.3) | collective-permute-done | bytes 524320 | tf_op jit(solution)/shard_map/ppermute | solution.py:99
  73.2 4.8 %collective-permute-done.2 = bf16[256,1024]{1,0:T(8,128)(2,1)S(1)} collective-permute-done((bf16[256,1024]{1,0:T(8,128)(2,1)S(1)}, bf16[256,1024]{1,0:T(8,128)(2,1)S(1)}, u32[]{:S(2)}, u32[]{:S(2)}) %collective-permute-start.2) | collective-permute-done | bytes 524320 | tf_op jit(solution)/shard_map/ppermute | solution.py:103
  80.3 24.1 %all-to-all-start.1 = ((bf16[32,2,2,8,1024]{4,3,1,2,0:T(8,128)(2,1)}), bf16[32,2,2,8,1024]{4,3,1,2,0:T(8,128)(2,1)S(1)}, u32[]{:S(2)}, u32[]{:S(2)}) async-start(bf16[32,2,2,8,1024]{4,3,1,2,0:T(8,128)(2,1)} %bitcast.63), calls=%async_computation.1 | async-start | bytes 4194304 | tf_op jit(solution)/shard_map/all_to_all | solution.py:81
  104.4 2.6 collective-permute-start.4
  107.2 18.2 %collective-permute-done.4 = bf16[256,1024]{1,0:T(8,128)(2,1)} collective-permute-done((bf16[256,1024]{1,0:T(8,128)(2,1)}, bf16[256,1024]{1,0:T(8,128)(2,1)}, u32[]{:S(2)}, u32[]{:S(2)}) %collective-permute-start.4) | collective-permute-done | bytes 524320 | tf_op jit(solution)/shard_map/ppermute | solution.py:103
  125.4 5.8 %all-to-all-done.1 = bf16[32,2,2,8,1024]{4,3,1,2,0:T(8,128)(2,1)S(1)} async-done(((bf16[32,2,2,8,1024]{4,3,1,2,0:T(8,128)(2,1)}), bf16[32,2,2,8,1024]{4,3,1,2,0:T(8,128)(2,1)S(1)}, u32[]{:S(2)}, u32[]{:S(2)}) %all-to-all-start.1) | async-done | bytes 2097184 | tf_op jit(solution)/shard_map/all_to_all | solution.py:81
  133.8 18.4 %all-to-all-start.2 = ((bf16[32,2,2,2,1024]{4,3,2,1,0:T(2,128)(2,1)}), bf16[32,2,2,2,1024]{4,3,2,1,0:T(2,128)(2,1)S(1)}, u32[]{:S(2)}, u32[]{:S(2)}) async-start(bf16[32,2,2,2,1024]{4,3,2,1,0:T(2,128)(2,1)} %copy.40), calls=%async_computation.2 | async-start | bytes 1048576 | tf_op jit(solution)/shard_map/all_to_all | solution.py:81
  153.3 3.2 %fusion.7 = (bf16[2,512,1024]{2,1,0:T(8,128)(2,1)S(1)}, f32[2,512,1024]{2,1,0:T(8,128)}) fusion(f32[2,32,2,8,1024]{4,3,2,1,0:T(8,128)S(1)} %copy.37), kind=kLoop, calls=%fused_computation.10 | loop fusion | flops 5242880 | bytes 10485760 | tf_op jit(solution)/shard_map/convert_element_type | solution.py:163
  165.3 6.3 %all-to-all-start.3 = ((bf16[32,2,2,2,1024]{4,3,1,2,0:T(2,128)(2,1)}), bf16[32,2,2,2,1024]{4,3,1,2,0:T(2,128)(2,1)S(1)}, u32[]{:S(2)}, u32[]{:S(2)}) async-start(bf16[32,2,2,2,1024]{4,3,1,2,0:T(2,128)(2,1)} %bitcast.58), calls=%async_computation.3 | async-start | bytes 1048576 | tf_op jit(solution)/shard_map/all_to_all | solution.py:81
  173.5 4.9 %fusion.5 = bf16[2,512,1024]{2,1,0:T(8,128)(2,1)S(1)} fusion(f32[2,32,2,8,1024]{4,3,2,1,0:T(8,128)} %copy-done, f32[2,512,1024]{2,1,0:T(8,128)} %get-tuple-element.23, bf16[2,512,128]{2,1,0:T(8,128)(2,1)S(1)} %copy-done.4, bf16[2,128,1024]{2,1,0:T(8,128)(2,1)S(1)} %copy-done.5), kind=kOutput, calls=%fused_computation.6 | convolution fusion | flops 276824064 | bytes 11272192 | tf_op jit(solution)/shard_map/gmc,gct->gmt/dot_general | solution.py:168
  180.0 11.7 %collective-permute-done.6 = bf16[16,2,8,512]{3,2,1,0:T(8,128)(2,1)S(1)} collective-permute-done((bf16[16,2,8,512]{3,2,1,0:T(8,128)(2,1)S(1)}, bf16[16,2,8,512]{3,2,1,0:T(8,128)(2,1)S(1)}, u32[]{:S(2)}, u32[]{:S(2)}) %collective-permute-start.6) | collective-permute-done | bytes 262176 | tf_op jit(solution)/shard_map/ppermute | solution.py:136
  192.4 8.5 %all-to-all-start.4 = ((bf16[32,2,2,8,1024]{4,3,1,2,0:T(8,128)(2,1)}), bf16[32,2,2,8,1024]{4,3,1,2,0:T(8,128)(2,1)S(1)}, u32[]{:S(2)}, u32[]{:S(2)}) async-start(bf16[32,2,2,8,1024]{4,3,1,2,0:T(8,128)(2,1)} %bitcast.56), calls=%async_computation.4 | async-start | bytes 4194304 | tf_op jit(solution)/shard_map/all_to_all | solution.py:81
  204.1 29.9 %collective-permute-done.5 = bf16[256,1024]{1,0:T(8,128)(2,1)S(1)} collective-permute-done((bf16[256,1024]{1,0:T(8,128)(2,1)}, bf16[256,1024]{1,0:T(8,128)(2,1)S(1)}, u32[]{:S(2)}, u32[]{:S(2)}) %collective-permute-start.5) | collective-permute-done | bytes 524320 | tf_op jit(solution)/shard_map/ppermute | solution.py:107
  235.6 2.3 collective-permute-start.7
  239.8 16.0 %collective-permute-done.7 = bf16[16,2,8,512]{3,2,1,0:T(8,128)(2,1)S(1)} collective-permute-done((bf16[16,2,8,512]{3,2,1,0:T(8,128)(2,1)S(1)}, bf16[16,2,8,512]{3,2,1,0:T(8,128)(2,1)S(1)}, u32[]{:S(2)}, u32[]{:S(2)}) %collective-permute-start.7) | collective-permute-done | bytes 262176 | tf_op jit(solution)/shard_map/ppermute | solution.py:136
  256.6 30.2 %all-to-all-start.5 = ((bf16[16,4,8,512]{3,2,1,0:T(8,128)(2,1)}), bf16[16,4,8,512]{3,2,1,0:T(8,128)(2,1)S(1)}, u32[]{:S(2)}, u32[]{:S(2)}) async-start(bf16[16,4,8,512]{3,2,1,0:T(8,128)(2,1)} %pad_maximum_fusion), calls=%async_computation.5 | async-start | bytes 1048576 | tf_op jit(solution)/shard_map/all_to_all | solution.py:141
  289.0 8.6 %all-to-all-done.5 = bf16[16,4,8,512]{3,2,1,0:T(8,128)(2,1)S(1)} async-done(((bf16[16,4,8,512]{3,2,1,0:T(8,128)(2,1)}), bf16[16,4,8,512]{3,2,1,0:T(8,128)(2,1)S(1)}, u32[]{:S(2)}, u32[]{:S(2)}) %all-to-all-start.5) | async-done | bytes 524320 | tf_op jit(solution)/shard_map/all_to_all | solution.py:141
  298.9 9.9 %collective-permute-done.8 = bf16[256,1024]{1,0:T(8,128)(2,1)S(1)} collective-permute-done((bf16[256,1024]{1,0:T(8,128)(2,1)S(1)}, bf16[256,1024]{1,0:T(8,128)(2,1)S(1)}, u32[]{:S(2)}, u32[]{:S(2)}) %collective-permute-start.8) | collective-permute-done | bytes 524320 | tf_op jit(solution)/shard_map/ppermute | solution.py:111
  (61 shorter events, 34.1 us)
Async XLA Ops:
  2.1 6.1 %collective-permute-start = (bf16[4,8,512]{2,1,0:T(8,128)(2,1)S(1)}, bf16[4,8,512]{2,1,0:T(8,128)(2,1)S(1)}, u32[]{:S(2)}, u32[]{:S(2)}) collective-permute-start(bf16[4,8,512]{2,1,0:T(8,128)(2,1)S(1)} %pad_maximum_fusion.1), channel_id=1, source_target_pairs={{0,0},{1,1},{64,64},{65,65},{128,128},{129,129},{192,192},{193,193... | collective-permute-start | bytes 98312 | tf_op jit(solution)/shard_map/ppermute | solution.py:123
  4.9 49.9 %collective-permute-start.1 = (bf16[256,1024]{1,0:T(8,128)(2,1)}, bf16[256,1024]{1,0:T(8,128)(2,1)S(1)}, u32[]{:S(2)}, u32[]{:S(2)}) collective-permute-start(bf16[256,1024]{1,0:T(8,128)(2,1)} %param.4), channel_id=1, source_target_pairs={{0,0},{1,1},{64,64},{65,65},{128,128},{129,129},{192,192},{193,193... | collective-permute-start | bytes 1572872 | tf_op jit(solution)/shard_map/ppermute | solution.py:99
  42.8 21.7 %all-to-all-start = ((bf16[16,4,8,512]{3,2,1,0:T(8,128)(2,1)}), bf16[16,4,8,512]{3,2,1,0:T(8,128)(2,1)S(1)}, u32[]{:S(2)}, u32[]{:S(2)}) async-start(bf16[16,4,8,512]{3,2,1,0:T(8,128)(2,1)} %fusion.11), calls=%async_computation | async-start | bytes 1048576 | tf_op jit(solution)/shard_map/all_to_all | solution.py:81
  54.8 18.3 %collective-permute-start.3 = (bf16[256,1024]{1,0:T(8,128)(2,1)}, bf16[256,1024]{1,0:T(8,128)(2,1)}, u32[]{:S(2)}, u32[]{:S(2)}) collective-permute-start(bf16[256,1024]{1,0:T(8,128)(2,1)} %param.7), channel_id=1, source_target_pairs={{0,0},{1,1},{64,64},{65,65},{128,128},{129,129},{192,192},{193,193... | collective-permute-start | bytes 1572872 | tf_op jit(solution)/shard_map/ppermute | solution.py:99
  57.9 20.0 %collective-permute-start.2 = (bf16[256,1024]{1,0:T(8,128)(2,1)S(1)}, bf16[256,1024]{1,0:T(8,128)(2,1)S(1)}, u32[]{:S(2)}, u32[]{:S(2)}) collective-permute-start(bf16[256,1024]{1,0:T(8,128)(2,1)S(1)} %collective-permute-done.1), channel_id=1, source_target_pairs={{0,0},{1,1},{64,66},{65,67},{128,132},{129,133},{192,198},{193,199... | collective-permute-start | bytes 1572872 | tf_op jit(solution)/shard_map/ppermute | solution.py:103
  78.0 2.3 copy-start.1
  80.3 51.0 %all-to-all-start.1 = ((bf16[32,2,2,8,1024]{4,3,1,2,0:T(8,128)(2,1)}), bf16[32,2,2,8,1024]{4,3,1,2,0:T(8,128)(2,1)S(1)}, u32[]{:S(2)}, u32[]{:S(2)}) async-start(bf16[32,2,2,8,1024]{4,3,1,2,0:T(8,128)(2,1)} %bitcast.63), calls=%async_computation.1 | async-start | bytes 4194304 | tf_op jit(solution)/shard_map/all_to_all | solution.py:81
  104.4 21.0 %collective-permute-start.4 = (bf16[256,1024]{1,0:T(8,128)(2,1)}, bf16[256,1024]{1,0:T(8,128)(2,1)}, u32[]{:S(2)}, u32[]{:S(2)}) collective-permute-start(bf16[256,1024]{1,0:T(8,128)(2,1)} %collective-permute-done.3), channel_id=1, source_target_pairs={{0,0},{1,1},{64,66},{65,67},{128,132},{129,133},{192,198},{193,199... | collective-permute-start | bytes 1572872 | tf_op jit(solution)/shard_map/ppermute | solution.py:103
  107.2 49.5 %copy-start.3 = (bf16[2,512,128]{2,1,0:T(8,128)(2,1)}, bf16[2,512,128]{2,1,0:T(8,128)(2,1)S(1)}, u32[]{:S(2)}) copy-start(bf16[2,512,128]{2,1,0:T(8,128)(2,1)S(1)} %reshape_reshape.3) | copy-start | bytes 786436
  133.8 28.0 %all-to-all-start.2 = ((bf16[32,2,2,2,1024]{4,3,2,1,0:T(2,128)(2,1)}), bf16[32,2,2,2,1024]{4,3,2,1,0:T(2,128)(2,1)S(1)}, u32[]{:S(2)}, u32[]{:S(2)}) async-start(bf16[32,2,2,2,1024]{4,3,2,1,0:T(2,128)(2,1)} %copy.40), calls=%async_computation.2 | async-start | bytes 1048576 | tf_op jit(solution)/shard_map/all_to_all | solution.py:81
  153.3 3.3 %copy-start = (f32[2,32,2,8,1024]{4,3,2,1,0:T(8,128)}, f32[2,32,2,8,1024]{4,3,2,1,0:T(8,128)S(1)}, u32[]{:S(2)}) copy-start(f32[2,32,2,8,1024]{4,3,2,1,0:T(8,128)S(1)} %copy.37) | copy-start | bytes 12582916
  162.2 11.3 %copy-start.4 = (bf16[2,512,128]{2,1,0:T(8,128)(2,1)S(1)}, bf16[2,512,128]{2,1,0:T(8,128)(2,1)}, u32[]{:S(2)}) copy-start(bf16[2,512,128]{2,1,0:T(8,128)(2,1)} %copy-done.3) | copy-start | bytes 786436
  163.2 10.3 %copy-start.5 = (bf16[2,128,1024]{2,1,0:T(8,128)(2,1)S(1)}, bf16[2,128,1024]{2,1,0:T(8,128)(2,1)}, u32[]{:S(2)}) copy-start(bf16[2,128,1024]{2,1,0:T(8,128)(2,1)} %reshape.64) | copy-start | bytes 1572868
  165.3 26.4 %all-to-all-start.3 = ((bf16[32,2,2,2,1024]{4,3,1,2,0:T(2,128)(2,1)}), bf16[32,2,2,2,1024]{4,3,1,2,0:T(2,128)(2,1)S(1)}, u32[]{:S(2)}, u32[]{:S(2)}) async-start(bf16[32,2,2,2,1024]{4,3,1,2,0:T(2,128)(2,1)} %bitcast.58), calls=%async_computation.3 | async-start | bytes 1048576 | tf_op jit(solution)/shard_map/all_to_all | solution.py:81
  171.6 20.1 %collective-permute-start.6 = (bf16[16,2,8,512]{3,2,1,0:T(8,128)(2,1)S(1)}, bf16[16,2,8,512]{3,2,1,0:T(8,128)(2,1)S(1)}, u32[]{:S(2)}, u32[]{:S(2)}) collective-permute-start(bf16[16,2,8,512]{3,2,1,0:T(8,128)(2,1)S(1)} %bitcast.76), channel_id=1, source_target_pairs={{0,0},{1,1},{66,64},{67,65},{132,128},{133,129},{198,192},{199,193... | collective-permute-start | bytes 786440 | tf_op jit(solution)/shard_map/ppermute | solution.py:136
  191.7 0.7 copy-start.6
  192.4 41.7 %all-to-all-start.4 = ((bf16[32,2,2,8,1024]{4,3,1,2,0:T(8,128)(2,1)}), bf16[32,2,2,8,1024]{4,3,1,2,0:T(8,128)(2,1)S(1)}, u32[]{:S(2)}, u32[]{:S(2)}) async-start(bf16[32,2,2,8,1024]{4,3,1,2,0:T(8,128)(2,1)} %bitcast.56), calls=%async_computation.4 | async-start | bytes 4194304 | tf_op jit(solution)/shard_map/all_to_all | solution.py:81
  201.2 33.5 %copy-start.2 = (bf16[256,1024]{1,0:T(8,128)(2,1)S(1)}, bf16[256,1024]{1,0:T(8,128)(2,1)}, u32[]{:S(2)}) copy-start(bf16[256,1024]{1,0:T(8,128)(2,1)} %copy-done.1) | copy-start | bytes 1572868
  202.2 31.8 %collective-permute-start.5 = (bf16[256,1024]{1,0:T(8,128)(2,1)}, bf16[256,1024]{1,0:T(8,128)(2,1)S(1)}, u32[]{:S(2)}, u32[]{:S(2)}) collective-permute-start(bf16[256,1024]{1,0:T(8,128)(2,1)} %reshape.63), channel_id=1, source_target_pairs={{0,0},{1,1},{66,64},{67,65},{132,128},{133,129},{198,192},{199,193... | collective-permute-start | bytes 1572872 | tf_op jit(solution)/shard_map/ppermute | solution.py:107
  234.2 21.5 %copy-start.7 = (bf16[16,2,8,512]{3,2,1,0:T(8,128)(2,1)S(1)}, bf16[16,2,8,512]{3,2,1,0:T(8,128)(2,1)}, u32[]{:S(2)}) copy-start(bf16[16,2,8,512]{3,2,1,0:T(8,128)(2,1)} %copy-done.6) | copy-start | bytes 786436
  235.6 20.2 %collective-permute-start.7 = (bf16[16,2,8,512]{3,2,1,0:T(8,128)(2,1)S(1)}, bf16[16,2,8,512]{3,2,1,0:T(8,128)(2,1)S(1)}, u32[]{:S(2)}, u32[]{:S(2)}) collective-permute-start(bf16[16,2,8,512]{3,2,1,0:T(8,128)(2,1)S(1)} %bitcast.77), channel_id=1, source_target_pairs={{0,0},{1,1},{66,64},{67,65},{132,128},{133,129},{198,192},{199,193... | collective-permute-start | bytes 786440 | tf_op jit(solution)/shard_map/ppermute | solution.py:136
  237.9 51.1 %collective-permute-start.9 = (bf16[256,1024]{1,0:T(8,128)(2,1)S(1)}, bf16[256,1024]{1,0:T(8,128)(2,1)S(1)}, u32[]{:S(2)}, u32[]{:S(2)}) collective-permute-start(bf16[256,1024]{1,0:T(8,128)(2,1)S(1)} %bitcast.75), channel_id=1, source_target_pairs={{0,0},{1,1},{66,64},{67,65},{132,128},{133,129},{198,192},{199,193... | collective-permute-start | bytes 1572872 | tf_op jit(solution)/shard_map/ppermute | solution.py:115
  256.6 41.0 %all-to-all-start.5 = ((bf16[16,4,8,512]{3,2,1,0:T(8,128)(2,1)}), bf16[16,4,8,512]{3,2,1,0:T(8,128)(2,1)S(1)}, u32[]{:S(2)}, u32[]{:S(2)}) async-start(bf16[16,4,8,512]{3,2,1,0:T(8,128)(2,1)} %pad_maximum_fusion), calls=%async_computation.5 | async-start | bytes 1048576 | tf_op jit(solution)/shard_map/all_to_all | solution.py:141
  286.8 22.0 %collective-permute-start.8 = (bf16[256,1024]{1,0:T(8,128)(2,1)S(1)}, bf16[256,1024]{1,0:T(8,128)(2,1)S(1)}, u32[]{:S(2)}, u32[]{:S(2)}) collective-permute-start(bf16[256,1024]{1,0:T(8,128)(2,1)S(1)} %collective-permute-done.5), channel_id=1, source_target_pairs={{0,0},{1,1},{64,64},{65,65},{128,128},{129,129},{192,192},{193,193... | collective-permute-start | bytes 1572872 | tf_op jit(solution)/shard_map/ppermute | solution.py:111

commit v8 on v5

--- a/solution.py
+++ b/solution.py
@@ -98,25 +98,28 @@
     return got[:, :nb], got[:, nb:]
 
 
+def to_class(rows):
+    return lax.ppermute(rows, DEVICES, PLAN.weights)
+
+
 def whole(rows, height, width):
     n, nb = rows.shape[:2]
-    rows = lax.ppermute(rows, DEVICES, PLAN.weights)
     return rows.reshape(n, nb, height // n, width).transpose(1, 0, 2, 3).reshape(nb, height, width)
 
 
-def sum_rows(up_term, down_term):
+def to_rows(term):
     n = lax.axis_size("dp")
-    nb, hu, wu = up_term.shape
-    hd, wd = down_term.shape[1:]
-    ru, rd = hu // n, hd // n
-    u = up_term.astype(BF16).reshape(nb, n, ru, wu).transpose(1, 0, 2, 3)
-    d = down_term.astype(BF16).reshape(nb, n, ru, wu).transpose(1, 0, 2, 3)
-    u = lax.ppermute(u, DEVICES, back(PLAN.weights))
-    d = lax.ppermute(d, DEVICES, back(PLAN.weights))
-    both = jnp.concatenate([u, d], axis=1)
+    nb = term.shape[0]
+    rows = term.astype(BF16).reshape(nb, n, -1, BOUT).transpose(1, 0, 2, 3)
+    return lax.ppermute(rows, DEVICES, back(PLAN.weights))
+
+
+def sum_rows(up_term, down_term, down_shape):
+    both = jnp.concatenate([up_term, down_term], axis=1)
     got = lax.all_to_all(both, "dp", split_axis=0, concat_axis=0, tiled=True)
     s = jnp.sum(got.astype(F32), axis=0)
-    return s[:nb], s[nb:].reshape(nb, rd, wd)
+    nb = down_shape[0]
+    return s[:nb], s[nb:].reshape(down_shape)
 
 
 def per_device(features, up_blocks, down_blocks, out_cotangent):
@@ -124,15 +127,17 @@
     t = features.shape[1]
     n = NB // nb
     moved = shuffle(features)
-    cot = mirror(shuffle(out_cotangent))
+    moved_cot = shuffle(out_cotangent)
     up_rows, down_rows = gather_rows(up_blocks, down_blocks)
+    cot = mirror(after(moved_cot, up_rows))
+    up_rows = to_class(up_rows)
     up = whole(up_rows, BIN, BOUT)
     x_flat = mirror(after(moved, cot))
-    dblock = exchange(cot.reshape(nb, n, nb, J_DN, t).transpose(1, 2, 0, 3, 4))
+    dblock = exchange(after(cot, up_rows).reshape(nb, n, nb, J_DN, t).transpose(1, 2, 0, 3, 4))
     x = after(x_flat, dblock).reshape(nb, BIN, t)
     pre = jnp.einsum("bkn,bkt->bnt", up, x, preferred_element_type=F32).astype(BF16)
     permuted = exchange(pre.reshape(nb, n, nb, J_UP, t).transpose(1, 2, 0, 3, 4))
-    down = whole(after(down_rows, x_flat), BOUT, BIN)
+    down = whole(to_class(after(down_rows, x_flat)), BOUT, BIN)
     permuted = permuted.transpose(1, 0, 2, 3, 4).reshape(nb, BOUT, t)
     pf = permuted.astype(F32)
     act = gelu_value(pf).astype(BF16)
@@ -146,13 +151,14 @@
     dpre = exchange(after(dperm, mixed))
     mixed = unmirror(mixed.transpose(1, 0, 2, 3, 4).reshape(nb * BIN, t))
     down_term = jnp.einsum("gmt,gct->gmc", act, dblock, preferred_element_type=F32)
-    dpre = after(dpre, mixed).transpose(1, 0, 2, 3, 4).reshape(nb, BOUT, t)
+    dpre = dpre.transpose(1, 0, 2, 3, 4).reshape(nb, BOUT, t)
     fgrad = jnp.einsum("bkn,bnt->bkt", up, dpre, preferred_element_type=F32).astype(BF16)
     fgrad = fgrad.reshape(nb * BIN, t)
-    dpre = after(dpre, fgrad)
+    dpre = after(dpre, fgrad, mixed)
     up_term = jnp.einsum("bkt,bnt->bkn", x, dpre, preferred_element_type=F32)
-    up_grad, down_grad = sum_rows(up_term, down_term)
-    return unshuffle(mixed), to_store(fgrad), up_grad, down_grad
+    up_term = to_rows(up_term)
+    up_grad, down_grad = sum_rows(up_term, to_rows(down_term), down_blocks.shape)
+    return unshuffle(after(mixed, up_term)), to_store(fgrad), up_grad, down_grad
 
 
 def solution(mesh):

time: 297 us -> 309 us (1.040)
  the two profiles are of different devices: /device:TPU:32 before, /device:TPU:161 now
where the time goes in v8:
time: 309 us; the launch traced here: 308 us
  waiting for transfers between devices  108 us (35%)
  starting transfers between devices  107 us (35%)
  blocking collectives  61.5 us (20%)
  local copies, waits for them, and re-layouts  16 us (5%)
  matrix products  9.33 us (3%)
  other arithmetic  5.31 us (2%)
    all_to_all x1, blocking collectives, exchange(): lax.all_to_all(x, DEVICES, split_axis=0, concat_axis=0, tiled=True, axis_...  61.5 us
    all_to_all x3, waiting for transfers between devices, exchange(): lax.all_to_all(x, DEVICES, split_axis=0, concat_axis=0, tiled=True, axis_...  38 us
    all_to_all x1, starting transfers between devices, sum_rows(): got = lax.all_to_all(both, 'dp', split_axis=0, concat_axis=0, tiled=True)  37.5 us
    all_to_all x3, starting transfers between devices, exchange(): lax.all_to_all(x, DEVICES, split_axis=0, concat_axis=0, tiled=True, axis_...  26.7 us
    ppermute x2, waiting for transfers between devices, to_class(): return lax.ppermute(rows, DEVICES, PLAN.weights)  14.2 us
    ppermute x2, waiting for transfers between devices, mirror(): return lax.ppermute(x, DEVICES, PLAN.mirror)  13.1 us
    ppermute x2, waiting for transfers between devices, shuffle(): return lax.ppermute(x, DEVICES, PLAN.shuffle)  12.4 us
    ppermute x2, waiting for transfers between devices, to_rows(): return lax.ppermute(rows, DEVICES, back(PLAN.weights))  11.3 us
  transfers between devices with their start and end apart: 16, of which 12 were waited for; matrix products, arithmetic and copies ran while one was open for 6% of the time, Pallas kernels for 0%

profile of v8, /device:TPU:161, one launch (start us, length us, event | category | flops | bytes accessed | tf_op | source)
XLA Modules:
  0.0 307.8 jit_solution(1589900936665427329)
XLA Ops:
  2.9 7.6 %all-to-all-start = ((bf16[16,4,8,512]{3,2,1,0:T(8,128)(2,1)}), bf16[16,4,8,512]{3,2,1,0:T(8,128)(2,1)S(1)}, u32[]{:S(2)}, u32[]{:S(2)}) async-start(bf16[16,4,8,512]{3,2,1,0:T(8,128)(2,1)} %broadcast_in_dim.3), calls=%async_computation | async-start | bytes 1048576 | tf_op jit(solution)/shard_map/all_to_all | solution.py:97
  10.6 5.4 %collective-permute-start.1 = (bf16[256,1024]{1,0:T(8,128)(2,1)}, bf16[256,1024]{1,0:T(8,128)(2,1)S(1)}, u32[]{:S(2)}, u32[]{:S(2)}) collective-permute-start(bf16[256,1024]{1,0:T(8,128)(2,1)} %param.7), channel_id=1, source_target_pairs={{0,0},{1,1},{32,32},{33,33},{64,64},{65,65},{96,96},{97,97},{128,1... | collective-permute-start | bytes 1572872 | tf_op jit(solution)/shard_map/ppermute | solution.py:73
  16.0 3.3 %collective-permute-start = (bf16[256,1024]{1,0:T(8,128)(2,1)}, bf16[256,1024]{1,0:T(8,128)(2,1)S(1)}, u32[]{:S(2)}, u32[]{:S(2)}) collective-permute-start(bf16[256,1024]{1,0:T(8,128)(2,1)} %param.4), channel_id=1, source_target_pairs={{0,0},{1,1},{32,32},{33,33},{64,64},{65,65},{96,96},{97,97},{128,1... | collective-permute-start | bytes 1572872 | tf_op jit(solution)/shard_map/ppermute | solution.py:73
  22.6 9.2 %collective-permute-done.1 = bf16[256,1024]{1,0:T(8,128)(2,1)S(1)} collective-permute-done((bf16[256,1024]{1,0:T(8,128)(2,1)}, bf16[256,1024]{1,0:T(8,128)(2,1)S(1)}, u32[]{:S(2)}, u32[]{:S(2)}) %collective-permute-start.1) | collective-permute-done | bytes 524320 | tf_op jit(solution)/shard_map/ppermute | solution.py:73
  34.0 5.2 %collective-permute-start.5 = (bf16[16,2,8,512]{3,2,0,1:T(8,128)(2,1)S(1)}, bf16[16,2,8,512]{3,2,0,1:T(8,128)(2,1)S(1)}, u32[]{:S(2)}, u32[]{:S(2)}) collective-permute-start(bf16[16,2,8,512]{3,2,0,1:T(8,128)(2,1)S(1)} %copy.51), channel_id=1, source_target_pairs={{0,0},{1,1},{32,48},{33,49},{64,66},{65,67},{96,114},{97,115},{128... | collective-permute-start | bytes 786440 | tf_op jit(solution)/shard_map/ppermute | solution.py:102
  39.2 3.2 %collective-permute-done = bf16[256,1024]{1,0:T(8,128)(2,1)S(1)} collective-permute-done((bf16[256,1024]{1,0:T(8,128)(2,1)}, bf16[256,1024]{1,0:T(8,128)(2,1)S(1)}, u32[]{:S(2)}, u32[]{:S(2)}) %collective-permute-start) | collective-permute-done | bytes 524320 | tf_op jit(solution)/shard_map/ppermute | solution.py:73
  42.4 13.1 %collective-permute-done.2 = bf16[256,1024]{1,0:T(8,128)(2,1)S(1)} collective-permute-done((bf16[256,1024]{1,0:T(8,128)(2,1)S(1)}, bf16[256,1024]{1,0:T(8,128)(2,1)S(1)}, u32[]{:S(2)}, u32[]{:S(2)}) %collective-permute-start.2) | collective-permute-done | bytes 524320 | tf_op jit(solution)/shard_map/ppermute | solution.py:77
  57.4 6.8 %collective-permute-done.5 = bf16[16,2,8,512]{3,2,0,1:T(8,128)(2,1)S(1)} collective-permute-done((bf16[16,2,8,512]{3,2,0,1:T(8,128)(2,1)S(1)}, bf16[16,2,8,512]{3,2,0,1:T(8,128)(2,1)S(1)}, u32[]{:S(2)}, u32[]{:S(2)}) %collective-permute-start.5) | collective-permute-done | bytes 262176 | tf_op jit(solution)/shard_map/ppermute | solution.py:102
  65.0 61.5 %all_to_all.30 = bf16[32,2,2,2,1024]{4,3,2,1,0:T(2,128)(2,1)S(1)} all-to-all(bf16[32,2,2,2,1024]{4,3,2,1,0:T(2,128)(2,1)S(1)} %copy.37), channel_id=1, replica_groups={{0,1,64,65,128,129,192,193,257,256,321,320,385,384,449,448,32,33,96,97,..., dimensions={0} | all-to-all | bytes 1048576 | tf_op jit(solution)/shard_map/all_to_all | solution.py:63
  128.7 7.2 %all-to-all-start.2 = ((bf16[32,2,2,8,1024]{4,3,1,2,0:T(8,128)(2,1)}), bf16[32,2,2,8,1024]{4,3,1,2,0:T(8,128)(2,1)S(1)}, u32[]{:S(2)}, u32[]{:S(2)}) async-start(bf16[32,2,2,8,1024]{4,3,1,2,0:T(8,128)(2,1)} %bitcast.65), calls=%async_computation.2 | async-start | bytes 4194304 | tf_op jit(solution)/shard_map/all_to_all | solution.py:63
  139.2 7.4 %collective-permute-done.4 = bf16[16,2,8,512]{3,2,1,0:T(8,128)(2,1)S(1)} collective-permute-done((bf16[16,2,8,512]{3,2,1,0:T(8,128)(2,1)}, bf16[16,2,8,512]{3,2,1,0:T(8,128)(2,1)S(1)}, u32[]{:S(2)}, u32[]{:S(2)}) %collective-permute-start.4) | collective-permute-done | bytes 262176 | tf_op jit(solution)/shard_map/ppermute | solution.py:102
  146.8 17.4 %all-to-all-done.2 = bf16[32,2,2,8,1024]{4,3,1,2,0:T(8,128)(2,1)S(1)} async-done(((bf16[32,2,2,8,1024]{4,3,1,2,0:T(8,128)(2,1)}), bf16[32,2,2,8,1024]{4,3,1,2,0:T(8,128)(2,1)S(1)}, u32[]{:S(2)}, u32[]{:S(2)}) %all-to-all-start.2) | async-done | bytes 2097184 | tf_op jit(solution)/shard_map/all_to_all | solution.py:63
  165.3 3.2 %fusion.7 = (bf16[2,512,1024]{2,1,0:T(8,128)(2,1)S(1)}, f32[2,512,1024]{2,1,0:T(8,128)}) fusion(f32[2,32,2,8,1024]{4,3,2,1,0:T(8,128)S(1)} %copy.40), kind=kLoop, calls=%fused_computation.10 | loop fusion | flops 5242880 | bytes 10485760 | tf_op jit(solution)/shard_map/convert_element_type | solution.py:143
  170.6 11.6 %all-to-all-start.3 = ((bf16[32,2,2,2,1024]{4,3,1,2,0:T(2,128)(2,1)}), bf16[32,2,2,2,1024]{4,3,1,2,0:T(2,128)(2,1)S(1)}, u32[]{:S(2)}, u32[]{:S(2)}) async-start(bf16[32,2,2,2,1024]{4,3,1,2,0:T(2,128)(2,1)} %bitcast.59), calls=%async_computation.3 | async-start | bytes 1048576 | tf_op jit(solution)/shard_map/all_to_all | solution.py:63
  182.2 5.1 %fusion.5 = bf16[2,512,1024]{2,1,0:T(8,128)(2,1)S(1)} fusion(f32[2,32,2,8,1024]{4,3,2,1,0:T(8,128)} %copy-done, f32[2,512,1024]{2,1,0:T(8,128)} %get-tuple-element.21, bf16[2,512,128]{2,1,0:T(8,128)(2,1)S(1)} %bitcast.75, bf16[2,128,1024]{2,1,0:T(8,128)(2,1)} %reshape.68), kind=kOutput, calls=%fused_computation.6 | convolution fusion | flops 276824064 | bytes 11272192 | tf_op jit(solution)/shard_map/gmc,gct->gmt/dot_general | solution.py:148
  188.8 2.6 all-to-all-done.3
  191.3 7.9 %all-to-all-start.4 = ((bf16[32,2,2,8,1024]{4,3,1,2,0:T(8,128)(2,1)}), bf16[32,2,2,8,1024]{4,3,1,2,0:T(8,128)(2,1)}, u32[]{:S(2)}, u32[]{:S(2)}) async-start(bf16[32,2,2,8,1024]{4,3,1,2,0:T(8,128)(2,1)} %bitcast.64), calls=%async_computation.4 | async-start | bytes 4194304 | tf_op jit(solution)/shard_map/all_to_all | solution.py:63
  204.6 4.9 %collective-permute-start.10 = (bf16[16,2,8,512]{3,2,1,0:T(8,128)(2,1)S(1)}, bf16[16,2,8,512]{3,2,1,0:T(8,128)(2,1)S(1)}, u32[]{:S(2)}, u32[]{:S(2)}) collective-permute-start(bf16[16,2,8,512]{3,2,1,0:T(8,128)(2,1)S(1)} %bitcast.77), channel_id=1, source_target_pairs={{0,0},{1,1},{48,32},{49,33},{66,64},{67,65},{114,96},{115,97},{132... | collective-permute-start | bytes 786440 | tf_op jit(solution)/shard_map/ppermute | solution.py:114
  209.5 18.1 %all-to-all-done.4 = bf16[32,2,2,8,1024]{4,3,1,2,0:T(8,128)(2,1)} async-done(((bf16[32,2,2,8,1024]{4,3,1,2,0:T(8,128)(2,1)}), bf16[32,2,2,8,1024]{4,3,1,2,0:T(8,128)(2,1)}, u32[]{:S(2)}, u32[]{:S(2)}) %all-to-all-start.4) | async-done | bytes 2097184 | tf_op jit(solution)/shard_map/all_to_all | solution.py:63
  234.5 11.3 %collective-permute-done.7 = bf16[16,2,8,512]{3,2,1,0:T(8,128)(2,1)S(1)} collective-permute-done((bf16[16,2,8,512]{3,2,1,0:T(8,128)(2,1)S(1)}, bf16[16,2,8,512]{3,2,1,0:T(8,128)(2,1)S(1)}, u32[]{:S(2)}, u32[]{:S(2)}) %collective-permute-start.7) | collective-permute-done | bytes 262176 | tf_op jit(solution)/shard_map/ppermute | solution.py:114
  246.7 37.5 %all-to-all-start.5 = ((bf16[16,4,8,512]{3,2,1,0:T(8,128)(2,1)}), bf16[16,4,8,512]{3,2,1,0:T(8,128)(2,1)S(1)}, u32[]{:S(2)}, u32[]{:S(2)}) async-start(bf16[16,4,8,512]{3,2,1,0:T(8,128)(2,1)} %pad_maximum_fusion), calls=%async_computation.5 | async-start | bytes 1048576 | tf_op jit(solution)/shard_map/all_to_all | solution.py:119
  284.2 4.7 %collective-permute-start.8 = (bf16[256,1024]{1,0:T(8,128)(2,1)S(1)}, bf16[256,1024]{1,0:T(8,128)(2,1)S(1)}, u32[]{:S(2)}, u32[]{:S(2)}) collective-permute-start(bf16[256,1024]{1,0:T(8,128)(2,1)S(1)} %collective-permute-done.6), channel_id=1, source_target_pairs={{0,0},{1,1},{32,32},{33,33},{64,64},{65,65},{96,96},{97,97},{128,1... | collective-permute-start | bytes 1572872 | tf_op jit(solution)/shard_map/ppermute | solution.py:85
  289.0 6.6 %all-to-all-done.5 = bf16[16,4,8,512]{3,2,1,0:T(8,128)(2,1)S(1)} async-done(((bf16[16,4,8,512]{3,2,1,0:T(8,128)(2,1)}), bf16[16,4,8,512]{3,2,1,0:T(8,128)(2,1)S(1)}, u32[]{:S(2)}, u32[]{:S(2)}) %all-to-all-start.5) | async-done | bytes 524320 | tf_op jit(solution)/shard_map/all_to_all | solution.py:119
  296.9 9.3 %collective-permute-done.8 = bf16[256,1024]{1,0:T(8,128)(2,1)S(1)} collective-permute-done((bf16[256,1024]{1,0:T(8,128)(2,1)S(1)}, bf16[256,1024]{1,0:T(8,128)(2,1)S(1)}, u32[]{:S(2)}, u32[]{:S(2)}) %collective-permute-start.8) | collective-permute-done | bytes 524320 | tf_op jit(solution)/shard_map/ppermute | solution.py:85
  (55 shorter events, 36.9 us)
Async XLA Ops:
  2.9 18.9 %all-to-all-start = ((bf16[16,4,8,512]{3,2,1,0:T(8,128)(2,1)}), bf16[16,4,8,512]{3,2,1,0:T(8,128)(2,1)S(1)}, u32[]{:S(2)}, u32[]{:S(2)}) async-start(bf16[16,4,8,512]{3,2,1,0:T(8,128)(2,1)} %broadcast_in_dim.3), calls=%async_computation | async-start | bytes 1048576 | tf_op jit(solution)/shard_map/all_to_all | solution.py:97
  10.6 21.2 %collective-permute-start.1 = (bf16[256,1024]{1,0:T(8,128)(2,1)}, bf16[256,1024]{1,0:T(8,128)(2,1)S(1)}, u32[]{:S(2)}, u32[]{:S(2)}) collective-permute-start(bf16[256,1024]{1,0:T(8,128)(2,1)} %param.7), channel_id=1, source_target_pairs={{0,0},{1,1},{32,32},{33,33},{64,64},{65,65},{96,96},{97,97},{128,1... | collective-permute-start | bytes 1572872 | tf_op jit(solution)/shard_map/ppermute | solution.py:73
  16.0 26.4 %collective-permute-start = (bf16[256,1024]{1,0:T(8,128)(2,1)}, bf16[256,1024]{1,0:T(8,128)(2,1)S(1)}, u32[]{:S(2)}, u32[]{:S(2)}) collective-permute-start(bf16[256,1024]{1,0:T(8,128)(2,1)} %param.4), channel_id=1, source_target_pairs={{0,0},{1,1},{32,32},{33,33},{64,64},{65,65},{96,96},{97,97},{128,1... | collective-permute-start | bytes 1572872 | tf_op jit(solution)/shard_map/ppermute | solution.py:73
  31.8 23.7 %collective-permute-start.2 = (bf16[256,1024]{1,0:T(8,128)(2,1)S(1)}, bf16[256,1024]{1,0:T(8,128)(2,1)S(1)}, u32[]{:S(2)}, u32[]{:S(2)}) collective-permute-start(bf16[256,1024]{1,0:T(8,128)(2,1)S(1)} %collective-permute-done.1), channel_id=1, source_target_pairs={{0,0},{1,1},{32,48},{33,49},{64,66},{65,67},{96,114},{97,115},{128... | collective-permute-start | bytes 1572872 | tf_op jit(solution)/shard_map/ppermute | solution.py:77
  34.0 30.2 %collective-permute-start.5 = (bf16[16,2,8,512]{3,2,0,1:T(8,128)(2,1)S(1)}, bf16[16,2,8,512]{3,2,0,1:T(8,128)(2,1)S(1)}, u32[]{:S(2)}, u32[]{:S(2)}) collective-permute-start(bf16[16,2,8,512]{3,2,0,1:T(8,128)(2,1)S(1)} %copy.51), channel_id=1, source_target_pairs={{0,0},{1,1},{32,48},{33,49},{64,66},{65,67},{96,114},{97,115},{128... | collective-permute-start | bytes 786440 | tf_op jit(solution)/shard_map/ppermute | solution.py:102
  55.5 70.9 %collective-permute-start.3 = (bf16[256,1024]{1,0:T(8,128)(2,1)S(1)}, bf16[256,1024]{1,0:T(8,128)(2,1)S(1)}, u32[]{:S(2)}, u32[]{:S(2)}) collective-permute-start(bf16[256,1024]{1,0:T(8,128)(2,1)S(1)} %collective-permute-done), channel_id=1, source_target_pairs={{0,0},{1,1},{32,48},{33,49},{64,66},{65,67},{96,114},{97,115},{128... | collective-permute-start | bytes 1572872 | tf_op jit(solution)/shard_map/ppermute | solution.py:77
  64.2 64.5 %copy-start.3 = (bf16[16,2,8,512]{3,2,0,1:T(8,128)(2,1)}, bf16[16,2,8,512]{3,2,0,1:T(8,128)(2,1)S(1)}, u32[]{:S(2)}) copy-start(bf16[16,2,8,512]{3,2,0,1:T(8,128)(2,1)S(1)} %collective-permute-done.5) | copy-start | bytes 786436
  126.4 2.3 copy-start.1
  128.7 35.5 %all-to-all-start.2 = ((bf16[32,2,2,8,1024]{4,3,1,2,0:T(8,128)(2,1)}), bf16[32,2,2,8,1024]{4,3,1,2,0:T(8,128)(2,1)S(1)}, u32[]{:S(2)}, u32[]{:S(2)}) async-start(bf16[32,2,2,8,1024]{4,3,1,2,0:T(8,128)(2,1)} %bitcast.65), calls=%async_computation.2 | async-start | bytes 4194304 | tf_op jit(solution)/shard_map/all_to_all | solution.py:63
  135.9 10.7 %collective-permute-start.4 = (bf16[16,2,8,512]{3,2,1,0:T(8,128)(2,1)}, bf16[16,2,8,512]{3,2,1,0:T(8,128)(2,1)S(1)}, u32[]{:S(2)}, u32[]{:S(2)}) collective-permute-start(bf16[16,2,8,512]{3,2,1,0:T(8,128)(2,1)} %get-tuple-element.14), channel_id=1, source_target_pairs={{0,0},{1,1},{32,48},{33,49},{64,66},{65,67},{96,114},{97,115},{128... | collective-permute-start | bytes 786440 | tf_op jit(solution)/shard_map/ppermute | solution.py:102
  165.3 3.3 %copy-start = (f32[2,32,2,8,1024]{4,3,2,1,0:T(8,128)}, f32[2,32,2,8,1024]{4,3,2,1,0:T(8,128)S(1)}, u32[]{:S(2)}) copy-start(f32[2,32,2,8,1024]{4,3,2,1,0:T(8,128)S(1)} %copy.40) | copy-start | bytes 12582916
  170.6 20.7 %all-to-all-start.3 = ((bf16[32,2,2,2,1024]{4,3,1,2,0:T(2,128)(2,1)}), bf16[32,2,2,2,1024]{4,3,1,2,0:T(2,128)(2,1)S(1)}, u32[]{:S(2)}, u32[]{:S(2)}) async-start(bf16[32,2,2,2,1024]{4,3,1,2,0:T(2,128)(2,1)} %bitcast.59), calls=%async_computation.3 | async-start | bytes 1048576 | tf_op jit(solution)/shard_map/all_to_all | solution.py:63
  191.3 36.2 %all-to-all-start.4 = ((bf16[32,2,2,8,1024]{4,3,1,2,0:T(8,128)(2,1)}), bf16[32,2,2,8,1024]{4,3,1,2,0:T(8,128)(2,1)}, u32[]{:S(2)}, u32[]{:S(2)}) async-start(bf16[32,2,2,8,1024]{4,3,1,2,0:T(8,128)(2,1)} %bitcast.64), calls=%async_computation.4 | async-start | bytes 4194304 | tf_op jit(solution)/shard_map/all_to_all | solution.py:63
  200.6 28.7 %copy-start.4 = (bf16[16,2,8,512]{3,2,0,1:T(8,128)(2,1)S(1)}, bf16[16,2,8,512]{3,2,0,1:T(8,128)(2,1)}, u32[]{:S(2)}) copy-start(bf16[16,2,8,512]{3,2,0,1:T(8,128)(2,1)} %copy-done.3) | copy-start | bytes 786436
  200.6 29.2 %collective-permute-start.6 = (bf16[256,1024]{1,0:T(8,128)(2,1)}, bf16[256,1024]{1,0:T(8,128)(2,1)S(1)}, u32[]{:S(2)}, u32[]{:S(2)}) collective-permute-start(bf16[256,1024]{1,0:T(8,128)(2,1)} %reshape.67), channel_id=1, source_target_pairs={{0,0},{1,1},{48,32},{49,33},{66,64},{67,65},{114,96},{115,97},{132... | collective-permute-start | bytes 1572872 | tf_op jit(solution)/shard_map/ppermute | solution.py:81
  204.4 25.4 %copy-start.2 = (bf16[256,1024]{1,0:T(8,128)(2,1)S(1)}, bf16[256,1024]{1,0:T(8,128)(2,1)}, u32[]{:S(2)}) copy-start(bf16[256,1024]{1,0:T(8,128)(2,1)} %copy-done.1) | copy-start | bytes 1572868
  204.6 29.9 %collective-permute-start.10 = (bf16[16,2,8,512]{3,2,1,0:T(8,128)(2,1)S(1)}, bf16[16,2,8,512]{3,2,1,0:T(8,128)(2,1)S(1)}, u32[]{:S(2)}, u32[]{:S(2)}) collective-permute-start(bf16[16,2,8,512]{3,2,1,0:T(8,128)(2,1)S(1)} %bitcast.77), channel_id=1, source_target_pairs={{0,0},{1,1},{48,32},{49,33},{66,64},{67,65},{114,96},{115,97},{132... | collective-permute-start | bytes 786440 | tf_op jit(solution)/shard_map/ppermute | solution.py:114
  230.7 15.2 %collective-permute-start.7 = (bf16[16,2,8,512]{3,2,1,0:T(8,128)(2,1)S(1)}, bf16[16,2,8,512]{3,2,1,0:T(8,128)(2,1)S(1)}, u32[]{:S(2)}, u32[]{:S(2)}) collective-permute-start(bf16[16,2,8,512]{3,2,1,0:T(8,128)(2,1)S(1)} %bitcast.78), channel_id=1, source_target_pairs={{0,0},{1,1},{48,32},{49,33},{66,64},{67,65},{114,96},{115,97},{132... | collective-permute-start | bytes 786440 | tf_op jit(solution)/shard_map/ppermute | solution.py:114
  232.6 56.3 %collective-permute-start.9 = (bf16[256,1024]{1,0:T(8,128)(2,1)S(1)}, bf16[256,1024]{1,0:T(8,128)(2,1)S(1)}, u32[]{:S(2)}, u32[]{:S(2)}) collective-permute-start(bf16[256,1024]{1,0:T(8,128)(2,1)S(1)} %bitcast.76), channel_id=1, source_target_pairs={{0,0},{1,1},{48,32},{49,33},{66,64},{67,65},{114,96},{115,97},{132... | collective-permute-start | bytes 1572872 | tf_op jit(solution)/shard_map/ppermute | solution.py:89
  246.7 48.9 %all-to-all-start.5 = ((bf16[16,4,8,512]{3,2,1,0:T(8,128)(2,1)}), bf16[16,4,8,512]{3,2,1,0:T(8,128)(2,1)S(1)}, u32[]{:S(2)}, u32[]{:S(2)}) async-start(bf16[16,4,8,512]{3,2,1,0:T(8,128)(2,1)} %pad_maximum_fusion), calls=%async_computation.5 | async-start | bytes 1048576 | tf_op jit(solution)/shard_map/all_to_all | solution.py:119
  284.2 22.0 %collective-permute-start.8 = (bf16[256,1024]{1,0:T(8,128)(2,1)S(1)}, bf16[256,1024]{1,0:T(8,128)(2,1)S(1)}, u32[]{:S(2)}, u32[]{:S(2)}) collective-permute-start(bf16[256,1024]{1,0:T(8,128)(2,1)S(1)} %collective-permute-done.6), channel_id=1, source_target_pairs={{0,0},{1,1},{32,32},{33,33},{64,64},{65,65},{96,96},{97,97},{128,1... | collective-permute-start | bytes 1572872 | tf_op jit(solution)/shard_map/ppermute | solution.py:85

commit v9 on v8

--- a/solution.py
+++ b/solution.py
@@ -98,12 +98,9 @@
     return got[:, :nb], got[:, nb:]
 
 
-def to_class(rows):
-    return lax.ppermute(rows, DEVICES, PLAN.weights)
-
-
 def whole(rows, height, width):
     n, nb = rows.shape[:2]
+    rows = lax.ppermute(rows, DEVICES, PLAN.weights)
     return rows.reshape(n, nb, height // n, width).transpose(1, 0, 2, 3).reshape(nb, height, width)
 
 
@@ -127,38 +124,34 @@
     t = features.shape[1]
     n = NB // nb
     moved = shuffle(features)
-    moved_cot = shuffle(out_cotangent)
+    cot = mirror(shuffle(out_cotangent))
     up_rows, down_rows = gather_rows(up_blocks, down_blocks)
-    cot = mirror(after(moved_cot, up_rows))
-    up_rows = to_class(up_rows)
     up = whole(up_rows, BIN, BOUT)
     x_flat = mirror(after(moved, cot))
-    dblock = exchange(after(cot, up_rows).reshape(nb, n, nb, J_DN, t).transpose(1, 2, 0, 3, 4))
+    dblock = exchange(cot.reshape(nb, n, nb, J_DN, t).transpose(1, 2, 0, 3, 4))
     x = after(x_flat, dblock).reshape(nb, BIN, t)
     pre = jnp.einsum("bkn,bkt->bnt", up, x, preferred_element_type=F32).astype(BF16)
     permuted = exchange(pre.reshape(nb, n, nb, J_UP, t).transpose(1, 2, 0, 3, 4))
-    down = whole(to_class(after(down_rows, x_flat)), BOUT, BIN)
+    down = whole(after(down_rows, x_flat), BOUT, BIN)
     permuted = permuted.transpose(1, 0, 2, 3, 4).reshape(nb, BOUT, t)
     pf = permuted.astype(F32)
-    act = gelu_value(pf).astype(BF16)
-    blockout = jnp.einsum("gmc,gmt->gct", down, act, preferred_element_type=F32).astype(BF16)
-    blockout = blockout.reshape(nb, n, nb, J_DN, t).transpose(1, 2, 0, 3, 4)
-    mixed = exchange(blockout)
     dblock = dblock.transpose(1, 0, 2, 3, 4).reshape(nb, BIN, t)
     dact = jnp.einsum("gmc,gct->gmt", down, dblock, preferred_element_type=F32)
     dperm = (dact * gelu_slope(pf)).astype(BF16)
-    dperm = dperm.reshape(nb, n, nb, J_UP, t).transpose(1, 2, 0, 3, 4)
-    dpre = exchange(after(dperm, mixed))
-    mixed = unmirror(mixed.transpose(1, 0, 2, 3, 4).reshape(nb * BIN, t))
-    down_term = jnp.einsum("gmt,gct->gmc", act, dblock, preferred_element_type=F32)
+    dpre = exchange(dperm.reshape(nb, n, nb, J_UP, t).transpose(1, 2, 0, 3, 4))
+    act = gelu_value(pf).astype(BF16)
+    down_term = to_rows(jnp.einsum("gmt,gct->gmc", act, dblock, preferred_element_type=F32))
+    blockout = jnp.einsum("gmc,gmt->gct", down, act, preferred_element_type=F32).astype(BF16)
+    blockout = blockout.reshape(nb, n, nb, J_DN, t).transpose(1, 2, 0, 3, 4)
+    mixed = exchange(after(blockout, dpre, down_term))
     dpre = dpre.transpose(1, 0, 2, 3, 4).reshape(nb, BOUT, t)
     fgrad = jnp.einsum("bkn,bnt->bkt", up, dpre, preferred_element_type=F32).astype(BF16)
-    fgrad = fgrad.reshape(nb * BIN, t)
-    dpre = after(dpre, fgrad, mixed)
-    up_term = jnp.einsum("bkt,bnt->bkn", x, dpre, preferred_element_type=F32)
-    up_term = to_rows(up_term)
-    up_grad, down_grad = sum_rows(up_term, to_rows(down_term), down_blocks.shape)
-    return unshuffle(after(mixed, up_term)), to_store(fgrad), up_grad, down_grad
+    fgrad = unmirror(fgrad.reshape(nb * BIN, t))
+    up_term = to_rows(jnp.einsum("bkt,bnt->bkn", x, dpre, preferred_element_type=F32))
+    mixed = mixed.transpose(1, 0, 2, 3, 4).reshape(nb * BIN, t)
+    mixed = to_store(after(mixed, fgrad))
+    up_grad, down_grad = sum_rows(up_term, down_term, down_blocks.shape)
+    return mixed, unshuffle(fgrad), up_grad, down_grad
 
 
 def solution(mesh):

time: 309 us -> 300 us (0.971)
  the two profiles are of different devices: /device:TPU:161 before, /device:TPU:1 now
where the time goes in v9:
time: 300 us; the launch traced here: 299 us
  starting transfers between devices  142 us (47%)
  waiting for transfers between devices  131 us (44%)
  local copies, waits for them, and re-layouts  16.9 us (6%)
  matrix products  4.68 us (2%)
  other arithmetic  4.23 us (1%)
    all_to_all x4, starting transfers between devices, exchange(): lax.all_to_all(x, DEVICES, split_axis=0, concat_axis=0, tiled=True, axis_...  55.3 us
    ppermute x2, waiting for transfers between devices, to_rows(): return lax.ppermute(rows, DEVICES, back(PLAN.weights))  41.1 us
    ppermute x1, waiting for transfers between devices, to_store(): return lax.ppermute(x, DEVICES, PLAN.home)  31.9 us
    all_to_all x4, waiting for transfers between devices, exchange(): lax.all_to_all(x, DEVICES, split_axis=0, concat_axis=0, tiled=True, axis_...  25.7 us
    ppermute x2, starting transfers between devices, mirror(): return lax.ppermute(x, DEVICES, PLAN.mirror)  24.8 us
    ppermute x2, waiting for transfers between devices, whole(): rows = lax.ppermute(rows, DEVICES, PLAN.weights)  24.1 us
    all_to_all x1, starting transfers between devices, gather_rows(): got = lax.all_to_all(sent, 'dp', split_axis=0, concat_axis=0, tiled=True)  18.9 us
    ppermute x2, starting transfers between devices, to_rows(): return lax.ppermute(rows, DEVICES, back(PLAN.weights))  14.4 us
  transfers between devices with their start and end apart: 17, of which 11 were waited for; matrix products, arithmetic and copies ran while one was open for 6% of the time, Pallas kernels for 0%

profile of v9, /device:TPU:1, one launch (start us, length us, event | category | flops | bytes accessed | tf_op | source)
XLA Modules:
  0.0 299.2 jit_solution(18055393985160761978)
XLA Ops:
  4.8 17.4 %collective-permute-start.2 = (bf16[256,1024]{1,0:T(8,128)(2,1)S(1)}, bf16[256,1024]{1,0:T(8,128)(2,1)S(1)}, u32[]{:S(2)}, u32[]{:S(2)}) collective-permute-start(bf16[256,1024]{1,0:T(8,128)(2,1)S(1)} %collective-permute-done.1), channel_id=1, source_target_pairs={{0,0},{1,1},{32,48},{33,49},{64,66},{65,67},{96,114},{97,115},{128... | collective-permute-start | bytes 1572872 | tf_op jit(solution)/shard_map/ppermute | solution.py:77
  23.8 18.9 %all-to-all-start = ((bf16[16,4,8,512]{3,2,1,0:T(8,128)(2,1)}), bf16[16,4,8,512]{3,2,1,0:T(8,128)(2,1)S(1)}, u32[]{:S(2)}, u32[]{:S(2)}) async-start(bf16[16,4,8,512]{3,2,1,0:T(8,128)(2,1)} %broadcast_in_dim.3), calls=%async_computation | async-start | bytes 1048576 | tf_op jit(solution)/shard_map/all_to_all | solution.py:97
  42.7 7.4 %collective-permute-start.3 = (bf16[256,1024]{1,0:T(8,128)(2,1)S(1)}, bf16[256,1024]{1,0:T(8,128)(2,1)S(1)}, u32[]{:S(2)}, u32[]{:S(2)}) collective-permute-start(bf16[256,1024]{1,0:T(8,128)(2,1)S(1)} %collective-permute-done), channel_id=1, source_target_pairs={{0,0},{1,1},{32,48},{33,49},{64,66},{65,67},{96,114},{97,115},{128... | collective-permute-start | bytes 1572872 | tf_op jit(solution)/shard_map/ppermute | solution.py:77
  51.6 2.4 all-to-all-done
  53.9 29.8 %all-to-all-start.1 = ((bf16[32,2,2,2,1024]{4,3,2,1,0:T(2,128)(2,1)}), bf16[32,2,2,2,1024]{4,3,2,1,0:T(2,128)(2,1)S(1)}, u32[]{:S(2)}, u32[]{:S(2)}) async-start(bf16[32,2,2,2,1024]{4,3,2,1,0:T(2,128)(2,1)} %copy.37), calls=%async_computation.1 | async-start | bytes 1048576 | tf_op jit(solution)/shard_map/all_to_all | solution.py:63
  84.5 1.9 collective-permute-start.5
  86.4 9.3 %all-to-all-done.1 = bf16[32,2,2,2,1024]{4,3,2,1,0:T(2,128)(2,1)S(1)} async-done(((bf16[32,2,2,2,1024]{4,3,2,1,0:T(2,128)(2,1)}), bf16[32,2,2,2,1024]{4,3,2,1,0:T(2,128)(2,1)S(1)}, u32[]{:S(2)}, u32[]{:S(2)}) %all-to-all-start.1) | async-done | bytes 524320 | tf_op jit(solution)/shard_map/all_to_all | solution.py:63
  95.7 7.4 %collective-permute-done.5 = bf16[16,2,8,512]{3,2,0,1:T(8,128)(2,1)S(1)} collective-permute-done((bf16[16,2,8,512]{3,2,0,1:T(8,128)(2,1)S(1)}, bf16[16,2,8,512]{3,2,0,1:T(8,128)(2,1)S(1)}, u32[]{:S(2)}, u32[]{:S(2)}) %collective-permute-start.5) | collective-permute-done | bytes 262176 | tf_op jit(solution)/shard_map/ppermute | solution.py:103
  105.3 16.9 %all-to-all-start.2 = ((bf16[32,2,2,8,1024]{4,3,1,2,0:T(8,128)(2,1)}), bf16[32,2,2,8,1024]{4,3,1,2,0:T(8,128)(2,1)S(1)}, u32[]{:S(2)}, u32[]{:S(2)}) async-start(bf16[32,2,2,8,1024]{4,3,1,2,0:T(8,128)(2,1)} %bitcast.65), calls=%async_computation.2 | async-start | bytes 4194304 | tf_op jit(solution)/shard_map/all_to_all | solution.py:63
  122.2 8.4 %collective-permute-start.4 = (bf16[16,2,8,512]{3,2,1,0:T(8,128)(2,1)}, bf16[16,2,8,512]{3,2,1,0:T(8,128)(2,1)}, u32[]{:S(2)}, u32[]{:S(2)}) collective-permute-start(bf16[16,2,8,512]{3,2,1,0:T(8,128)(2,1)} %get-tuple-element.10), channel_id=1, source_target_pairs={{0,0},{1,1},{32,48},{33,49},{64,66},{65,67},{96,114},{97,115},{128... | collective-permute-start | bytes 786440 | tf_op jit(solution)/shard_map/ppermute | solution.py:103
  132.0 16.8 %collective-permute-done.4 = bf16[16,2,8,512]{3,2,1,0:T(8,128)(2,1)} collective-permute-done((bf16[16,2,8,512]{3,2,1,0:T(8,128)(2,1)}, bf16[16,2,8,512]{3,2,1,0:T(8,128)(2,1)}, u32[]{:S(2)}, u32[]{:S(2)}) %collective-permute-start.4) | collective-permute-done | bytes 262176 | tf_op jit(solution)/shard_map/ppermute | solution.py:103
  149.9 8.7 %all-to-all-done.2 = bf16[32,2,2,8,1024]{4,3,1,2,0:T(8,128)(2,1)S(1)} async-done(((bf16[32,2,2,8,1024]{4,3,1,2,0:T(8,128)(2,1)}), bf16[32,2,2,8,1024]{4,3,1,2,0:T(8,128)(2,1)S(1)}, u32[]{:S(2)}, u32[]{:S(2)}) %all-to-all-start.2) | async-done | bytes 2097184 | tf_op jit(solution)/shard_map/all_to_all | solution.py:63
  163.8 4.7 %all-to-all-start.3 = ((bf16[32,2,2,8,1024]{4,3,1,2,0:T(8,128)(2,1)}), bf16[32,2,2,8,1024]{4,3,1,2,0:T(8,128)(2,1)}, u32[]{:S(2)}, u32[]{:S(2)}) async-start(bf16[32,2,2,8,1024]{4,3,1,2,0:T(8,128)(2,1)} %bitcast.64), calls=%async_computation.3 | async-start | bytes 4194304 | tf_op jit(solution)/shard_map/all_to_all | solution.py:63
  169.4 8.1 %collective-permute-start.6 = (bf16[16,2,8,512]{3,2,1,0:T(8,128)(2,1)S(1)}, bf16[16,2,8,512]{3,2,1,0:T(8,128)(2,1)}, u32[]{:S(2)}, u32[]{:S(2)}) collective-permute-start(bf16[16,2,8,512]{3,2,1,0:T(8,128)(2,1)S(1)} %bitcast.77), channel_id=1, source_target_pairs={{0,0},{1,1},{48,32},{49,33},{66,64},{67,65},{114,96},{115,97},{132... | collective-permute-start | bytes 786440 | tf_op jit(solution)/shard_map/ppermute | solution.py:111
  179.6 14.1 %collective-permute-done.6 = bf16[16,2,8,512]{3,2,1,0:T(8,128)(2,1)} collective-permute-done((bf16[16,2,8,512]{3,2,1,0:T(8,128)(2,1)S(1)}, bf16[16,2,8,512]{3,2,1,0:T(8,128)(2,1)}, u32[]{:S(2)}, u32[]{:S(2)}) %collective-permute-start.6) | collective-permute-done | bytes 262176 | tf_op jit(solution)/shard_map/ppermute | solution.py:111
  193.7 7.7 %all-to-all-done.3 = bf16[32,2,2,8,1024]{4,3,1,2,0:T(8,128)(2,1)} async-done(((bf16[32,2,2,8,1024]{4,3,1,2,0:T(8,128)(2,1)}), bf16[32,2,2,8,1024]{4,3,1,2,0:T(8,128)(2,1)}, u32[]{:S(2)}, u32[]{:S(2)}) %all-to-all-start.3) | async-done | bytes 2097184 | tf_op jit(solution)/shard_map/all_to_all | solution.py:63
  201.4 3.9 %all-to-all-start.4 = ((bf16[32,2,2,2,1024]{4,3,1,2,0:T(2,128)(2,1)}), bf16[32,2,2,2,1024]{4,3,1,2,0:T(2,128)(2,1)S(1)}, u32[]{:S(2)}, u32[]{:S(2)}) async-start(bf16[32,2,2,2,1024]{4,3,1,2,0:T(2,128)(2,1)} %bitcast.59), calls=%async_computation.4 | async-start | bytes 1048576 | tf_op jit(solution)/shard_map/all_to_all | solution.py:63
  208.0 6.4 %collective-permute-start.10 = (bf16[16,2,8,512]{3,2,1,0:T(8,128)(2,1)S(1)}, bf16[16,2,8,512]{3,2,1,0:T(8,128)(2,1)S(1)}, u32[]{:S(2)}, u32[]{:S(2)}) collective-permute-start(bf16[16,2,8,512]{3,2,1,0:T(8,128)(2,1)S(1)} %bitcast.78), channel_id=1, source_target_pairs={{0,0},{1,1},{48,32},{49,33},{66,64},{67,65},{114,96},{115,97},{132... | collective-permute-start | bytes 786440 | tf_op jit(solution)/shard_map/ppermute | solution.py:111
  214.9 7.6 %collective-permute-start.7 = (bf16[256,1024]{1,0:T(8,128)(2,1)S(1)}, bf16[256,1024]{1,0:T(8,128)(2,1)}, u32[]{:S(2)}, u32[]{:S(2)}) collective-permute-start(bf16[256,1024]{1,0:T(8,128)(2,1)S(1)} %bitcast.76), channel_id=1, source_target_pairs={{0,0},{1,1},{48,32},{49,33},{66,64},{67,65},{114,96},{115,97},{132... | collective-permute-start | bytes 1572872 | tf_op jit(solution)/shard_map/ppermute | solution.py:81
  222.5 27.0 %collective-permute-done.10 = bf16[16,2,8,512]{3,2,1,0:T(8,128)(2,1)S(1)} collective-permute-done((bf16[16,2,8,512]{3,2,1,0:T(8,128)(2,1)S(1)}, bf16[16,2,8,512]{3,2,1,0:T(8,128)(2,1)S(1)}, u32[]{:S(2)}, u32[]{:S(2)}) %collective-permute-start.10) | collective-permute-done | bytes 262176 | tf_op jit(solution)/shard_map/ppermute | solution.py:111
  251.3 3.5 %all-to-all-start.5 = ((bf16[16,4,8,512]{3,2,1,0:T(8,128)(2,1)}), bf16[16,4,8,512]{3,2,1,0:T(8,128)(2,1)S(1)}, u32[]{:S(2)}, u32[]{:S(2)}) async-start(bf16[16,4,8,512]{3,2,1,0:T(8,128)(2,1)} %pad_maximum_fusion), calls=%async_computation.5 | async-start | bytes 1048576 | tf_op jit(solution)/shard_map/all_to_all | solution.py:116
  255.3 4.4 %collective-permute-done.7 = bf16[256,1024]{1,0:T(8,128)(2,1)} collective-permute-done((bf16[256,1024]{1,0:T(8,128)(2,1)S(1)}, bf16[256,1024]{1,0:T(8,128)(2,1)}, u32[]{:S(2)}, u32[]{:S(2)}) %collective-permute-start.7) | collective-permute-done | bytes 524320 | tf_op jit(solution)/shard_map/ppermute | solution.py:81
  259.8 1.9 collective-permute-start.8
  265.7 31.9 %collective-permute-done.8 = bf16[256,1024]{1,0:T(8,128)(2,1)S(1)} collective-permute-done((bf16[256,1024]{1,0:T(8,128)(2,1)S(1)}, bf16[256,1024]{1,0:T(8,128)(2,1)S(1)}, u32[]{:S(2)}, u32[]{:S(2)}) %collective-permute-start.8) | collective-permute-done | bytes 524320 | tf_op jit(solution)/shard_map/ppermute | solution.py:89
  (52 shorter events, 31.9 us)
Async XLA Ops:
  0.6 4.1 %collective-permute-start.1 = (bf16[256,1024]{1,0:T(8,128)(2,1)}, bf16[256,1024]{1,0:T(8,128)(2,1)S(1)}, u32[]{:S(2)}, u32[]{:S(2)}) collective-permute-start(bf16[256,1024]{1,0:T(8,128)(2,1)} %param.7), channel_id=1, source_target_pairs={{0,0},{1,1},{32,32},{33,33},{64,64},{65,65},{96,96},{97,97},{128,1... | collective-permute-start | bytes 1572872 | tf_op jit(solution)/shard_map/ppermute | solution.py:73
  2.3 40.3 %collective-permute-start = (bf16[256,1024]{1,0:T(8,128)(2,1)}, bf16[256,1024]{1,0:T(8,128)(2,1)S(1)}, u32[]{:S(2)}, u32[]{:S(2)}) collective-permute-start(bf16[256,1024]{1,0:T(8,128)(2,1)} %param.4), channel_id=1, source_target_pairs={{0,0},{1,1},{32,32},{33,33},{64,64},{65,65},{96,96},{97,97},{128,1... | collective-permute-start | bytes 1572872 | tf_op jit(solution)/shard_map/ppermute | solution.py:73
  4.8 37.9 %collective-permute-start.2 = (bf16[256,1024]{1,0:T(8,128)(2,1)S(1)}, bf16[256,1024]{1,0:T(8,128)(2,1)S(1)}, u32[]{:S(2)}, u32[]{:S(2)}) collective-permute-start(bf16[256,1024]{1,0:T(8,128)(2,1)S(1)} %collective-permute-done.1), channel_id=1, source_target_pairs={{0,0},{1,1},{32,48},{33,49},{64,66},{65,67},{96,114},{97,115},{128... | collective-permute-start | bytes 1572872 | tf_op jit(solution)/shard_map/ppermute | solution.py:77
  23.8 30.2 %all-to-all-start = ((bf16[16,4,8,512]{3,2,1,0:T(8,128)(2,1)}), bf16[16,4,8,512]{3,2,1,0:T(8,128)(2,1)S(1)}, u32[]{:S(2)}, u32[]{:S(2)}) async-start(bf16[16,4,8,512]{3,2,1,0:T(8,128)(2,1)} %broadcast_in_dim.3), calls=%async_computation | async-start | bytes 1048576 | tf_op jit(solution)/shard_map/all_to_all | solution.py:97
  42.7 53.0 %collective-permute-start.3 = (bf16[256,1024]{1,0:T(8,128)(2,1)S(1)}, bf16[256,1024]{1,0:T(8,128)(2,1)S(1)}, u32[]{:S(2)}, u32[]{:S(2)}) collective-permute-start(bf16[256,1024]{1,0:T(8,128)(2,1)S(1)} %collective-permute-done), channel_id=1, source_target_pairs={{0,0},{1,1},{32,48},{33,49},{64,66},{65,67},{96,114},{97,115},{128... | collective-permute-start | bytes 1572872 | tf_op jit(solution)/shard_map/ppermute | solution.py:77
  53.9 41.8 %all-to-all-start.1 = ((bf16[32,2,2,2,1024]{4,3,2,1,0:T(2,128)(2,1)}), bf16[32,2,2,2,1024]{4,3,2,1,0:T(2,128)(2,1)S(1)}, u32[]{:S(2)}, u32[]{:S(2)}) async-start(bf16[32,2,2,2,1024]{4,3,2,1,0:T(2,128)(2,1)} %copy.37), calls=%async_computation.1 | async-start | bytes 1048576 | tf_op jit(solution)/shard_map/all_to_all | solution.py:63
  84.5 18.6 %collective-permute-start.5 = (bf16[16,2,8,512]{3,2,0,1:T(8,128)(2,1)S(1)}, bf16[16,2,8,512]{3,2,0,1:T(8,128)(2,1)S(1)}, u32[]{:S(2)}, u32[]{:S(2)}) collective-permute-start(bf16[16,2,8,512]{3,2,0,1:T(8,128)(2,1)S(1)} %copy.51), channel_id=1, source_target_pairs={{0,0},{1,1},{32,48},{33,49},{64,66},{65,67},{96,114},{97,115},{128... | collective-permute-start | bytes 786440 | tf_op jit(solution)/shard_map/ppermute | solution.py:103
  95.7 9.6 %copy-start = (bf16[256,1024]{1,0:T(8,128)(2,1)}, bf16[256,1024]{1,0:T(8,128)(2,1)S(1)}, u32[]{:S(2)}) copy-start(bf16[256,1024]{1,0:T(8,128)(2,1)S(1)} %collective-permute-done.3) | copy-start | bytes 1572868
  105.3 53.3 %all-to-all-start.2 = ((bf16[32,2,2,8,1024]{4,3,1,2,0:T(8,128)(2,1)}), bf16[32,2,2,8,1024]{4,3,1,2,0:T(8,128)(2,1)S(1)}, u32[]{:S(2)}, u32[]{:S(2)}) async-start(bf16[32,2,2,8,1024]{4,3,1,2,0:T(8,128)(2,1)} %bitcast.65), calls=%async_computation.2 | async-start | bytes 4194304 | tf_op jit(solution)/shard_map/all_to_all | solution.py:63
  122.2 26.5 %collective-permute-start.4 = (bf16[16,2,8,512]{3,2,1,0:T(8,128)(2,1)}, bf16[16,2,8,512]{3,2,1,0:T(8,128)(2,1)}, u32[]{:S(2)}, u32[]{:S(2)}) collective-permute-start(bf16[16,2,8,512]{3,2,1,0:T(8,128)(2,1)} %get-tuple-element.10), channel_id=1, source_target_pairs={{0,0},{1,1},{32,48},{33,49},{64,66},{65,67},{96,114},{97,115},{128... | collective-permute-start | bytes 786440 | tf_op jit(solution)/shard_map/ppermute | solution.py:103
  159.7 1.2 copy-start.2
  163.8 37.6 %all-to-all-start.3 = ((bf16[32,2,2,8,1024]{4,3,1,2,0:T(8,128)(2,1)}), bf16[32,2,2,8,1024]{4,3,1,2,0:T(8,128)(2,1)}, u32[]{:S(2)}, u32[]{:S(2)}) async-start(bf16[32,2,2,8,1024]{4,3,1,2,0:T(8,128)(2,1)} %bitcast.64), calls=%async_computation.3 | async-start | bytes 4194304 | tf_op jit(solution)/shard_map/all_to_all | solution.py:63
  169.4 24.3 %collective-permute-start.6 = (bf16[16,2,8,512]{3,2,1,0:T(8,128)(2,1)S(1)}, bf16[16,2,8,512]{3,2,1,0:T(8,128)(2,1)}, u32[]{:S(2)}, u32[]{:S(2)}) collective-permute-start(bf16[16,2,8,512]{3,2,1,0:T(8,128)(2,1)S(1)} %bitcast.77), channel_id=1, source_target_pairs={{0,0},{1,1},{48,32},{49,33},{66,64},{67,65},{114,96},{115,97},{132... | collective-permute-start | bytes 786440 | tf_op jit(solution)/shard_map/ppermute | solution.py:111
  178.0 29.2 %copy-start.1 = (bf16[256,1024]{1,0:T(8,128)(2,1)S(1)}, bf16[256,1024]{1,0:T(8,128)(2,1)}, u32[]{:S(2)}) copy-start(bf16[256,1024]{1,0:T(8,128)(2,1)} %copy-done) | copy-start | bytes 1572868
  201.4 49.8 %all-to-all-start.4 = ((bf16[32,2,2,2,1024]{4,3,1,2,0:T(2,128)(2,1)}), bf16[32,2,2,2,1024]{4,3,1,2,0:T(2,128)(2,1)S(1)}, u32[]{:S(2)}, u32[]{:S(2)}) async-start(bf16[32,2,2,2,1024]{4,3,1,2,0:T(2,128)(2,1)} %bitcast.59), calls=%async_computation.4 | async-start | bytes 1048576 | tf_op jit(solution)/shard_map/all_to_all | solution.py:63
  208.0 41.4 %collective-permute-start.10 = (bf16[16,2,8,512]{3,2,1,0:T(8,128)(2,1)S(1)}, bf16[16,2,8,512]{3,2,1,0:T(8,128)(2,1)S(1)}, u32[]{:S(2)}, u32[]{:S(2)}) collective-permute-start(bf16[16,2,8,512]{3,2,1,0:T(8,128)(2,1)S(1)} %bitcast.78), channel_id=1, source_target_pairs={{0,0},{1,1},{48,32},{49,33},{66,64},{67,65},{114,96},{115,97},{132... | collective-permute-start | bytes 786440 | tf_op jit(solution)/shard_map/ppermute | solution.py:111
  214.9 44.9 %collective-permute-start.7 = (bf16[256,1024]{1,0:T(8,128)(2,1)S(1)}, bf16[256,1024]{1,0:T(8,128)(2,1)}, u32[]{:S(2)}, u32[]{:S(2)}) collective-permute-start(bf16[256,1024]{1,0:T(8,128)(2,1)S(1)} %bitcast.76), channel_id=1, source_target_pairs={{0,0},{1,1},{48,32},{49,33},{66,64},{67,65},{114,96},{115,97},{132... | collective-permute-start | bytes 1572872 | tf_op jit(solution)/shard_map/ppermute | solution.py:81
  251.3 13.1 %all-to-all-start.5 = ((bf16[16,4,8,512]{3,2,1,0:T(8,128)(2,1)}), bf16[16,4,8,512]{3,2,1,0:T(8,128)(2,1)S(1)}, u32[]{:S(2)}, u32[]{:S(2)}) async-start(bf16[16,4,8,512]{3,2,1,0:T(8,128)(2,1)} %pad_maximum_fusion), calls=%async_computation.5 | async-start | bytes 1048576 | tf_op jit(solution)/shard_map/all_to_all | solution.py:116
  259.8 37.8 %collective-permute-start.8 = (bf16[256,1024]{1,0:T(8,128)(2,1)S(1)}, bf16[256,1024]{1,0:T(8,128)(2,1)S(1)}, u32[]{:S(2)}, u32[]{:S(2)}) collective-permute-start(bf16[256,1024]{1,0:T(8,128)(2,1)S(1)} %reshape.70), channel_id=1, source_target_pairs={{0,0},{1,1},{48,32},{49,33},{66,64},{67,65},{114,96},{115,97},{132... | collective-permute-start | bytes 1572872 | tf_op jit(solution)/shard_map/ppermute | solution.py:89
  261.7 35.9 %collective-permute-start.9 = (bf16[256,1024]{1,0:T(8,128)(2,1)}, bf16[256,1024]{1,0:T(8,128)(2,1)S(1)}, u32[]{:S(2)}, u32[]{:S(2)}) collective-permute-start(bf16[256,1024]{1,0:T(8,128)(2,1)} %collective-permute-done.7), channel_id=1, source_target_pairs={{0,0},{1,1},{32,32},{33,33},{64,64},{65,65},{96,96},{97,97},{128,1... | collective-permute-start | bytes 1572872 | tf_op jit(solution)/shard_map/ppermute | solution.py:85

commit v10 on v9

--- a/solution.py
+++ b/solution.py
@@ -147,10 +147,11 @@
     dpre = dpre.transpose(1, 0, 2, 3, 4).reshape(nb, BOUT, t)
     fgrad = jnp.einsum("bkn,bnt->bkt", up, dpre, preferred_element_type=F32).astype(BF16)
     fgrad = unmirror(fgrad.reshape(nb * BIN, t))
-    up_term = to_rows(jnp.einsum("bkt,bnt->bkn", x, dpre, preferred_element_type=F32))
+    up_term = jnp.einsum("bkt,bnt->bkn", x, dpre, preferred_element_type=F32).astype(BF16)
+    up_term = to_rows(after(up_term, mixed))
     mixed = mixed.transpose(1, 0, 2, 3, 4).reshape(nb * BIN, t)
-    mixed = to_store(after(mixed, fgrad))
-    up_grad, down_grad = sum_rows(up_term, down_term, down_blocks.shape)
+    mixed = to_store(mixed)
+    up_grad, down_grad = sum_rows(after(up_term, fgrad), down_term, down_blocks.shape)
     return mixed, unshuffle(fgrad), up_grad, down_grad
 
 

time: 300 us -> 303 us (1.010)
  the two profiles are of different devices: /device:TPU:1 before, /device:TPU:130 now
where the time goes in v10:
time: 303 us; the launch traced here: 301 us
  waiting for transfers between devices  156 us (51%)
  starting transfers between devices  118 us (39%)
  local copies, waits for them, and re-layouts  16.9 us (6%)
  matrix products  4.69 us (2%)
  other arithmetic  4.23 us (1%)
    ppermute x1, waiting for transfers between devices, unmirror(): return lax.ppermute(x, DEVICES, back(PLAN.mirror))  44.4 us
    all_to_all x4, starting transfers between devices, exchange(): lax.all_to_all(x, DEVICES, split_axis=0, concat_axis=0, tiled=True, axis_...  37 us
    ppermute x2, waiting for transfers between devices, whole(): rows = lax.ppermute(rows, DEVICES, PLAN.weights)  29.2 us
    all_to_all x4, waiting for transfers between devices, exchange(): lax.all_to_all(x, DEVICES, split_axis=0, concat_axis=0, tiled=True, axis_...  24.5 us
    ppermute x2, starting transfers between devices, to_rows(): return lax.ppermute(rows, DEVICES, back(PLAN.weights))  19.6 us
    ppermute x2, starting transfers between devices, mirror(): return lax.ppermute(x, DEVICES, PLAN.mirror)  19 us
    ppermute x2, waiting for transfers between devices, to_rows(): return lax.ppermute(rows, DEVICES, back(PLAN.weights))  17.9 us
    ppermute x2, waiting for transfers between devices, mirror(): return lax.ppermute(x, DEVICES, PLAN.mirror)  17.6 us
  transfers between devices with their start and end apart: 17, of which 11 were waited for; matrix products, arithmetic and copies ran while one was open for 5% of the time, Pallas kernels for 0%

profile of v10, /device:TPU:130, one launch (start us, length us, event | category | flops | bytes accessed | tf_op | source)
XLA Modules:
  0.0 301.3 jit_solution(9397670267242615083)
XLA Ops:
  0.6 3.4 %collective-permute-start.1 = (bf16[256,1024]{1,0:T(8,128)(2,1)}, bf16[256,1024]{1,0:T(8,128)(2,1)S(1)}, u32[]{:S(2)}, u32[]{:S(2)}) collective-permute-start(bf16[256,1024]{1,0:T(8,128)(2,1)} %param.7), channel_id=1, source_target_pairs={{0,0},{1,1},{32,32},{33,33},{64,64},{65,65},{96,96},{97,97},{128,1... | collective-permute-start | bytes 1572872 | tf_op jit(solution)/shard_map/ppermute | solution.py:73
  6.7 10.2 %collective-permute-done.1 = bf16[256,1024]{1,0:T(8,128)(2,1)S(1)} collective-permute-done((bf16[256,1024]{1,0:T(8,128)(2,1)}, bf16[256,1024]{1,0:T(8,128)(2,1)S(1)}, u32[]{:S(2)}, u32[]{:S(2)}) %collective-permute-start.1) | collective-permute-done | bytes 524320 | tf_op jit(solution)/shard_map/ppermute | solution.py:73
  16.9 11.5 %collective-permute-start.2 = (bf16[256,1024]{1,0:T(8,128)(2,1)S(1)}, bf16[256,1024]{1,0:T(8,128)(2,1)S(1)}, u32[]{:S(2)}, u32[]{:S(2)}) collective-permute-start(bf16[256,1024]{1,0:T(8,128)(2,1)S(1)} %collective-permute-done.1), channel_id=1, source_target_pairs={{0,0},{1,1},{32,48},{33,49},{64,66},{65,67},{96,114},{97,115},{128... | collective-permute-start | bytes 1572872 | tf_op jit(solution)/shard_map/ppermute | solution.py:77
  30.0 6.1 %all-to-all-start = ((bf16[16,4,8,512]{3,2,1,0:T(8,128)(2,1)}), bf16[16,4,8,512]{3,2,1,0:T(8,128)(2,1)S(1)}, u32[]{:S(2)}, u32[]{:S(2)}) async-start(bf16[16,4,8,512]{3,2,1,0:T(8,128)(2,1)} %broadcast_in_dim.3), calls=%async_computation | async-start | bytes 1048576 | tf_op jit(solution)/shard_map/all_to_all | solution.py:97
  36.1 17.6 %collective-permute-done.2 = bf16[256,1024]{1,0:T(8,128)(2,1)S(1)} collective-permute-done((bf16[256,1024]{1,0:T(8,128)(2,1)S(1)}, bf16[256,1024]{1,0:T(8,128)(2,1)S(1)}, u32[]{:S(2)}, u32[]{:S(2)}) %collective-permute-start.2) | collective-permute-done | bytes 524320 | tf_op jit(solution)/shard_map/ppermute | solution.py:77
  53.7 7.4 %collective-permute-start.3 = (bf16[256,1024]{1,0:T(8,128)(2,1)S(1)}, bf16[256,1024]{1,0:T(8,128)(2,1)S(1)}, u32[]{:S(2)}, u32[]{:S(2)}) collective-permute-start(bf16[256,1024]{1,0:T(8,128)(2,1)S(1)} %collective-permute-done), channel_id=1, source_target_pairs={{0,0},{1,1},{32,48},{33,49},{64,66},{65,67},{96,114},{97,115},{128... | collective-permute-start | bytes 1572872 | tf_op jit(solution)/shard_map/ppermute | solution.py:77
  62.7 15.7 %all-to-all-start.1 = ((bf16[32,2,2,2,1024]{4,3,2,1,0:T(2,128)(2,1)}), bf16[32,2,2,2,1024]{4,3,2,1,0:T(2,128)(2,1)S(1)}, u32[]{:S(2)}, u32[]{:S(2)}) async-start(bf16[32,2,2,2,1024]{4,3,2,1,0:T(2,128)(2,1)} %copy.37), calls=%async_computation.1 | async-start | bytes 1048576 | tf_op jit(solution)/shard_map/all_to_all | solution.py:63
  81.1 7.4 %all-to-all-done.1 = bf16[32,2,2,2,1024]{4,3,2,1,0:T(2,128)(2,1)S(1)} async-done(((bf16[32,2,2,2,1024]{4,3,2,1,0:T(2,128)(2,1)}), bf16[32,2,2,2,1024]{4,3,2,1,0:T(2,128)(2,1)S(1)}, u32[]{:S(2)}, u32[]{:S(2)}) %all-to-all-start.1) | async-done | bytes 524320 | tf_op jit(solution)/shard_map/all_to_all | solution.py:63
  88.5 19.7 %collective-permute-done.5 = bf16[16,2,8,512]{3,2,0,1:T(8,128)(2,1)S(1)} collective-permute-done((bf16[16,2,8,512]{3,2,0,1:T(8,128)(2,1)S(1)}, bf16[16,2,8,512]{3,2,0,1:T(8,128)(2,1)S(1)}, u32[]{:S(2)}, u32[]{:S(2)}) %collective-permute-start.5) | collective-permute-done | bytes 262176 | tf_op jit(solution)/shard_map/ppermute | solution.py:103
  110.5 4.2 %all-to-all-start.2 = ((bf16[32,2,2,8,1024]{4,3,1,2,0:T(8,128)(2,1)}), bf16[32,2,2,8,1024]{4,3,1,2,0:T(8,128)(2,1)S(1)}, u32[]{:S(2)}, u32[]{:S(2)}) async-start(bf16[32,2,2,8,1024]{4,3,1,2,0:T(8,128)(2,1)} %bitcast.65), calls=%async_computation.2 | async-start | bytes 4194304 | tf_op jit(solution)/shard_map/all_to_all | solution.py:63
  114.7 10.8 %collective-permute-start.4 = (bf16[16,2,8,512]{3,2,1,0:T(8,128)(2,1)}, bf16[16,2,8,512]{3,2,1,0:T(8,128)(2,1)}, u32[]{:S(2)}, u32[]{:S(2)}) collective-permute-start(bf16[16,2,8,512]{3,2,1,0:T(8,128)(2,1)} %get-tuple-element.11), channel_id=1, source_target_pairs={{0,0},{1,1},{32,48},{33,49},{64,66},{65,67},{96,114},{97,115},{128... | collective-permute-start | bytes 786440 | tf_op jit(solution)/shard_map/ppermute | solution.py:103
  126.9 9.5 %collective-permute-done.4 = bf16[16,2,8,512]{3,2,1,0:T(8,128)(2,1)} collective-permute-done((bf16[16,2,8,512]{3,2,1,0:T(8,128)(2,1)}, bf16[16,2,8,512]{3,2,1,0:T(8,128)(2,1)}, u32[]{:S(2)}, u32[]{:S(2)}) %collective-permute-start.4) | collective-permute-done | bytes 262176 | tf_op jit(solution)/shard_map/ppermute | solution.py:103
  137.5 7.1 %all-to-all-done.2 = bf16[32,2,2,8,1024]{4,3,1,2,0:T(8,128)(2,1)S(1)} async-done(((bf16[32,2,2,8,1024]{4,3,1,2,0:T(8,128)(2,1)}), bf16[32,2,2,8,1024]{4,3,1,2,0:T(8,128)(2,1)S(1)}, u32[]{:S(2)}, u32[]{:S(2)}) %all-to-all-start.2) | async-done | bytes 2097184 | tf_op jit(solution)/shard_map/all_to_all | solution.py:63
  149.8 11.1 %all-to-all-start.3 = ((bf16[32,2,2,8,1024]{4,3,1,2,0:T(8,128)(2,1)}), bf16[32,2,2,8,1024]{4,3,1,2,0:T(8,128)(2,1)}, u32[]{:S(2)}, u32[]{:S(2)}) async-start(bf16[32,2,2,8,1024]{4,3,1,2,0:T(8,128)(2,1)} %bitcast.64), calls=%async_computation.3 | async-start | bytes 4194304 | tf_op jit(solution)/shard_map/all_to_all | solution.py:63
  161.8 11.3 %collective-permute-start.6 = (bf16[16,2,8,512]{3,2,1,0:T(8,128)(2,1)S(1)}, bf16[16,2,8,512]{3,2,1,0:T(8,128)(2,1)}, u32[]{:S(2)}, u32[]{:S(2)}) collective-permute-start(bf16[16,2,8,512]{3,2,1,0:T(8,128)(2,1)S(1)} %bitcast.77), channel_id=1, source_target_pairs={{0,0},{1,1},{48,32},{49,33},{66,64},{67,65},{114,96},{115,97},{132... | collective-permute-start | bytes 786440 | tf_op jit(solution)/shard_map/ppermute | solution.py:111
  175.2 9.0 %collective-permute-done.6 = bf16[16,2,8,512]{3,2,1,0:T(8,128)(2,1)} collective-permute-done((bf16[16,2,8,512]{3,2,1,0:T(8,128)(2,1)S(1)}, bf16[16,2,8,512]{3,2,1,0:T(8,128)(2,1)}, u32[]{:S(2)}, u32[]{:S(2)}) %collective-permute-start.6) | collective-permute-done | bytes 262176 | tf_op jit(solution)/shard_map/ppermute | solution.py:111
  184.2 10.0 %all-to-all-done.3 = bf16[32,2,2,8,1024]{4,3,1,2,0:T(8,128)(2,1)} async-done(((bf16[32,2,2,8,1024]{4,3,1,2,0:T(8,128)(2,1)}), bf16[32,2,2,8,1024]{4,3,1,2,0:T(8,128)(2,1)}, u32[]{:S(2)}, u32[]{:S(2)}) %all-to-all-start.3) | async-done | bytes 2097184 | tf_op jit(solution)/shard_map/all_to_all | solution.py:63
  194.2 6.0 %all-to-all-start.4 = ((bf16[32,2,2,2,1024]{4,3,1,2,0:T(2,128)(2,1)}), bf16[32,2,2,2,1024]{4,3,1,2,0:T(2,128)(2,1)S(1)}, u32[]{:S(2)}, u32[]{:S(2)}) async-start(bf16[32,2,2,2,1024]{4,3,1,2,0:T(2,128)(2,1)} %bitcast.60), calls=%async_computation.4 | async-start | bytes 1048576 | tf_op jit(solution)/shard_map/all_to_all | solution.py:63
  202.4 10.5 %collective-permute-start.8 = (bf16[256,1024]{1,0:T(8,128)(2,1)S(1)}, bf16[256,1024]{1,0:T(8,128)(2,1)}, u32[]{:S(2)}, u32[]{:S(2)}) collective-permute-start(bf16[256,1024]{1,0:T(8,128)(2,1)S(1)} %bitcast.76), channel_id=1, source_target_pairs={{0,0},{1,1},{48,32},{49,33},{66,64},{67,65},{114,96},{115,97},{132... | collective-permute-start | bytes 1572872 | tf_op jit(solution)/shard_map/ppermute | solution.py:81
  213.8 8.2 %collective-permute-start.10 = (bf16[16,2,8,512]{3,2,1,0:T(8,128)(2,1)S(1)}, bf16[16,2,8,512]{3,2,1,0:T(8,128)(2,1)S(1)}, u32[]{:S(2)}, u32[]{:S(2)}) collective-permute-start(bf16[16,2,8,512]{3,2,1,0:T(8,128)(2,1)S(1)} %copy_bitcast_fusion.3), channel_id=1, source_target_pairs={{0,0},{1,1},{48,32},{49,33},{66,64},{67,65},{114,96},{115,97},{132... | collective-permute-start | bytes 786440 | tf_op jit(solution)/shard_map/ppermute | solution.py:111
  225.5 44.4 %collective-permute-done.8 = bf16[256,1024]{1,0:T(8,128)(2,1)} collective-permute-done((bf16[256,1024]{1,0:T(8,128)(2,1)S(1)}, bf16[256,1024]{1,0:T(8,128)(2,1)}, u32[]{:S(2)}, u32[]{:S(2)}) %collective-permute-start.8) | collective-permute-done | bytes 524320 | tf_op jit(solution)/shard_map/ppermute | solution.py:81
  271.8 9.0 %collective-permute-done.10 = bf16[16,2,8,512]{3,2,1,0:T(8,128)(2,1)S(1)} collective-permute-done((bf16[16,2,8,512]{3,2,1,0:T(8,128)(2,1)S(1)}, bf16[16,2,8,512]{3,2,1,0:T(8,128)(2,1)S(1)}, u32[]{:S(2)}, u32[]{:S(2)}) %collective-permute-start.10) | collective-permute-done | bytes 262176 | tf_op jit(solution)/shard_map/ppermute | solution.py:111
  282.5 3.6 %all-to-all-start.5 = ((bf16[16,4,8,512]{3,2,1,0:T(8,128)(2,1)}), bf16[16,4,8,512]{3,2,1,0:T(8,128)(2,1)S(1)}, u32[]{:S(2)}, u32[]{:S(2)}) async-start(bf16[16,4,8,512]{3,2,1,0:T(8,128)(2,1)} %pad_maximum_fusion), calls=%async_computation.5 | async-start | bytes 1048576 | tf_op jit(solution)/shard_map/all_to_all | solution.py:116
  286.1 12.3 %all-to-all-done.5 = bf16[16,4,8,512]{3,2,1,0:T(8,128)(2,1)S(1)} async-done(((bf16[16,4,8,512]{3,2,1,0:T(8,128)(2,1)}), bf16[16,4,8,512]{3,2,1,0:T(8,128)(2,1)S(1)}, u32[]{:S(2)}, u32[]{:S(2)}) %all-to-all-start.5) | async-done | bytes 524320 | tf_op jit(solution)/shard_map/all_to_all | solution.py:116
  (52 shorter events, 34.4 us)
Async XLA Ops:
  0.6 16.3 %collective-permute-start.1 = (bf16[256,1024]{1,0:T(8,128)(2,1)}, bf16[256,1024]{1,0:T(8,128)(2,1)S(1)}, u32[]{:S(2)}, u32[]{:S(2)}) collective-permute-start(bf16[256,1024]{1,0:T(8,128)(2,1)} %param.7), channel_id=1, source_target_pairs={{0,0},{1,1},{32,32},{33,33},{64,64},{65,65},{96,96},{97,97},{128,1... | collective-permute-start | bytes 1572872 | tf_op jit(solution)/shard_map/ppermute | solution.py:73
  4.0 32.1 %collective-permute-start = (bf16[256,1024]{1,0:T(8,128)(2,1)}, bf16[256,1024]{1,0:T(8,128)(2,1)S(1)}, u32[]{:S(2)}, u32[]{:S(2)}) collective-permute-start(bf16[256,1024]{1,0:T(8,128)(2,1)} %param.4), channel_id=1, source_target_pairs={{0,0},{1,1},{32,32},{33,33},{64,64},{65,65},{96,96},{97,97},{128,1... | collective-permute-start | bytes 1572872 | tf_op jit(solution)/shard_map/ppermute | solution.py:73
  16.9 36.8 %collective-permute-start.2 = (bf16[256,1024]{1,0:T(8,128)(2,1)S(1)}, bf16[256,1024]{1,0:T(8,128)(2,1)S(1)}, u32[]{:S(2)}, u32[]{:S(2)}) collective-permute-start(bf16[256,1024]{1,0:T(8,128)(2,1)S(1)} %collective-permute-done.1), channel_id=1, source_target_pairs={{0,0},{1,1},{32,48},{33,49},{64,66},{65,67},{96,114},{97,115},{128... | collective-permute-start | bytes 1572872 | tf_op jit(solution)/shard_map/ppermute | solution.py:77
  30.0 32.7 %all-to-all-start = ((bf16[16,4,8,512]{3,2,1,0:T(8,128)(2,1)}), bf16[16,4,8,512]{3,2,1,0:T(8,128)(2,1)S(1)}, u32[]{:S(2)}, u32[]{:S(2)}) async-start(bf16[16,4,8,512]{3,2,1,0:T(8,128)(2,1)} %broadcast_in_dim.3), calls=%async_computation | async-start | bytes 1048576 | tf_op jit(solution)/shard_map/all_to_all | solution.py:97
  53.7 34.8 %collective-permute-start.3 = (bf16[256,1024]{1,0:T(8,128)(2,1)S(1)}, bf16[256,1024]{1,0:T(8,128)(2,1)S(1)}, u32[]{:S(2)}, u32[]{:S(2)}) collective-permute-start(bf16[256,1024]{1,0:T(8,128)(2,1)S(1)} %collective-permute-done), channel_id=1, source_target_pairs={{0,0},{1,1},{32,48},{33,49},{64,66},{65,67},{96,114},{97,115},{128... | collective-permute-start | bytes 1572872 | tf_op jit(solution)/shard_map/ppermute | solution.py:77
  62.7 25.8 %all-to-all-start.1 = ((bf16[32,2,2,2,1024]{4,3,2,1,0:T(2,128)(2,1)}), bf16[32,2,2,2,1024]{4,3,2,1,0:T(2,128)(2,1)S(1)}, u32[]{:S(2)}, u32[]{:S(2)}) async-start(bf16[32,2,2,2,1024]{4,3,2,1,0:T(2,128)(2,1)} %copy.37), calls=%async_computation.1 | async-start | bytes 1048576 | tf_op jit(solution)/shard_map/all_to_all | solution.py:63
  79.2 29.0 %collective-permute-start.5 = (bf16[16,2,8,512]{3,2,0,1:T(8,128)(2,1)S(1)}, bf16[16,2,8,512]{3,2,0,1:T(8,128)(2,1)S(1)}, u32[]{:S(2)}, u32[]{:S(2)}) collective-permute-start(bf16[16,2,8,512]{3,2,0,1:T(8,128)(2,1)S(1)} %copy.51), channel_id=1, source_target_pairs={{0,0},{1,1},{32,48},{33,49},{64,66},{65,67},{96,114},{97,115},{128... | collective-permute-start | bytes 786440 | tf_op jit(solution)/shard_map/ppermute | solution.py:103
  88.5 22.0 %copy-start = (bf16[256,1024]{1,0:T(8,128)(2,1)}, bf16[256,1024]{1,0:T(8,128)(2,1)S(1)}, u32[]{:S(2)}) copy-start(bf16[256,1024]{1,0:T(8,128)(2,1)S(1)} %collective-permute-done.3) | copy-start | bytes 1572868
  110.5 34.1 %all-to-all-start.2 = ((bf16[32,2,2,8,1024]{4,3,1,2,0:T(8,128)(2,1)}), bf16[32,2,2,8,1024]{4,3,1,2,0:T(8,128)(2,1)S(1)}, u32[]{:S(2)}, u32[]{:S(2)}) async-start(bf16[32,2,2,8,1024]{4,3,1,2,0:T(8,128)(2,1)} %bitcast.65), calls=%async_computation.2 | async-start | bytes 4194304 | tf_op jit(solution)/shard_map/all_to_all | solution.py:63
  114.7 21.7 %collective-permute-start.4 = (bf16[16,2,8,512]{3,2,1,0:T(8,128)(2,1)}, bf16[16,2,8,512]{3,2,1,0:T(8,128)(2,1)}, u32[]{:S(2)}, u32[]{:S(2)}) collective-permute-start(bf16[16,2,8,512]{3,2,1,0:T(8,128)(2,1)} %get-tuple-element.11), channel_id=1, source_target_pairs={{0,0},{1,1},{32,48},{33,49},{64,66},{65,67},{96,114},{97,115},{128... | collective-permute-start | bytes 786440 | tf_op jit(solution)/shard_map/ppermute | solution.py:103
  145.6 1.2 copy-start.2
  149.8 44.4 %all-to-all-start.3 = ((bf16[32,2,2,8,1024]{4,3,1,2,0:T(8,128)(2,1)}), bf16[32,2,2,8,1024]{4,3,1,2,0:T(8,128)(2,1)}, u32[]{:S(2)}, u32[]{:S(2)}) async-start(bf16[32,2,2,8,1024]{4,3,1,2,0:T(8,128)(2,1)} %bitcast.64), calls=%async_computation.3 | async-start | bytes 4194304 | tf_op jit(solution)/shard_map/all_to_all | solution.py:63
  161.8 22.4 %collective-permute-start.6 = (bf16[16,2,8,512]{3,2,1,0:T(8,128)(2,1)S(1)}, bf16[16,2,8,512]{3,2,1,0:T(8,128)(2,1)}, u32[]{:S(2)}, u32[]{:S(2)}) collective-permute-start(bf16[16,2,8,512]{3,2,1,0:T(8,128)(2,1)S(1)} %bitcast.77), channel_id=1, source_target_pairs={{0,0},{1,1},{48,32},{49,33},{66,64},{67,65},{114,96},{115,97},{132... | collective-permute-start | bytes 786440 | tf_op jit(solution)/shard_map/ppermute | solution.py:111
  175.2 37.8 %copy-start.1 = (bf16[256,1024]{1,0:T(8,128)(2,1)S(1)}, bf16[256,1024]{1,0:T(8,128)(2,1)}, u32[]{:S(2)}) copy-start(bf16[256,1024]{1,0:T(8,128)(2,1)} %copy-done) | copy-start | bytes 1572868
  194.2 19.6 %all-to-all-start.4 = ((bf16[32,2,2,2,1024]{4,3,1,2,0:T(2,128)(2,1)}), bf16[32,2,2,2,1024]{4,3,1,2,0:T(2,128)(2,1)S(1)}, u32[]{:S(2)}, u32[]{:S(2)}) async-start(bf16[32,2,2,2,1024]{4,3,1,2,0:T(2,128)(2,1)} %bitcast.60), calls=%async_computation.4 | async-start | bytes 1048576 | tf_op jit(solution)/shard_map/all_to_all | solution.py:63
  202.4 67.4 %collective-permute-start.8 = (bf16[256,1024]{1,0:T(8,128)(2,1)S(1)}, bf16[256,1024]{1,0:T(8,128)(2,1)}, u32[]{:S(2)}, u32[]{:S(2)}) collective-permute-start(bf16[256,1024]{1,0:T(8,128)(2,1)S(1)} %bitcast.76), channel_id=1, source_target_pairs={{0,0},{1,1},{48,32},{49,33},{66,64},{67,65},{114,96},{115,97},{132... | collective-permute-start | bytes 1572872 | tf_op jit(solution)/shard_map/ppermute | solution.py:81
  213.8 66.9 %collective-permute-start.10 = (bf16[16,2,8,512]{3,2,1,0:T(8,128)(2,1)S(1)}, bf16[16,2,8,512]{3,2,1,0:T(8,128)(2,1)S(1)}, u32[]{:S(2)}, u32[]{:S(2)}) collective-permute-start(bf16[16,2,8,512]{3,2,1,0:T(8,128)(2,1)S(1)} %copy_bitcast_fusion.3), channel_id=1, source_target_pairs={{0,0},{1,1},{48,32},{49,33},{66,64},{67,65},{114,96},{115,97},{132... | collective-permute-start | bytes 786440 | tf_op jit(solution)/shard_map/ppermute | solution.py:111
  222.7 63.4 %collective-permute-start.7 = (bf16[256,1024]{1,0:T(8,128)(2,1)S(1)}, bf16[256,1024]{1,0:T(8,128)(2,1)S(1)}, u32[]{:S(2)}, u32[]{:S(2)}) collective-permute-start(bf16[256,1024]{1,0:T(8,128)(2,1)S(1)} %reshape.70), channel_id=1, source_target_pairs={{0,0},{1,1},{48,32},{49,33},{66,64},{67,65},{114,96},{115,97},{132... | collective-permute-start | bytes 1572872 | tf_op jit(solution)/shard_map/ppermute | solution.py:89
  269.8 16.3 %collective-permute-start.9 = (bf16[256,1024]{1,0:T(8,128)(2,1)}, bf16[256,1024]{1,0:T(8,128)(2,1)S(1)}, u32[]{:S(2)}, u32[]{:S(2)}) collective-permute-start(bf16[256,1024]{1,0:T(8,128)(2,1)} %collective-permute-done.8), channel_id=1, source_target_pairs={{0,0},{1,1},{32,32},{33,33},{64,64},{65,65},{96,96},{97,97},{128,1... | collective-permute-start | bytes 1572872 | tf_op jit(solution)/shard_map/ppermute | solution.py:85
  282.5 15.9 %all-to-all-start.5 = ((bf16[16,4,8,512]{3,2,1,0:T(8,128)(2,1)}), bf16[16,4,8,512]{3,2,1,0:T(8,128)(2,1)S(1)}, u32[]{:S(2)}, u32[]{:S(2)}) async-start(bf16[16,4,8,512]{3,2,1,0:T(8,128)(2,1)} %pad_maximum_fusion), calls=%async_computation.5 | async-start | bytes 1048576 | tf_op jit(solution)/shard_map/all_to_all | solution.py:116

commit v11 on v9

--- a/solution.py
+++ b/solution.py
@@ -77,14 +77,6 @@
     return lax.ppermute(x, DEVICES, PLAN.mirror)
 
 
-def unmirror(x):
-    return lax.ppermute(x, DEVICES, back(PLAN.mirror))
-
-
-def unshuffle(x):
-    return lax.ppermute(x, DEVICES, back(PLAN.shuffle))
-
-
 def to_store(x):
     return lax.ppermute(x, DEVICES, PLAN.home)
 
@@ -140,18 +132,20 @@
     dperm = (dact * gelu_slope(pf)).astype(BF16)
     dpre = exchange(dperm.reshape(nb, n, nb, J_UP, t).transpose(1, 2, 0, 3, 4))
     act = gelu_value(pf).astype(BF16)
-    down_term = to_rows(jnp.einsum("gmt,gct->gmc", act, dblock, preferred_element_type=F32))
+    down_term = jnp.einsum("gmt,gct->gmc", act, dblock, preferred_element_type=F32).astype(BF16)
+    early = to_rows(down_term[:1])
     blockout = jnp.einsum("gmc,gmt->gct", down, act, preferred_element_type=F32).astype(BF16)
     blockout = blockout.reshape(nb, n, nb, J_DN, t).transpose(1, 2, 0, 3, 4)
-    mixed = exchange(after(blockout, dpre, down_term))
+    mixed = exchange(after(blockout, dpre, early))
     dpre = dpre.transpose(1, 0, 2, 3, 4).reshape(nb, BOUT, t)
     fgrad = jnp.einsum("bkn,bnt->bkt", up, dpre, preferred_element_type=F32).astype(BF16)
-    fgrad = unmirror(fgrad.reshape(nb * BIN, t))
+    fgrad = to_store(fgrad.reshape(nb * BIN, t))
     up_term = to_rows(jnp.einsum("bkt,bnt->bkn", x, dpre, preferred_element_type=F32))
     mixed = mixed.transpose(1, 0, 2, 3, 4).reshape(nb * BIN, t)
-    mixed = to_store(after(mixed, fgrad))
+    down_term = jnp.concatenate([early, to_rows(after(down_term[1:], mixed))], axis=1)
+    mixed = to_store(mixed)
     up_grad, down_grad = sum_rows(up_term, down_term, down_blocks.shape)
-    return mixed, unshuffle(fgrad), up_grad, down_grad
+    return mixed, fgrad, up_grad, down_grad
 
 
 def solution(mesh):

time: 300 us -> 305 us (1.017)
  the two profiles are of different devices: /device:TPU:1 before, /device:TPU:111 now
where the time goes in v11:
time: 305 us; the launch traced here: 303 us
  starting transfers between devices  191 us (63%)
  waiting for transfers between devices  83.1 us (27%)
  local copies, waits for them, and re-layouts  19 us (6%)
  matrix products  4.69 us (2%)
  other arithmetic  4.31 us (1%)
    all_to_all x4, starting transfers between devices, exchange(): lax.all_to_all(x, DEVICES, split_axis=0, concat_axis=0, tiled=True, axis_...  53.9 us
    all_to_all x1, starting transfers between devices, sum_rows(): got = lax.all_to_all(both, 'dp', split_axis=0, concat_axis=0, tiled=True)  41.1 us
    ppermute x3, starting transfers between devices, to_rows(): return lax.ppermute(rows, DEVICES, back(PLAN.weights))  29.7 us
    ppermute x2, waiting for transfers between devices, to_store(): return lax.ppermute(x, DEVICES, PLAN.home)  28.3 us
    ppermute x2, starting transfers between devices, whole(): rows = lax.ppermute(rows, DEVICES, PLAN.weights)  22.9 us
    all_to_all x4, waiting for transfers between devices, exchange(): lax.all_to_all(x, DEVICES, split_axis=0, concat_axis=0, tiled=True, axis_...  21.8 us
    ppermute x2, starting transfers between devices, mirror(): return lax.ppermute(x, DEVICES, PLAN.mirror)  17.4 us
    ppermute x2, waiting for transfers between devices, mirror(): return lax.ppermute(x, DEVICES, PLAN.mirror)  17.2 us
  transfers between devices with their start and end apart: 17, of which 10 were waited for; matrix products, arithmetic and copies ran while one was open for 6% of the time, Pallas kernels for 0%

profile of v11, /device:TPU:111, one launch (start us, length us, event | category | flops | bytes accessed | tf_op | source)
XLA Modules:
  0.0 303.5 jit_solution(6474180336821125083)
XLA Ops:
  3.2 4.9 %collective-permute-start = (bf16[256,1024]{1,0:T(8,128)(2,1)}, bf16[256,1024]{1,0:T(8,128)(2,1)S(1)}, u32[]{:S(2)}, u32[]{:S(2)}) collective-permute-start(bf16[256,1024]{1,0:T(8,128)(2,1)} %param.4), channel_id=1, source_target_pairs={{0,0},{1,1},{32,32},{33,33},{64,64},{65,65},{96,96},{97,97},{128,1... | collective-permute-start | bytes 1572872 | tf_op jit(solution)/shard_map/ppermute | solution.py:73
  8.9 8.8 %collective-permute-done.1 = bf16[256,1024]{1,0:T(8,128)(2,1)S(1)} collective-permute-done((bf16[256,1024]{1,0:T(8,128)(2,1)}, bf16[256,1024]{1,0:T(8,128)(2,1)S(1)}, u32[]{:S(2)}, u32[]{:S(2)}) %collective-permute-start.1) | collective-permute-done | bytes 524320 | tf_op jit(solution)/shard_map/ppermute | solution.py:73
  17.6 15.5 %collective-permute-start.2 = (bf16[256,1024]{1,0:T(8,128)(2,1)S(1)}, bf16[256,1024]{1,0:T(8,128)(2,1)S(1)}, u32[]{:S(2)}, u32[]{:S(2)}) collective-permute-start(bf16[256,1024]{1,0:T(8,128)(2,1)S(1)} %collective-permute-done.1), channel_id=1, source_target_pairs={{0,0},{1,1},{32,48},{33,49},{64,66},{65,67},{96,114},{97,115},{128... | collective-permute-start | bytes 1572872 | tf_op jit(solution)/shard_map/ppermute | solution.py:77
  34.7 6.0 %all-to-all-start = ((bf16[16,4,8,512]{3,2,1,0:T(8,128)(2,1)}), bf16[16,4,8,512]{3,2,1,0:T(8,128)(2,1)S(1)}, u32[]{:S(2)}, u32[]{:S(2)}) async-start(bf16[16,4,8,512]{3,2,1,0:T(8,128)(2,1)} %broadcast_in_dim.3), calls=%async_computation | async-start | bytes 1048576 | tf_op jit(solution)/shard_map/all_to_all | solution.py:89
  40.8 13.6 %collective-permute-done.2 = bf16[256,1024]{1,0:T(8,128)(2,1)S(1)} collective-permute-done((bf16[256,1024]{1,0:T(8,128)(2,1)S(1)}, bf16[256,1024]{1,0:T(8,128)(2,1)S(1)}, u32[]{:S(2)}, u32[]{:S(2)}) %collective-permute-start.2) | collective-permute-done | bytes 524320 | tf_op jit(solution)/shard_map/ppermute | solution.py:77
  57.8 14.4 %all-to-all-start.1 = ((bf16[32,2,2,2,1024]{4,3,2,1,0:T(2,128)(2,1)}), bf16[32,2,2,2,1024]{4,3,2,1,0:T(2,128)(2,1)S(1)}, u32[]{:S(2)}, u32[]{:S(2)}) async-start(bf16[32,2,2,2,1024]{4,3,2,1,0:T(2,128)(2,1)} %copy.38), calls=%async_computation.1 | async-start | bytes 1048576 | tf_op jit(solution)/shard_map/all_to_all | solution.py:63
  73.0 10.6 %collective-permute-start.5 = (bf16[16,2,8,512]{3,2,0,1:T(8,128)(2,1)S(1)}, bf16[16,2,8,512]{3,2,0,1:T(8,128)(2,1)S(1)}, u32[]{:S(2)}, u32[]{:S(2)}) collective-permute-start(bf16[16,2,8,512]{3,2,0,1:T(8,128)(2,1)S(1)} %copy.53), channel_id=1, source_target_pairs={{0,0},{1,1},{32,48},{33,49},{64,66},{65,67},{96,114},{97,115},{128... | collective-permute-start | bytes 786440 | tf_op jit(solution)/shard_map/ppermute | solution.py:95
  83.6 3.7 %collective-permute-done.3 = bf16[256,1024]{1,0:T(8,128)(2,1)S(1)} collective-permute-done((bf16[256,1024]{1,0:T(8,128)(2,1)S(1)}, bf16[256,1024]{1,0:T(8,128)(2,1)S(1)}, u32[]{:S(2)}, u32[]{:S(2)}) %collective-permute-start.3) | collective-permute-done | bytes 524320 | tf_op jit(solution)/shard_map/ppermute | solution.py:77
  87.3 3.1 %collective-permute-done.5 = bf16[16,2,8,512]{3,2,0,1:T(8,128)(2,1)S(1)} collective-permute-done((bf16[16,2,8,512]{3,2,0,1:T(8,128)(2,1)S(1)}, bf16[16,2,8,512]{3,2,0,1:T(8,128)(2,1)S(1)}, u32[]{:S(2)}, u32[]{:S(2)}) %collective-permute-start.5) | collective-permute-done | bytes 262176 | tf_op jit(solution)/shard_map/ppermute | solution.py:95
  92.6 20.5 %all-to-all-start.2 = ((bf16[32,2,2,8,1024]{4,3,1,2,0:T(8,128)(2,1)}), bf16[32,2,2,8,1024]{4,3,1,2,0:T(8,128)(2,1)S(1)}, u32[]{:S(2)}, u32[]{:S(2)}) async-start(bf16[32,2,2,8,1024]{4,3,1,2,0:T(8,128)(2,1)} %bitcast.64), calls=%async_computation.2 | async-start | bytes 4194304 | tf_op jit(solution)/shard_map/all_to_all | solution.py:63
  113.1 12.3 %collective-permute-start.4 = (bf16[16,2,8,512]{3,2,1,0:T(8,128)(2,1)}, bf16[16,2,8,512]{3,2,1,0:T(8,128)(2,1)}, u32[]{:S(2)}, u32[]{:S(2)}) collective-permute-start(bf16[16,2,8,512]{3,2,1,0:T(8,128)(2,1)} %get-tuple-element.10), channel_id=1, source_target_pairs={{0,0},{1,1},{32,48},{33,49},{64,66},{65,67},{96,114},{97,115},{128... | collective-permute-start | bytes 786440 | tf_op jit(solution)/shard_map/ppermute | solution.py:95
  126.8 3.1 %collective-permute-done.4 = bf16[16,2,8,512]{3,2,1,0:T(8,128)(2,1)} collective-permute-done((bf16[16,2,8,512]{3,2,1,0:T(8,128)(2,1)}, bf16[16,2,8,512]{3,2,1,0:T(8,128)(2,1)}, u32[]{:S(2)}, u32[]{:S(2)}) %collective-permute-start.4) | collective-permute-done | bytes 262176 | tf_op jit(solution)/shard_map/ppermute | solution.py:95
  131.1 10.5 %all-to-all-done.2 = bf16[32,2,2,8,1024]{4,3,1,2,0:T(8,128)(2,1)S(1)} async-done(((bf16[32,2,2,8,1024]{4,3,1,2,0:T(8,128)(2,1)}), bf16[32,2,2,8,1024]{4,3,1,2,0:T(8,128)(2,1)S(1)}, u32[]{:S(2)}, u32[]{:S(2)}) %all-to-all-start.2) | async-done | bytes 2097184 | tf_op jit(solution)/shard_map/all_to_all | solution.py:63
  146.9 10.9 %all-to-all-start.3 = ((bf16[32,2,2,8,1024]{4,3,1,2,0:T(8,128)(2,1)}), bf16[32,2,2,8,1024]{4,3,1,2,0:T(8,128)(2,1)}, u32[]{:S(2)}, u32[]{:S(2)}) async-start(bf16[32,2,2,8,1024]{4,3,1,2,0:T(8,128)(2,1)} %bitcast.63), calls=%async_computation.3 | async-start | bytes 4194304 | tf_op jit(solution)/shard_map/all_to_all | solution.py:63
  159.2 12.4 %collective-permute-start.6 = (bf16[16,1,8,512]{3,2,1,0:T(8,128)(2,1)}, bf16[16,1,8,512]{3,2,1,0:T(8,128)(2,1)}, u32[]{:S(2)}, u32[]{:S(2)}) collective-permute-start(bf16[16,1,8,512]{3,2,1,0:T(8,128)(2,1)} %bitcast.14), channel_id=1, source_target_pairs={{0,0},{1,1},{48,32},{49,33},{66,64},{67,65},{114,96},{115,97},{132... | collective-permute-start | bytes 393224 | tf_op jit(solution)/shard_map/ppermute | solution.py:103
  174.5 11.3 %all-to-all-done.3 = bf16[32,2,2,8,1024]{4,3,1,2,0:T(8,128)(2,1)} async-done(((bf16[32,2,2,8,1024]{4,3,1,2,0:T(8,128)(2,1)}), bf16[32,2,2,8,1024]{4,3,1,2,0:T(8,128)(2,1)}, u32[]{:S(2)}, u32[]{:S(2)}) %all-to-all-start.3) | async-done | bytes 2097184 | tf_op jit(solution)/shard_map/all_to_all | solution.py:63
  185.9 8.1 %all-to-all-start.4 = ((bf16[32,2,2,2,1024]{4,3,1,2,0:T(2,128)(2,1)}), bf16[32,2,2,2,1024]{4,3,1,2,0:T(2,128)(2,1)S(1)}, u32[]{:S(2)}, u32[]{:S(2)}) async-start(bf16[32,2,2,2,1024]{4,3,1,2,0:T(2,128)(2,1)} %bitcast.59), calls=%async_computation.4 | async-start | bytes 1048576 | tf_op jit(solution)/shard_map/all_to_all | solution.py:63
  197.4 12.0 %collective-permute-start.9 = (bf16[16,2,8,512]{3,2,1,0:T(8,128)(2,1)}, bf16[16,2,8,512]{3,2,1,0:T(8,128)(2,1)}, u32[]{:S(2)}, u32[]{:S(2)}) collective-permute-start(bf16[16,2,8,512]{3,2,1,0:T(8,128)(2,1)} %bitcast.60), channel_id=1, source_target_pairs={{0,0},{1,1},{48,32},{49,33},{66,64},{67,65},{114,96},{115,97},{132... | collective-permute-start | bytes 786440 | tf_op jit(solution)/shard_map/ppermute | solution.py:103
  210.8 5.2 %collective-permute-start.10 = (bf16[16,1,8,512]{3,2,1,0:T(8,128)(2,1)}, bf16[16,1,8,512]{3,2,1,0:T(8,128)(2,1)S(1)}, u32[]{:S(2)}, u32[]{:S(2)}) collective-permute-start(bf16[16,1,8,512]{3,2,1,0:T(8,128)(2,1)} %bitcast.22), channel_id=1, source_target_pairs={{0,0},{1,1},{48,32},{49,33},{66,64},{67,65},{114,96},{115,97},{132... | collective-permute-start | bytes 393224 | tf_op jit(solution)/shard_map/ppermute | solution.py:103
  216.4 4.9 %collective-permute-start.8 = (bf16[256,1024]{1,0:T(8,128)(2,1)S(1)}, bf16[256,1024]{1,0:T(8,128)(2,1)S(1)}, u32[]{:S(2)}, u32[]{:S(2)}) collective-permute-start(bf16[256,1024]{1,0:T(8,128)(2,1)S(1)} %bitcast.75), channel_id=1, source_target_pairs={{0,0},{1,1},{48,32},{49,33},{66,64},{67,65},{114,96},{115,97},{132... | collective-permute-start | bytes 1572872 | tf_op jit(solution)/shard_map/ppermute | solution.py:81
  221.3 7.9 %collective-permute-start.7 = (bf16[256,1024]{1,0:T(8,128)(2,1)S(1)}, bf16[256,1024]{1,0:T(8,128)(2,1)S(1)}, u32[]{:S(2)}, u32[]{:S(2)}) collective-permute-start(bf16[256,1024]{1,0:T(8,128)(2,1)S(1)} %reshape.66), channel_id=1, source_target_pairs={{0,0},{1,1},{48,32},{49,33},{66,64},{67,65},{114,96},{115,97},{132... | collective-permute-start | bytes 1572872 | tf_op jit(solution)/shard_map/ppermute | solution.py:81
  231.1 41.1 %all-to-all-start.5 = ((bf16[16,4,8,512]{3,2,1,0:T(8,128)(2,1)}), bf16[16,4,8,512]{3,2,1,0:T(8,128)(2,1)S(1)}, u32[]{:S(2)}, u32[]{:S(2)}) async-start(bf16[16,4,8,512]{3,2,1,0:T(8,128)(2,1)} %pad_maximum_fusion), calls=%async_computation.5 | async-start | bytes 1048576 | tf_op jit(solution)/shard_map/all_to_all | solution.py:108
  272.3 9.4 %collective-permute-done.8 = bf16[256,1024]{1,0:T(8,128)(2,1)S(1)} collective-permute-done((bf16[256,1024]{1,0:T(8,128)(2,1)S(1)}, bf16[256,1024]{1,0:T(8,128)(2,1)S(1)}, u32[]{:S(2)}, u32[]{:S(2)}) %collective-permute-start.8) | collective-permute-done | bytes 524320 | tf_op jit(solution)/shard_map/ppermute | solution.py:81
  281.7 18.9 %collective-permute-done.7 = bf16[256,1024]{1,0:T(8,128)(2,1)S(1)} collective-permute-done((bf16[256,1024]{1,0:T(8,128)(2,1)S(1)}, bf16[256,1024]{1,0:T(8,128)(2,1)S(1)}, u32[]{:S(2)}, u32[]{:S(2)}) %collective-permute-start.7) | collective-permute-done | bytes 524320 | tf_op jit(solution)/shard_map/ppermute | solution.py:81
  (53 shorter events, 33.2 us)
Async XLA Ops:
  0.6 17.0 %collective-permute-start.1 = (bf16[256,1024]{1,0:T(8,128)(2,1)}, bf16[256,1024]{1,0:T(8,128)(2,1)S(1)}, u32[]{:S(2)}, u32[]{:S(2)}) collective-permute-start(bf16[256,1024]{1,0:T(8,128)(2,1)} %param.7), channel_id=1, source_target_pairs={{0,0},{1,1},{32,32},{33,33},{64,64},{65,65},{96,96},{97,97},{128,1... | collective-permute-start | bytes 1572872 | tf_op jit(solution)/shard_map/ppermute | solution.py:73
  3.2 37.6 %collective-permute-start = (bf16[256,1024]{1,0:T(8,128)(2,1)}, bf16[256,1024]{1,0:T(8,128)(2,1)S(1)}, u32[]{:S(2)}, u32[]{:S(2)}) collective-permute-start(bf16[256,1024]{1,0:T(8,128)(2,1)} %param.4), channel_id=1, source_target_pairs={{0,0},{1,1},{32,32},{33,33},{64,64},{65,65},{96,96},{97,97},{128,1... | collective-permute-start | bytes 1572872 | tf_op jit(solution)/shard_map/ppermute | solution.py:73
  17.6 36.7 %collective-permute-start.2 = (bf16[256,1024]{1,0:T(8,128)(2,1)S(1)}, bf16[256,1024]{1,0:T(8,128)(2,1)S(1)}, u32[]{:S(2)}, u32[]{:S(2)}) collective-permute-start(bf16[256,1024]{1,0:T(8,128)(2,1)S(1)} %collective-permute-done.1), channel_id=1, source_target_pairs={{0,0},{1,1},{32,48},{33,49},{64,66},{65,67},{96,114},{97,115},{128... | collective-permute-start | bytes 1572872 | tf_op jit(solution)/shard_map/ppermute | solution.py:77
  34.7 23.1 %all-to-all-start = ((bf16[16,4,8,512]{3,2,1,0:T(8,128)(2,1)}), bf16[16,4,8,512]{3,2,1,0:T(8,128)(2,1)S(1)}, u32[]{:S(2)}, u32[]{:S(2)}) async-start(bf16[16,4,8,512]{3,2,1,0:T(8,128)(2,1)} %broadcast_in_dim.3), calls=%async_computation | async-start | bytes 1048576 | tf_op jit(solution)/shard_map/all_to_all | solution.py:89
  54.3 33.0 %collective-permute-start.3 = (bf16[256,1024]{1,0:T(8,128)(2,1)S(1)}, bf16[256,1024]{1,0:T(8,128)(2,1)S(1)}, u32[]{:S(2)}, u32[]{:S(2)}) collective-permute-start(bf16[256,1024]{1,0:T(8,128)(2,1)S(1)} %collective-permute-done), channel_id=1, source_target_pairs={{0,0},{1,1},{32,48},{33,49},{64,66},{65,67},{96,114},{97,115},{128... | collective-permute-start | bytes 1572872 | tf_op jit(solution)/shard_map/ppermute | solution.py:77
  57.8 25.8 %all-to-all-start.1 = ((bf16[32,2,2,2,1024]{4,3,2,1,0:T(2,128)(2,1)}), bf16[32,2,2,2,1024]{4,3,2,1,0:T(2,128)(2,1)S(1)}, u32[]{:S(2)}, u32[]{:S(2)}) async-start(bf16[32,2,2,2,1024]{4,3,2,1,0:T(2,128)(2,1)} %copy.38), calls=%async_computation.1 | async-start | bytes 1048576 | tf_op jit(solution)/shard_map/all_to_all | solution.py:63
  73.0 17.3 %collective-permute-start.5 = (bf16[16,2,8,512]{3,2,0,1:T(8,128)(2,1)S(1)}, bf16[16,2,8,512]{3,2,0,1:T(8,128)(2,1)S(1)}, u32[]{:S(2)}, u32[]{:S(2)}) collective-permute-start(bf16[16,2,8,512]{3,2,0,1:T(8,128)(2,1)S(1)} %copy.53), channel_id=1, source_target_pairs={{0,0},{1,1},{32,48},{33,49},{64,66},{65,67},{96,114},{97,115},{128... | collective-permute-start | bytes 786440 | tf_op jit(solution)/shard_map/ppermute | solution.py:95
  87.3 5.3 %copy-start = (bf16[256,1024]{1,0:T(8,128)(2,1)}, bf16[256,1024]{1,0:T(8,128)(2,1)S(1)}, u32[]{:S(2)}) copy-start(bf16[256,1024]{1,0:T(8,128)(2,1)S(1)} %collective-permute-done.3) | copy-start | bytes 1572868
  92.6 49.0 %all-to-all-start.2 = ((bf16[32,2,2,8,1024]{4,3,1,2,0:T(8,128)(2,1)}), bf16[32,2,2,8,1024]{4,3,1,2,0:T(8,128)(2,1)S(1)}, u32[]{:S(2)}, u32[]{:S(2)}) async-start(bf16[32,2,2,8,1024]{4,3,1,2,0:T(8,128)(2,1)} %bitcast.64), calls=%async_computation.2 | async-start | bytes 4194304 | tf_op jit(solution)/shard_map/all_to_all | solution.py:63
  113.1 16.9 %collective-permute-start.4 = (bf16[16,2,8,512]{3,2,1,0:T(8,128)(2,1)}, bf16[16,2,8,512]{3,2,1,0:T(8,128)(2,1)}, u32[]{:S(2)}, u32[]{:S(2)}) collective-permute-start(bf16[16,2,8,512]{3,2,1,0:T(8,128)(2,1)} %get-tuple-element.10), channel_id=1, source_target_pairs={{0,0},{1,1},{32,48},{33,49},{64,66},{65,67},{96,114},{97,115},{128... | collective-permute-start | bytes 786440 | tf_op jit(solution)/shard_map/ppermute | solution.py:95
  142.7 1.2 copy-start.2
  146.9 39.0 %all-to-all-start.3 = ((bf16[32,2,2,8,1024]{4,3,1,2,0:T(8,128)(2,1)}), bf16[32,2,2,8,1024]{4,3,1,2,0:T(8,128)(2,1)}, u32[]{:S(2)}, u32[]{:S(2)}) async-start(bf16[32,2,2,8,1024]{4,3,1,2,0:T(8,128)(2,1)} %bitcast.63), calls=%async_computation.3 | async-start | bytes 4194304 | tf_op jit(solution)/shard_map/all_to_all | solution.py:63
  159.2 15.3 %collective-permute-start.6 = (bf16[16,1,8,512]{3,2,1,0:T(8,128)(2,1)}, bf16[16,1,8,512]{3,2,1,0:T(8,128)(2,1)}, u32[]{:S(2)}, u32[]{:S(2)}) collective-permute-start(bf16[16,1,8,512]{3,2,1,0:T(8,128)(2,1)} %bitcast.14), channel_id=1, source_target_pairs={{0,0},{1,1},{48,32},{49,33},{66,64},{67,65},{114,96},{115,97},{132... | collective-permute-start | bytes 393224 | tf_op jit(solution)/shard_map/ppermute | solution.py:103
  172.2 23.7 %copy-start.1 = (bf16[256,1024]{1,0:T(8,128)(2,1)S(1)}, bf16[256,1024]{1,0:T(8,128)(2,1)}, u32[]{:S(2)}) copy-start(bf16[256,1024]{1,0:T(8,128)(2,1)} %copy-done) | copy-start | bytes 1572868
  185.9 23.6 %all-to-all-start.4 = ((bf16[32,2,2,2,1024]{4,3,1,2,0:T(2,128)(2,1)}), bf16[32,2,2,2,1024]{4,3,1,2,0:T(2,128)(2,1)S(1)}, u32[]{:S(2)}, u32[]{:S(2)}) async-start(bf16[32,2,2,2,1024]{4,3,1,2,0:T(2,128)(2,1)} %bitcast.59), calls=%async_computation.4 | async-start | bytes 1048576 | tf_op jit(solution)/shard_map/all_to_all | solution.py:63
  197.4 31.9 %collective-permute-start.9 = (bf16[16,2,8,512]{3,2,1,0:T(8,128)(2,1)}, bf16[16,2,8,512]{3,2,1,0:T(8,128)(2,1)}, u32[]{:S(2)}, u32[]{:S(2)}) collective-permute-start(bf16[16,2,8,512]{3,2,1,0:T(8,128)(2,1)} %bitcast.60), channel_id=1, source_target_pairs={{0,0},{1,1},{48,32},{49,33},{66,64},{67,65},{114,96},{115,97},{132... | collective-permute-start | bytes 786440 | tf_op jit(solution)/shard_map/ppermute | solution.py:103
  210.8 18.5 %collective-permute-start.10 = (bf16[16,1,8,512]{3,2,1,0:T(8,128)(2,1)}, bf16[16,1,8,512]{3,2,1,0:T(8,128)(2,1)S(1)}, u32[]{:S(2)}, u32[]{:S(2)}) collective-permute-start(bf16[16,1,8,512]{3,2,1,0:T(8,128)(2,1)} %bitcast.22), channel_id=1, source_target_pairs={{0,0},{1,1},{48,32},{49,33},{66,64},{67,65},{114,96},{115,97},{132... | collective-permute-start | bytes 393224 | tf_op jit(solution)/shard_map/ppermute | solution.py:103
  216.4 65.2 %collective-permute-start.8 = (bf16[256,1024]{1,0:T(8,128)(2,1)S(1)}, bf16[256,1024]{1,0:T(8,128)(2,1)S(1)}, u32[]{:S(2)}, u32[]{:S(2)}) collective-permute-start(bf16[256,1024]{1,0:T(8,128)(2,1)S(1)} %bitcast.75), channel_id=1, source_target_pairs={{0,0},{1,1},{48,32},{49,33},{66,64},{67,65},{114,96},{115,97},{132... | collective-permute-start | bytes 1572872 | tf_op jit(solution)/shard_map/ppermute | solution.py:81
  221.3 79.3 %collective-permute-start.7 = (bf16[256,1024]{1,0:T(8,128)(2,1)S(1)}, bf16[256,1024]{1,0:T(8,128)(2,1)S(1)}, u32[]{:S(2)}, u32[]{:S(2)}) collective-permute-start(bf16[256,1024]{1,0:T(8,128)(2,1)S(1)} %reshape.66), channel_id=1, source_target_pairs={{0,0},{1,1},{48,32},{49,33},{66,64},{67,65},{114,96},{115,97},{132... | collective-permute-start | bytes 1572872 | tf_op jit(solution)/shard_map/ppermute | solution.py:81
  231.1 69.4 %all-to-all-start.5 = ((bf16[16,4,8,512]{3,2,1,0:T(8,128)(2,1)}), bf16[16,4,8,512]{3,2,1,0:T(8,128)(2,1)S(1)}, u32[]{:S(2)}, u32[]{:S(2)}) async-start(bf16[16,4,8,512]{3,2,1,0:T(8,128)(2,1)} %pad_maximum_fusion), calls=%async_computation.5 | async-start | bytes 1048576 | tf_op jit(solution)/shard_map/all_to_all | solution.py:108

commit v12 on v5

--- a/solution.py
+++ b/solution.py
@@ -146,10 +146,10 @@
     dpre = exchange(after(dperm, mixed))
     mixed = unmirror(mixed.transpose(1, 0, 2, 3, 4).reshape(nb * BIN, t))
     down_term = jnp.einsum("gmt,gct->gmc", act, dblock, preferred_element_type=F32)
-    dpre = after(dpre, mixed).transpose(1, 0, 2, 3, 4).reshape(nb, BOUT, t)
+    dpre = dpre.transpose(1, 0, 2, 3, 4).reshape(nb, BOUT, t)
     fgrad = jnp.einsum("bkn,bnt->bkt", up, dpre, preferred_element_type=F32).astype(BF16)
     fgrad = fgrad.reshape(nb * BIN, t)
-    dpre = after(dpre, fgrad)
+    dpre = after(dpre, fgrad, mixed)
     up_term = jnp.einsum("bkt,bnt->bkn", x, dpre, preferred_element_type=F32)
     up_grad, down_grad = sum_rows(up_term, down_term)
     return unshuffle(mixed), to_store(fgrad), up_grad, down_grad

time: 297 us -> 297 us (level)
  the two profiles are of different devices: /device:TPU:32 before, /device:TPU:162 now
where the time goes in v12:
time: 297 us; the launch traced here: 296 us
  starting transfers between devices  159 us (54%)
  waiting for transfers between devices  104 us (35%)
  local copies, waits for them, and re-layouts  16.8 us (6%)
  matrix products  9.33 us (3%)
  other arithmetic  5.3 us (2%)
    all_to_all x4, starting transfers between devices, exchange(): lax.all_to_all(x, DEVICES, split_axis=0, concat_axis=0, tiled=True, axis_...  55.4 us
    all_to_all x1, starting transfers between devices, sum_rows(): got = lax.all_to_all(both, 'dp', split_axis=0, concat_axis=0, tiled=True)  42.3 us
    all_to_all x4, waiting for transfers between devices, exchange(): lax.all_to_all(x, DEVICES, split_axis=0, concat_axis=0, tiled=True, axis_...  38.8 us
    ppermute x2, waiting for transfers between devices, whole(): rows = lax.ppermute(rows, DEVICES, PLAN.weights)  21 us
    ppermute x2, starting transfers between devices, mirror(): return lax.ppermute(x, DEVICES, PLAN.mirror)  19.9 us
    ppermute x2, waiting for transfers between devices, mirror(): return lax.ppermute(x, DEVICES, PLAN.mirror)  14.4 us
    all_to_all x1, waiting for transfers between devices, sum_rows(): got = lax.all_to_all(both, 'dp', split_axis=0, concat_axis=0, tiled=True)  12.3 us
    ppermute x1, starting transfers between devices, sum_rows(): d = lax.ppermute(d, DEVICES, back(PLAN.weights))  11.1 us
  transfers between devices with their start and end apart: 17, of which 10 were waited for; matrix products, arithmetic and copies ran while one was open for 7% of the time, Pallas kernels for 0%

profile of v12, /device:TPU:162, one launch (start us, length us, event | category | flops | bytes accessed | tf_op | source)
XLA Modules:
  0.0 295.8 jit_solution(12881950441696038197)
XLA Ops:
  0.6 4.4 %collective-permute-start.1 = (bf16[256,1024]{1,0:T(8,128)(2,1)}, bf16[256,1024]{1,0:T(8,128)(2,1)S(1)}, u32[]{:S(2)}, u32[]{:S(2)}) collective-permute-start(bf16[256,1024]{1,0:T(8,128)(2,1)} %param.7), channel_id=1, source_target_pairs={{0,0},{1,1},{32,32},{33,33},{64,64},{65,65},{96,96},{97,97},{128,1... | collective-permute-start | bytes 1572872 | tf_op jit(solution)/shard_map/ppermute | solution.py:73
  5.0 2.9 collective-permute-start
  8.7 9.2 %collective-permute-done.1 = bf16[256,1024]{1,0:T(8,128)(2,1)S(1)} collective-permute-done((bf16[256,1024]{1,0:T(8,128)(2,1)}, bf16[256,1024]{1,0:T(8,128)(2,1)S(1)}, u32[]{:S(2)}, u32[]{:S(2)}) %collective-permute-start.1) | collective-permute-done | bytes 524320 | tf_op jit(solution)/shard_map/ppermute | solution.py:73
  17.9 9.6 %collective-permute-start.2 = (bf16[256,1024]{1,0:T(8,128)(2,1)S(1)}, bf16[256,1024]{1,0:T(8,128)(2,1)S(1)}, u32[]{:S(2)}, u32[]{:S(2)}) collective-permute-start(bf16[256,1024]{1,0:T(8,128)(2,1)S(1)} %collective-permute-done.1), channel_id=1, source_target_pairs={{0,0},{1,1},{32,48},{33,49},{64,66},{65,67},{96,114},{97,115},{128... | collective-permute-start | bytes 1572872 | tf_op jit(solution)/shard_map/ppermute | solution.py:77
  29.1 6.4 %all-to-all-start = ((bf16[16,4,8,512]{3,2,1,0:T(8,128)(2,1)}), bf16[16,4,8,512]{3,2,1,0:T(8,128)(2,1)S(1)}, u32[]{:S(2)}, u32[]{:S(2)}) async-start(bf16[16,4,8,512]{3,2,1,0:T(8,128)(2,1)} %broadcast_in_dim.3), calls=%async_computation | async-start | bytes 1048576 | tf_op jit(solution)/shard_map/all_to_all | solution.py:97
  35.5 14.4 %collective-permute-done.2 = bf16[256,1024]{1,0:T(8,128)(2,1)S(1)} collective-permute-done((bf16[256,1024]{1,0:T(8,128)(2,1)S(1)}, bf16[256,1024]{1,0:T(8,128)(2,1)S(1)}, u32[]{:S(2)}, u32[]{:S(2)}) %collective-permute-start.2) | collective-permute-done | bytes 524320 | tf_op jit(solution)/shard_map/ppermute | solution.py:77
  49.9 10.2 %collective-permute-start.3 = (bf16[256,1024]{1,0:T(8,128)(2,1)S(1)}, bf16[256,1024]{1,0:T(8,128)(2,1)S(1)}, u32[]{:S(2)}, u32[]{:S(2)}) collective-permute-start(bf16[256,1024]{1,0:T(8,128)(2,1)S(1)} %collective-permute-done), channel_id=1, source_target_pairs={{0,0},{1,1},{32,48},{33,49},{64,66},{65,67},{96,114},{97,115},{128... | collective-permute-start | bytes 1572872 | tf_op jit(solution)/shard_map/ppermute | solution.py:77
  61.6 23.8 %all-to-all-start.1 = ((bf16[32,2,2,2,1024]{4,3,2,1,0:T(2,128)(2,1)}), bf16[32,2,2,2,1024]{4,3,2,1,0:T(2,128)(2,1)S(1)}, u32[]{:S(2)}, u32[]{:S(2)}) async-start(bf16[32,2,2,2,1024]{4,3,2,1,0:T(2,128)(2,1)} %copy.37), calls=%async_computation.1 | async-start | bytes 1048576 | tf_op jit(solution)/shard_map/all_to_all | solution.py:63
  88.1 8.7 %all-to-all-done.1 = bf16[32,2,2,2,1024]{4,3,2,1,0:T(2,128)(2,1)S(1)} async-done(((bf16[32,2,2,2,1024]{4,3,2,1,0:T(2,128)(2,1)}), bf16[32,2,2,2,1024]{4,3,2,1,0:T(2,128)(2,1)S(1)}, u32[]{:S(2)}, u32[]{:S(2)}) %all-to-all-start.1) | async-done | bytes 524320 | tf_op jit(solution)/shard_map/all_to_all | solution.py:63
  96.8 4.2 %collective-permute-done.5 = bf16[16,2,8,512]{3,2,0,1:T(8,128)(2,1)S(1)} collective-permute-done((bf16[16,2,8,512]{3,2,0,1:T(8,128)(2,1)S(1)}, bf16[16,2,8,512]{3,2,0,1:T(8,128)(2,1)S(1)}, u32[]{:S(2)}, u32[]{:S(2)}) %collective-permute-start.5) | collective-permute-done | bytes 262176 | tf_op jit(solution)/shard_map/ppermute | solution.py:103
  103.3 12.8 %all-to-all-start.2 = ((bf16[32,2,2,8,1024]{4,3,1,2,0:T(8,128)(2,1)}), bf16[32,2,2,8,1024]{4,3,1,2,0:T(8,128)(2,1)S(1)}, u32[]{:S(2)}, u32[]{:S(2)}) async-start(bf16[32,2,2,8,1024]{4,3,1,2,0:T(8,128)(2,1)} %bitcast.65), calls=%async_computation.2 | async-start | bytes 4194304 | tf_op jit(solution)/shard_map/all_to_all | solution.py:63
  119.4 16.8 %collective-permute-done.4 = bf16[16,2,8,512]{3,2,1,0:T(8,128)(2,1)S(1)} collective-permute-done((bf16[16,2,8,512]{3,2,1,0:T(8,128)(2,1)}, bf16[16,2,8,512]{3,2,1,0:T(8,128)(2,1)S(1)}, u32[]{:S(2)}, u32[]{:S(2)}) %collective-permute-start.4) | collective-permute-done | bytes 262176 | tf_op jit(solution)/shard_map/ppermute | solution.py:103
  136.4 8.9 %all-to-all-done.2 = bf16[32,2,2,8,1024]{4,3,1,2,0:T(8,128)(2,1)S(1)} async-done(((bf16[32,2,2,8,1024]{4,3,1,2,0:T(8,128)(2,1)}), bf16[32,2,2,8,1024]{4,3,1,2,0:T(8,128)(2,1)S(1)}, u32[]{:S(2)}, u32[]{:S(2)}) %all-to-all-start.2) | async-done | bytes 2097184 | tf_op jit(solution)/shard_map/all_to_all | solution.py:63
  146.4 3.2 %fusion.7 = (bf16[2,512,1024]{2,1,0:T(8,128)(2,1)S(1)}, f32[2,512,1024]{2,1,0:T(8,128)}) fusion(f32[2,32,2,8,1024]{4,3,2,1,0:T(8,128)S(1)} %copy.40), kind=kLoop, calls=%fused_computation.10 | loop fusion | flops 5242880 | bytes 10485760 | tf_op jit(solution)/shard_map/convert_element_type | solution.py:138
  151.8 11.0 %all-to-all-start.3 = ((bf16[32,2,2,2,1024]{4,3,1,2,0:T(2,128)(2,1)}), bf16[32,2,2,2,1024]{4,3,1,2,0:T(2,128)(2,1)S(1)}, u32[]{:S(2)}, u32[]{:S(2)}) async-start(bf16[32,2,2,2,1024]{4,3,1,2,0:T(2,128)(2,1)} %bitcast.59), calls=%async_computation.3 | async-start | bytes 1048576 | tf_op jit(solution)/shard_map/all_to_all | solution.py:63
  162.8 5.1 %fusion.5 = bf16[2,512,1024]{2,1,0:T(8,128)(2,1)S(1)} fusion(f32[2,32,2,8,1024]{4,3,2,1,0:T(8,128)} %copy-done, f32[2,512,1024]{2,1,0:T(8,128)} %get-tuple-element.15, bf16[2,512,128]{2,1,0:T(8,128)(2,1)S(1)} %bitcast.75, bf16[2,128,1024]{2,1,0:T(8,128)(2,1)} %reshape.68), kind=kOutput, calls=%fused_computation.6 | convolution fusion | flops 276824064 | bytes 11272192 | tf_op jit(solution)/shard_map/gmc,gct->gmt/dot_general | solution.py:143
  169.4 2.7 all-to-all-done.3
  172.0 7.8 %all-to-all-start.4 = ((bf16[32,2,2,8,1024]{4,3,1,2,0:T(8,128)(2,1)}), bf16[32,2,2,8,1024]{4,3,1,2,0:T(8,128)(2,1)}, u32[]{:S(2)}, u32[]{:S(2)}) async-start(bf16[32,2,2,8,1024]{4,3,1,2,0:T(8,128)(2,1)} %bitcast.64), calls=%async_computation.4 | async-start | bytes 4194304 | tf_op jit(solution)/shard_map/all_to_all | solution.py:63
  185.2 11.1 %collective-permute-start.10 = (bf16[16,2,8,512]{3,2,1,0:T(8,128)(2,1)S(1)}, bf16[16,2,8,512]{3,2,1,0:T(8,128)(2,1)S(1)}, u32[]{:S(2)}, u32[]{:S(2)}) collective-permute-start(bf16[16,2,8,512]{3,2,1,0:T(8,128)(2,1)S(1)} %bitcast.77), channel_id=1, source_target_pairs={{0,0},{1,1},{48,32},{49,33},{66,64},{67,65},{114,96},{115,97},{132... | collective-permute-start | bytes 786440 | tf_op jit(solution)/shard_map/ppermute | solution.py:115
  196.4 18.5 %all-to-all-done.4 = bf16[32,2,2,8,1024]{4,3,1,2,0:T(8,128)(2,1)} async-done(((bf16[32,2,2,8,1024]{4,3,1,2,0:T(8,128)(2,1)}), bf16[32,2,2,8,1024]{4,3,1,2,0:T(8,128)(2,1)}, u32[]{:S(2)}, u32[]{:S(2)}) %all-to-all-start.4) | async-done | bytes 2097184 | tf_op jit(solution)/shard_map/all_to_all | solution.py:63
  219.9 7.0 %collective-permute-start.7 = (bf16[256,1024]{1,0:T(8,128)(2,1)S(1)}, bf16[256,1024]{1,0:T(8,128)(2,1)S(1)}, u32[]{:S(2)}, u32[]{:S(2)}) collective-permute-start(bf16[256,1024]{1,0:T(8,128)(2,1)S(1)} %collective-permute-done.6), channel_id=1, source_target_pairs={{0,0},{1,1},{32,32},{33,33},{64,64},{65,65},{96,96},{97,97},{128,1... | collective-permute-start | bytes 1572872 | tf_op jit(solution)/shard_map/ppermute | solution.py:85
  228.9 8.6 %collective-permute-done.9 = bf16[16,2,8,512]{3,2,1,0:T(8,128)(2,1)S(1)} collective-permute-done((bf16[16,2,8,512]{3,2,1,0:T(8,128)(2,1)S(1)}, bf16[16,2,8,512]{3,2,1,0:T(8,128)(2,1)S(1)}, u32[]{:S(2)}, u32[]{:S(2)}) %collective-permute-start.9) | collective-permute-done | bytes 262176 | tf_op jit(solution)/shard_map/ppermute | solution.py:114
  238.2 42.3 %all-to-all-start.5 = ((bf16[16,4,8,512]{3,2,1,0:T(8,128)(2,1)}), bf16[16,4,8,512]{3,2,1,0:T(8,128)(2,1)S(1)}, u32[]{:S(2)}, u32[]{:S(2)}) async-start(bf16[16,4,8,512]{3,2,1,0:T(8,128)(2,1)} %pad_maximum_fusion), calls=%async_computation.5 | async-start | bytes 1048576 | tf_op jit(solution)/shard_map/all_to_all | solution.py:117
  280.6 12.3 %all-to-all-done.5 = bf16[16,4,8,512]{3,2,1,0:T(8,128)(2,1)S(1)} async-done(((bf16[16,4,8,512]{3,2,1,0:T(8,128)(2,1)}), bf16[16,4,8,512]{3,2,1,0:T(8,128)(2,1)S(1)}, u32[]{:S(2)}, u32[]{:S(2)}) %all-to-all-start.5) | async-done | bytes 524320 | tf_op jit(solution)/shard_map/all_to_all | solution.py:117
  (56 shorter events, 33.0 us)
Async XLA Ops:
  0.6 17.3 %collective-permute-start.1 = (bf16[256,1024]{1,0:T(8,128)(2,1)}, bf16[256,1024]{1,0:T(8,128)(2,1)S(1)}, u32[]{:S(2)}, u32[]{:S(2)}) collective-permute-start(bf16[256,1024]{1,0:T(8,128)(2,1)} %param.7), channel_id=1, source_target_pairs={{0,0},{1,1},{32,32},{33,33},{64,64},{65,65},{96,96},{97,97},{128,1... | collective-permute-start | bytes 1572872 | tf_op jit(solution)/shard_map/ppermute | solution.py:73
  5.0 30.4 %collective-permute-start = (bf16[256,1024]{1,0:T(8,128)(2,1)}, bf16[256,1024]{1,0:T(8,128)(2,1)S(1)}, u32[]{:S(2)}, u32[]{:S(2)}) collective-permute-start(bf16[256,1024]{1,0:T(8,128)(2,1)} %param.4), channel_id=1, source_target_pairs={{0,0},{1,1},{32,32},{33,33},{64,64},{65,65},{96,96},{97,97},{128,1... | collective-permute-start | bytes 1572872 | tf_op jit(solution)/shard_map/ppermute | solution.py:73
  17.9 32.0 %collective-permute-start.2 = (bf16[256,1024]{1,0:T(8,128)(2,1)S(1)}, bf16[256,1024]{1,0:T(8,128)(2,1)S(1)}, u32[]{:S(2)}, u32[]{:S(2)}) collective-permute-start(bf16[256,1024]{1,0:T(8,128)(2,1)S(1)} %collective-permute-done.1), channel_id=1, source_target_pairs={{0,0},{1,1},{32,48},{33,49},{64,66},{65,67},{96,114},{97,115},{128... | collective-permute-start | bytes 1572872 | tf_op jit(solution)/shard_map/ppermute | solution.py:77
  29.1 32.5 %all-to-all-start = ((bf16[16,4,8,512]{3,2,1,0:T(8,128)(2,1)}), bf16[16,4,8,512]{3,2,1,0:T(8,128)(2,1)S(1)}, u32[]{:S(2)}, u32[]{:S(2)}) async-start(bf16[16,4,8,512]{3,2,1,0:T(8,128)(2,1)} %broadcast_in_dim.3), calls=%async_computation | async-start | bytes 1048576 | tf_op jit(solution)/shard_map/all_to_all | solution.py:97
  49.9 47.0 %collective-permute-start.3 = (bf16[256,1024]{1,0:T(8,128)(2,1)S(1)}, bf16[256,1024]{1,0:T(8,128)(2,1)S(1)}, u32[]{:S(2)}, u32[]{:S(2)}) collective-permute-start(bf16[256,1024]{1,0:T(8,128)(2,1)S(1)} %collective-permute-done), channel_id=1, source_target_pairs={{0,0},{1,1},{32,48},{33,49},{64,66},{65,67},{96,114},{97,115},{128... | collective-permute-start | bytes 1572872 | tf_op jit(solution)/shard_map/ppermute | solution.py:77
  61.6 35.2 %all-to-all-start.1 = ((bf16[32,2,2,2,1024]{4,3,2,1,0:T(2,128)(2,1)}), bf16[32,2,2,2,1024]{4,3,2,1,0:T(2,128)(2,1)S(1)}, u32[]{:S(2)}, u32[]{:S(2)}) async-start(bf16[32,2,2,2,1024]{4,3,2,1,0:T(2,128)(2,1)} %copy.37), calls=%async_computation.1 | async-start | bytes 1048576 | tf_op jit(solution)/shard_map/all_to_all | solution.py:63
  86.2 14.9 %collective-permute-start.5 = (bf16[16,2,8,512]{3,2,0,1:T(8,128)(2,1)S(1)}, bf16[16,2,8,512]{3,2,0,1:T(8,128)(2,1)S(1)}, u32[]{:S(2)}, u32[]{:S(2)}) collective-permute-start(bf16[16,2,8,512]{3,2,0,1:T(8,128)(2,1)S(1)} %copy.51), channel_id=1, source_target_pairs={{0,0},{1,1},{32,48},{33,49},{64,66},{65,67},{96,114},{97,115},{128... | collective-permute-start | bytes 786440 | tf_op jit(solution)/shard_map/ppermute | solution.py:103
  96.8 6.5 %copy-start.1 = (bf16[256,1024]{1,0:T(8,128)(2,1)}, bf16[256,1024]{1,0:T(8,128)(2,1)S(1)}, u32[]{:S(2)}) copy-start(bf16[256,1024]{1,0:T(8,128)(2,1)S(1)} %collective-permute-done.3) | copy-start | bytes 1572868
  101.1 2.3 copy-start.3
  103.3 42.0 %all-to-all-start.2 = ((bf16[32,2,2,8,1024]{4,3,1,2,0:T(8,128)(2,1)}), bf16[32,2,2,8,1024]{4,3,1,2,0:T(8,128)(2,1)S(1)}, u32[]{:S(2)}, u32[]{:S(2)}) async-start(bf16[32,2,2,8,1024]{4,3,1,2,0:T(8,128)(2,1)} %bitcast.65), calls=%async_computation.2 | async-start | bytes 4194304 | tf_op jit(solution)/shard_map/all_to_all | solution.py:63
  116.1 20.1 %collective-permute-start.4 = (bf16[16,2,8,512]{3,2,1,0:T(8,128)(2,1)}, bf16[16,2,8,512]{3,2,1,0:T(8,128)(2,1)S(1)}, u32[]{:S(2)}, u32[]{:S(2)}) collective-permute-start(bf16[16,2,8,512]{3,2,1,0:T(8,128)(2,1)} %get-tuple-element.10), channel_id=1, source_target_pairs={{0,0},{1,1},{32,48},{33,49},{64,66},{65,67},{96,114},{97,115},{128... | collective-permute-start | bytes 786440 | tf_op jit(solution)/shard_map/ppermute | solution.py:103
  146.4 3.3 %copy-start = (f32[2,32,2,8,1024]{4,3,2,1,0:T(8,128)}, f32[2,32,2,8,1024]{4,3,2,1,0:T(8,128)S(1)}, u32[]{:S(2)}) copy-start(f32[2,32,2,8,1024]{4,3,2,1,0:T(8,128)S(1)} %copy.40) | copy-start | bytes 12582916
  151.8 20.3 %all-to-all-start.3 = ((bf16[32,2,2,2,1024]{4,3,1,2,0:T(2,128)(2,1)}), bf16[32,2,2,2,1024]{4,3,1,2,0:T(2,128)(2,1)S(1)}, u32[]{:S(2)}, u32[]{:S(2)}) async-start(bf16[32,2,2,2,1024]{4,3,1,2,0:T(2,128)(2,1)} %bitcast.59), calls=%async_computation.3 | async-start | bytes 1048576 | tf_op jit(solution)/shard_map/all_to_all | solution.py:63
  172.0 42.8 %all-to-all-start.4 = ((bf16[32,2,2,8,1024]{4,3,1,2,0:T(8,128)(2,1)}), bf16[32,2,2,8,1024]{4,3,1,2,0:T(8,128)(2,1)}, u32[]{:S(2)}, u32[]{:S(2)}) async-start(bf16[32,2,2,8,1024]{4,3,1,2,0:T(8,128)(2,1)} %bitcast.64), calls=%async_computation.4 | async-start | bytes 4194304 | tf_op jit(solution)/shard_map/all_to_all | solution.py:63
  181.2 35.4 %copy-start.4 = (bf16[16,2,8,512]{3,2,0,1:T(8,128)(2,1)S(1)}, bf16[16,2,8,512]{3,2,0,1:T(8,128)(2,1)}, u32[]{:S(2)}) copy-start(bf16[16,2,8,512]{3,2,0,1:T(8,128)(2,1)} %copy-done.3) | copy-start | bytes 786436
  181.2 35.9 %collective-permute-start.6 = (bf16[256,1024]{1,0:T(8,128)(2,1)}, bf16[256,1024]{1,0:T(8,128)(2,1)S(1)}, u32[]{:S(2)}, u32[]{:S(2)}) collective-permute-start(bf16[256,1024]{1,0:T(8,128)(2,1)} %reshape.67), channel_id=1, source_target_pairs={{0,0},{1,1},{48,32},{49,33},{66,64},{67,65},{114,96},{115,97},{132... | collective-permute-start | bytes 1572872 | tf_op jit(solution)/shard_map/ppermute | solution.py:81
  185.0 32.1 %copy-start.2 = (bf16[256,1024]{1,0:T(8,128)(2,1)S(1)}, bf16[256,1024]{1,0:T(8,128)(2,1)}, u32[]{:S(2)}) copy-start(bf16[256,1024]{1,0:T(8,128)(2,1)} %copy-done.1) | copy-start | bytes 1572868
  185.2 43.6 %collective-permute-start.10 = (bf16[16,2,8,512]{3,2,1,0:T(8,128)(2,1)S(1)}, bf16[16,2,8,512]{3,2,1,0:T(8,128)(2,1)S(1)}, u32[]{:S(2)}, u32[]{:S(2)}) collective-permute-start(bf16[16,2,8,512]{3,2,1,0:T(8,128)(2,1)S(1)} %bitcast.77), channel_id=1, source_target_pairs={{0,0},{1,1},{48,32},{49,33},{66,64},{67,65},{114,96},{115,97},{132... | collective-permute-start | bytes 786440 | tf_op jit(solution)/shard_map/ppermute | solution.py:115
  218.0 19.4 %collective-permute-start.9 = (bf16[16,2,8,512]{3,2,1,0:T(8,128)(2,1)S(1)}, bf16[16,2,8,512]{3,2,1,0:T(8,128)(2,1)S(1)}, u32[]{:S(2)}, u32[]{:S(2)}) collective-permute-start(bf16[16,2,8,512]{3,2,1,0:T(8,128)(2,1)S(1)} %bitcast.78), channel_id=1, source_target_pairs={{0,0},{1,1},{48,32},{49,33},{66,64},{67,65},{114,96},{115,97},{132... | collective-permute-start | bytes 786440 | tf_op jit(solution)/shard_map/ppermute | solution.py:114
  219.9 60.7 %collective-permute-start.7 = (bf16[256,1024]{1,0:T(8,128)(2,1)S(1)}, bf16[256,1024]{1,0:T(8,128)(2,1)S(1)}, u32[]{:S(2)}, u32[]{:S(2)}) collective-permute-start(bf16[256,1024]{1,0:T(8,128)(2,1)S(1)} %collective-permute-done.6), channel_id=1, source_target_pairs={{0,0},{1,1},{32,32},{33,33},{64,64},{65,65},{96,96},{97,97},{128,1... | collective-permute-start | bytes 1572872 | tf_op jit(solution)/shard_map/ppermute | solution.py:85
  226.9 53.7 %collective-permute-start.8 = (bf16[256,1024]{1,0:T(8,128)(2,1)S(1)}, bf16[256,1024]{1,0:T(8,128)(2,1)S(1)}, u32[]{:S(2)}, u32[]{:S(2)}) collective-permute-start(bf16[256,1024]{1,0:T(8,128)(2,1)S(1)} %bitcast.76), channel_id=1, source_target_pairs={{0,0},{1,1},{48,32},{49,33},{66,64},{67,65},{114,96},{115,97},{132... | collective-permute-start | bytes 1572872 | tf_op jit(solution)/shard_map/ppermute | solution.py:89
  238.2 54.7 %all-to-all-start.5 = ((bf16[16,4,8,512]{3,2,1,0:T(8,128)(2,1)}), bf16[16,4,8,512]{3,2,1,0:T(8,128)(2,1)S(1)}, u32[]{:S(2)}, u32[]{:S(2)}) async-start(bf16[16,4,8,512]{3,2,1,0:T(8,128)(2,1)} %pad_maximum_fusion), calls=%async_computation.5 | async-start | bytes 1048576 | tf_op jit(solution)/shard_map/all_to_all | solution.py:117

commit v13 on v12

--- a/solution.py
+++ b/solution.py
@@ -134,8 +134,8 @@
     permuted = exchange(pre.reshape(nb, n, nb, J_UP, t).transpose(1, 2, 0, 3, 4))
     down = whole(after(down_rows, x_flat), BOUT, BIN)
     permuted = permuted.transpose(1, 0, 2, 3, 4).reshape(nb, BOUT, t)
-    pf = permuted.astype(F32)
-    act = gelu_value(pf).astype(BF16)
+    act = gelu_value(permuted.astype(F32)).astype(BF16)
+    pf = lax.optimization_barrier(permuted).astype(F32)
     blockout = jnp.einsum("gmc,gmt->gct", down, act, preferred_element_type=F32).astype(BF16)
     blockout = blockout.reshape(nb, n, nb, J_DN, t).transpose(1, 2, 0, 3, 4)
     mixed = exchange(blockout)

time: 297 us -> 290 us (0.976)
  the two profiles are of different devices: /device:TPU:162 before, /device:TPU:1 now
where the time goes in v13:
time: 290 us; the launch traced here: 285 us
  starting transfers between devices  146 us (50%)
  waiting for transfers between devices  111 us (38%)
  local copies, waits for them, and re-layouts  15.8 us (5%)
  matrix products  7.55 us (3%)
    all_to_all x4, starting transfers between devices, exchange(): lax.all_to_all(x, DEVICES, split_axis=0, concat_axis=0, tiled=True, axis_...  55.3 us
    all_to_all x4, waiting for transfers between devices, exchange(): lax.all_to_all(x, DEVICES, split_axis=0, concat_axis=0, tiled=True, axis_...  42.7 us
    ppermute x2, starting transfers between devices, mirror(): return lax.ppermute(x, DEVICES, PLAN.mirror)  24.8 us
    ppermute x2, waiting for transfers between devices, whole(): rows = lax.ppermute(rows, DEVICES, PLAN.weights)  24 us
    all_to_all x1, starting transfers between devices, gather_rows(): got = lax.all_to_all(sent, 'dp', split_axis=0, concat_axis=0, tiled=True)  18.9 us
    ppermute x1, waiting for transfers between devices, sum_rows(): u = lax.ppermute(u, DEVICES, back(PLAN.weights))  17.6 us
    ppermute x1, waiting for transfers between devices, unmirror(): return lax.ppermute(x, DEVICES, back(PLAN.mirror))  14.8 us
    ppermute x1, starting transfers between devices, to_store(): return lax.ppermute(x, DEVICES, PLAN.home)  13.1 us
  transfers between devices with their start and end apart: 17, of which 11 were waited for; matrix products, arithmetic and copies ran while one was open for 6% of the time, Pallas kernels for 0%

profile of v13, /device:TPU:1, one launch (start us, length us, event | category | flops | bytes accessed | tf_op | source)
XLA Modules:
  0.0 284.5 jit_solution(6085940358129752363)
XLA Ops:
  4.8 17.4 %collective-permute-start.2 = (bf16[256,1024]{1,0:T(8,128)(2,1)S(1)}, bf16[256,1024]{1,0:T(8,128)(2,1)S(1)}, u32[]{:S(2)}, u32[]{:S(2)}) collective-permute-start(bf16[256,1024]{1,0:T(8,128)(2,1)S(1)} %collective-permute-done.1), channel_id=1, source_target_pairs={{0,0},{1,1},{32,48},{33,49},{64,66},{65,67},{96,114},{97,115},{128... | collective-permute-start | bytes 1572872 | tf_op jit(solution)/shard_map/ppermute | solution.py:77
  23.8 18.9 %all-to-all-start = ((bf16[16,4,8,512]{3,2,1,0:T(8,128)(2,1)}), bf16[16,4,8,512]{3,2,1,0:T(8,128)(2,1)S(1)}, u32[]{:S(2)}, u32[]{:S(2)}) async-start(bf16[16,4,8,512]{3,2,1,0:T(8,128)(2,1)} %broadcast_in_dim.3), calls=%async_computation | async-start | bytes 1048576 | tf_op jit(solution)/shard_map/all_to_all | solution.py:97
  42.7 7.4 %collective-permute-start.3 = (bf16[256,1024]{1,0:T(8,128)(2,1)S(1)}, bf16[256,1024]{1,0:T(8,128)(2,1)S(1)}, u32[]{:S(2)}, u32[]{:S(2)}) collective-permute-start(bf16[256,1024]{1,0:T(8,128)(2,1)S(1)} %collective-permute-done), channel_id=1, source_target_pairs={{0,0},{1,1},{32,48},{33,49},{64,66},{65,67},{96,114},{97,115},{128... | collective-permute-start | bytes 1572872 | tf_op jit(solution)/shard_map/ppermute | solution.py:77
  53.9 29.8 %all-to-all-start.1 = ((bf16[32,2,2,2,1024]{4,3,2,1,0:T(2,128)(2,1)}), bf16[32,2,2,2,1024]{4,3,2,1,0:T(2,128)(2,1)S(1)}, u32[]{:S(2)}, u32[]{:S(2)}) async-start(bf16[32,2,2,2,1024]{4,3,2,1,0:T(2,128)(2,1)} %copy.37), calls=%async_computation.1 | async-start | bytes 1048576 | tf_op jit(solution)/shard_map/all_to_all | solution.py:63
  86.4 9.3 %all-to-all-done.1 = bf16[32,2,2,2,1024]{4,3,2,1,0:T(2,128)(2,1)S(1)} async-done(((bf16[32,2,2,2,1024]{4,3,2,1,0:T(2,128)(2,1)}), bf16[32,2,2,2,1024]{4,3,2,1,0:T(2,128)(2,1)S(1)}, u32[]{:S(2)}, u32[]{:S(2)}) %all-to-all-start.1) | async-done | bytes 524320 | tf_op jit(solution)/shard_map/all_to_all | solution.py:63
  95.7 7.4 %collective-permute-done.5 = bf16[16,2,8,512]{3,2,0,1:T(8,128)(2,1)S(1)} collective-permute-done((bf16[16,2,8,512]{3,2,0,1:T(8,128)(2,1)S(1)}, bf16[16,2,8,512]{3,2,0,1:T(8,128)(2,1)S(1)}, u32[]{:S(2)}, u32[]{:S(2)}) %collective-permute-start.5) | collective-permute-done | bytes 262176 | tf_op jit(solution)/shard_map/ppermute | solution.py:103
  105.3 16.9 %all-to-all-start.2 = ((bf16[32,2,2,8,1024]{4,3,1,2,0:T(8,128)(2,1)}), bf16[32,2,2,8,1024]{4,3,1,2,0:T(8,128)(2,1)S(1)}, u32[]{:S(2)}, u32[]{:S(2)}) async-start(bf16[32,2,2,8,1024]{4,3,1,2,0:T(8,128)(2,1)} %bitcast.54), calls=%async_computation.2 | async-start | bytes 4194304 | tf_op jit(solution)/shard_map/all_to_all | solution.py:63
  122.2 8.4 %collective-permute-start.4 = (bf16[16,2,8,512]{3,2,1,0:T(8,128)(2,1)}, bf16[16,2,8,512]{3,2,1,0:T(8,128)(2,1)S(1)}, u32[]{:S(2)}, u32[]{:S(2)}) collective-permute-start(bf16[16,2,8,512]{3,2,1,0:T(8,128)(2,1)} %get-tuple-element.10), channel_id=1, source_target_pairs={{0,0},{1,1},{32,48},{33,49},{64,66},{65,67},{96,114},{97,115},{128... | collective-permute-start | bytes 786440 | tf_op jit(solution)/shard_map/ppermute | solution.py:103
  132.0 16.6 %collective-permute-done.4 = bf16[16,2,8,512]{3,2,1,0:T(8,128)(2,1)S(1)} collective-permute-done((bf16[16,2,8,512]{3,2,1,0:T(8,128)(2,1)}, bf16[16,2,8,512]{3,2,1,0:T(8,128)(2,1)S(1)}, u32[]{:S(2)}, u32[]{:S(2)}) %collective-permute-start.4) | collective-permute-done | bytes 262176 | tf_op jit(solution)/shard_map/ppermute | solution.py:103
  148.8 9.8 %all-to-all-done.2 = bf16[32,2,2,8,1024]{4,3,1,2,0:T(8,128)(2,1)S(1)} async-done(((bf16[32,2,2,8,1024]{4,3,1,2,0:T(8,128)(2,1)}), bf16[32,2,2,8,1024]{4,3,1,2,0:T(8,128)(2,1)S(1)}, u32[]{:S(2)}, u32[]{:S(2)}) %all-to-all-start.2) | async-done | bytes 2097184 | tf_op jit(solution)/shard_map/all_to_all | solution.py:63
  162.2 3.9 %all-to-all-start.3 = ((bf16[32,2,2,2,1024]{4,3,1,2,0:T(2,128)(2,1)}), bf16[32,2,2,2,1024]{4,3,1,2,0:T(2,128)(2,1)S(1)}, u32[]{:S(2)}, u32[]{:S(2)}) async-start(bf16[32,2,2,2,1024]{4,3,1,2,0:T(2,128)(2,1)} %bitcast.47), calls=%async_computation.3 | async-start | bytes 1048576 | tf_op jit(solution)/shard_map/all_to_all | solution.py:63
  166.1 3.3 %fusion.11 = bf16[2,512,1024]{2,1,0:T(8,128)(2,1)S(1)} fusion(bf16[2,512,1024]{2,1,0:T(8,128)(2,1)} %bitcast.55, bf16[2,512,128]{2,1,0:T(8,128)(2,1)S(1)} %bitcast.65, bf16[2,128,1024]{2,1,0:T(8,128)(2,1)S(1)} %copy-done.5), kind=kOutput, calls=%fused_computation.17 | convolution fusion | flops 279969792 | bytes 4980736 | tf_op jit(solution)/shard_map/gmc,gct->gmt/dot_general | solution.py:143
  170.9 7.3 %all-to-all-done.3 = bf16[32,2,2,2,1024]{4,3,1,2,0:T(2,128)(2,1)S(1)} async-done(((bf16[32,2,2,2,1024]{4,3,1,2,0:T(2,128)(2,1)}), bf16[32,2,2,2,1024]{4,3,1,2,0:T(2,128)(2,1)S(1)}, u32[]{:S(2)}, u32[]{:S(2)}) %all-to-all-start.3) | async-done | bytes 524320 | tf_op jit(solution)/shard_map/all_to_all | solution.py:63
  178.1 4.7 %all-to-all-start.4 = ((bf16[32,2,2,8,1024]{4,3,1,2,0:T(8,128)(2,1)}), bf16[32,2,2,8,1024]{4,3,1,2,0:T(8,128)(2,1)}, u32[]{:S(2)}, u32[]{:S(2)}) async-start(bf16[32,2,2,8,1024]{4,3,1,2,0:T(8,128)(2,1)} %bitcast.52), calls=%async_computation.4 | async-start | bytes 4194304 | tf_op jit(solution)/shard_map/all_to_all | solution.py:63
  183.5 7.8 %collective-permute-start.6 = (bf16[256,1024]{1,0:T(8,128)(2,1)S(1)}, bf16[256,1024]{1,0:T(8,128)(2,1)S(1)}, u32[]{:S(2)}, u32[]{:S(2)}) collective-permute-start(bf16[256,1024]{1,0:T(8,128)(2,1)S(1)} %reshape.68), channel_id=1, source_target_pairs={{0,0},{1,1},{48,32},{49,33},{66,64},{67,65},{114,96},{115,97},{132... | collective-permute-start | bytes 1572872 | tf_op jit(solution)/shard_map/ppermute | solution.py:81
  193.2 6.2 %collective-permute-start.10 = (bf16[16,2,8,512]{3,2,1,0:T(8,128)(2,1)S(1)}, bf16[16,2,8,512]{3,2,1,0:T(8,128)(2,1)S(1)}, u32[]{:S(2)}, u32[]{:S(2)}) collective-permute-start(bf16[16,2,8,512]{3,2,1,0:T(8,128)(2,1)S(1)} %bitcast.67), channel_id=1, source_target_pairs={{0,0},{1,1},{48,32},{49,33},{66,64},{67,65},{114,96},{115,97},{132... | collective-permute-start | bytes 786440 | tf_op jit(solution)/shard_map/ppermute | solution.py:115
  199.4 16.4 %all-to-all-done.4 = bf16[32,2,2,8,1024]{4,3,1,2,0:T(8,128)(2,1)} async-done(((bf16[32,2,2,8,1024]{4,3,1,2,0:T(8,128)(2,1)}), bf16[32,2,2,8,1024]{4,3,1,2,0:T(8,128)(2,1)}, u32[]{:S(2)}, u32[]{:S(2)}) %all-to-all-start.4) | async-done | bytes 2097184 | tf_op jit(solution)/shard_map/all_to_all | solution.py:63
  218.1 14.8 %collective-permute-done.6 = bf16[256,1024]{1,0:T(8,128)(2,1)S(1)} collective-permute-done((bf16[256,1024]{1,0:T(8,128)(2,1)S(1)}, bf16[256,1024]{1,0:T(8,128)(2,1)S(1)}, u32[]{:S(2)}, u32[]{:S(2)}) %collective-permute-start.6) | collective-permute-done | bytes 524320 | tf_op jit(solution)/shard_map/ppermute | solution.py:81
  233.8 2.5 collective-permute-start.9
  237.0 13.1 %collective-permute-start.8 = (bf16[256,1024]{1,0:T(8,128)(2,1)S(1)}, bf16[256,1024]{1,0:T(8,128)(2,1)S(1)}, u32[]{:S(2)}, u32[]{:S(2)}) collective-permute-start(bf16[256,1024]{1,0:T(8,128)(2,1)S(1)} %bitcast.66), channel_id=1, source_target_pairs={{0,0},{1,1},{48,32},{49,33},{66,64},{67,65},{114,96},{115,97},{132... | collective-permute-start | bytes 1572872 | tf_op jit(solution)/shard_map/ppermute | solution.py:89
  250.1 17.6 %collective-permute-done.9 = bf16[16,2,8,512]{3,2,1,0:T(8,128)(2,1)S(1)} collective-permute-done((bf16[16,2,8,512]{3,2,1,0:T(8,128)(2,1)S(1)}, bf16[16,2,8,512]{3,2,1,0:T(8,128)(2,1)S(1)}, u32[]{:S(2)}, u32[]{:S(2)}) %collective-permute-start.9) | collective-permute-done | bytes 262176 | tf_op jit(solution)/shard_map/ppermute | solution.py:114
  268.5 3.5 %all-to-all-start.5 = ((bf16[16,4,8,512]{3,2,1,0:T(8,128)(2,1)}), bf16[16,4,8,512]{3,2,1,0:T(8,128)(2,1)S(1)}, u32[]{:S(2)}, u32[]{:S(2)}) async-start(bf16[16,4,8,512]{3,2,1,0:T(8,128)(2,1)} %pad_maximum_fusion), calls=%async_computation.5 | async-start | bytes 1048576 | tf_op jit(solution)/shard_map/all_to_all | solution.py:117
  272.0 5.3 %collective-permute-done.8 = bf16[256,1024]{1,0:T(8,128)(2,1)S(1)} collective-permute-done((bf16[256,1024]{1,0:T(8,128)(2,1)S(1)}, bf16[256,1024]{1,0:T(8,128)(2,1)S(1)}, u32[]{:S(2)}, u32[]{:S(2)}) %collective-permute-start.8) | collective-permute-done | bytes 524320 | tf_op jit(solution)/shard_map/ppermute | solution.py:89
  277.3 4.3 %all-to-all-done.5 = bf16[16,4,8,512]{3,2,1,0:T(8,128)(2,1)S(1)} async-done(((bf16[16,4,8,512]{3,2,1,0:T(8,128)(2,1)}), bf16[16,4,8,512]{3,2,1,0:T(8,128)(2,1)S(1)}, u32[]{:S(2)}, u32[]{:S(2)}) %all-to-all-start.5) | async-done | bytes 524320 | tf_op jit(solution)/shard_map/all_to_all | solution.py:117
  (57 shorter events, 31.2 us)
Async XLA Ops:
  0.6 4.1 %collective-permute-start.1 = (bf16[256,1024]{1,0:T(8,128)(2,1)}, bf16[256,1024]{1,0:T(8,128)(2,1)S(1)}, u32[]{:S(2)}, u32[]{:S(2)}) collective-permute-start(bf16[256,1024]{1,0:T(8,128)(2,1)} %param.7), channel_id=1, source_target_pairs={{0,0},{1,1},{32,32},{33,33},{64,64},{65,65},{96,96},{97,97},{128,1... | collective-permute-start | bytes 1572872 | tf_op jit(solution)/shard_map/ppermute | solution.py:73
  2.3 40.3 %collective-permute-start = (bf16[256,1024]{1,0:T(8,128)(2,1)}, bf16[256,1024]{1,0:T(8,128)(2,1)S(1)}, u32[]{:S(2)}, u32[]{:S(2)}) collective-permute-start(bf16[256,1024]{1,0:T(8,128)(2,1)} %param.4), channel_id=1, source_target_pairs={{0,0},{1,1},{32,32},{33,33},{64,64},{65,65},{96,96},{97,97},{128,1... | collective-permute-start | bytes 1572872 | tf_op jit(solution)/shard_map/ppermute | solution.py:73
  4.8 37.9 %collective-permute-start.2 = (bf16[256,1024]{1,0:T(8,128)(2,1)S(1)}, bf16[256,1024]{1,0:T(8,128)(2,1)S(1)}, u32[]{:S(2)}, u32[]{:S(2)}) collective-permute-start(bf16[256,1024]{1,0:T(8,128)(2,1)S(1)} %collective-permute-done.1), channel_id=1, source_target_pairs={{0,0},{1,1},{32,48},{33,49},{64,66},{65,67},{96,114},{97,115},{128... | collective-permute-start | bytes 1572872 | tf_op jit(solution)/shard_map/ppermute | solution.py:77
  23.8 30.2 %all-to-all-start = ((bf16[16,4,8,512]{3,2,1,0:T(8,128)(2,1)}), bf16[16,4,8,512]{3,2,1,0:T(8,128)(2,1)S(1)}, u32[]{:S(2)}, u32[]{:S(2)}) async-start(bf16[16,4,8,512]{3,2,1,0:T(8,128)(2,1)} %broadcast_in_dim.3), calls=%async_computation | async-start | bytes 1048576 | tf_op jit(solution)/shard_map/all_to_all | solution.py:97
  42.7 53.0 %collective-permute-start.3 = (bf16[256,1024]{1,0:T(8,128)(2,1)S(1)}, bf16[256,1024]{1,0:T(8,128)(2,1)S(1)}, u32[]{:S(2)}, u32[]{:S(2)}) collective-permute-start(bf16[256,1024]{1,0:T(8,128)(2,1)S(1)} %collective-permute-done), channel_id=1, source_target_pairs={{0,0},{1,1},{32,48},{33,49},{64,66},{65,67},{96,114},{97,115},{128... | collective-permute-start | bytes 1572872 | tf_op jit(solution)/shard_map/ppermute | solution.py:77
  53.9 41.8 %all-to-all-start.1 = ((bf16[32,2,2,2,1024]{4,3,2,1,0:T(2,128)(2,1)}), bf16[32,2,2,2,1024]{4,3,2,1,0:T(2,128)(2,1)S(1)}, u32[]{:S(2)}, u32[]{:S(2)}) async-start(bf16[32,2,2,2,1024]{4,3,2,1,0:T(2,128)(2,1)} %copy.37), calls=%async_computation.1 | async-start | bytes 1048576 | tf_op jit(solution)/shard_map/all_to_all | solution.py:63
  84.5 18.6 %collective-permute-start.5 = (bf16[16,2,8,512]{3,2,0,1:T(8,128)(2,1)S(1)}, bf16[16,2,8,512]{3,2,0,1:T(8,128)(2,1)S(1)}, u32[]{:S(2)}, u32[]{:S(2)}) collective-permute-start(bf16[16,2,8,512]{3,2,0,1:T(8,128)(2,1)S(1)} %copy.51), channel_id=1, source_target_pairs={{0,0},{1,1},{32,48},{33,49},{64,66},{65,67},{96,114},{97,115},{128... | collective-permute-start | bytes 786440 | tf_op jit(solution)/shard_map/ppermute | solution.py:103
  95.7 9.6 %copy-start.1 = (bf16[256,1024]{1,0:T(8,128)(2,1)}, bf16[256,1024]{1,0:T(8,128)(2,1)S(1)}, u32[]{:S(2)}) copy-start(bf16[256,1024]{1,0:T(8,128)(2,1)S(1)} %collective-permute-done.3) | copy-start | bytes 1572868
  103.1 2.3 copy-start.3
  105.3 53.3 %all-to-all-start.2 = ((bf16[32,2,2,8,1024]{4,3,1,2,0:T(8,128)(2,1)}), bf16[32,2,2,8,1024]{4,3,1,2,0:T(8,128)(2,1)S(1)}, u32[]{:S(2)}, u32[]{:S(2)}) async-start(bf16[32,2,2,8,1024]{4,3,1,2,0:T(8,128)(2,1)} %bitcast.54), calls=%async_computation.2 | async-start | bytes 4194304 | tf_op jit(solution)/shard_map/all_to_all | solution.py:63
  122.2 26.4 %collective-permute-start.4 = (bf16[16,2,8,512]{3,2,1,0:T(8,128)(2,1)}, bf16[16,2,8,512]{3,2,1,0:T(8,128)(2,1)S(1)}, u32[]{:S(2)}, u32[]{:S(2)}) collective-permute-start(bf16[16,2,8,512]{3,2,1,0:T(8,128)(2,1)} %get-tuple-element.10), channel_id=1, source_target_pairs={{0,0},{1,1},{32,48},{33,49},{64,66},{65,67},{96,114},{97,115},{128... | collective-permute-start | bytes 786440 | tf_op jit(solution)/shard_map/ppermute | solution.py:103
  158.8 1.3 copy-start
  160.8 5.3 %copy-start.5 = (bf16[2,128,1024]{2,1,0:T(8,128)(2,1)S(1)}, bf16[2,128,1024]{2,1,0:T(8,128)(2,1)}, u32[]{:S(2)}) copy-start(bf16[2,128,1024]{2,1,0:T(8,128)(2,1)} %reshape.69) | copy-start | bytes 1572868
  162.2 15.9 %all-to-all-start.3 = ((bf16[32,2,2,2,1024]{4,3,1,2,0:T(2,128)(2,1)}), bf16[32,2,2,2,1024]{4,3,1,2,0:T(2,128)(2,1)S(1)}, u32[]{:S(2)}, u32[]{:S(2)}) async-start(bf16[32,2,2,2,1024]{4,3,1,2,0:T(2,128)(2,1)} %bitcast.47), calls=%async_computation.3 | async-start | bytes 1048576 | tf_op jit(solution)/shard_map/all_to_all | solution.py:63
  178.1 37.7 %all-to-all-start.4 = ((bf16[32,2,2,8,1024]{4,3,1,2,0:T(8,128)(2,1)}), bf16[32,2,2,8,1024]{4,3,1,2,0:T(8,128)(2,1)}, u32[]{:S(2)}, u32[]{:S(2)}) async-start(bf16[32,2,2,8,1024]{4,3,1,2,0:T(8,128)(2,1)} %bitcast.52), calls=%async_computation.4 | async-start | bytes 4194304 | tf_op jit(solution)/shard_map/all_to_all | solution.py:63
  183.5 49.4 %collective-permute-start.6 = (bf16[256,1024]{1,0:T(8,128)(2,1)S(1)}, bf16[256,1024]{1,0:T(8,128)(2,1)S(1)}, u32[]{:S(2)}, u32[]{:S(2)}) collective-permute-start(bf16[256,1024]{1,0:T(8,128)(2,1)S(1)} %reshape.68), channel_id=1, source_target_pairs={{0,0},{1,1},{48,32},{49,33},{66,64},{67,65},{114,96},{115,97},{132... | collective-permute-start | bytes 1572872 | tf_op jit(solution)/shard_map/ppermute | solution.py:81
  193.2 56.9 %collective-permute-start.10 = (bf16[16,2,8,512]{3,2,1,0:T(8,128)(2,1)S(1)}, bf16[16,2,8,512]{3,2,1,0:T(8,128)(2,1)S(1)}, u32[]{:S(2)}, u32[]{:S(2)}) collective-permute-start(bf16[16,2,8,512]{3,2,1,0:T(8,128)(2,1)S(1)} %bitcast.67), channel_id=1, source_target_pairs={{0,0},{1,1},{48,32},{49,33},{66,64},{67,65},{114,96},{115,97},{132... | collective-permute-start | bytes 786440 | tf_op jit(solution)/shard_map/ppermute | solution.py:115
  215.8 1.8 copy-start.4
  217.6 15.3 %copy-start.2 = (bf16[256,1024]{1,0:T(8,128)(2,1)S(1)}, bf16[256,1024]{1,0:T(8,128)(2,1)}, u32[]{:S(2)}) copy-start(bf16[256,1024]{1,0:T(8,128)(2,1)} %copy-done.1) | copy-start | bytes 1572868
  233.8 33.9 %collective-permute-start.9 = (bf16[16,2,8,512]{3,2,1,0:T(8,128)(2,1)S(1)}, bf16[16,2,8,512]{3,2,1,0:T(8,128)(2,1)S(1)}, u32[]{:S(2)}, u32[]{:S(2)}) collective-permute-start(bf16[16,2,8,512]{3,2,1,0:T(8,128)(2,1)S(1)} %bitcast.68), channel_id=1, source_target_pairs={{0,0},{1,1},{48,32},{49,33},{66,64},{67,65},{114,96},{115,97},{132... | collective-permute-start | bytes 786440 | tf_op jit(solution)/shard_map/ppermute | solution.py:114
  236.3 35.7 %collective-permute-start.7 = (bf16[256,1024]{1,0:T(8,128)(2,1)S(1)}, bf16[256,1024]{1,0:T(8,128)(2,1)S(1)}, u32[]{:S(2)}, u32[]{:S(2)}) collective-permute-start(bf16[256,1024]{1,0:T(8,128)(2,1)S(1)} %collective-permute-done.6), channel_id=1, source_target_pairs={{0,0},{1,1},{32,32},{33,33},{64,64},{65,65},{96,96},{97,97},{128,1... | collective-permute-start | bytes 1572872 | tf_op jit(solution)/shard_map/ppermute | solution.py:85
  237.0 40.4 %collective-permute-start.8 = (bf16[256,1024]{1,0:T(8,128)(2,1)S(1)}, bf16[256,1024]{1,0:T(8,128)(2,1)S(1)}, u32[]{:S(2)}, u32[]{:S(2)}) collective-permute-start(bf16[256,1024]{1,0:T(8,128)(2,1)S(1)} %bitcast.66), channel_id=1, source_target_pairs={{0,0},{1,1},{48,32},{49,33},{66,64},{67,65},{114,96},{115,97},{132... | collective-permute-start | bytes 1572872 | tf_op jit(solution)/shard_map/ppermute | solution.py:89
  268.5 13.1 %all-to-all-start.5 = ((bf16[16,4,8,512]{3,2,1,0:T(8,128)(2,1)}), bf16[16,4,8,512]{3,2,1,0:T(8,128)(2,1)S(1)}, u32[]{:S(2)}, u32[]{:S(2)}) async-start(bf16[16,4,8,512]{3,2,1,0:T(8,128)(2,1)} %pad_maximum_fusion), calls=%async_computation.5 | async-start | bytes 1048576 | tf_op jit(solution)/shard_map/all_to_all | solution.py:117

commit v14 on v13

--- a/solution.py
+++ b/solution.py
@@ -145,11 +145,12 @@
     dperm = dperm.reshape(nb, n, nb, J_UP, t).transpose(1, 2, 0, 3, 4)
     dpre = exchange(after(dperm, mixed))
     mixed = unmirror(mixed.transpose(1, 0, 2, 3, 4).reshape(nb * BIN, t))
-    down_term = jnp.einsum("gmt,gct->gmc", act, dblock, preferred_element_type=F32)
+    down_term = jnp.einsum("gmt,gct->gmc", act, dblock, preferred_element_type=F32).astype(BF16)
+    down_term = after(down_term, mixed)
     dpre = dpre.transpose(1, 0, 2, 3, 4).reshape(nb, BOUT, t)
     fgrad = jnp.einsum("bkn,bnt->bkt", up, dpre, preferred_element_type=F32).astype(BF16)
     fgrad = fgrad.reshape(nb * BIN, t)
-    dpre = after(dpre, fgrad, mixed)
+    dpre = after(dpre, fgrad)
     up_term = jnp.einsum("bkt,bnt->bkn", x, dpre, preferred_element_type=F32)
     up_grad, down_grad = sum_rows(up_term, down_term)
     return unshuffle(mixed), to_store(fgrad), up_grad, down_grad

time: 290 us -> 296 us (1.021)
  the two profiles are of different devices: /device:TPU:1 before, /device:TPU:64 now
where the time goes in v14:
time: 296 us; the launch traced here: 295 us
  starting transfers between devices  179 us (60%)
  waiting for transfers between devices  88.3 us (30%)
  local copies, waits for them, and re-layouts  16.4 us (6%)
  matrix products  7.55 us (3%)
    all_to_all x4, starting transfers between devices, exchange(): lax.all_to_all(x, DEVICES, split_axis=0, concat_axis=0, tiled=True, axis_...  53.8 us
    all_to_all x1, starting transfers between devices, sum_rows(): got = lax.all_to_all(both, 'dp', split_axis=0, concat_axis=0, tiled=True)  45.6 us
    all_to_all x4, waiting for transfers between devices, exchange(): lax.all_to_all(x, DEVICES, split_axis=0, concat_axis=0, tiled=True, axis_...  23.9 us
    ppermute x2, starting transfers between devices, whole(): rows = lax.ppermute(rows, DEVICES, PLAN.weights)  17.8 us
    ppermute x1, waiting for transfers between devices, unmirror(): return lax.ppermute(x, DEVICES, back(PLAN.mirror))  16.8 us
    ppermute x2, waiting for transfers between devices, mirror(): return lax.ppermute(x, DEVICES, PLAN.mirror)  13.3 us
    ppermute x2, starting transfers between devices, mirror(): return lax.ppermute(x, DEVICES, PLAN.mirror)  12.7 us
    ppermute x2, waiting for transfers between devices, whole(): rows = lax.ppermute(rows, DEVICES, PLAN.weights)  12.6 us
  transfers between devices with their start and end apart: 17, of which 9 were waited for; matrix products, arithmetic and copies ran while one was open for 6% of the time, Pallas kernels for 0%

profile of v14, /device:TPU:64, one launch (start us, length us, event | category | flops | bytes accessed | tf_op | source)
XLA Modules:
  0.0 295.1 jit_solution(9360895398143570648)
XLA Ops:
  0.6 5.1 %collective-permute-start.1 = (bf16[256,1024]{1,0:T(8,128)(2,1)}, bf16[256,1024]{1,0:T(8,128)(2,1)S(1)}, u32[]{:S(2)}, u32[]{:S(2)}) collective-permute-start(bf16[256,1024]{1,0:T(8,128)(2,1)} %param.7), channel_id=1, source_target_pairs={{0,0},{1,1},{32,32},{33,33},{64,64},{65,65},{96,96},{97,97},{128,1... | collective-permute-start | bytes 1572872 | tf_op jit(solution)/shard_map/ppermute | solution.py:73
  5.7 4.4 %collective-permute-start = (bf16[256,1024]{1,0:T(8,128)(2,1)}, bf16[256,1024]{1,0:T(8,128)(2,1)S(1)}, u32[]{:S(2)}, u32[]{:S(2)}) collective-permute-start(bf16[256,1024]{1,0:T(8,128)(2,1)} %param.4), channel_id=1, source_target_pairs={{0,0},{1,1},{32,32},{33,33},{64,64},{65,65},{96,96},{97,97},{128,1... | collective-permute-start | bytes 1572872 | tf_op jit(solution)/shard_map/ppermute | solution.py:73
  10.9 9.3 %collective-permute-done.1 = bf16[256,1024]{1,0:T(8,128)(2,1)S(1)} collective-permute-done((bf16[256,1024]{1,0:T(8,128)(2,1)}, bf16[256,1024]{1,0:T(8,128)(2,1)S(1)}, u32[]{:S(2)}, u32[]{:S(2)}) %collective-permute-start.1) | collective-permute-done | bytes 524320 | tf_op jit(solution)/shard_map/ppermute | solution.py:73
  20.2 10.7 %collective-permute-start.2 = (bf16[256,1024]{1,0:T(8,128)(2,1)S(1)}, bf16[256,1024]{1,0:T(8,128)(2,1)S(1)}, u32[]{:S(2)}, u32[]{:S(2)}) collective-permute-start(bf16[256,1024]{1,0:T(8,128)(2,1)S(1)} %collective-permute-done.1), channel_id=1, source_target_pairs={{0,0},{1,1},{32,48},{33,49},{64,66},{65,67},{96,114},{97,115},{128... | collective-permute-start | bytes 1572872 | tf_op jit(solution)/shard_map/ppermute | solution.py:77
  32.5 6.2 %all-to-all-start = ((bf16[16,4,8,512]{3,2,1,0:T(8,128)(2,1)}), bf16[16,4,8,512]{3,2,1,0:T(8,128)(2,1)S(1)}, u32[]{:S(2)}, u32[]{:S(2)}) async-start(bf16[16,4,8,512]{3,2,1,0:T(8,128)(2,1)} %broadcast_in_dim.3), calls=%async_computation | async-start | bytes 1048576 | tf_op jit(solution)/shard_map/all_to_all | solution.py:97
  38.7 13.3 %collective-permute-done.2 = bf16[256,1024]{1,0:T(8,128)(2,1)S(1)} collective-permute-done((bf16[256,1024]{1,0:T(8,128)(2,1)S(1)}, bf16[256,1024]{1,0:T(8,128)(2,1)S(1)}, u32[]{:S(2)}, u32[]{:S(2)}) %collective-permute-start.2) | collective-permute-done | bytes 524320 | tf_op jit(solution)/shard_map/ppermute | solution.py:77
  55.6 15.7 %all-to-all-start.1 = ((bf16[32,2,2,2,1024]{4,3,2,1,0:T(2,128)(2,1)}), bf16[32,2,2,2,1024]{4,3,2,1,0:T(2,128)(2,1)S(1)}, u32[]{:S(2)}, u32[]{:S(2)}) async-start(bf16[32,2,2,2,1024]{4,3,2,1,0:T(2,128)(2,1)} %copy.37), calls=%async_computation.1 | async-start | bytes 1048576 | tf_op jit(solution)/shard_map/all_to_all | solution.py:63
  72.0 10.6 %collective-permute-start.5 = (bf16[16,2,8,512]{3,2,0,1:T(8,128)(2,1)S(1)}, bf16[16,2,8,512]{3,2,0,1:T(8,128)(2,1)S(1)}, u32[]{:S(2)}, u32[]{:S(2)}) collective-permute-start(bf16[16,2,8,512]{3,2,0,1:T(8,128)(2,1)S(1)} %copy.51), channel_id=1, source_target_pairs={{0,0},{1,1},{32,48},{33,49},{64,66},{65,67},{96,114},{97,115},{128... | collective-permute-start | bytes 786440 | tf_op jit(solution)/shard_map/ppermute | solution.py:103
  82.7 5.7 %collective-permute-done.5 = bf16[16,2,8,512]{3,2,0,1:T(8,128)(2,1)S(1)} collective-permute-done((bf16[16,2,8,512]{3,2,0,1:T(8,128)(2,1)S(1)}, bf16[16,2,8,512]{3,2,0,1:T(8,128)(2,1)S(1)}, u32[]{:S(2)}, u32[]{:S(2)}) %collective-permute-start.5) | collective-permute-done | bytes 262176 | tf_op jit(solution)/shard_map/ppermute | solution.py:103
  90.7 24.8 %all-to-all-start.2 = ((bf16[32,2,2,8,1024]{4,3,1,2,0:T(8,128)(2,1)}), bf16[32,2,2,8,1024]{4,3,1,2,0:T(8,128)(2,1)S(1)}, u32[]{:S(2)}, u32[]{:S(2)}) async-start(bf16[32,2,2,8,1024]{4,3,1,2,0:T(8,128)(2,1)} %bitcast.54), calls=%async_computation.2 | async-start | bytes 4194304 | tf_op jit(solution)/shard_map/all_to_all | solution.py:63
  115.5 7.1 %collective-permute-start.4 = (bf16[16,2,8,512]{3,2,1,0:T(8,128)(2,1)}, bf16[16,2,8,512]{3,2,1,0:T(8,128)(2,1)S(1)}, u32[]{:S(2)}, u32[]{:S(2)}) collective-permute-start(bf16[16,2,8,512]{3,2,1,0:T(8,128)(2,1)} %get-tuple-element.11), channel_id=1, source_target_pairs={{0,0},{1,1},{32,48},{33,49},{64,66},{65,67},{96,114},{97,115},{128... | collective-permute-start | bytes 786440 | tf_op jit(solution)/shard_map/ppermute | solution.py:103
  124.0 6.9 %collective-permute-done.4 = bf16[16,2,8,512]{3,2,1,0:T(8,128)(2,1)S(1)} collective-permute-done((bf16[16,2,8,512]{3,2,1,0:T(8,128)(2,1)}, bf16[16,2,8,512]{3,2,1,0:T(8,128)(2,1)S(1)}, u32[]{:S(2)}, u32[]{:S(2)}) %collective-permute-start.4) | collective-permute-done | bytes 262176 | tf_op jit(solution)/shard_map/ppermute | solution.py:103
  131.2 16.8 %all-to-all-done.2 = bf16[32,2,2,8,1024]{4,3,1,2,0:T(8,128)(2,1)S(1)} async-done(((bf16[32,2,2,8,1024]{4,3,1,2,0:T(8,128)(2,1)}), bf16[32,2,2,8,1024]{4,3,1,2,0:T(8,128)(2,1)S(1)}, u32[]{:S(2)}, u32[]{:S(2)}) %all-to-all-start.2) | async-done | bytes 2097184 | tf_op jit(solution)/shard_map/all_to_all | solution.py:63
  151.5 6.5 %all-to-all-start.3 = ((bf16[32,2,2,2,1024]{4,3,1,2,0:T(2,128)(2,1)}), bf16[32,2,2,2,1024]{4,3,1,2,0:T(2,128)(2,1)S(1)}, u32[]{:S(2)}, u32[]{:S(2)}) async-start(bf16[32,2,2,2,1024]{4,3,1,2,0:T(2,128)(2,1)} %bitcast.47), calls=%async_computation.3 | async-start | bytes 1048576 | tf_op jit(solution)/shard_map/all_to_all | solution.py:63
  158.1 3.3 %fusion.11 = bf16[2,512,1024]{2,1,0:T(8,128)(2,1)S(1)} fusion(bf16[2,512,1024]{2,1,0:T(8,128)(2,1)} %bitcast.55, bf16[2,512,128]{2,1,0:T(8,128)(2,1)S(1)} %bitcast.65, bf16[2,128,1024]{2,1,0:T(8,128)(2,1)S(1)} %copy-done.5), kind=kOutput, calls=%fused_computation.17 | convolution fusion | flops 279969792 | bytes 4980736 | tf_op jit(solution)/shard_map/gmc,gct->gmt/dot_general | solution.py:143
  162.8 4.4 %all-to-all-done.3 = bf16[32,2,2,2,1024]{4,3,1,2,0:T(2,128)(2,1)S(1)} async-done(((bf16[32,2,2,2,1024]{4,3,1,2,0:T(2,128)(2,1)}), bf16[32,2,2,2,1024]{4,3,1,2,0:T(2,128)(2,1)S(1)}, u32[]{:S(2)}, u32[]{:S(2)}) %all-to-all-start.3) | async-done | bytes 524320 | tf_op jit(solution)/shard_map/all_to_all | solution.py:63
  167.2 6.7 %all-to-all-start.4 = ((bf16[32,2,2,8,1024]{4,3,1,2,0:T(8,128)(2,1)}), bf16[32,2,2,8,1024]{4,3,1,2,0:T(8,128)(2,1)}, u32[]{:S(2)}, u32[]{:S(2)}) async-start(bf16[32,2,2,8,1024]{4,3,1,2,0:T(8,128)(2,1)} %bitcast.52), calls=%async_computation.4 | async-start | bytes 4194304 | tf_op jit(solution)/shard_map/all_to_all | solution.py:63
  174.5 6.2 %collective-permute-start.6 = (bf16[256,1024]{1,0:T(8,128)(2,1)S(1)}, bf16[256,1024]{1,0:T(8,128)(2,1)S(1)}, u32[]{:S(2)}, u32[]{:S(2)}) collective-permute-start(bf16[256,1024]{1,0:T(8,128)(2,1)S(1)} %reshape.68), channel_id=1, source_target_pairs={{0,0},{1,1},{48,32},{49,33},{66,64},{67,65},{114,96},{115,97},{132... | collective-permute-start | bytes 1572872 | tf_op jit(solution)/shard_map/ppermute | solution.py:81
  182.5 16.8 %collective-permute-done.6 = bf16[256,1024]{1,0:T(8,128)(2,1)S(1)} collective-permute-done((bf16[256,1024]{1,0:T(8,128)(2,1)S(1)}, bf16[256,1024]{1,0:T(8,128)(2,1)S(1)}, u32[]{:S(2)}, u32[]{:S(2)}) %collective-permute-start.6) | collective-permute-done | bytes 524320 | tf_op jit(solution)/shard_map/ppermute | solution.py:81
  207.8 6.0 %collective-permute-start.9 = (bf16[16,2,8,512]{3,2,1,0:T(8,128)(2,1)S(1)}, bf16[16,2,8,512]{3,2,1,0:T(8,128)(2,1)S(1)}, u32[]{:S(2)}, u32[]{:S(2)}) collective-permute-start(bf16[16,2,8,512]{3,2,1,0:T(8,128)(2,1)S(1)} %bitcast.68), channel_id=1, source_target_pairs={{0,0},{1,1},{48,32},{49,33},{66,64},{67,65},{114,96},{115,97},{132... | collective-permute-start | bytes 786440 | tf_op jit(solution)/shard_map/ppermute | solution.py:114
  213.9 11.4 %collective-permute-start.7 = (bf16[256,1024]{1,0:T(8,128)(2,1)S(1)}, bf16[256,1024]{1,0:T(8,128)(2,1)S(1)}, u32[]{:S(2)}, u32[]{:S(2)}) collective-permute-start(bf16[256,1024]{1,0:T(8,128)(2,1)S(1)} %collective-permute-done.6), channel_id=1, source_target_pairs={{0,0},{1,1},{32,32},{33,33},{64,64},{65,65},{96,96},{97,97},{128,1... | collective-permute-start | bytes 1572872 | tf_op jit(solution)/shard_map/ppermute | solution.py:85
  225.3 8.1 %collective-permute-start.8 = (bf16[256,1024]{1,0:T(8,128)(2,1)S(1)}, bf16[256,1024]{1,0:T(8,128)(2,1)S(1)}, u32[]{:S(2)}, u32[]{:S(2)}) collective-permute-start(bf16[256,1024]{1,0:T(8,128)(2,1)S(1)} %bitcast.66), channel_id=1, source_target_pairs={{0,0},{1,1},{48,32},{49,33},{66,64},{67,65},{114,96},{115,97},{132... | collective-permute-start | bytes 1572872 | tf_op jit(solution)/shard_map/ppermute | solution.py:89
  234.3 45.6 %all-to-all-start.5 = ((bf16[16,4,8,512]{3,2,1,0:T(8,128)(2,1)}), bf16[16,4,8,512]{3,2,1,0:T(8,128)(2,1)S(1)}, u32[]{:S(2)}, u32[]{:S(2)}) async-start(bf16[16,4,8,512]{3,2,1,0:T(8,128)(2,1)} %pad_maximum_fusion), calls=%async_computation.5 | async-start | bytes 1048576 | tf_op jit(solution)/shard_map/all_to_all | solution.py:117
  279.9 12.3 %all-to-all-done.5 = bf16[16,4,8,512]{3,2,1,0:T(8,128)(2,1)S(1)} async-done(((bf16[16,4,8,512]{3,2,1,0:T(8,128)(2,1)}), bf16[16,4,8,512]{3,2,1,0:T(8,128)(2,1)S(1)}, u32[]{:S(2)}, u32[]{:S(2)}) %all-to-all-start.5) | async-done | bytes 524320 | tf_op jit(solution)/shard_map/all_to_all | solution.py:117
  (57 shorter events, 30.0 us)
Async XLA Ops:
  0.6 19.6 %collective-permute-start.1 = (bf16[256,1024]{1,0:T(8,128)(2,1)}, bf16[256,1024]{1,0:T(8,128)(2,1)S(1)}, u32[]{:S(2)}, u32[]{:S(2)}) collective-permute-start(bf16[256,1024]{1,0:T(8,128)(2,1)} %param.7), channel_id=1, source_target_pairs={{0,0},{1,1},{32,32},{33,33},{64,64},{65,65},{96,96},{97,97},{128,1... | collective-permute-start | bytes 1572872 | tf_op jit(solution)/shard_map/ppermute | solution.py:73
  5.7 33.0 %collective-permute-start = (bf16[256,1024]{1,0:T(8,128)(2,1)}, bf16[256,1024]{1,0:T(8,128)(2,1)S(1)}, u32[]{:S(2)}, u32[]{:S(2)}) collective-permute-start(bf16[256,1024]{1,0:T(8,128)(2,1)} %param.4), channel_id=1, source_target_pairs={{0,0},{1,1},{32,32},{33,33},{64,64},{65,65},{96,96},{97,97},{128,1... | collective-permute-start | bytes 1572872 | tf_op jit(solution)/shard_map/ppermute | solution.py:73
  20.2 31.8 %collective-permute-start.2 = (bf16[256,1024]{1,0:T(8,128)(2,1)S(1)}, bf16[256,1024]{1,0:T(8,128)(2,1)S(1)}, u32[]{:S(2)}, u32[]{:S(2)}) collective-permute-start(bf16[256,1024]{1,0:T(8,128)(2,1)S(1)} %collective-permute-done.1), channel_id=1, source_target_pairs={{0,0},{1,1},{32,48},{33,49},{64,66},{65,67},{96,114},{97,115},{128... | collective-permute-start | bytes 1572872 | tf_op jit(solution)/shard_map/ppermute | solution.py:77
  32.5 23.1 %all-to-all-start = ((bf16[16,4,8,512]{3,2,1,0:T(8,128)(2,1)}), bf16[16,4,8,512]{3,2,1,0:T(8,128)(2,1)S(1)}, u32[]{:S(2)}, u32[]{:S(2)}) async-start(bf16[16,4,8,512]{3,2,1,0:T(8,128)(2,1)} %broadcast_in_dim.3), calls=%async_computation | async-start | bytes 1048576 | tf_op jit(solution)/shard_map/all_to_all | solution.py:97
  52.0 30.6 %collective-permute-start.3 = (bf16[256,1024]{1,0:T(8,128)(2,1)S(1)}, bf16[256,1024]{1,0:T(8,128)(2,1)S(1)}, u32[]{:S(2)}, u32[]{:S(2)}) collective-permute-start(bf16[256,1024]{1,0:T(8,128)(2,1)S(1)} %collective-permute-done), channel_id=1, source_target_pairs={{0,0},{1,1},{32,48},{33,49},{64,66},{65,67},{96,114},{97,115},{128... | collective-permute-start | bytes 1572872 | tf_op jit(solution)/shard_map/ppermute | solution.py:77
  55.6 27.1 %all-to-all-start.1 = ((bf16[32,2,2,2,1024]{4,3,2,1,0:T(2,128)(2,1)}), bf16[32,2,2,2,1024]{4,3,2,1,0:T(2,128)(2,1)S(1)}, u32[]{:S(2)}, u32[]{:S(2)}) async-start(bf16[32,2,2,2,1024]{4,3,2,1,0:T(2,128)(2,1)} %copy.37), calls=%async_computation.1 | async-start | bytes 1048576 | tf_op jit(solution)/shard_map/all_to_all | solution.py:63
  72.0 16.4 %collective-permute-start.5 = (bf16[16,2,8,512]{3,2,0,1:T(8,128)(2,1)S(1)}, bf16[16,2,8,512]{3,2,0,1:T(8,128)(2,1)S(1)}, u32[]{:S(2)}, u32[]{:S(2)}) collective-permute-start(bf16[16,2,8,512]{3,2,0,1:T(8,128)(2,1)S(1)} %copy.51), channel_id=1, source_target_pairs={{0,0},{1,1},{32,48},{33,49},{64,66},{65,67},{96,114},{97,115},{128... | collective-permute-start | bytes 786440 | tf_op jit(solution)/shard_map/ppermute | solution.py:103
  82.7 8.0 %copy-start.1 = (bf16[256,1024]{1,0:T(8,128)(2,1)}, bf16[256,1024]{1,0:T(8,128)(2,1)S(1)}, u32[]{:S(2)}) copy-start(bf16[256,1024]{1,0:T(8,128)(2,1)S(1)} %collective-permute-done.3) | copy-start | bytes 1572868
  88.4 2.3 copy-start.3
  90.7 57.2 %all-to-all-start.2 = ((bf16[32,2,2,8,1024]{4,3,1,2,0:T(8,128)(2,1)}), bf16[32,2,2,8,1024]{4,3,1,2,0:T(8,128)(2,1)S(1)}, u32[]{:S(2)}, u32[]{:S(2)}) async-start(bf16[32,2,2,8,1024]{4,3,1,2,0:T(8,128)(2,1)} %bitcast.54), calls=%async_computation.2 | async-start | bytes 4194304 | tf_op jit(solution)/shard_map/all_to_all | solution.py:63
  115.5 15.4 %collective-permute-start.4 = (bf16[16,2,8,512]{3,2,1,0:T(8,128)(2,1)}, bf16[16,2,8,512]{3,2,1,0:T(8,128)(2,1)S(1)}, u32[]{:S(2)}, u32[]{:S(2)}) collective-permute-start(bf16[16,2,8,512]{3,2,1,0:T(8,128)(2,1)} %get-tuple-element.11), channel_id=1, source_target_pairs={{0,0},{1,1},{32,48},{33,49},{64,66},{65,67},{96,114},{97,115},{128... | collective-permute-start | bytes 786440 | tf_op jit(solution)/shard_map/ppermute | solution.py:103
  148.1 1.3 copy-start
  150.1 7.9 %copy-start.5 = (bf16[2,128,1024]{2,1,0:T(8,128)(2,1)S(1)}, bf16[2,128,1024]{2,1,0:T(8,128)(2,1)}, u32[]{:S(2)}) copy-start(bf16[2,128,1024]{2,1,0:T(8,128)(2,1)} %reshape.69) | copy-start | bytes 1572868
  151.5 15.7 %all-to-all-start.3 = ((bf16[32,2,2,2,1024]{4,3,1,2,0:T(2,128)(2,1)}), bf16[32,2,2,2,1024]{4,3,1,2,0:T(2,128)(2,1)S(1)}, u32[]{:S(2)}, u32[]{:S(2)}) async-start(bf16[32,2,2,2,1024]{4,3,1,2,0:T(2,128)(2,1)} %bitcast.47), calls=%async_computation.3 | async-start | bytes 1048576 | tf_op jit(solution)/shard_map/all_to_all | solution.py:63
  167.2 36.9 %all-to-all-start.4 = ((bf16[32,2,2,8,1024]{4,3,1,2,0:T(8,128)(2,1)}), bf16[32,2,2,8,1024]{4,3,1,2,0:T(8,128)(2,1)}, u32[]{:S(2)}, u32[]{:S(2)}) async-start(bf16[32,2,2,8,1024]{4,3,1,2,0:T(8,128)(2,1)} %bitcast.52), calls=%async_computation.4 | async-start | bytes 4194304 | tf_op jit(solution)/shard_map/all_to_all | solution.py:63
  174.5 24.7 %collective-permute-start.6 = (bf16[256,1024]{1,0:T(8,128)(2,1)S(1)}, bf16[256,1024]{1,0:T(8,128)(2,1)S(1)}, u32[]{:S(2)}, u32[]{:S(2)}) collective-permute-start(bf16[256,1024]{1,0:T(8,128)(2,1)S(1)} %reshape.68), channel_id=1, source_target_pairs={{0,0},{1,1},{48,32},{49,33},{66,64},{67,65},{114,96},{115,97},{132... | collective-permute-start | bytes 1572872 | tf_op jit(solution)/shard_map/ppermute | solution.py:81
  199.5 34.0 %collective-permute-start.10 = (bf16[16,2,8,512]{3,2,1,0:T(8,128)(2,1)S(1)}, bf16[16,2,8,512]{3,2,1,0:T(8,128)(2,1)S(1)}, u32[]{:S(2)}, u32[]{:S(2)}) collective-permute-start(bf16[16,2,8,512]{3,2,1,0:T(8,128)(2,1)S(1)} %bitcast.67), channel_id=1, source_target_pairs={{0,0},{1,1},{48,32},{49,33},{66,64},{67,65},{114,96},{115,97},{132... | collective-permute-start | bytes 786440 | tf_op jit(solution)/shard_map/ppermute | solution.py:115
  204.1 1.8 copy-start.4
  205.9 1.0 copy-start.2
  207.8 25.6 %collective-permute-start.9 = (bf16[16,2,8,512]{3,2,1,0:T(8,128)(2,1)S(1)}, bf16[16,2,8,512]{3,2,1,0:T(8,128)(2,1)S(1)}, u32[]{:S(2)}, u32[]{:S(2)}) collective-permute-start(bf16[16,2,8,512]{3,2,1,0:T(8,128)(2,1)S(1)} %bitcast.68), channel_id=1, source_target_pairs={{0,0},{1,1},{48,32},{49,33},{66,64},{67,65},{114,96},{115,97},{132... | collective-permute-start | bytes 786440 | tf_op jit(solution)/shard_map/ppermute | solution.py:114
  213.9 66.0 %collective-permute-start.7 = (bf16[256,1024]{1,0:T(8,128)(2,1)S(1)}, bf16[256,1024]{1,0:T(8,128)(2,1)S(1)}, u32[]{:S(2)}, u32[]{:S(2)}) collective-permute-start(bf16[256,1024]{1,0:T(8,128)(2,1)S(1)} %collective-permute-done.6), channel_id=1, source_target_pairs={{0,0},{1,1},{32,32},{33,33},{64,64},{65,65},{96,96},{97,97},{128,1... | collective-permute-start | bytes 1572872 | tf_op jit(solution)/shard_map/ppermute | solution.py:85
  225.3 54.6 %collective-permute-start.8 = (bf16[256,1024]{1,0:T(8,128)(2,1)S(1)}, bf16[256,1024]{1,0:T(8,128)(2,1)S(1)}, u32[]{:S(2)}, u32[]{:S(2)}) collective-permute-start(bf16[256,1024]{1,0:T(8,128)(2,1)S(1)} %bitcast.66), channel_id=1, source_target_pairs={{0,0},{1,1},{48,32},{49,33},{66,64},{67,65},{114,96},{115,97},{132... | collective-permute-start | bytes 1572872 | tf_op jit(solution)/shard_map/ppermute | solution.py:89
  234.3 58.0 %all-to-all-start.5 = ((bf16[16,4,8,512]{3,2,1,0:T(8,128)(2,1)}), bf16[16,4,8,512]{3,2,1,0:T(8,128)(2,1)S(1)}, u32[]{:S(2)}, u32[]{:S(2)}) async-start(bf16[16,4,8,512]{3,2,1,0:T(8,128)(2,1)} %pad_maximum_fusion), calls=%async_computation.5 | async-start | bytes 1048576 | tf_op jit(solution)/shard_map/all_to_all | solution.py:117
